TPU v7x, 32 devices: a whole 2x2x4 slice. The times are simulated.
32 devices in a mesh: groups: 2 (over y), leaf: 4 (over z), sub: 2 (over x), vec: 2 (over core).
Axes of the slice: x: 2, y: 2, z: 4, core: 2. Of those that a mesh axis runs over, the one named last changes fastest.
Arguments:
- points: float32 [6, 262144], P('groups', ('leaf', 'sub')), parts along dimension 0, may hold values from 0 to 1
- inv_scale: float32 [6], P('groups'), parts along dimension 0, may hold values from 2 to 6
- noise: float32 [524288], P(('groups', 'leaf', 'sub')), parts along dimension 0, may hold values from 0.05 to 0.5
- vectors: bfloat16 [32, 262144], P(('groups', 'vec'), ('leaf', 'sub')), parts along dimension 0, may hold values from -6 to 6
- leaf_basis: bfloat16 [2048, 64, 256], P(('groups', 'leaf', 'sub')), parts along dimension 0, may hold values from -0.375 to 0.375
- local_transfer: bfloat16 [2032, 2, 64, 64], P(('groups', 'leaf', 'sub')), parts along dimension 0, may hold values from -0.5 to 0.5
- top_transfer: bfloat16 [8, 2, 64, 64], P('groups'), parts along dimension 0, may hold values from -0.5 to 0.5
- local_coupling: bfloat16 [4080, 3, 64, 64], P(('groups', 'leaf', 'sub')), parts along dimension 0, may hold values from -0.4375 to 0.4375
- top_coupling: bfloat16 [8, 3, 64, 64], P('groups'), parts along dimension 0, may hold values from -0.4375 to 0.4375
- local_partners: int32 [4080, 3], P(('groups', 'leaf', 'sub')), parts along dimension 0, may hold values from 0 to 1023, as said below
- top_partners: int32 [8, 3], P('groups'), parts along dimension 0, may hold values from 0 to 3, as said below
- near_offsets: int32 [2048], P(('groups', 'leaf', 'sub')), parts along dimension 0, may hold values from 0 to 511, as said below
- near_cols: int32 [8192], P(('groups', 'leaf', 'sub')), parts along dimension 0, may hold values from 0 to 1023, as said below
Outputs:
- product: float32 [32, 262144], P(('groups', 'vec'), ('leaf', 'sub')), parts along dimension 0
There are 2 independent parts, one for each index of `groups`. A program takes and returns all parts, laid end to end along the dimension named above; each array names one. Nothing has to cross between parts.
Inputs may be any that keep to these rules, and one draw needn't show every extreme that they name: `local_partners`: row e * 255 + 2 ** k - 1 + h lists the far-field partners of node e * 2 ** k + h of level t + k (see the steps): 3 distinct nodes of that level, never the node itself, all in the node's aligned group of 2 ** 3 nodes. `top_partners`: row 2 ** m - 4 + i lists the far-field partners of node i of level m: 3 distinct nodes of that level, never the node itself, all in the node's aligned group of 2 ** 3 nodes (at level 2, the other three nodes). `near_offsets`: within each device's 128 leaves the offsets rise from 0; each leaf owns 1 to 7 consecutive blocks, some leaf of every device exactly 7, and a device's leaves own exactly 512 blocks. `near_cols`: A leaf's first block is the leaf itself; its column leaves are distinct and each lies within 128 leaves of the row leaf in tree order.
All inputs are finite; a program needn't handle non-finite values.
Results may differ from a plain program's by a relative error of at most 0.0028.
Values may be sent and summed in bfloat16 or wider, within the bound.
No kernel may reach another device: no remote copies, remote signals or barrier semaphores. Data moves between devices by JAX's collectives and lax.ppermute only.
A program may use at most 128 MiB of HBM per device.

v0:
```python
import functools
import math

import jax
import jax.numpy as jnp
from jax import lax
from jax.experimental import pallas as pl
from jax.experimental.pallas import tpu as pltpu
from jax.sharding import PartitionSpec as P

BF = jnp.bfloat16
F32 = jnp.float32
LEAF = 256
RANK = 64
SPAN = 3
PART = 8
EXPORT = 2**SPAN - 1
NEG_LOG2E = -1.0 / math.log(2.0)
ROOT3 = math.sqrt(3.0)
TINY = 1e-12
PAIR = 2
PAD = 16
CODE = 1024
VMEM = pltpu.VMEM
SMEM = pltpu.SMEM
NT = (((1,), (1,)), ((), ()))


def vspec():
    return pl.BlockSpec(memory_space=pltpu.VMEM)


def sspec():
    return pl.BlockSpec(memory_space=pltpu.SMEM)


def aspec():
    return pl.BlockSpec(memory_space=pl.ANY)


def params(mib):
    return pltpu.CompilerParams(vmem_limit_bytes=mib << 20)


def lanes(index):
    return pl.ds(pl.multiple_of(index * LEAF, LEAF), LEAF)


def coordinate_rows(raw, scale_ref):
    width = raw.shape[1]
    row = lax.broadcasted_iota(jnp.int32, (8, width), 0)
    scale = jnp.where(
        row == 0, scale_ref[0], jnp.where(row == 1, scale_ref[1], scale_ref[2])
    )
    full = jnp.concatenate([raw, jnp.zeros((5, width), F32)], axis=0)
    scaled = (full - 0.5) * (scale * ROOT3)
    scaled = jnp.where(row < 3, scaled, 0.0)
    high = scaled.astype(BF).astype(F32)
    rest = (scaled - high).astype(BF).astype(F32)
    return high + pltpu.roll(rest, 4, 0)


def norm_parts(rows):
    swapped = pltpu.roll(rows, 4, 0)
    norm = jnp.sum(rows * (rows + swapped), axis=0, keepdims=True)
    high = norm.astype(BF).astype(F32)
    rest = norm - high
    mid = rest.astype(BF).astype(F32)
    return swapped, high, mid, rest - mid


def row_features(rows):
    swapped, high, mid, low = norm_parts(rows)
    row = lax.broadcasted_iota(jnp.int32, rows.shape, 0)
    tail = jnp.where(
        row < 3,
        1.0,
        jnp.where(row == 3, high, jnp.where(row == 4, mid, jnp.where(row == 5, low, 0.0))),
    )
    return jnp.concatenate([rows, swapped, tail, jnp.zeros_like(rows)], axis=0).astype(BF)


def col_features(rows):
    _, high, mid, low = norm_parts(rows)
    row = lax.broadcasted_iota(jnp.int32, rows.shape, 0)
    tail = jnp.where(
        row == 0,
        high,
        jnp.where(row == 1, mid, jnp.where(row == 2, low, jnp.where(row < 6, 1.0, 0.0))),
    )
    both = -2.0 * rows
    return jnp.concatenate([both, both, tail, jnp.zeros_like(rows)], axis=0).T.astype(BF)


def matern(squared):
    squared = jnp.maximum(squared, TINY)
    dist = squared * lax.rsqrt(squared)
    return ((1.0 + dist) * jnp.exp2(dist * NEG_LOG2E)).astype(BF)


def pack_kernel(where_ref, scale_ref, points_ref, vec_ref, got_ref, out_ref):
    half = got_ref.shape[1]
    base = where_ref[1] * half

    def step(i, _):
        here = pl.ds(pl.multiple_of(i * 2048, 2048), 2048)
        there = pl.ds(pl.multiple_of(base + i * 2048, 2048), 2048)
        rows = coordinate_rows(points_ref[:, there], scale_ref)
        out_ref[:, here] = jnp.concatenate(
            [vec_ref[:, there].astype(F32), got_ref[:, here].astype(F32), rows], axis=0
        ).astype(BF)
        return 0

    lax.fori_loop(0, half // 2048, step, 0)


def block_loop(count, list_ref, row_ref, col_ref, val_ref, acc_ref, s0, s1, k0, k1):
    def accumulate(first, kern):
        for q in range(PAIR):
            code = list_ref[first + q]
            here = lanes(code // CODE)
            acc_ref[:, here] += jnp.dot(
                val_ref[code % CODE], kern[q], preferred_element_type=F32
            )

    def distance(first, out):
        for q in range(PAIR):
            code = list_ref[first + q]
            out[q] = jnp.dot(
                col_ref[code % CODE], row_ref[code // CODE], preferred_element_type=F32
            )

    def evaluate(squared, kern):
        for q in range(PAIR):
            kern[q] = matern(squared[q])

    k1[...] = jnp.zeros_like(k1)
    distance(0, s0)

    def step(it, _):
        first = it * 2 * PAIR
        accumulate(jnp.maximum(first - PAIR, 0), k1)
        distance(first + PAIR, s1)
        evaluate(s0, k0)
        accumulate(first, k0)
        distance(first + 2 * PAIR, s0)
        evaluate(s1, k1)
        return 0

    turns = (count + 2 * PAIR - 1) // (2 * PAIR)
    lax.fori_loop(0, turns, step, 0)
    accumulate(jnp.maximum(turns * 2 * PAIR - PAIR, 0), k1)


def load_columns(pack_ref, base, count, col_ref, val_ref):
    def step(i, _):
        for q in range(4):
            leaf = i * 4 + q
            val_ref[base + leaf] = pack_ref[0:16, lanes(leaf)]
            col_ref[base + leaf] = col_features(pack_ref[16:24, lanes(leaf)].astype(F32))
        return 0

    lax.fori_loop(0, count // 4, step, 0)


def near_local_kernel(
    where_ref, scale_ref, offs_ref, cols_ref, points_ref, pack_ref,
    acc_ref, row_ref, far_list, far_count,
    col_ref, val_ref, s0, s1, k0, k1, own_list,
):
    device, half_id = where_ref[0], where_ref[1]
    leaves = offs_ref.shape[0]
    half = leaves // 2
    slots = cols_ref.shape[0]
    each = slots // leaves

    def rows_step(i, carry):
        row, own, far = carry
        for q in range(2):
            leaf = i * 2 + q
            row_ref[leaf] = row_features(coordinate_rows(points_ref[:, lanes(leaf)], scale_ref))
            acc_ref[:, lanes(leaf)] = jnp.zeros((16, LEAF), F32)
            for w in range(each):
                slot = leaf * each + w
                nxt = jnp.minimum(row + 1, leaves - 1)
                row = jnp.where((nxt > row) & (offs_ref[nxt] <= slot), nxt, row)
                col = cols_ref[slot] - device * leaves + leaves
                seg = col // leaves
                inner = col % leaves
                mine = inner // half == half_id
                local = mine & (seg == 1)
                apart = mine & (seg != 1)
                own_list[own] = row * CODE + inner % half
                far_list[far] = row * CODE + (seg // 2) * half + inner % half
                own = own + local.astype(jnp.int32)
                far = far + apart.astype(jnp.int32)
        return row, own, far

    zero = jnp.int32(0)
    _, own, far = lax.fori_loop(0, leaves // 2, rows_step, (zero, zero, zero))
    for q in range(PAD):
        own_list[own + q] = half
        far_list[far + q] = leaves
    far_count[0] = far
    load_columns(pack_ref, 0, half, col_ref, val_ref)
    val_ref[half] = jnp.zeros((16, LEAF), BF)
    col_ref[half] = jnp.zeros(col_ref.shape[1:], BF)
    block_loop(own, own_list, row_ref, col_ref, val_ref, acc_ref, s0, s1, k0, k1)


def near_halo_kernel(
    far_list, far_count, row_ref, left_ref, right_ref, start_ref,
    mine_ref, other_ref,
    acc_ref, col_ref, val_ref, s0, s1, k0, k1,
):
    half = left_ref.shape[1] // LEAF
    acc_ref[...] = start_ref[...]
    load_columns(left_ref, 0, half, col_ref, val_ref)
    load_columns(right_ref, half, half, col_ref, val_ref)
    val_ref[2 * half] = jnp.zeros((16, LEAF), BF)
    col_ref[2 * half] = jnp.zeros(col_ref.shape[1:], BF)
    block_loop(far_count[0], far_list, row_ref, col_ref, val_ref, acc_ref, s0, s1, k0, k1)
    mine_ref[...] = acc_ref[0:8]
    other_ref[...] = acc_ref[8:16]


def split_parts(value):
    high = value.astype(BF).astype(F32)
    return jnp.concatenate([high, value - high], axis=0).astype(BF)


def join_parts(value):
    return value[0:8] + value[8:16]


def mul_nt(left, right):
    return lax.dot_general(left, right, NT, preferred_element_type=F32)


def over_nodes(count, unroll, work):
    group = min(unroll, count)
    if count == group:
        work([jnp.int32(i) for i in range(count)])
        return

    def step(i, _):
        work([i * group + q for q in range(group)])
        return 0

    lax.fori_loop(0, count // group, step, 0)


def up_kernel(vec_ref, basis_hbm, transfer_hbm, coef_ref, export_ref, basis, transfer, sems):
    leaves = basis.shape[0]
    levels = leaves.bit_length() - 1
    chunks = 4
    per = leaves // chunks
    copies = [
        pltpu.make_async_copy(
            basis_hbm.at[pl.ds(c * per, per)], basis.at[pl.ds(c * per, per)], sems.at[c]
        )
        for c in range(chunks)
    ]
    last = pltpu.make_async_copy(transfer_hbm, transfer, sems.at[chunks])
    for copy in copies:
        copy.start()
    last.start()
    for c in range(chunks):
        copies[c].wait()

        def work(nodes, c=c):
            outs = [
                mul_nt(vec_ref[:, lanes(c * per + n)], basis[c * per + n]) for n in nodes
            ]
            for n, out in zip(nodes, outs):
                coef_ref[leaves - 1 + c * per + n] = split_parts(out)

        over_nodes(per, 8, work)
    last.wait()
    for depth in range(levels - 1, -1, -1):
        first = 2**depth - 1

        def work(nodes, first=first):
            outs = []
            for i in nodes:
                node = first + i
                outs.append(
                    mul_nt(coef_ref[2 * node + 1], transfer[node, 0])
                    + mul_nt(coef_ref[2 * node + 2], transfer[node, 1])
                )
            for i, out in zip(nodes, outs):
                coef_ref[first + i] = split_parts(join_parts(out))

        over_nodes(2**depth, 8, work)
    export_ref[...] = coef_ref[0:EXPORT]


def down_kernel(
    dev_levels, where_ref, partners_ref, top_partners_ref, coef_ref, gather_ref, top_e, top_b,
    coupling_hbm, transfer_hbm, out_ref, coupling, transfer, local, down, tree, sems,
):
    device = where_ref[0]
    total = coupling.shape[0]
    leaves = (total + 1) // 2
    levels = leaves.bit_length() - 1
    copy_b0 = pltpu.make_async_copy(
        coupling_hbm.at[pl.ds(0, leaves - 1)], coupling.at[pl.ds(0, leaves - 1)], sems.at[0]
    )
    copy_b1 = pltpu.make_async_copy(
        coupling_hbm.at[pl.ds(leaves - 1, leaves)],
        coupling.at[pl.ds(leaves - 1, leaves)],
        sems.at[1],
    )
    copy_e = pltpu.make_async_copy(transfer_hbm, transfer, sems.at[2])
    copy_b0.start()
    copy_b1.start()
    copy_e.start()

    for level in range(dev_levels - 1, 1, -1):

        def work(nodes, level=level):
            outs = []
            for i in nodes:
                row = 2**level - 4 + i
                if level == dev_levels - 1:
                    kids = [gather_ref[2 * i, 0], gather_ref[2 * i + 1, 0]]
                else:
                    kids = [tree[2 ** (level + 1) + 2 * i + c] for c in range(2)]
                outs.append(mul_nt(kids[0], top_e[row, 0]) + mul_nt(kids[1], top_e[row, 1]))
            for i, out in zip(nodes, outs):
                tree[2**level + i] = split_parts(join_parts(out))

        over_nodes(2**level, 8, work)
    pushed = jnp.zeros((PART, RANK), F32)
    for level in range(2, dev_levels):
        node = device >> (dev_levels - level)
        row = 2**level - 4 + node
        side = device >> (dev_levels - level - 1) & 1
        parts = sum(
            mul_nt(tree[2**level + top_partners_ref[row, f]], top_b[row, f]) for f in range(3)
        )
        here = split_parts(join_parts(parts) + pushed)
        pushed = join_parts(jnp.dot(here, top_e[row, side], preferred_element_type=F32))

    copy_b0.wait()
    for depth in range(levels + 1):
        first = 2**depth - 1
        if depth == levels:
            copy_b1.wait()

        def work(nodes, depth=depth, first=first):
            outs = []
            for i in nodes:
                node = first + i
                part = None
                for f in range(3):
                    mate = partners_ref[node, f]
                    if depth < SPAN:
                        picked = gather_ref[mate >> depth, first + (mate & first)]
                    else:
                        picked = coef_ref[mate - device * 2**depth + first]
                    term = mul_nt(picked, coupling[node, f])
                    part = term if part is None else part + term
                outs.append(part)
            for i, part in zip(nodes, outs):
                local[first + i] = join_parts(part)

        over_nodes(2**depth, 8, work)
    copy_e.wait()
    down[0] = split_parts(local[0] + pushed)
    for depth in range(levels):
        first = 2**depth - 1

        def work(nodes, depth=depth, first=first):
            outs = []
            for i in nodes:
                for c in range(2):
                    outs.append(
                        jnp.dot(down[first + i], transfer[first + i, c], preferred_element_type=F32)
                    )
            for j, i in enumerate(nodes):
                for c in range(2):
                    kid = 2 * (first + i) + 1 + c
                    value = local[kid] + join_parts(outs[2 * j + c])
                    if depth == levels - 1:
                        out_ref[2 * i + c] = value.astype(BF)
                    else:
                        down[kid] = split_parts(value)

        over_nodes(2**depth, 8, work)


def final_kernel(low_ref, basis_ref, noise_ref, vec_ref, mine_ref, got_ref, out_ref):
    for leaf in range(low_ref.shape[0]):
        here = slice(leaf * LEAF, (leaf + 1) * LEAF)
        far = jnp.dot(low_ref[leaf], basis_ref[leaf], preferred_element_type=F32)
        out_ref[:, here] = (
            mine_ref[:, here]
            + got_ref[:, here]
            + noise_ref[:, here] * vec_ref[:, here].astype(F32)
            + far
        )


def body(
    points, inv_scale, noise, vectors, leaf_basis, local_transfer, top_transfer,
    local_coupling, top_coupling, local_partners, top_partners, near_offsets, near_cols,
):
    subs = lax.axis_size("sub")
    count = lax.axis_size("leaf") * subs
    dev_levels = count.bit_length() - 1
    device = lax.axis_index("leaf") * subs + lax.axis_index("sub")
    core = lax.axis_index("vec")
    where = jnp.stack([device, core]).astype(jnp.int32)
    size = vectors.shape[1]
    leaves = near_offsets.shape[0]
    slots = near_cols.shape[0]
    half = size // 2
    sds = jax.ShapeDtypeStruct
    scratch_blocks = [
        VMEM((PAIR, LEAF, LEAF), F32), VMEM((PAIR, LEAF, LEAF), F32),
        VMEM((PAIR, LEAF, LEAF), BF), VMEM((PAIR, LEAF, LEAF), BF),
    ]

    send = lax.dynamic_slice(vectors, (0, (1 - core) * half), (PART, half))
    got = lax.ppermute(send, "vec", [(0, 1), (1, 0)])

    coef, export = pl.pallas_call(
        up_kernel,
        name="up",
        out_shape=(sds((2 * leaves - 1, 16, RANK), BF), sds((EXPORT, 16, RANK), BF)),
        in_specs=[vspec(), aspec(), aspec()],
        out_specs=(vspec(), vspec()),
        scratch_shapes=[
            VMEM(leaf_basis.shape, BF), VMEM(local_transfer.shape, BF),
            pltpu.SemaphoreType.DMA((5,)),
        ],
        compiler_params=params(28),
    )(vectors, leaf_basis, local_transfer)
    gathered = lax.all_gather(export, ("leaf", "sub"))

    pack = pl.pallas_call(
        pack_kernel,
        name="pack",
        out_shape=sds((24, half), BF),
        in_specs=[sspec(), sspec(), vspec(), vspec(), vspec()],
        out_specs=vspec(),
        compiler_params=params(16),
    )(where, inv_scale, points, vectors, got)
    axes = ("leaf", "sub")
    left = lax.ppermute(pack, axes, [(i, i + 1) for i in range(count - 1)])
    right = lax.ppermute(pack, axes, [(i + 1, i) for i in range(count - 1)])

    start, row_feat, far_list, far_count = pl.pallas_call(
        near_local_kernel,
        name="near_local",
        out_shape=(
            sds((16, size), F32), sds((leaves, 32, LEAF), BF),
            sds((slots + PAD,), jnp.int32), sds((1,), jnp.int32),
        ),
        in_specs=[sspec()] * 4 + [vspec()] * 2,
        out_specs=(vspec(), vspec(), sspec(), sspec()),
        scratch_shapes=[
            VMEM((leaves // 2 + 1, LEAF, 32), BF), VMEM((leaves // 2 + 1, 16, LEAF), BF),
            *scratch_blocks, SMEM((slots + PAD,), jnp.int32),
        ],
        compiler_params=params(28),
        cost_estimate=pl.CostEstimate(
            flops=190 * 2 * 256 * 256 * 48, bytes_accessed=8 << 20, transcendentals=190 * 2**17
        ),
    )(where, inv_scale, near_offsets, near_cols, points, pack)

    mine, other = pl.pallas_call(
        near_halo_kernel,
        name="near_halo",
        out_shape=(sds((PART, size), F32), sds((PART, size), F32)),
        in_specs=[sspec(), sspec()] + [vspec()] * 4,
        out_specs=(vspec(), vspec()),
        scratch_shapes=[
            VMEM((16, size), F32),
            VMEM((leaves + 1, LEAF, 32), BF), VMEM((leaves + 1, 16, LEAF), BF),
            *scratch_blocks,
        ],
        compiler_params=params(36),
        cost_estimate=pl.CostEstimate(
            flops=60 * 2 * 256 * 256 * 48, bytes_accessed=8 << 20, transcendentals=60 * 2**17
        ),
    )(far_list, far_count, row_feat, left, right, start)
    swapped = lax.ppermute(other, "vec", [(0, 1), (1, 0)])

    low = pl.pallas_call(
        functools.partial(down_kernel, dev_levels),
        name="down",
        out_shape=sds((leaves, PART, RANK), BF),
        in_specs=[sspec()] * 3 + [vspec()] * 4 + [aspec(), aspec()],
        out_specs=vspec(),
        scratch_shapes=[
            VMEM(local_coupling.shape, BF), VMEM(local_transfer.shape, BF),
            VMEM((2 * leaves - 1, PART, RANK), F32), VMEM((leaves - 1, 16, RANK), BF),
            VMEM((count, 16, RANK), BF), pltpu.SemaphoreType.DMA((3,)),
        ],
        compiler_params=params(36),
        cost_estimate=pl.CostEstimate(
            flops=1300 * 2 * 16 * 64 * 64, bytes_accessed=17 << 20, transcendentals=0
        ),
    )(
        where, local_partners, top_partners, coef, gathered, top_transfer, top_coupling,
        local_coupling, local_transfer,
    )

    per = 16
    wide = per * LEAF
    return pl.pallas_call(
        final_kernel,
        name="final",
        out_shape=sds((PART, size), F32),
        grid=(leaves // per,),
        in_specs=[
            pl.BlockSpec((per, PART, RANK), lambda i: (i, 0, 0)),
            pl.BlockSpec((per, RANK, LEAF), lambda i: (i, 0, 0)),
            pl.BlockSpec((1, wide), lambda i: (0, i)),
            pl.BlockSpec((PART, wide), lambda i: (0, i)),
            pl.BlockSpec((PART, wide), lambda i: (0, i)),
            pl.BlockSpec((PART, wide), lambda i: (0, i)),
        ],
        out_specs=pl.BlockSpec((PART, wide), lambda i: (0, i)),
        compiler_params=params(24),
    )(low, leaf_basis, noise.reshape(1, size), vectors, mine, swapped)


def solution(mesh):
    return jax.shard_map(
        body,
        mesh=mesh,
        in_specs=(
            P("groups", ("leaf", "sub")),
            P("groups"),
            P(("groups", "leaf", "sub")),
            P(("groups", "vec"), ("leaf", "sub")),
            P(("groups", "leaf", "sub"), None, None),
            P(("groups", "leaf", "sub"), None, None, None),
            P("groups", None, None, None),
            P(("groups", "leaf", "sub"), None, None, None),
            P("groups", None, None, None),
            P(("groups", "leaf", "sub"), None),
            P("groups", None),
            P(("groups", "leaf", "sub")),
            P(("groups", "leaf", "sub")),
        ),
        out_specs=P(("groups", "vec"), ("leaf", "sub")),
        check_vma=False,
    )
```

profile of v0, /device:TPU:0, one launch (start us, length us, event | category | flops | bytes accessed | tf_op | source)
XLA Modules:
  0.0 165.0 jit_solution(11135511494987642107)
XLA Ops:
  0.0 1.0 constant_dynamic-slice_fusion
  1.0 0.5 collective-permute-start
  1.6 1.1 collective-permute-done.got_ref
  2.7 1.0 copy-done.5
  3.7 1.0 copy-done.7
  4.7 0.7 copy-done.13
  5.4 0.9 pack.1.pack_ref
  6.3 4.8 %collective-permute-start.1 = (bf16[24,16384]{1,0:T(8,128)(2,1)S(1)}, bf16[24,16384]{1,0:T(8,128)(2,1)S(1)}, u32[]{:S(2)}, u32[]{:S(2)}) collective-permute-start(bf16[24,16384]{1,0:T(8,128)(2,1)S(1)} %pack.1.pack_ref), channel_id=1, source_target_pairs={{0,2},{2,4},{4,6},{6,8},{8,10},{10,12},{12,14},{1,3},{3,5},{5,7},{... | collective-permute-start | bytes 2359304 | tf_op jit(solution)/shard_map/ppermute | solution.py:451
  11.1 1.3 collective-permute-start.2
  12.4 1.0 copy-done.8
  13.4 0.7 copy-done.14
  14.1 0.7 copy-done.15
  14.8 0.7 copy-done.16
  15.4 42.6 %near_local.1 = (f32[16,32768]{1,0:T(8,128)S(1)}, bf16[128,32,256]{2,1,0:T(8,128)(2,1)S(1)}, s32[528]{0:T(1024)S(1)}, s32[1]{0:T(128)}) custom-call(s32[2]{0:T(128)S(1)} %pad_add_fusion.where_ref, f32[3]{0:T(128)S(1)} %copy-done.14, s32[128]{0:T(128)S(1)} %copy-done.16, s32[512]{0:T(512)S(1)} %copy-done.15, f32[3,32768]{1,0:T(4,128)S(1)} %copy-done.8, ...), custom_call_target="tpu_custom_call" | custom-call | flops 1195376640 | bytes 8388608 | tf_op jit(solution)/shard_map/near_local/pallas_call | solution.py:454
  58.0 9.7 %near_halo.1 = (f32[8,32768]{1,0:T(8,128)S(1)}, f32[8,32768]{1,0:T(8,128)}) custom-call(s32[528]{0:T(1024)S(1)} %get-tuple-element.15.far_list, s32[1]{0:T(128)} %get-tuple-element.16.far_count, bf16[128,32,256]{2,1,0:T(8,128)(2,1)S(1)} %get-tuple-element.17.row_ref, bf16[24,16384]{1,0:T(8,128)(2,1)S(1)} %collective-permute-done.1.left_ref, ...), custom_call_target="tpu_custom_call" | custom-call | flops 377487360 | bytes 8388608 | tf_op jit(solution)/shard_map/near_halo/pallas_call | solution.py:473
  67.9 8.0 %copy.18.transfer_hbm = bf16[127,2,64,64]{3,2,1,0:T(8,128)(2,1)} copy(bf16[127,2,64,64]{0,3,2,1:T(8,128)(2,1)} %param.18) | data formatting | bytes 4161536 | tf_op args[5]
  75.9 15.8 %copy.20.coupling_hbm = bf16[255,3,64,64]{3,2,1,0:T(8,128)(2,1)} copy(bf16[255,3,64,64]{0,3,2,1:T(8,128)(2,1)} %param.20) | data formatting | bytes 12533760 | tf_op args[7]
  91.7 2.2 %copy-done.1 = bf16[127,2,64,64]{3,2,1,0:T(8,128)(2,1)S(1)} copy-done((bf16[127,2,64,64]{3,2,1,0:T(8,128)(2,1)S(1)}, bf16[127,2,64,64]{3,2,1,0:T(8,128)(2,1)}, u32[]{:S(2)}) %copy-start.1) | copy-done | bytes 2080792
  93.9 2.2 %copy-done.3 = bf16[128,64,256]{2,1,0:T(8,128)(2,1)S(1)} copy-done((bf16[128,64,256]{2,1,0:T(8,128)(2,1)S(1)}, bf16[128,64,256]{2,1,0:T(8,128)(2,1)}, u32[]{:S(2)}) %copy-start.3) | copy-done | bytes 4194328
  96.1 8.2 %up.1 = (bf16[255,16,64]{2,1,0:T(8,128)(2,1)S(1)}, bf16[7,16,64]{2,1,0:T(8,128)(2,1)S(1)}) custom-call(bf16[8,32768]{1,0:T(8,128)(2,1)S(1)} %copy-done.6, bf16[128,64,256]{2,1,0:T(8,128)(2,1)S(1)} %copy-done.3, bf16[127,2,64,64]{3,2,1,0:T(8,128)(2,1)S(1)} %copy-done.1), custom_call_target="tpu_custom_call" | custom-call | tf_op jit(solution)/shard_map/up/pallas_call | solution.py:428
  104.3 31.8 %all-gather = bf16[56,16,64]{2,1,0:T(8,128)(2,1)S(1)} all-gather(bf16[7,16,64]{2,1,0:T(8,128)(2,1)S(1)} %get-tuple-element.14), channel_id=2, replica_groups=mesh['groups'=2,'leaf'=4,'sub'=2,'vec'=2] {'leaf','sub'}, dimensions={0}, use_global_device_ids=true | all-gather | bytes 129024 | tf_op jit(solution)/shard_map/all_gather | solution.py:440
  136.1 4.6 %copy-done = bf16[255,3,64,64]{3,2,1,0:T(8,128)(2,1)S(1)} copy-done((bf16[255,3,64,64]{3,2,1,0:T(8,128)(2,1)S(1)}, bf16[255,3,64,64]{3,2,1,0:T(8,128)(2,1)}, u32[]{:S(2)}) %copy-start) | copy-done | bytes 6266904
  140.7 18.4 %down.1.low_ref = bf16[128,8,64]{2,1,0:T(8,128)(2,1)S(1)} custom-call(s32[2]{0:T(128)S(1)} %pad_add_fusion.where_ref, s32[255,3]{1,0:T(8,128)S(1)} %copy.19.partners_ref, s32[4,3]{1,0:T(4,128)S(1)} %copy-done.12, bf16[255,16,64]{2,1,0:T(8,128)(2,1)S(1)} %get-tuple-element.13.coef_ref, bf16[8,7,16,64]{3,2,1,0:T(8,128)(2,1)S(1)} %bitcast.4, ...), custom_call_target="tpu_custom_call" | custom-call | flops 170393600 | bytes 17825792 | tf_op jit(solution)/shard_map/down/pallas_call | solution.py:491
  159.1 5.9 %final.1 = f32[8,32768]{1,0:T(8,128)} custom-call(bf16[128,8,64]{2,1,0:T(8,128)(2,1)S(1)} %down.1.low_ref, bf16[128,64,256]{2,1,0:T(8,128)(2,1)S(1)} %copy-done.4, f32[1,32768]{1,0:T(1,128)S(1)} %bitcast.5, bf16[8,32768]{1,0:T(8,128)(2,1)S(1)} %copy-done.6, f32[8,32768]{1,0:T(8,128)S(1)} %get-tuple-element.19.mine_ref, f32[8,32768]{1,0:T(8,128)} %collective-permute-done.3.got_ref), custom_call_target="tpu_custom_call" | custom-call | tf_op jit(solution)/shard_map/final/pallas_call | solution.py:513
  (32 shorter events, 0.3 us)
Async XLA Ops:
  1.0 1.7 %collective-permute-start = (bf16[8,16384]{1,0:T(8,128)(2,1)S(1)}, bf16[8,16384]{1,0:T(8,128)(2,1)S(1)}, u32[]{:S(2)}, u32[]{:S(2)}) collective-permute-start(bf16[8,16384]{1,0:T(8,128)(2,1)S(1)} %constant_dynamic-slice_fusion), channel_id=1, source_target_pairs={{0,1},{1,0},{2,3},{3,2},{4,5},{5,4},{6,7},{7,6},{8,9},{9,8},{10,11... | collective-permute-start | bytes 786440 | tf_op jit(solution)/shard_map/ppermute | solution.py:426
  2.7 1.0 copy-start.5
  3.7 1.0 copy-start.7
  4.7 0.7 copy-start.13
  6.3 51.7 %collective-permute-start.1 = (bf16[24,16384]{1,0:T(8,128)(2,1)S(1)}, bf16[24,16384]{1,0:T(8,128)(2,1)S(1)}, u32[]{:S(2)}, u32[]{:S(2)}) collective-permute-start(bf16[24,16384]{1,0:T(8,128)(2,1)S(1)} %pack.1.pack_ref), channel_id=1, source_target_pairs={{0,2},{2,4},{4,6},{6,8},{8,10},{10,12},{12,14},{1,3},{3,5},{5,7},{... | collective-permute-start | bytes 2359304 | tf_op jit(solution)/shard_map/ppermute | solution.py:451
  11.1 46.9 %collective-permute-start.2 = (bf16[24,16384]{1,0:T(8,128)(2,1)S(1)}, bf16[24,16384]{1,0:T(8,128)(2,1)S(1)}, u32[]{:S(2)}, u32[]{:S(2)}) collective-permute-start(bf16[24,16384]{1,0:T(8,128)(2,1)S(1)} %pack.1.pack_ref), channel_id=1, source_target_pairs={{2,0},{4,2},{6,4},{8,6},{10,8},{12,10},{14,12},{3,1},{5,3},{7,5},{... | collective-permute-start | bytes 2359304 | tf_op jit(solution)/shard_map/ppermute | solution.py:452
  12.4 1.0 copy-start.8
  13.4 0.7 copy-start.14
  14.1 0.7 copy-start.15
  14.8 0.7 copy-start.16
  58.0 9.7 %copy-start.17 = (s32[255,3]{0,1:T(4,128)S(1)}, s32[255,3]{0,1:T(4,128)}, u32[]{:S(2)}) copy-start(s32[255,3]{0,1:T(4,128)} %param.22) | copy-start | bytes 9184
  67.7 91.4 %collective-permute-start.3 = (f32[8,32768]{1,0:T(8,128)}, f32[8,32768]{1,0:T(8,128)}, u32[]{:S(2)}, u32[]{:S(2)}) collective-permute-start(f32[8,32768]{1,0:T(8,128)} %get-tuple-element.20), channel_id=1, source_target_pairs={{0,1},{1,0},{2,3},{3,2},{4,5},{5,4},{6,7},{7,6},{8,9},{9,8},{10,11... | collective-permute-start | bytes 3145736 | tf_op jit(solution)/shard_map/ppermute | solution.py:489
  75.9 15.8 %copy-start.6 = (bf16[8,32768]{1,0:T(8,128)(2,1)S(1)}, bf16[8,32768]{1,0:T(8,128)(2,1)}, u32[]{:S(2)}) copy-start(bf16[8,32768]{1,0:T(8,128)(2,1)} %vec_ref.5) | copy-start | bytes 1572868
  91.7 2.2 %copy-start.1 = (bf16[127,2,64,64]{3,2,1,0:T(8,128)(2,1)S(1)}, bf16[127,2,64,64]{3,2,1,0:T(8,128)(2,1)}, u32[]{:S(2)}) copy-start(bf16[127,2,64,64]{3,2,1,0:T(8,128)(2,1)} %copy.18.transfer_hbm) | copy-start | bytes 6242308
  93.9 2.2 %copy-start.3 = (bf16[128,64,256]{2,1,0:T(8,128)(2,1)S(1)}, bf16[128,64,256]{2,1,0:T(8,128)(2,1)}, u32[]{:S(2)}) copy-start(bf16[128,64,256]{2,1,0:T(8,128)(2,1)} %basis_ref.1) | copy-start | bytes 12582916
  96.1 40.0 %copy-start.2 = (bf16[127,2,64,64]{3,2,1,0:T(8,128)(2,1)S(1)}, bf16[127,2,64,64]{3,2,1,0:T(8,128)(2,1)}, u32[]{:S(2)}) copy-start(bf16[127,2,64,64]{3,2,1,0:T(8,128)(2,1)} %copy.18.transfer_hbm) | copy-start | bytes 6242308
  96.1 40.0 %copy-start.9 = (bf16[4,3,64,64]{3,2,1,0:T(8,128)(2,1)S(1)}, bf16[4,3,64,64]{3,2,1,0:T(8,128)(2,1)}, u32[]{:S(2)}) copy-start(bf16[4,3,64,64]{3,2,1,0:T(8,128)(2,1)} %top_b.1) | copy-start | bytes 294916
  96.1 40.0 %copy-start.10 = (bf16[4,2,64,64]{3,2,1,0:T(8,128)(2,1)S(1)}, bf16[4,2,64,64]{3,2,1,0:T(8,128)(2,1)}, u32[]{:S(2)}) copy-start(bf16[4,2,64,64]{3,2,1,0:T(8,128)(2,1)} %top_e.1) | copy-start | bytes 196612
  96.1 40.0 %copy-start.12 = (s32[4,3]{1,0:T(4,128)S(1)}, s32[4,3]{1,0:T(4,128)}, u32[]{:S(2)}) copy-start(s32[4,3]{1,0:T(4,128)} %top_partners_ref.1) | copy-start | bytes 148
  136.1 4.6 %copy-start = (bf16[255,3,64,64]{3,2,1,0:T(8,128)(2,1)S(1)}, bf16[255,3,64,64]{3,2,1,0:T(8,128)(2,1)}, u32[]{:S(2)}) copy-start(bf16[255,3,64,64]{3,2,1,0:T(8,128)(2,1)} %copy.20.coupling_hbm) | copy-start | bytes 18800644
  140.7 18.5 %copy-start.4 = (bf16[128,64,256]{2,1,0:T(8,128)(2,1)S(1)}, bf16[128,64,256]{2,1,0:T(8,128)(2,1)}, u32[]{:S(2)}) copy-start(bf16[128,64,256]{2,1,0:T(8,128)(2,1)} %basis_ref.1) | copy-start | bytes 12582916
  140.7 18.5 %copy-start.11 = (f32[32768]{0:T(1024)S(1)}, f32[32768]{0:T(1024)}, u32[]{:S(2)}) copy-start(f32[32768]{0:T(1024)} %param.15) | copy-start | bytes 393220
where the time goes:
time: 166 us; the launch traced here: 165 us
  Pallas kernels  85.7 us (52%)
  local copies, waits for them, and re-layouts  39.6 us (24%)
  blocking collectives  31.8 us (19%)
  starting transfers between devices  6.63 us (4%)
    pallas_call x1, Pallas kernels, body(): pl.pallas_call(near_local_kernel, name='near_local', out_shape=(sds((16,...  42.6 us
    unnamed x39, local copies, waits for them, and re-layouts  38.6 us
    all_gather x1, blocking collectives, body(): gathered = lax.all_gather(export, ('leaf', 'sub'))  31.8 us
    pallas_call x1, Pallas kernels, body(): pl.pallas_call(functools.partial(down_kernel, dev_levels), name='down', o...  18.4 us
    pallas_call x1, Pallas kernels, body(): pl.pallas_call(near_halo_kernel, name='near_halo', out_shape=(sds((PART,...  9.72 us
    pallas_call x1, Pallas kernels, body(): pl.pallas_call(up_kernel, name='up', out_shape=(sds((2 * leaves - 1, 16,...  8.21 us
    pallas_call x1, Pallas kernels, body(): pl.pallas_call(final_kernel, name='final', out_shape=sds((PART, size), F3...  5.88 us
    ppermute x1, starting transfers between devices, body(): left = lax.ppermute(pack, axes, [(i, i + 1) for i in range(count - 1)])  4.81 us
  transfers between devices with their start and end apart: 4, of which 1 were waited for; matrix products, arithmetic and copies ran while one was open for 15% of the time, Pallas kernels for 42%

commit v1 on v0

--- a/solution.py
+++ b/solution.py
@@ -20,7 +20,8 @@
 TINY = 1e-12
 PAIR = 2
 PAD = 16
-CODE = 1024
+CODE_BITS = 10
+CODE = 2**CODE_BITS
 VMEM = pltpu.VMEM
 SMEM = pltpu.SMEM
 NT = (((1,), (1,)), ((), ()))
@@ -114,20 +115,22 @@
     lax.fori_loop(0, half // 2048, step, 0)
 
 
-def block_loop(count, list_ref, row_ref, col_ref, val_ref, acc_ref, s0, s1, k0, k1):
+def block_loop(count, place, list_ref, row_ref, col_ref, val_ref, acc_ref, s0, s1, k0, k1):
     def accumulate(first, kern):
         for q in range(PAIR):
             code = list_ref[first + q]
-            here = lanes(code // CODE)
+            here = lanes(code >> CODE_BITS)
             acc_ref[:, here] += jnp.dot(
-                val_ref[code % CODE], kern[q], preferred_element_type=F32
+                val_ref[place(code & (CODE - 1))], kern[q], preferred_element_type=F32
             )
 
     def distance(first, out):
         for q in range(PAIR):
             code = list_ref[first + q]
             out[q] = jnp.dot(
-                col_ref[code % CODE], row_ref[code // CODE], preferred_element_type=F32
+                col_ref[place(code & (CODE - 1))],
+                row_ref[code >> CODE_BITS],
+                preferred_element_type=F32,
             )
 
     def evaluate(squared, kern):
@@ -174,38 +177,38 @@
     slots = cols_ref.shape[0]
     each = slots // leaves
 
+    far_base = device * leaves - leaves + half_id * half
+    half_bits = half.bit_length() - 1
+
     def rows_step(i, carry):
-        row, own, far = carry
+        row, code, own, far = carry
         for q in range(2):
             leaf = i * 2 + q
             row_ref[leaf] = row_features(coordinate_rows(points_ref[:, lanes(leaf)], scale_ref))
             acc_ref[:, lanes(leaf)] = jnp.zeros((16, LEAF), F32)
             for w in range(each):
                 slot = leaf * each + w
-                nxt = jnp.minimum(row + 1, leaves - 1)
-                row = jnp.where((nxt > row) & (offs_ref[nxt] <= slot), nxt, row)
-                col = cols_ref[slot] - device * leaves + leaves
-                seg = col // leaves
-                inner = col % leaves
-                mine = inner // half == half_id
-                local = mine & (seg == 1)
-                apart = mine & (seg != 1)
-                own_list[own] = row * CODE + inner % half
-                far_list[far] = row * CODE + (seg // 2) * half + inner % half
-                own = own + local.astype(jnp.int32)
-                far = far + apart.astype(jnp.int32)
-        return row, own, far
+                begins = offs_ref[jnp.minimum(row + 1, leaves - 1)] == slot
+                row = jnp.where(begins, row + 1, row)
+                code = jnp.where(begins, code + CODE, code)
+                place = cols_ref[slot] - far_base
+                own_list[own] = code + (place - leaves)
+                far_list[far] = code + place
+                block = place >> half_bits
+                own = jnp.where(block == 2, own + 1, own)
+                far = jnp.where((block & 3) == 0, far + 1, far)
+        return row, code, own, far
 
     zero = jnp.int32(0)
-    _, own, far = lax.fori_loop(0, leaves // 2, rows_step, (zero, zero, zero))
+    _, _, own, far = lax.fori_loop(0, leaves // 2, rows_step, (zero, zero, zero, zero))
     for q in range(PAD):
         own_list[own + q] = half
-        far_list[far + q] = leaves
+        far_list[far + q] = 8 * half
     far_count[0] = far
     load_columns(pack_ref, 0, half, col_ref, val_ref)
     val_ref[half] = jnp.zeros((16, LEAF), BF)
     col_ref[half] = jnp.zeros(col_ref.shape[1:], BF)
-    block_loop(own, own_list, row_ref, col_ref, val_ref, acc_ref, s0, s1, k0, k1)
+    block_loop(own, lambda c: c, own_list, row_ref, col_ref, val_ref, acc_ref, s0, s1, k0, k1)
 
 
 def near_halo_kernel(
@@ -219,7 +222,12 @@
     load_columns(right_ref, half, half, col_ref, val_ref)
     val_ref[2 * half] = jnp.zeros((16, LEAF), BF)
     col_ref[2 * half] = jnp.zeros(col_ref.shape[1:], BF)
-    block_loop(far_count[0], far_list, row_ref, col_ref, val_ref, acc_ref, s0, s1, k0, k1)
+    bits = half.bit_length() - 1
+
+    def place(code):
+        return (code & (half - 1)) | ((code >> (bits + 2)) << bits)
+
+    block_loop(far_count[0], place, far_list, row_ref, col_ref, val_ref, acc_ref, s0, s1, k0, k1)
     mine_ref[...] = acc_ref[0:8]
     other_ref[...] = acc_ref[8:16]
 
@@ -250,71 +258,121 @@
     lax.fori_loop(0, count // group, step, 0)
 
 
-def up_kernel(vec_ref, basis_hbm, transfer_hbm, coef_ref, export_ref, basis, transfer, sems):
-    leaves = basis.shape[0]
+def side_by_side(first, second):
+    return jnp.concatenate([first, second], axis=1)
+
+
+def doubled(pair):
+    low = lax.broadcasted_iota(jnp.int32, pair.shape, 1) < RANK
+    turned = pltpu.roll(pair, RANK, 1)
+    return jnp.where(low, pair, turned), jnp.where(low, turned, pair)
+
+
+def up_kernel(vec_ref, basis_ref, raw_ref, coef_ref, export_ref, move_ref, flat, pairs):
+    leaves = basis_ref.shape[0]
     levels = leaves.bit_length() - 1
-    chunks = 4
-    per = leaves // chunks
-    copies = [
-        pltpu.make_async_copy(
-            basis_hbm.at[pl.ds(c * per, per)], basis.at[pl.ds(c * per, per)], sems.at[c]
-        )
-        for c in range(chunks)
-    ]
-    last = pltpu.make_async_copy(transfer_hbm, transfer, sems.at[chunks])
-    for copy in copies:
-        copy.start()
-    last.start()
-    for c in range(chunks):
-        copies[c].wait()
-
-        def work(nodes, c=c):
-            outs = [
-                mul_nt(vec_ref[:, lanes(c * per + n)], basis[c * per + n]) for n in nodes
-            ]
-            for n, out in zip(nodes, outs):
-                coef_ref[leaves - 1 + c * per + n] = split_parts(out)
-
-        over_nodes(per, 8, work)
-    last.wait()
-    for depth in range(levels - 1, -1, -1):
+    inner = raw_ref.shape[3]
+
+    def keep(parent, first, second):
+        pair = side_by_side(first, second)
+        pairs[parent] = split_parts(pair)
+        one, two = doubled(pair)
+        coef_ref[2 * parent + 1] = split_parts(one)
+        coef_ref[2 * parent + 2] = split_parts(two)
+
+    def leaf_step(it, _):
+        outs = []
+        for q in range(8):
+            leaf = it * 8 + q
+            outs.append(mul_nt(vec_ref[:, lanes(leaf)], basis_ref[leaf]))
+        for q in range(4):
+            r = it * 4 + q
+            block = jnp.concatenate([raw_ref[0, r], raw_ref[1, r]], axis=0).astype(F32)
+            flat[pl.ds(r * leaves, inner)] = block.T
+        for q in range(4):
+            keep(leaves // 2 - 1 + it * 4 + q, outs[2 * q], outs[2 * q + 1])
+        return 0
+
+    lax.fori_loop(0, leaves // 8, leaf_step, 0)
+    for depth in range(levels - 1, 0, -1):
         first = 2**depth - 1
-
-        def work(nodes, first=first):
+        above = 2 ** (depth - 1) - 1
+
+        def work(nodes, first=first, above=above):
             outs = []
-            for i in nodes:
-                node = first + i
-                outs.append(
-                    mul_nt(coef_ref[2 * node + 1], transfer[node, 0])
-                    + mul_nt(coef_ref[2 * node + 2], transfer[node, 1])
-                )
-            for i, out in zip(nodes, outs):
-                coef_ref[first + i] = split_parts(join_parts(out))
-
-        over_nodes(2**depth, 8, work)
-    export_ref[...] = coef_ref[0:EXPORT]
-
-
-def down_kernel(
-    dev_levels, where_ref, partners_ref, top_partners_ref, coef_ref, gather_ref, top_e, top_b,
-    coupling_hbm, transfer_hbm, out_ref, coupling, transfer, local, down, tree, sems,
+            for j in nodes:
+                for c in range(2):
+                    node = first + 2 * j + c
+                    move = flat[pl.ds(node, RANK, stride=leaves)].astype(BF)
+                    move_ref[node] = move
+                    outs.append(mul_nt(pairs[node], move))
+            for j, i in enumerate(nodes):
+                keep(above + i, join_parts(outs[2 * j]), join_parts(outs[2 * j + 1]))
+
+        over_nodes(2 ** (depth - 1), 8, work)
+    move = flat[pl.ds(0, RANK, stride=leaves)].astype(BF)
+    move_ref[0] = move
+    root = join_parts(mul_nt(pairs[0], move))
+    coef_ref[0] = split_parts(side_by_side(root, root))
+    export_ref[0] = coef_ref[0:EXPORT]
+
+
+def couple_kernel(
+    where_ref, partners_ref, coef_ref, raw_ref, local_ref, wide_ref, thin_ref, wide, thin
 ):
     device = where_ref[0]
-    total = coupling.shape[0]
-    leaves = (total + 1) // 2
+    total = raw_ref.shape[3]
+    span = total + 1
+    levels = span.bit_length() - 2
+    low = lax.broadcasted_iota(jnp.int32, (16, 2 * RANK), 1) < RANK
+
+    def turn(i, _):
+        for q in range(2):
+            r = i * 2 + q
+            block = jnp.concatenate([raw_ref[0, r], raw_ref[1, r]], axis=0).astype(F32)
+            wide[pl.ds(r * span, total)] = block.T
+            thin[pl.ds(r * span, total)] = raw_ref[2, r].astype(F32).T
+        return 0
+
+    lax.fori_loop(0, RANK // 2, turn, 0)
+    for node in range(EXPORT):
+        wide_ref[node] = wide[pl.ds(node, RANK, stride=span)].astype(BF)
+        thin_ref[node] = thin[pl.ds(node, RANK, stride=span)].astype(BF)
+    for depth in range(SPAN, levels + 1):
+        first = 2**depth - 1
+        above = 2 ** (depth - 1) - 1
+        shift = first - device * 2**depth
+
+        def work(nodes, first=first, above=above, shift=shift):
+            outs = []
+            for j in nodes:
+                for c in range(2):
+                    node = first + 2 * j + c
+                    mates = [coef_ref[partners_ref[node, f] + shift] for f in range(3)]
+                    left = jnp.where(low, mates[0], mates[1])
+                    outs.append(
+                        mul_nt(left, wide[pl.ds(node, RANK, stride=span)].astype(BF))
+                        + mul_nt(
+                            mates[2][:, :RANK],
+                            thin[pl.ds(node, RANK, stride=span)].astype(BF),
+                        )
+                    )
+            for j, i in enumerate(nodes):
+                local_ref[above + i] = side_by_side(
+                    join_parts(outs[2 * j]), join_parts(outs[2 * j + 1])
+                )
+
+        over_nodes(2 ** (depth - 1), 4, work)
+
+
+def down_kernel(
+    dev_levels, where_ref, partners_ref, top_partners_ref, gather_ref, tops_ref, top_e, top_b,
+    wide_ref, thin_ref, local_ref, move_ref, out_ref, down, tree,
+):
+    device = where_ref[0]
+    leaves = out_ref.shape[0]
     levels = leaves.bit_length() - 1
-    copy_b0 = pltpu.make_async_copy(
-        coupling_hbm.at[pl.ds(0, leaves - 1)], coupling.at[pl.ds(0, leaves - 1)], sems.at[0]
-    )
-    copy_b1 = pltpu.make_async_copy(
-        coupling_hbm.at[pl.ds(leaves - 1, leaves)],
-        coupling.at[pl.ds(leaves - 1, leaves)],
-        sems.at[1],
-    )
-    copy_e = pltpu.make_async_copy(transfer_hbm, transfer, sems.at[2])
-    copy_b0.start()
-    copy_b1.start()
-    copy_e.start()
+    low = lax.broadcasted_iota(jnp.int32, (16, 2 * RANK), 1) < RANK
 
     for level in range(dev_levels - 1, 1, -1):
 
@@ -323,14 +381,27 @@
             for i in nodes:
                 row = 2**level - 4 + i
                 if level == dev_levels - 1:
-                    kids = [gather_ref[2 * i, 0], gather_ref[2 * i + 1, 0]]
+                    kids = [tops_ref[(2 * i + c) ^ device, 0][:, :RANK] for c in range(2)]
                 else:
                     kids = [tree[2 ** (level + 1) + 2 * i + c] for c in range(2)]
                 outs.append(mul_nt(kids[0], top_e[row, 0]) + mul_nt(kids[1], top_e[row, 1]))
             for i, out in zip(nodes, outs):
                 tree[2**level + i] = split_parts(join_parts(out))
 
-        over_nodes(2**level, 8, work)
+        over_nodes(2**level, 4, work)
+
+    def near_root(node, depth):
+        mates = []
+        for f in range(3):
+            mate = partners_ref[node, f]
+            at = ((mate >> depth) ^ device) & (2**SPAN - 1)
+            mates.append(gather_ref[at, 2**depth - 1 + (mate & (2**depth - 1))])
+        left = jnp.where(low, mates[0], mates[1])
+        return join_parts(
+            mul_nt(left, wide_ref[node]) + mul_nt(mates[2][:, :RANK], thin_ref[node])
+        )
+
+    shallow = [near_root(node, (node + 1).bit_length() - 1) for node in range(EXPORT)]
     pushed = jnp.zeros((PART, RANK), F32)
     for level in range(2, dev_levels):
         node = device >> (dev_levels - level)
@@ -342,52 +413,34 @@
         here = split_parts(join_parts(parts) + pushed)
         pushed = join_parts(jnp.dot(here, top_e[row, side], preferred_element_type=F32))
 
-    copy_b0.wait()
-    for depth in range(levels + 1):
-        first = 2**depth - 1
-        if depth == levels:
-            copy_b1.wait()
-
-        def work(nodes, depth=depth, first=first):
-            outs = []
-            for i in nodes:
-                node = first + i
-                part = None
-                for f in range(3):
-                    mate = partners_ref[node, f]
-                    if depth < SPAN:
-                        picked = gather_ref[mate >> depth, first + (mate & first)]
-                    else:
-                        picked = coef_ref[mate - device * 2**depth + first]
-                    term = mul_nt(picked, coupling[node, f])
-                    part = term if part is None else part + term
-                outs.append(part)
-            for i, part in zip(nodes, outs):
-                local[first + i] = join_parts(part)
-
-        over_nodes(2**depth, 8, work)
-    copy_e.wait()
-    down[0] = split_parts(local[0] + pushed)
+    down[0] = split_parts(shallow[0] + pushed)
     for depth in range(levels):
         first = 2**depth - 1
 
         def work(nodes, depth=depth, first=first):
-            outs = []
-            for i in nodes:
-                for c in range(2):
-                    outs.append(
-                        jnp.dot(down[first + i], transfer[first + i, c], preferred_element_type=F32)
-                    )
-            for j, i in enumerate(nodes):
-                for c in range(2):
-                    kid = 2 * (first + i) + 1 + c
-                    value = local[kid] + join_parts(outs[2 * j + c])
-                    if depth == levels - 1:
-                        out_ref[2 * i + c] = value.astype(BF)
-                    else:
-                        down[kid] = split_parts(value)
-
-        over_nodes(2**depth, 8, work)
+            outs = [
+                jnp.dot(down[first + i], move_ref[first + i], preferred_element_type=F32)
+                for i in nodes
+            ]
+            for i, out in zip(nodes, outs):
+                node = first + i
+                if depth < SPAN - 1:
+                    base = side_by_side(shallow[2 * node + 1], shallow[2 * node + 2])
+                else:
+                    base = local_ref[node]
+                pair = base + join_parts(out)
+                if depth == levels - 1:
+                    out_ref[2 * i] = pair[:, :RANK].astype(BF)
+                    out_ref[2 * i + 1] = pair[:, RANK:].astype(BF)
+                else:
+                    down[2 * node + 1] = split_parts(pair[:, :RANK])
+                    down[2 * node + 2] = split_parts(pair[:, RANK:])
+
+        if depth < SPAN:
+            first_nodes = list(range(2**depth))
+            work(first_nodes)
+        else:
+            over_nodes(2**depth, 8, work)
 
 
 def final_kernel(low_ref, basis_ref, noise_ref, vec_ref, mine_ref, got_ref, out_ref):
@@ -400,6 +453,13 @@
             + noise_ref[:, here] * vec_ref[:, here].astype(F32)
             + far
         )
+
+
+def swap_bit(value, bit):
+    sub_bits = lax.axis_size("sub").bit_length() - 1
+    axis, apart = ("sub", 2**bit) if bit < sub_bits else ("leaf", 2 ** (bit - sub_bits))
+    pairs = [(i, i ^ apart) for i in range(lax.axis_size(axis))]
+    return lax.ppermute(value, axis, pairs)
 
 
 def body(
@@ -425,19 +485,30 @@
     send = lax.dynamic_slice(vectors, (0, (1 - core) * half), (PART, half))
     got = lax.ppermute(send, "vec", [(0, 1), (1, 0)])
 
-    coef, export = pl.pallas_call(
+    coef, export, moves = pl.pallas_call(
         up_kernel,
         name="up",
-        out_shape=(sds((2 * leaves - 1, 16, RANK), BF), sds((EXPORT, 16, RANK), BF)),
-        in_specs=[vspec(), aspec(), aspec()],
-        out_specs=(vspec(), vspec()),
+        out_shape=(
+            sds((2 * leaves - 1, 16, 2 * RANK), BF), sds((1, EXPORT, 16, 2 * RANK), BF),
+            sds((leaves - 1, RANK, 2 * RANK), BF),
+        ),
+        in_specs=[vspec()] * 3,
+        out_specs=(vspec(),) * 3,
         scratch_shapes=[
-            VMEM(leaf_basis.shape, BF), VMEM(local_transfer.shape, BF),
-            pltpu.SemaphoreType.DMA((5,)),
+            VMEM((RANK * leaves, 2 * RANK), F32), VMEM((leaves - 1, 16, 2 * RANK), BF),
         ],
         compiler_params=params(28),
-    )(vectors, leaf_basis, local_transfer)
-    gathered = lax.all_gather(export, ("leaf", "sub"))
+        cost_estimate=pl.CostEstimate(
+            flops=300 * 2 * 256 * 256 * 48, bytes_accessed=8 << 20, transcendentals=0
+        ),
+    )(vectors, leaf_basis, jnp.transpose(local_transfer, (1, 2, 3, 0)))
+    gathered = export
+    for bit in range(SPAN):
+        gathered = jnp.concatenate([gathered, swap_bit(gathered, bit)], axis=0)
+    tops = gathered
+    for bit in range(SPAN, dev_levels):
+        tops = tops[:, 0:1]
+        tops = jnp.concatenate([tops, swap_bit(tops, bit)], axis=0)
 
     pack = pl.pallas_call(
         pack_kernel,
@@ -451,6 +522,7 @@
     left = lax.ppermute(pack, axes, [(i, i + 1) for i in range(count - 1)])
     right = lax.ppermute(pack, axes, [(i + 1, i) for i in range(count - 1)])
 
+    pack, _ = lax.optimization_barrier((pack, export))
     start, row_feat, far_list, far_count = pl.pallas_call(
         near_local_kernel,
         name="near_local",
@@ -488,24 +560,39 @@
     )(far_list, far_count, row_feat, left, right, start)
     swapped = lax.ppermute(other, "vec", [(0, 1), (1, 0)])
 
+    _, coef_late = lax.optimization_barrier((mine, coef))
+    local, wide, thin = pl.pallas_call(
+        couple_kernel,
+        name="couple",
+        out_shape=(
+            sds((leaves - 1, PART, 2 * RANK), F32), sds((EXPORT, RANK, 2 * RANK), BF),
+            sds((EXPORT, RANK, RANK), BF),
+        ),
+        in_specs=[sspec()] * 2 + [vspec()] * 2,
+        out_specs=(vspec(),) * 3,
+        scratch_shapes=[
+            VMEM((2 * leaves * RANK, 2 * RANK), F32), VMEM((2 * leaves * RANK, RANK), F32),
+        ],
+        compiler_params=params(36),
+        cost_estimate=pl.CostEstimate(
+            flops=300 * 2 * 256 * 256 * 48, bytes_accessed=8 << 20, transcendentals=0
+        ),
+    )(where, local_partners, coef_late, jnp.transpose(local_coupling, (1, 2, 3, 0)))
+
     low = pl.pallas_call(
         functools.partial(down_kernel, dev_levels),
         name="down",
         out_shape=sds((leaves, PART, RANK), BF),
-        in_specs=[sspec()] * 3 + [vspec()] * 4 + [aspec(), aspec()],
+        in_specs=[sspec()] * 3 + [vspec()] * 8,
         out_specs=vspec(),
-        scratch_shapes=[
-            VMEM(local_coupling.shape, BF), VMEM(local_transfer.shape, BF),
-            VMEM((2 * leaves - 1, PART, RANK), F32), VMEM((leaves - 1, 16, RANK), BF),
-            VMEM((count, 16, RANK), BF), pltpu.SemaphoreType.DMA((3,)),
-        ],
-        compiler_params=params(36),
+        scratch_shapes=[VMEM((leaves - 1, 16, RANK), BF), VMEM((count, 16, RANK), BF)],
+        compiler_params=params(24),
         cost_estimate=pl.CostEstimate(
-            flops=1300 * 2 * 16 * 64 * 64, bytes_accessed=17 << 20, transcendentals=0
+            flops=100 * 2 * 256 * 256 * 48, bytes_accessed=8 << 20, transcendentals=0
         ),
     )(
-        where, local_partners, top_partners, coef, gathered, top_transfer, top_coupling,
-        local_coupling, local_transfer,
+        where, local_partners, top_partners, gathered, tops, top_transfer, top_coupling,
+        wide, thin, local, moves,
     )
 
     per = 16

time: 166 us -> 125 us (0.75)
  blocking collectives: 31.8 us -> 0 us
  local copies, waits for them, and re-layouts: 39.6 us -> 11.2 us
  starting transfers between devices: 6.63 us -> 14 us
  waiting for transfers between devices: 1.09 us -> 7.92 us
  Pallas kernels: 85.7 us -> 90.7 us
    all_gather x1 -> x0, blocking collectives: 31.8 us -> none  [body(): gathered = lax.all_gather(export, ('leaf', 'sub'))]
    unnamed x39 -> x43, local copies, waits for them, and re-layouts: 38.6 us -> 10.1 us
    pallas_call x0 -> x1, Pallas kernels: none -> 22.1 us  [body(): pl.pallas_call(couple_kernel, name='couple', out_shape=(sds((leaves - 1,...]
    pallas_call x1, Pallas kernels: 18.4 us -> 7.21 us  [body(): pl.pallas_call(functools.partial(down_kernel, dev_levels), name='down', o...]
    ppermute x0 -> x3, starting transfers between devices: none -> 7.34 us  [swap_bit(): return lax.ppermute(value, axis, pairs)]
    ppermute x0 -> x3, waiting for transfers between devices: none -> 6.83 us  [swap_bit(): return lax.ppermute(value, axis, pairs)]
    pallas_call x1, Pallas kernels: 42.6 us -> 35.8 us  [body(): pl.pallas_call(near_local_kernel, name='near_local', out_shape=(sds((16,...]
    pallas_call x1, Pallas kernels: 8.21 us -> 10.2 us  [body(): pl.pallas_call(up_kernel, name='up', out_shape=(sds((2 * leaves - 1, 16,...]
  transfers between devices with their start and end apart: 4 -> 7, of which waited for: 1 -> 4; matrix products, arithmetic and copies ran while one was open for 15% -> 0% of each run, Pallas kernels for 42% -> 61%
where the time goes in v1:
time: 125 us; the launch traced here: 124 us
  Pallas kernels  90.7 us (73%)
  starting transfers between devices  14 us (11%)
  local copies, waits for them, and re-layouts  11.2 us (9%)
  waiting for transfers between devices  7.92 us (6%)
    pallas_call x1, Pallas kernels, body(): pl.pallas_call(near_local_kernel, name='near_local', out_shape=(sds((16,...  35.8 us
    pallas_call x1, Pallas kernels, body(): pl.pallas_call(couple_kernel, name='couple', out_shape=(sds((leaves - 1,...  22.1 us
    pallas_call x1, Pallas kernels, body(): pl.pallas_call(up_kernel, name='up', out_shape=(sds((2 * leaves - 1, 16,...  10.2 us
    unnamed x43, local copies, waits for them, and re-layouts  10.1 us
    pallas_call x1, Pallas kernels, body(): pl.pallas_call(near_halo_kernel, name='near_halo', out_shape=(sds((PART,...  8.59 us
    ppermute x3, starting transfers between devices, swap_bit(): return lax.ppermute(value, axis, pairs)  7.34 us
    pallas_call x1, Pallas kernels, body(): pl.pallas_call(functools.partial(down_kernel, dev_levels), name='down', o...  7.21 us
    ppermute x3, waiting for transfers between devices, swap_bit(): return lax.ppermute(value, axis, pairs)  6.83 us
  transfers between devices with their start and end apart: 7, of which 4 were waited for; matrix products, arithmetic and copies ran while one was open for 0% of the time, Pallas kernels for 61%

profile of v1, /device:TPU:0, one launch (start us, length us, event | category | flops | bytes accessed | tf_op | source)
XLA Modules:
  0.0 124.1 jit_solution(12667516642818162765)
XLA Ops:
  0.0 1.0 constant_dynamic-slice_fusion
  1.6 1.1 collective-permute-done.3.got_ref
  2.7 1.0 copy-done.3
  3.8 1.0 copy-done.9
  4.8 0.7 copy-done.15
  5.5 0.9 pack.1.pack_ref
  6.3 4.8 %collective-permute-start.4 = (bf16[24,16384]{1,0:T(8,128)(2,1)S(1)}, bf16[24,16384]{1,0:T(8,128)(2,1)S(1)}, u32[]{:S(2)}, u32[]{:S(2)}) collective-permute-start(bf16[24,16384]{1,0:T(8,128)(2,1)S(1)} %pack.1.pack_ref), channel_id=1, source_target_pairs={{0,2},{2,4},{4,6},{6,8},{8,10},{10,12},{12,14},{1,3},{3,5},{5,7},{... | collective-permute-start | bytes 2359304 | tf_op jit(solution)/shard_map/ppermute | solution.py:522
  11.2 1.3 %collective-permute-start.5 = (bf16[24,16384]{1,0:T(8,128)(2,1)S(1)}, bf16[24,16384]{1,0:T(8,128)(2,1)S(1)}, u32[]{:S(2)}, u32[]{:S(2)}) collective-permute-start(bf16[24,16384]{1,0:T(8,128)(2,1)S(1)} %pack.1.pack_ref), channel_id=1, source_target_pairs={{2,0},{4,2},{6,4},{8,6},{10,8},{12,10},{14,12},{3,1},{5,3},{7,5},{... | collective-permute-start | bytes 2359304 | tf_op jit(solution)/shard_map/ppermute | solution.py:523
  12.5 2.2 %copy-done.1 = bf16[128,64,256]{2,1,0:T(8,128)(2,1)S(1)} copy-done((bf16[128,64,256]{2,1,0:T(8,128)(2,1)S(1)}, bf16[128,64,256]{2,1,0:T(8,128)(2,1)}, u32[]{:S(2)}) %copy-start.1) | copy-done | bytes 4194328
  14.7 10.2 %up.1 = (bf16[255,16,128]{2,1,0:T(8,128)(2,1)S(1)}, bf16[1,7,16,128]{3,2,1,0:T(8,128)(2,1)S(1)}, bf16[127,64,128]{2,1,0:T(8,128)(2,1)S(1)}) custom-call(bf16[8,32768]{1,0:T(8,128)(2,1)S(1)} %copy-done.4, bf16[128,64,256]{2,1,0:T(8,128)(2,1)S(1)} %copy-done.1, bf16[2,64,64,127]{3,2,1,0:T(8,128)(2,1)S(1)} %bitcast.7), custom_call_target="tpu_custom_call" | custom-call | flops 1887436800 | bytes 8388608 | tf_op jit(solution)/shard_map/up/pallas_call | solution.py:488
  25.0 35.8 %near_local.1 = (f32[16,32768]{1,0:T(8,128)S(1)}, bf16[128,32,256]{2,1,0:T(8,128)(2,1)S(1)}, s32[528]{0:T(1024)S(1)}, s32[1]{0:T(128)}) custom-call(s32[2]{0:T(128)S(1)} %pad_add_fusion.where_ref, f32[3]{0:T(128)S(1)} %copy-done.16, s32[128]{0:T(128)S(1)} %copy-done.19, s32[512]{0:T(512)S(1)} %copy-done.18, f32[3,32768]{1,0:T(4,128)S(1)} %copy-done.10, ...), custom_call_target="tpu_custom_call" | custom-call | flops 1195376640 | bytes 8388608 | tf_op jit(solution)/shard_map/near_local/pallas_call | solution.py:526
  60.8 8.6 %near_halo.1 = (f32[8,32768]{1,0:T(8,128)S(1)}, f32[8,32768]{1,0:T(8,128)}) custom-call(s32[528]{0:T(1024)S(1)} %get-tuple-element.21.far_list, s32[1]{0:T(128)} %get-tuple-element.22.far_count, bf16[128,32,256]{2,1,0:T(8,128)(2,1)S(1)} %get-tuple-element.23.row_ref, bf16[24,16384]{1,0:T(8,128)(2,1)S(1)} %collective-permute-done.4.left_ref, ...), custom_call_target="tpu_custom_call" | custom-call | flops 377487360 | bytes 8388608 | tf_op jit(solution)/shard_map/near_halo/pallas_call | solution.py:545
  69.4 1.0 copy-done.5
  70.4 1.8 %collective-permute-start = (bf16[1,7,16,128]{3,2,1,0:T(8,128)(2,1)S(1)}, bf16[1,7,16,128]{3,2,1,0:T(8,128)(2,1)S(1)}, u32[]{:S(2)}, u32[]{:S(2)}) collective-permute-start(bf16[1,7,16,128]{3,2,1,0:T(8,128)(2,1)S(1)} %get-tuple-element.19), channel_id=1, source_target_pairs={{0,2},{2,0},{1,3},{3,1},{4,6},{6,4},{5,7},{7,5},{8,10},{10,8},{9,1... | collective-permute-start | bytes 86024 | tf_op jit(solution)/shard_map/ppermute | solution.py:462
  72.2 2.0 %collective-permute-done = bf16[1,7,16,128]{3,2,1,0:T(8,128)(2,1)S(1)} collective-permute-done((bf16[1,7,16,128]{3,2,1,0:T(8,128)(2,1)S(1)}, bf16[1,7,16,128]{3,2,1,0:T(8,128)(2,1)S(1)}, u32[]{:S(2)}, u32[]{:S(2)}) %collective-permute-start) | collective-permute-done | bytes 28704 | tf_op jit(solution)/shard_map/ppermute | solution.py:462
  74.3 2.4 %collective-permute-start.1 = (bf16[2,7,16,128]{3,2,1,0:T(8,128)(2,1)S(1)}, bf16[2,7,16,128]{3,2,1,0:T(8,128)(2,1)S(1)}, u32[]{:S(2)}, u32[]{:S(2)}) collective-permute-start(bf16[2,7,16,128]{3,2,1,0:T(8,128)(2,1)S(1)} %pad_maximum_fusion.2), channel_id=1, source_target_pairs={{0,4},{4,0},{8,12},{12,8},{1,5},{5,1},{9,13},{13,9},{2,6},{6,2},{1... | collective-permute-start | bytes 172040 | tf_op jit(solution)/shard_map/ppermute | solution.py:462
  76.7 2.2 %collective-permute-done.1 = bf16[2,7,16,128]{3,2,1,0:T(8,128)(2,1)S(1)} collective-permute-done((bf16[2,7,16,128]{3,2,1,0:T(8,128)(2,1)S(1)}, bf16[2,7,16,128]{3,2,1,0:T(8,128)(2,1)S(1)}, u32[]{:S(2)}, u32[]{:S(2)}) %collective-permute-start.1) | collective-permute-done | bytes 57376 | tf_op jit(solution)/shard_map/ppermute | solution.py:462
  78.9 3.1 %collective-permute-start.2 = (bf16[4,7,16,128]{3,2,1,0:T(8,128)(2,1)S(1)}, bf16[4,7,16,128]{3,2,1,0:T(8,128)(2,1)S(1)}, u32[]{:S(2)}, u32[]{:S(2)}) collective-permute-start(bf16[4,7,16,128]{3,2,1,0:T(8,128)(2,1)S(1)} %pad_maximum_fusion.1), channel_id=1, source_target_pairs={{0,8},{4,12},{8,0},{12,4},{1,9},{5,13},{9,1},{13,5},{2,10},{6,14},... | collective-permute-start | bytes 344072 | tf_op jit(solution)/shard_map/ppermute | solution.py:462
  82.1 2.6 %collective-permute-done.2 = bf16[4,7,16,128]{3,2,1,0:T(8,128)(2,1)S(1)} collective-permute-done((bf16[4,7,16,128]{3,2,1,0:T(8,128)(2,1)S(1)}, bf16[4,7,16,128]{3,2,1,0:T(8,128)(2,1)S(1)}, u32[]{:S(2)}, u32[]{:S(2)}) %collective-permute-start.2) | collective-permute-done | bytes 114720 | tf_op jit(solution)/shard_map/ppermute | solution.py:462
  84.8 2.8 %copy-done = bf16[255,3,64,64]{0,3,2,1:T(8,128)(2,1)S(1)} copy-done((bf16[255,3,64,64]{0,3,2,1:T(8,128)(2,1)S(1)}, bf16[255,3,64,64]{0,3,2,1:T(8,128)(2,1)}, u32[]{:S(2)}) %copy-start) | copy-done | bytes 6266904
  87.6 1.2 copy-done.8
  88.8 22.1 %couple.1 = (f32[127,8,128]{2,1,0:T(8,128)S(1)}, bf16[7,64,128]{2,1,0:T(8,128)(2,1)S(1)}, bf16[7,64,64]{2,1,0:T(8,128)(2,1)S(1)}) custom-call(s32[2]{0:T(128)S(1)} %pad_add_fusion.where_ref, s32[255,3]{1,0:T(8,128)S(1)} %copy.15.partners_ref, bf16[255,16,128]{2,1,0:T(8,128)(2,1)S(1)} %copy-done.8, bf16[3,64,64,255]{3,2,1,0:T(8,128)(2,1)S(1)} %bitcast.5), custom_call_target="tpu_custom_call" | custom-call | flops 1887436800 | bytes 8388608 | tf_op jit(solution)/shard_map/couple/pallas_call | solution.py:564
  111.0 7.2 %down.1.low_ref = bf16[128,8,64]{2,1,0:T(8,128)(2,1)S(1)} custom-call(s32[2]{0:T(128)S(1)} %pad_add_fusion.where_ref, s32[255,3]{1,0:T(8,128)S(1)} %copy.15.partners_ref, s32[4,3]{1,0:T(4,128)S(1)} %copy-done.14, bf16[8,7,16,128]{3,2,1,0:T(8,128)(2,1)S(1)} %pad_maximum_fusion.gather_ref.tops_ref, ...), custom_call_target="tpu_custom_call" | custom-call | flops 629145600 | bytes 8388608 | tf_op jit(solution)/shard_map/down/pallas_call | solution.py:582
  118.2 5.9 %final.1 = f32[8,32768]{1,0:T(8,128)} custom-call(bf16[128,8,64]{2,1,0:T(8,128)(2,1)S(1)} %down.1.low_ref, bf16[128,64,256]{2,1,0:T(8,128)(2,1)S(1)} %copy-done.2, f32[1,32768]{1,0:T(1,128)S(1)} %bitcast.6, bf16[8,32768]{1,0:T(8,128)(2,1)S(1)} %copy-done.4, f32[8,32768]{1,0:T(8,128)S(1)} %copy-done.6, f32[8,32768]{1,0:T(8,128)} %collective-permute-done.6.got_ref), custom_call_target="tpu_custom_call" | custom-call | tf_op jit(solution)/shard_map/final/pallas_call | solution.py:600
  (45 shorter events, 0.9 us)
Async XLA Ops:
  0.0 12.5 %copy-start.4 = (bf16[8,32768]{1,0:T(8,128)(2,1)S(1)}, bf16[8,32768]{1,0:T(8,128)(2,1)}, u32[]{:S(2)}) copy-start(bf16[8,32768]{1,0:T(8,128)(2,1)} %vec_ref.5) | copy-start | bytes 1572868
  1.0 1.7 %collective-permute-start.3 = (bf16[8,16384]{1,0:T(8,128)(2,1)S(1)}, bf16[8,16384]{1,0:T(8,128)(2,1)S(1)}, u32[]{:S(2)}, u32[]{:S(2)}) collective-permute-start(bf16[8,16384]{1,0:T(8,128)(2,1)S(1)} %constant_dynamic-slice_fusion), channel_id=1, source_target_pairs={{0,1},{1,0},{2,3},{3,2},{4,5},{5,4},{6,7},{7,6},{8,9},{9,8},{10,11... | collective-permute-start | bytes 786440 | tf_op jit(solution)/shard_map/ppermute | solution.py:486
  5.5 7.0 %copy-start.17 = (bf16[127,2,64,64]{0,3,2,1:T(8,128)(2,1)S(1)}, bf16[127,2,64,64]{0,3,2,1:T(8,128)(2,1)}, u32[]{:S(2)}) copy-start(bf16[127,2,64,64]{0,3,2,1:T(8,128)(2,1)} %param.18) | copy-start | bytes 6242308
  6.3 54.5 %collective-permute-start.4 = (bf16[24,16384]{1,0:T(8,128)(2,1)S(1)}, bf16[24,16384]{1,0:T(8,128)(2,1)S(1)}, u32[]{:S(2)}, u32[]{:S(2)}) collective-permute-start(bf16[24,16384]{1,0:T(8,128)(2,1)S(1)} %pack.1.pack_ref), channel_id=1, source_target_pairs={{0,2},{2,4},{4,6},{6,8},{8,10},{10,12},{12,14},{1,3},{3,5},{5,7},{... | collective-permute-start | bytes 2359304 | tf_op jit(solution)/shard_map/ppermute | solution.py:522
  11.2 49.7 %collective-permute-start.5 = (bf16[24,16384]{1,0:T(8,128)(2,1)S(1)}, bf16[24,16384]{1,0:T(8,128)(2,1)S(1)}, u32[]{:S(2)}, u32[]{:S(2)}) collective-permute-start(bf16[24,16384]{1,0:T(8,128)(2,1)S(1)} %pack.1.pack_ref), channel_id=1, source_target_pairs={{2,0},{4,2},{6,4},{8,6},{10,8},{12,10},{14,12},{3,1},{5,3},{7,5},{... | collective-permute-start | bytes 2359304 | tf_op jit(solution)/shard_map/ppermute | solution.py:523
  12.5 2.2 %copy-start.1 = (bf16[128,64,256]{2,1,0:T(8,128)(2,1)S(1)}, bf16[128,64,256]{2,1,0:T(8,128)(2,1)}, u32[]{:S(2)}) copy-start(bf16[128,64,256]{2,1,0:T(8,128)(2,1)} %basis_ref.3) | copy-start | bytes 12582916
  14.7 10.3 %copy-start.10 = (f32[3,32768]{1,0:T(4,128)S(1)}, f32[3,32768]{1,0:T(4,128)}, u32[]{:S(2)}) copy-start(f32[3,32768]{1,0:T(4,128)} %points_ref.3) | copy-start | bytes 1179652
  14.7 10.3 %copy-start.16 = (f32[3]{0:T(128)S(1)}, f32[3]{0:T(128)}, u32[]{:S(2)}) copy-start(f32[3]{0:T(128)} %scale_ref.3) | copy-start | bytes 40
  14.7 10.3 %copy-start.18 = (s32[512]{0:T(512)S(1)}, s32[512]{0:T(512)}, u32[]{:S(2)}) copy-start(s32[512]{0:T(512)} %cols_ref.1) | copy-start | bytes 6148
  14.7 10.3 %copy-start.19 = (s32[128]{0:T(128)S(1)}, s32[128]{0:T(128)}, u32[]{:S(2)}) copy-start(s32[128]{0:T(128)} %offs_ref.1) | copy-start | bytes 1540
  24.9 35.9 %copy-start.7 = (bf16[255,16,128]{2,1,0:T(8,128)(2,1)}, bf16[255,16,128]{2,1,0:T(8,128)(2,1)S(1)}, u32[]{:S(2)}) copy-start(bf16[255,16,128]{2,1,0:T(8,128)(2,1)S(1)} %get-tuple-element.27.coef_ref) | copy-start | bytes 3133444
  60.8 21.2 %copy-start.20 = (s32[255,3]{0,1:T(4,128)S(1)}, s32[255,3]{0,1:T(4,128)}, u32[]{:S(2)}) copy-start(s32[255,3]{0,1:T(4,128)} %param.22) | copy-start | bytes 9184
  70.4 47.8 %collective-permute-start.6 = (f32[8,32768]{1,0:T(8,128)}, f32[8,32768]{1,0:T(8,128)}, u32[]{:S(2)}, u32[]{:S(2)}) collective-permute-start(f32[8,32768]{1,0:T(8,128)} %get-tuple-element.32), channel_id=1, source_target_pairs={{0,1},{1,0},{2,3},{3,2},{4,5},{5,4},{6,7},{7,6},{8,9},{9,8},{10,11... | collective-permute-start | bytes 3145736 | tf_op jit(solution)/shard_map/ppermute | solution.py:561
  70.4 3.9 %collective-permute-start = (bf16[1,7,16,128]{3,2,1,0:T(8,128)(2,1)S(1)}, bf16[1,7,16,128]{3,2,1,0:T(8,128)(2,1)S(1)}, u32[]{:S(2)}, u32[]{:S(2)}) collective-permute-start(bf16[1,7,16,128]{3,2,1,0:T(8,128)(2,1)S(1)} %get-tuple-element.19), channel_id=1, source_target_pairs={{0,2},{2,0},{1,3},{3,1},{4,6},{6,4},{5,7},{7,5},{8,10},{10,8},{9,1... | collective-permute-start | bytes 86024 | tf_op jit(solution)/shard_map/ppermute | solution.py:462
  74.3 4.6 %collective-permute-start.1 = (bf16[2,7,16,128]{3,2,1,0:T(8,128)(2,1)S(1)}, bf16[2,7,16,128]{3,2,1,0:T(8,128)(2,1)S(1)}, u32[]{:S(2)}, u32[]{:S(2)}) collective-permute-start(bf16[2,7,16,128]{3,2,1,0:T(8,128)(2,1)S(1)} %pad_maximum_fusion.2), channel_id=1, source_target_pairs={{0,4},{4,0},{8,12},{12,8},{1,5},{5,1},{9,13},{13,9},{2,6},{6,2},{1... | collective-permute-start | bytes 172040 | tf_op jit(solution)/shard_map/ppermute | solution.py:462
  78.9 5.9 %collective-permute-start.2 = (bf16[4,7,16,128]{3,2,1,0:T(8,128)(2,1)S(1)}, bf16[4,7,16,128]{3,2,1,0:T(8,128)(2,1)S(1)}, u32[]{:S(2)}, u32[]{:S(2)}) collective-permute-start(bf16[4,7,16,128]{3,2,1,0:T(8,128)(2,1)S(1)} %pad_maximum_fusion.1), channel_id=1, source_target_pairs={{0,8},{4,12},{8,0},{12,4},{1,9},{5,13},{9,1},{13,5},{2,10},{6,14},... | collective-permute-start | bytes 344072 | tf_op jit(solution)/shard_map/ppermute | solution.py:462
  84.8 2.8 %copy-start = (bf16[255,3,64,64]{0,3,2,1:T(8,128)(2,1)S(1)}, bf16[255,3,64,64]{0,3,2,1:T(8,128)(2,1)}, u32[]{:S(2)}) copy-start(bf16[255,3,64,64]{0,3,2,1:T(8,128)(2,1)} %param.20) | copy-start | bytes 18800644
  87.6 1.2 copy-start.8
  88.8 22.2 %copy-start.11 = (bf16[4,3,64,64]{3,2,1,0:T(8,128)(2,1)S(1)}, bf16[4,3,64,64]{3,2,1,0:T(8,128)(2,1)}, u32[]{:S(2)}) copy-start(bf16[4,3,64,64]{3,2,1,0:T(8,128)(2,1)} %top_b.1) | copy-start | bytes 294916
  88.8 22.2 %copy-start.13 = (bf16[4,2,64,64]{3,2,1,0:T(8,128)(2,1)S(1)}, bf16[4,2,64,64]{3,2,1,0:T(8,128)(2,1)}, u32[]{:S(2)}) copy-start(bf16[4,2,64,64]{3,2,1,0:T(8,128)(2,1)} %top_e.1) | copy-start | bytes 196612
  88.8 22.2 %copy-start.14 = (s32[4,3]{1,0:T(4,128)S(1)}, s32[4,3]{1,0:T(4,128)}, u32[]{:S(2)}) copy-start(s32[4,3]{1,0:T(4,128)} %top_partners_ref.1) | copy-start | bytes 148
  88.8 29.4 %copy-start.2 = (bf16[128,64,256]{2,1,0:T(8,128)(2,1)S(1)}, bf16[128,64,256]{2,1,0:T(8,128)(2,1)}, u32[]{:S(2)}) copy-start(bf16[128,64,256]{2,1,0:T(8,128)(2,1)} %basis_ref.3) | copy-start | bytes 12582916
  110.9 7.3 %copy-start.6 = (f32[8,32768]{1,0:T(8,128)S(1)}, f32[8,32768]{1,0:T(8,128)}, u32[]{:S(2)}) copy-start(f32[8,32768]{1,0:T(8,128)} %copy-done.5) | copy-start | bytes 3145732
  110.9 7.3 %copy-start.12 = (f32[32768]{0:T(1024)S(1)}, f32[32768]{0:T(1024)}, u32[]{:S(2)}) copy-start(f32[32768]{0:T(1024)} %param.15) | copy-start | bytes 393220
  (4 other events, 3.7 us)

commit v2 on v1

--- a/solution.py
+++ b/solution.py
@@ -115,14 +115,16 @@
     lax.fori_loop(0, half // 2048, step, 0)
 
 
-def block_loop(count, place, list_ref, row_ref, col_ref, val_ref, acc_ref, s0, s1, k0, k1):
+def block_loop(count, place, list_ref, row_ref, col_ref, val_ref, sums, s0, s1, k0, k1):
     def accumulate(first, kern):
         for q in range(PAIR):
             code = list_ref[first + q]
             here = lanes(code >> CODE_BITS)
-            acc_ref[:, here] += jnp.dot(
+            part = jnp.dot(
                 val_ref[place(code & (CODE - 1))], kern[q], preferred_element_type=F32
             )
+            sums[0][:, here] += part[:PART]
+            sums[1][:, here] += part[PART:]
 
     def distance(first, out):
         for q in range(PAIR):
@@ -168,7 +170,7 @@
 
 def near_local_kernel(
     where_ref, scale_ref, offs_ref, cols_ref, points_ref, pack_ref,
-    acc_ref, row_ref, far_list, far_count,
+    mine_ref, other_ref, row_ref, far_list, far_count,
     col_ref, val_ref, s0, s1, k0, k1, own_list,
 ):
     device, half_id = where_ref[0], where_ref[1]
@@ -185,7 +187,8 @@
         for q in range(2):
             leaf = i * 2 + q
             row_ref[leaf] = row_features(coordinate_rows(points_ref[:, lanes(leaf)], scale_ref))
-            acc_ref[:, lanes(leaf)] = jnp.zeros((16, LEAF), F32)
+            mine_ref[:, lanes(leaf)] = jnp.zeros((PART, LEAF), F32)
+            other_ref[:, lanes(leaf)] = jnp.zeros((PART, LEAF), F32)
             for w in range(each):
                 slot = leaf * each + w
                 begins = offs_ref[jnp.minimum(row + 1, leaves - 1)] == slot
@@ -208,28 +211,40 @@
     load_columns(pack_ref, 0, half, col_ref, val_ref)
     val_ref[half] = jnp.zeros((16, LEAF), BF)
     col_ref[half] = jnp.zeros(col_ref.shape[1:], BF)
-    block_loop(own, lambda c: c, own_list, row_ref, col_ref, val_ref, acc_ref, s0, s1, k0, k1)
+    sums = (mine_ref, other_ref)
+    block_loop(own, lambda c: c, own_list, row_ref, col_ref, val_ref, sums, s0, s1, k0, k1)
 
 
 def near_halo_kernel(
-    far_list, far_count, row_ref, left_ref, right_ref, start_ref,
+    far_list, far_count, row_ref, left_ref, right_ref, mine_in, other_in,
     mine_ref, other_ref,
-    acc_ref, col_ref, val_ref, s0, s1, k0, k1,
+    col_ref, val_ref, s0, s1, k0, k1,
 ):
     half = left_ref.shape[1] // LEAF
-    acc_ref[...] = start_ref[...]
-    load_columns(left_ref, 0, half, col_ref, val_ref)
-    load_columns(right_ref, half, half, col_ref, val_ref)
+    bits = half.bit_length() - 1
+    count = far_count[0]
+
+    def place(code):
+        return (code & (half - 1)) | ((code >> (bits + 2)) << bits)
+
+    def load(i, _):
+        for q in range(4):
+            code = far_list[i * 4 + q] & (CODE - 1)
+            here = lanes(code & (half - 1))
+            after = code >= 4 * half
+            values = jnp.where(after, right_ref[0:16, here], left_ref[0:16, here])
+            rows = jnp.where(after, right_ref[16:24, here], left_ref[16:24, here])
+            val_ref[place(code)] = values
+            col_ref[place(code)] = col_features(rows.astype(F32))
+        return 0
+
+    mine_ref[...] = mine_in[...]
+    other_ref[...] = other_in[...]
+    lax.fori_loop(0, (count + 3) // 4, load, 0)
     val_ref[2 * half] = jnp.zeros((16, LEAF), BF)
     col_ref[2 * half] = jnp.zeros(col_ref.shape[1:], BF)
-    bits = half.bit_length() - 1
-
-    def place(code):
-        return (code & (half - 1)) | ((code >> (bits + 2)) << bits)
-
-    block_loop(far_count[0], place, far_list, row_ref, col_ref, val_ref, acc_ref, s0, s1, k0, k1)
-    mine_ref[...] = acc_ref[0:8]
-    other_ref[...] = acc_ref[8:16]
+    sums = (mine_ref, other_ref)
+    block_loop(count, place, far_list, row_ref, col_ref, val_ref, sums, s0, s1, k0, k1)
 
 
 def split_parts(value):
@@ -258,6 +273,20 @@
     lax.fori_loop(0, count // group, step, 0)
 
 
+def store_turned(flat, r, block):
+    turned = block.T
+    count = turned.shape[0] // 8
+    width = turned.shape[1]
+    rows = pl.ds(pl.multiple_of(r * 8, 8), 8)
+    flat[0:count, rows] = turned[: count * 8].reshape(count, 8, width)
+    rest = turned.shape[0] - count * 8
+    flat[count, pl.ds(pl.multiple_of(r * 8, 8), rest)] = turned[count * 8 :]
+
+
+def load_node(flat, node):
+    return flat[node >> 3, pl.ds(node & 7, RANK, stride=8)].astype(BF)
+
+
 def side_by_side(first, second):
     return jnp.concatenate([first, second], axis=1)
 
@@ -271,7 +300,6 @@
 def up_kernel(vec_ref, basis_ref, raw_ref, coef_ref, export_ref, move_ref, flat, pairs):
     leaves = basis_ref.shape[0]
     levels = leaves.bit_length() - 1
-    inner = raw_ref.shape[3]
 
     def keep(parent, first, second):
         pair = side_by_side(first, second)
@@ -288,7 +316,7 @@
         for q in range(4):
             r = it * 4 + q
             block = jnp.concatenate([raw_ref[0, r], raw_ref[1, r]], axis=0).astype(F32)
-            flat[pl.ds(r * leaves, inner)] = block.T
+            store_turned(flat, r, block)
         for q in range(4):
             keep(leaves // 2 - 1 + it * 4 + q, outs[2 * q], outs[2 * q + 1])
         return 0
@@ -303,14 +331,14 @@
             for j in nodes:
                 for c in range(2):
                     node = first + 2 * j + c
-                    move = flat[pl.ds(node, RANK, stride=leaves)].astype(BF)
+                    move = load_node(flat, node)
                     move_ref[node] = move
                     outs.append(mul_nt(pairs[node], move))
             for j, i in enumerate(nodes):
                 keep(above + i, join_parts(outs[2 * j]), join_parts(outs[2 * j + 1]))
 
         over_nodes(2 ** (depth - 1), 8, work)
-    move = flat[pl.ds(0, RANK, stride=leaves)].astype(BF)
+    move = load_node(flat, 0)
     move_ref[0] = move
     root = join_parts(mul_nt(pairs[0], move))
     coef_ref[0] = split_parts(side_by_side(root, root))
@@ -330,14 +358,14 @@
         for q in range(2):
             r = i * 2 + q
             block = jnp.concatenate([raw_ref[0, r], raw_ref[1, r]], axis=0).astype(F32)
-            wide[pl.ds(r * span, total)] = block.T
-            thin[pl.ds(r * span, total)] = raw_ref[2, r].astype(F32).T
+            store_turned(wide, r, block)
+            store_turned(thin, r, raw_ref[2, r].astype(F32))
         return 0
 
     lax.fori_loop(0, RANK // 2, turn, 0)
     for node in range(EXPORT):
-        wide_ref[node] = wide[pl.ds(node, RANK, stride=span)].astype(BF)
-        thin_ref[node] = thin[pl.ds(node, RANK, stride=span)].astype(BF)
+        wide_ref[node] = load_node(wide, node)
+        thin_ref[node] = load_node(thin, node)
     for depth in range(SPAN, levels + 1):
         first = 2**depth - 1
         above = 2 ** (depth - 1) - 1
@@ -351,10 +379,10 @@
                     mates = [coef_ref[partners_ref[node, f] + shift] for f in range(3)]
                     left = jnp.where(low, mates[0], mates[1])
                     outs.append(
-                        mul_nt(left, wide[pl.ds(node, RANK, stride=span)].astype(BF))
+                        mul_nt(left, load_node(wide, node))
                         + mul_nt(
                             mates[2][:, :RANK],
-                            thin[pl.ds(node, RANK, stride=span)].astype(BF),
+                            load_node(thin, node),
                         )
                     )
             for j, i in enumerate(nodes):
@@ -444,15 +472,16 @@
 
 
 def final_kernel(low_ref, basis_ref, noise_ref, vec_ref, mine_ref, got_ref, out_ref):
-    for leaf in range(low_ref.shape[0]):
-        here = slice(leaf * LEAF, (leaf + 1) * LEAF)
-        far = jnp.dot(low_ref[leaf], basis_ref[leaf], preferred_element_type=F32)
-        out_ref[:, here] = (
-            mine_ref[:, here]
-            + got_ref[:, here]
-            + noise_ref[:, here] * vec_ref[:, here].astype(F32)
-            + far
-        )
+    def work(nodes):
+        fars = [
+            jnp.dot(low_ref[n], basis_ref[n], preferred_element_type=F32) for n in nodes
+        ]
+        for n, far in zip(nodes, fars):
+            here = lanes(n)
+            near = mine_ref[:, here] + got_ref[:, here]
+            out_ref[:, here] = near + noise_ref[:, here] * vec_ref[:, here].astype(F32) + far
+
+    over_nodes(low_ref.shape[0], 8, work)
 
 
 def swap_bit(value, bit):
@@ -495,20 +524,14 @@
         in_specs=[vspec()] * 3,
         out_specs=(vspec(),) * 3,
         scratch_shapes=[
-            VMEM((RANK * leaves, 2 * RANK), F32), VMEM((leaves - 1, 16, 2 * RANK), BF),
+            VMEM((leaves // 8, RANK * 8, 2 * RANK), F32), VMEM((leaves - 1, 16, 2 * RANK), BF),
         ],
         compiler_params=params(28),
         cost_estimate=pl.CostEstimate(
             flops=300 * 2 * 256 * 256 * 48, bytes_accessed=8 << 20, transcendentals=0
         ),
     )(vectors, leaf_basis, jnp.transpose(local_transfer, (1, 2, 3, 0)))
-    gathered = export
-    for bit in range(SPAN):
-        gathered = jnp.concatenate([gathered, swap_bit(gathered, bit)], axis=0)
-    tops = gathered
-    for bit in range(SPAN, dev_levels):
-        tops = tops[:, 0:1]
-        tops = jnp.concatenate([tops, swap_bit(tops, bit)], axis=0)
+    gathered = jnp.concatenate([export, swap_bit(export, 0)], axis=0)
 
     pack = pl.pallas_call(
         pack_kernel,
@@ -523,15 +546,15 @@
     right = lax.ppermute(pack, axes, [(i + 1, i) for i in range(count - 1)])
 
     pack, _ = lax.optimization_barrier((pack, export))
-    start, row_feat, far_list, far_count = pl.pallas_call(
+    mine, other, row_feat, far_list, far_count = pl.pallas_call(
         near_local_kernel,
         name="near_local",
         out_shape=(
-            sds((16, size), F32), sds((leaves, 32, LEAF), BF),
+            sds((PART, size), F32), sds((PART, size), F32), sds((leaves, 32, LEAF), BF),
             sds((slots + PAD,), jnp.int32), sds((1,), jnp.int32),
         ),
         in_specs=[sspec()] * 4 + [vspec()] * 2,
-        out_specs=(vspec(), vspec(), sspec(), sspec()),
+        out_specs=(vspec(), vspec(), vspec(), sspec(), sspec()),
         scratch_shapes=[
             VMEM((leaves // 2 + 1, LEAF, 32), BF), VMEM((leaves // 2 + 1, 16, LEAF), BF),
             *scratch_blocks, SMEM((slots + PAD,), jnp.int32),
@@ -542,14 +565,15 @@
         ),
     )(where, inv_scale, near_offsets, near_cols, points, pack)
 
+    far_list, gathered = lax.optimization_barrier((far_list, gathered))
+    gathered = jnp.concatenate([gathered, swap_bit(gathered, 1)], axis=0)
     mine, other = pl.pallas_call(
         near_halo_kernel,
         name="near_halo",
         out_shape=(sds((PART, size), F32), sds((PART, size), F32)),
-        in_specs=[sspec(), sspec()] + [vspec()] * 4,
+        in_specs=[sspec(), sspec()] + [vspec()] * 5,
         out_specs=(vspec(), vspec()),
         scratch_shapes=[
-            VMEM((16, size), F32),
             VMEM((leaves + 1, LEAF, 32), BF), VMEM((leaves + 1, 16, LEAF), BF),
             *scratch_blocks,
         ],
@@ -557,10 +581,15 @@
         cost_estimate=pl.CostEstimate(
             flops=60 * 2 * 256 * 256 * 48, bytes_accessed=8 << 20, transcendentals=60 * 2**17
         ),
-    )(far_list, far_count, row_feat, left, right, start)
+    )(far_list, far_count, row_feat, left, right, mine, other)
     swapped = lax.ppermute(other, "vec", [(0, 1), (1, 0)])
 
-    _, coef_late = lax.optimization_barrier((mine, coef))
+    _, coef_late, gathered = lax.optimization_barrier((mine, coef, gathered))
+    gathered = jnp.concatenate([gathered, swap_bit(gathered, 2)], axis=0)
+    tops = gathered
+    for bit in range(SPAN, dev_levels):
+        tops = tops[:, 0:1]
+        tops = jnp.concatenate([tops, swap_bit(tops, bit)], axis=0)
     local, wide, thin = pl.pallas_call(
         couple_kernel,
         name="couple",
@@ -571,7 +600,8 @@
         in_specs=[sspec()] * 2 + [vspec()] * 2,
         out_specs=(vspec(),) * 3,
         scratch_shapes=[
-            VMEM((2 * leaves * RANK, 2 * RANK), F32), VMEM((2 * leaves * RANK, RANK), F32),
+            VMEM((leaves // 4, RANK * 8, 2 * RANK), F32),
+            VMEM((leaves // 4, RANK * 8, RANK), F32),
         ],
         compiler_params=params(36),
         cost_estimate=pl.CostEstimate(
@@ -595,23 +625,13 @@
         wide, thin, local, moves,
     )
 
-    per = 16
-    wide = per * LEAF
     return pl.pallas_call(
         final_kernel,
         name="final",
         out_shape=sds((PART, size), F32),
-        grid=(leaves // per,),
-        in_specs=[
-            pl.BlockSpec((per, PART, RANK), lambda i: (i, 0, 0)),
-            pl.BlockSpec((per, RANK, LEAF), lambda i: (i, 0, 0)),
-            pl.BlockSpec((1, wide), lambda i: (0, i)),
-            pl.BlockSpec((PART, wide), lambda i: (0, i)),
-            pl.BlockSpec((PART, wide), lambda i: (0, i)),
-            pl.BlockSpec((PART, wide), lambda i: (0, i)),
-        ],
-        out_specs=pl.BlockSpec((PART, wide), lambda i: (0, i)),
-        compiler_params=params(24),
+        in_specs=[vspec()] * 6,
+        out_specs=vspec(),
+        compiler_params=params(16),
     )(low, leaf_basis, noise.reshape(1, size), vectors, mine, swapped)
 
 

time: 125 us -> 130 us (1.040)
  waiting for transfers between devices: 7.92 us -> 22.2 us
  Pallas kernels: 90.7 us -> 80.7 us
    ppermute x3, waiting for transfers between devices: 6.83 us -> 21.1 us  [swap_bit(): return lax.ppermute(value, axis, pairs)]
    pallas_call x1, Pallas kernels: 22.1 us -> 17.8 us  [body(): pl.pallas_call(couple_kernel, name='couple', out_shape=(sds((leaves - 1,...]
    pallas_call x1, Pallas kernels: 8.59 us -> 5.08 us  [body(): pl.pallas_call(near_halo_kernel, name='near_halo', out_shape=(sds((PART,...]
  transfers between devices with their start and end apart: 7 -> 7, of which waited for: 4 -> 3; matrix products, arithmetic and copies ran while one was open for 0% -> 0% of each run, Pallas kernels for 61% -> 54%
where the time goes in v2:
time: 130 us
  Pallas kernels  80.7 us (62%)
  waiting for transfers between devices  22.2 us (17%)
  starting transfers between devices  15.2 us (12%)
  local copies, waits for them, and re-layouts  11.1 us (9%)
    pallas_call x1, Pallas kernels, body(): pl.pallas_call(near_local_kernel, name='near_local', out_shape=(sds((PART...  35.4 us
    ppermute x3, waiting for transfers between devices, swap_bit(): return lax.ppermute(value, axis, pairs)  21.1 us
    pallas_call x1, Pallas kernels, body(): pl.pallas_call(couple_kernel, name='couple', out_shape=(sds((leaves - 1,...  17.8 us
    unnamed x43, local copies, waits for them, and re-layouts  10.1 us
    pallas_call x1, Pallas kernels, body(): pl.pallas_call(up_kernel, name='up', out_shape=(sds((2 * leaves - 1, 16,...  9.64 us
    ppermute x3, starting transfers between devices, swap_bit(): return lax.ppermute(value, axis, pairs)  8.6 us
    pallas_call x1, Pallas kernels, body(): pl.pallas_call(functools.partial(down_kernel, dev_levels), name='down', o...  7.21 us
    pallas_call x1, Pallas kernels, body(): pl.pallas_call(near_halo_kernel, name='near_halo', out_shape=(sds((PART,...  5.08 us
  transfers between devices with their start and end apart: 7, of which 3 were waited for; matrix products, arithmetic and copies ran while one was open for 0% of the time, Pallas kernels for 54%

profile of v2, /device:TPU:0, one launch (start us, length us, event | category | flops | bytes accessed | tf_op | source)
XLA Modules:
  0.0 129.6 jit_solution(11593123201644701029)
XLA Ops:
  0.0 1.0 constant_dynamic-slice_fusion
  1.0 0.5 collective-permute-start
  1.6 1.1 collective-permute-done.got_ref
  2.7 1.0 copy-done.3
  3.8 1.0 copy-done.9
  4.8 0.7 copy-done.15
  5.5 0.9 pack.1.pack_ref
  6.3 4.8 %collective-permute-start.2 = (bf16[24,16384]{1,0:T(8,128)(2,1)S(1)}, bf16[24,16384]{1,0:T(8,128)(2,1)S(1)}, u32[]{:S(2)}, u32[]{:S(2)}) collective-permute-start(bf16[24,16384]{1,0:T(8,128)(2,1)S(1)} %pack.1.pack_ref), channel_id=1, source_target_pairs={{0,2},{2,4},{4,6},{6,8},{8,10},{10,12},{12,14},{1,3},{3,5},{5,7},{... | collective-permute-start | bytes 2359304 | tf_op jit(solution)/shard_map/ppermute | solution.py:545
  11.2 1.3 collective-permute-start.3
  12.5 2.2 %copy-done.1 = bf16[128,64,256]{2,1,0:T(8,128)(2,1)S(1)} copy-done((bf16[128,64,256]{2,1,0:T(8,128)(2,1)S(1)}, bf16[128,64,256]{2,1,0:T(8,128)(2,1)}, u32[]{:S(2)}) %copy-start.1) | copy-done | bytes 4194328
  14.7 9.6 %up.1 = (bf16[255,16,128]{2,1,0:T(8,128)(2,1)S(1)}, bf16[1,7,16,128]{3,2,1,0:T(8,128)(2,1)S(1)}, bf16[127,64,128]{2,1,0:T(8,128)(2,1)S(1)}) custom-call(bf16[8,32768]{1,0:T(8,128)(2,1)S(1)} %copy-done.4, bf16[128,64,256]{2,1,0:T(8,128)(2,1)S(1)} %copy-done.1, bf16[2,64,64,127]{3,2,1,0:T(8,128)(2,1)S(1)} %bitcast.7), custom_call_target="tpu_custom_call" | custom-call | flops 1887436800 | bytes 8388608 | tf_op jit(solution)/shard_map/up/pallas_call | solution.py:517
  24.3 2.7 %collective-permute-start.1 = (bf16[1,7,16,128]{3,2,1,0:T(8,128)(2,1)S(1)}, bf16[1,7,16,128]{3,2,1,0:T(8,128)(2,1)S(1)}, u32[]{:S(2)}, u32[]{:S(2)}) collective-permute-start(bf16[1,7,16,128]{3,2,1,0:T(8,128)(2,1)S(1)} %get-tuple-element.23), channel_id=1, source_target_pairs={{0,2},{2,0},{1,3},{3,1},{4,6},{6,4},{5,7},{7,5},{8,10},{10,8},{9,1... | collective-permute-start | bytes 86024 | tf_op jit(solution)/shard_map/ppermute | solution.py:491
  27.0 18.6 %collective-permute-done.1 = bf16[1,7,16,128]{3,2,1,0:T(8,128)(2,1)S(1)} collective-permute-done((bf16[1,7,16,128]{3,2,1,0:T(8,128)(2,1)S(1)}, bf16[1,7,16,128]{3,2,1,0:T(8,128)(2,1)S(1)}, u32[]{:S(2)}, u32[]{:S(2)}) %collective-permute-start.1) | collective-permute-done | bytes 28704 | tf_op jit(solution)/shard_map/ppermute | solution.py:491
  45.7 35.4 %near_local.1 = (f32[8,32768]{1,0:T(8,128)S(1)}, f32[8,32768]{1,0:T(8,128)S(1)}, bf16[128,32,256]{2,1,0:T(8,128)(2,1)S(1)}, s32[528]{0:T(1024)S(1)}, s32[1]{0:T(128)}) custom-call(s32[2]{0:T(128)S(1)} %pad_add_fusion.where_ref, f32[3]{0:T(128)S(1)} %copy-done.16, s32[128]{0:T(128)S(1)} %copy-done.19, s32[512]{0:T(512)S(1)} %copy-done.18, ...), custom_call_target="tpu_custom_call" | custom-call | flops 1195376640 | bytes 8388608 | tf_op jit(solution)/shard_map/near_local/pallas_call | solution.py:549
  81.1 5.1 %near_halo.1 = (f32[8,32768]{1,0:T(8,128)S(1)}, f32[8,32768]{1,0:T(8,128)}) custom-call(s32[528]{0:T(1024)S(1)} %get-tuple-element.26.far_list, s32[1]{0:T(128)} %get-tuple-element.27.far_count, bf16[128,32,256]{2,1,0:T(8,128)(2,1)S(1)} %get-tuple-element.28.row_ref, bf16[24,16384]{1,0:T(8,128)(2,1)S(1)} %collective-permute-done.2.left_ref, ...), custom_call_target="tpu_custom_call" | custom-call | flops 377487360 | bytes 8388608 | tf_op jit(solution)/shard_map/near_halo/pallas_call | solution.py:570
  86.2 1.0 copy-done.5
  87.2 2.4 %collective-permute-start.4 = (bf16[2,7,16,128]{3,2,1,0:T(8,128)(2,1)S(1)}, bf16[2,7,16,128]{3,2,1,0:T(8,128)(2,1)S(1)}, u32[]{:S(2)}, u32[]{:S(2)}) collective-permute-start(bf16[2,7,16,128]{3,2,1,0:T(8,128)(2,1)S(1)} %pad_maximum_fusion.2), channel_id=1, source_target_pairs={{0,4},{4,0},{8,12},{12,8},{1,5},{5,1},{9,13},{13,9},{2,6},{6,2},{1... | collective-permute-start | bytes 172040 | tf_op jit(solution)/shard_map/ppermute | solution.py:491
  89.7 2.4 %collective-permute-done.4 = bf16[2,7,16,128]{3,2,1,0:T(8,128)(2,1)S(1)} collective-permute-done((bf16[2,7,16,128]{3,2,1,0:T(8,128)(2,1)S(1)}, bf16[2,7,16,128]{3,2,1,0:T(8,128)(2,1)S(1)}, u32[]{:S(2)}, u32[]{:S(2)}) %collective-permute-start.4) | collective-permute-done | bytes 57376 | tf_op jit(solution)/shard_map/ppermute | solution.py:491
  92.2 3.5 %collective-permute-start.5 = (bf16[4,7,16,128]{3,2,1,0:T(8,128)(2,1)S(1)}, bf16[4,7,16,128]{3,2,1,0:T(8,128)(2,1)S(1)}, u32[]{:S(2)}, u32[]{:S(2)}) collective-permute-start(bf16[4,7,16,128]{3,2,1,0:T(8,128)(2,1)S(1)} %pad_maximum_fusion.1), channel_id=1, source_target_pairs={{0,8},{4,12},{8,0},{12,4},{1,9},{5,13},{9,1},{13,5},{2,10},{6,14},... | collective-permute-start | bytes 344072 | tf_op jit(solution)/shard_map/ppermute | solution.py:491
  95.7 2.8 %copy-done = bf16[255,3,64,64]{0,3,2,1:T(8,128)(2,1)S(1)} copy-done((bf16[255,3,64,64]{0,3,2,1:T(8,128)(2,1)S(1)}, bf16[255,3,64,64]{0,3,2,1:T(8,128)(2,1)}, u32[]{:S(2)}) %copy-start) | copy-done | bytes 6266904
  98.5 1.2 copy-done.8
  99.7 17.8 %couple.1 = (f32[127,8,128]{2,1,0:T(8,128)S(1)}, bf16[7,64,128]{2,1,0:T(8,128)(2,1)S(1)}, bf16[7,64,64]{2,1,0:T(8,128)(2,1)S(1)}) custom-call(s32[2]{0:T(128)S(1)} %pad_add_fusion.where_ref, s32[255,3]{1,0:T(8,128)S(1)} %copy.15.partners_ref, bf16[255,16,128]{2,1,0:T(8,128)(2,1)S(1)} %copy-done.8, bf16[3,64,64,255]{3,2,1,0:T(8,128)(2,1)S(1)} %bitcast.5), custom_call_target="tpu_custom_call" | custom-call | flops 1887436800 | bytes 8388608 | tf_op jit(solution)/shard_map/couple/pallas_call | solution.py:593
  117.6 7.2 %down.1.low_ref = bf16[128,8,64]{2,1,0:T(8,128)(2,1)S(1)} custom-call(s32[2]{0:T(128)S(1)} %pad_add_fusion.where_ref, s32[255,3]{1,0:T(8,128)S(1)} %copy.15.partners_ref, s32[4,3]{1,0:T(4,128)S(1)} %copy-done.14, bf16[8,7,16,128]{3,2,1,0:T(8,128)(2,1)S(1)} %pad_maximum_fusion.gather_ref.tops_ref, ...), custom_call_target="tpu_custom_call" | custom-call | flops 629145600 | bytes 8388608 | tf_op jit(solution)/shard_map/down/pallas_call | solution.py:612
  124.8 4.7 %final.1 = f32[8,32768]{1,0:T(8,128)} custom-call(bf16[128,8,64]{2,1,0:T(8,128)(2,1)S(1)} %down.1.low_ref, bf16[128,64,256]{2,1,0:T(8,128)(2,1)S(1)} %copy-done.2, f32[1,32768]{1,0:T(1,128)S(1)} %bitcast.6, bf16[8,32768]{1,0:T(8,128)(2,1)S(1)} %copy-done.4, f32[8,32768]{1,0:T(8,128)S(1)} %copy-done.6, f32[8,32768]{1,0:T(8,128)} %collective-permute-done.6.got_ref), custom_call_target="tpu_custom_call" | custom-call | tf_op jit(solution)/shard_map/final/pallas_call | solution.py:628
  (45 shorter events, 0.4 us)
Async XLA Ops:
  0.0 12.5 %copy-start.4 = (bf16[8,32768]{1,0:T(8,128)(2,1)S(1)}, bf16[8,32768]{1,0:T(8,128)(2,1)}, u32[]{:S(2)}) copy-start(bf16[8,32768]{1,0:T(8,128)(2,1)} %vec_ref.5) | copy-start | bytes 1572868
  1.0 1.7 %collective-permute-start = (bf16[8,16384]{1,0:T(8,128)(2,1)S(1)}, bf16[8,16384]{1,0:T(8,128)(2,1)S(1)}, u32[]{:S(2)}, u32[]{:S(2)}) collective-permute-start(bf16[8,16384]{1,0:T(8,128)(2,1)S(1)} %constant_dynamic-slice_fusion), channel_id=1, source_target_pairs={{0,1},{1,0},{2,3},{3,2},{4,5},{5,4},{6,7},{7,6},{8,9},{9,8},{10,11... | collective-permute-start | bytes 786440 | tf_op jit(solution)/shard_map/ppermute | solution.py:515
  5.5 7.0 %copy-start.17 = (bf16[127,2,64,64]{0,3,2,1:T(8,128)(2,1)S(1)}, bf16[127,2,64,64]{0,3,2,1:T(8,128)(2,1)}, u32[]{:S(2)}) copy-start(bf16[127,2,64,64]{0,3,2,1:T(8,128)(2,1)} %param.18) | copy-start | bytes 6242308
  6.3 74.8 %collective-permute-start.2 = (bf16[24,16384]{1,0:T(8,128)(2,1)S(1)}, bf16[24,16384]{1,0:T(8,128)(2,1)S(1)}, u32[]{:S(2)}, u32[]{:S(2)}) collective-permute-start(bf16[24,16384]{1,0:T(8,128)(2,1)S(1)} %pack.1.pack_ref), channel_id=1, source_target_pairs={{0,2},{2,4},{4,6},{6,8},{8,10},{10,12},{12,14},{1,3},{3,5},{5,7},{... | collective-permute-start | bytes 2359304 | tf_op jit(solution)/shard_map/ppermute | solution.py:545
  11.2 69.9 %collective-permute-start.3 = (bf16[24,16384]{1,0:T(8,128)(2,1)S(1)}, bf16[24,16384]{1,0:T(8,128)(2,1)S(1)}, u32[]{:S(2)}, u32[]{:S(2)}) collective-permute-start(bf16[24,16384]{1,0:T(8,128)(2,1)S(1)} %pack.1.pack_ref), channel_id=1, source_target_pairs={{2,0},{4,2},{6,4},{8,6},{10,8},{12,10},{14,12},{3,1},{5,3},{7,5},{... | collective-permute-start | bytes 2359304 | tf_op jit(solution)/shard_map/ppermute | solution.py:546
  12.5 2.2 %copy-start.1 = (bf16[128,64,256]{2,1,0:T(8,128)(2,1)S(1)}, bf16[128,64,256]{2,1,0:T(8,128)(2,1)}, u32[]{:S(2)}) copy-start(bf16[128,64,256]{2,1,0:T(8,128)(2,1)} %basis_ref.3) | copy-start | bytes 12582916
  14.7 31.0 %copy-start.10 = (f32[3,32768]{1,0:T(4,128)S(1)}, f32[3,32768]{1,0:T(4,128)}, u32[]{:S(2)}) copy-start(f32[3,32768]{1,0:T(4,128)} %points_ref.3) | copy-start | bytes 1179652
  14.7 31.0 %copy-start.16 = (f32[3]{0:T(128)S(1)}, f32[3]{0:T(128)}, u32[]{:S(2)}) copy-start(f32[3]{0:T(128)} %scale_ref.3) | copy-start | bytes 40
  14.7 31.0 %copy-start.18 = (s32[512]{0:T(512)S(1)}, s32[512]{0:T(512)}, u32[]{:S(2)}) copy-start(s32[512]{0:T(512)} %cols_ref.1) | copy-start | bytes 6148
  14.7 31.0 %copy-start.19 = (s32[128]{0:T(128)S(1)}, s32[128]{0:T(128)}, u32[]{:S(2)}) copy-start(s32[128]{0:T(128)} %offs_ref.1) | copy-start | bytes 1540
  24.3 56.8 %copy-start.7 = (bf16[255,16,128]{2,1,0:T(8,128)(2,1)}, bf16[255,16,128]{2,1,0:T(8,128)(2,1)S(1)}, u32[]{:S(2)}) copy-start(bf16[255,16,128]{2,1,0:T(8,128)(2,1)S(1)} %get-tuple-element.35.coef_ref) | copy-start | bytes 3133444
  24.3 21.3 %collective-permute-start.1 = (bf16[1,7,16,128]{3,2,1,0:T(8,128)(2,1)S(1)}, bf16[1,7,16,128]{3,2,1,0:T(8,128)(2,1)S(1)}, u32[]{:S(2)}, u32[]{:S(2)}) collective-permute-start(bf16[1,7,16,128]{3,2,1,0:T(8,128)(2,1)S(1)} %get-tuple-element.23), channel_id=1, source_target_pairs={{0,2},{2,0},{1,3},{3,1},{4,6},{6,4},{5,7},{7,5},{8,10},{10,8},{9,1... | collective-permute-start | bytes 86024 | tf_op jit(solution)/shard_map/ppermute | solution.py:491
  81.1 8.5 %copy-start.20 = (s32[255,3]{0,1:T(4,128)S(1)}, s32[255,3]{0,1:T(4,128)}, u32[]{:S(2)}) copy-start(s32[255,3]{0,1:T(4,128)} %param.22) | copy-start | bytes 9184
  87.2 37.6 %collective-permute-start.6 = (f32[8,32768]{1,0:T(8,128)}, f32[8,32768]{1,0:T(8,128)}, u32[]{:S(2)}, u32[]{:S(2)}) collective-permute-start(f32[8,32768]{1,0:T(8,128)} %get-tuple-element.40), channel_id=1, source_target_pairs={{0,1},{1,0},{2,3},{3,2},{4,5},{5,4},{6,7},{7,6},{8,9},{9,8},{10,11... | collective-permute-start | bytes 3145736 | tf_op jit(solution)/shard_map/ppermute | solution.py:585
  87.2 5.0 %collective-permute-start.4 = (bf16[2,7,16,128]{3,2,1,0:T(8,128)(2,1)S(1)}, bf16[2,7,16,128]{3,2,1,0:T(8,128)(2,1)S(1)}, u32[]{:S(2)}, u32[]{:S(2)}) collective-permute-start(bf16[2,7,16,128]{3,2,1,0:T(8,128)(2,1)S(1)} %pad_maximum_fusion.2), channel_id=1, source_target_pairs={{0,4},{4,0},{8,12},{12,8},{1,5},{5,1},{9,13},{13,9},{2,6},{6,2},{1... | collective-permute-start | bytes 172040 | tf_op jit(solution)/shard_map/ppermute | solution.py:491
  92.2 25.3 %collective-permute-start.5 = (bf16[4,7,16,128]{3,2,1,0:T(8,128)(2,1)S(1)}, bf16[4,7,16,128]{3,2,1,0:T(8,128)(2,1)S(1)}, u32[]{:S(2)}, u32[]{:S(2)}) collective-permute-start(bf16[4,7,16,128]{3,2,1,0:T(8,128)(2,1)S(1)} %pad_maximum_fusion.1), channel_id=1, source_target_pairs={{0,8},{4,12},{8,0},{12,4},{1,9},{5,13},{9,1},{13,5},{2,10},{6,14},... | collective-permute-start | bytes 344072 | tf_op jit(solution)/shard_map/ppermute | solution.py:491
  95.7 2.8 %copy-start = (bf16[255,3,64,64]{0,3,2,1:T(8,128)(2,1)S(1)}, bf16[255,3,64,64]{0,3,2,1:T(8,128)(2,1)}, u32[]{:S(2)}) copy-start(bf16[255,3,64,64]{0,3,2,1:T(8,128)(2,1)} %param.20) | copy-start | bytes 18800644
  98.5 1.2 copy-start.8
  99.7 17.9 %copy-start.11 = (bf16[4,3,64,64]{3,2,1,0:T(8,128)(2,1)S(1)}, bf16[4,3,64,64]{3,2,1,0:T(8,128)(2,1)}, u32[]{:S(2)}) copy-start(bf16[4,3,64,64]{3,2,1,0:T(8,128)(2,1)} %top_b.1) | copy-start | bytes 294916
  99.7 17.9 %copy-start.13 = (bf16[4,2,64,64]{3,2,1,0:T(8,128)(2,1)S(1)}, bf16[4,2,64,64]{3,2,1,0:T(8,128)(2,1)}, u32[]{:S(2)}) copy-start(bf16[4,2,64,64]{3,2,1,0:T(8,128)(2,1)} %top_e.1) | copy-start | bytes 196612
  99.7 17.9 %copy-start.14 = (s32[4,3]{1,0:T(4,128)S(1)}, s32[4,3]{1,0:T(4,128)}, u32[]{:S(2)}) copy-start(s32[4,3]{1,0:T(4,128)} %top_partners_ref.1) | copy-start | bytes 148
  99.7 25.1 %copy-start.6 = (f32[8,32768]{1,0:T(8,128)S(1)}, f32[8,32768]{1,0:T(8,128)}, u32[]{:S(2)}) copy-start(f32[8,32768]{1,0:T(8,128)} %copy-done.5) | copy-start | bytes 3145732
  117.5 7.3 %copy-start.2 = (bf16[128,64,256]{2,1,0:T(8,128)(2,1)S(1)}, bf16[128,64,256]{2,1,0:T(8,128)(2,1)}, u32[]{:S(2)}) copy-start(bf16[128,64,256]{2,1,0:T(8,128)(2,1)} %basis_ref.3) | copy-start | bytes 12582916
  117.5 7.3 %copy-start.12 = (f32[32768]{0:T(1024)S(1)}, f32[32768]{0:T(1024)}, u32[]{:S(2)}) copy-start(f32[32768]{0:T(1024)} %param.15) | copy-start | bytes 393220
  (4 other events, 3.7 us)

commit v3 on v2

--- a/solution.py
+++ b/solution.py
@@ -20,6 +20,7 @@
 TINY = 1e-12
 PAIR = 2
 PAD = 16
+TURNS = 2
 CODE_BITS = 10
 CODE = 2**CODE_BITS
 VMEM = pltpu.VMEM
@@ -35,8 +36,18 @@
     return pl.BlockSpec(memory_space=pltpu.SMEM)
 
 
-def aspec():
-    return pl.BlockSpec(memory_space=pl.ANY)
+def hspec():
+    return pl.BlockSpec(memory_space=pltpu.HBM)
+
+
+def fetch(pairs, sems):
+    copies = [
+        pltpu.make_async_copy(source, target, sems.at[i])
+        for i, (source, target) in enumerate(pairs)
+    ]
+    for copy in copies:
+        copy.start()
+    return copies
 
 
 def params(mib):
@@ -45,6 +56,10 @@
 
 def lanes(index):
     return pl.ds(pl.multiple_of(index * LEAF, LEAF), LEAF)
+
+
+def whole(scalar):
+    return scalar.astype(jnp.int32)
 
 
 def coordinate_rows(raw, scale_ref):
@@ -99,16 +114,25 @@
     return ((1.0 + dist) * jnp.exp2(dist * NEG_LOG2E)).astype(BF)
 
 
-def pack_kernel(where_ref, scale_ref, points_ref, vec_ref, got_ref, out_ref):
-    half = got_ref.shape[1]
-    base = where_ref[1] * half
+def pack_kernel(scale_ref, points_hbm, vec_hbm, got_hbm, out_ref, points, mine, got, sems):
+    half = out_ref.shape[1]
+    core = whole(scale_ref[4])
+    there = pl.ds(pl.multiple_of(core * half, half), half)
+    copies = fetch(
+        [
+            (points_hbm.at[:, there], points), (vec_hbm.at[:, there], mine),
+            (got_hbm.at[:, there], got),
+        ],
+        sems,
+    )
+    for copy in copies:
+        copy.wait()
 
     def step(i, _):
         here = pl.ds(pl.multiple_of(i * 2048, 2048), 2048)
-        there = pl.ds(pl.multiple_of(base + i * 2048, 2048), 2048)
-        rows = coordinate_rows(points_ref[:, there], scale_ref)
+        rows = coordinate_rows(points[:, here], scale_ref)
         out_ref[:, here] = jnp.concatenate(
-            [vec_ref[:, there].astype(F32), got_ref[:, here].astype(F32), rows], axis=0
+            [mine[:, here].astype(F32), got[:, here].astype(F32), rows], axis=0
         ).astype(BF)
         return 0
 
@@ -143,18 +167,19 @@
     distance(0, s0)
 
     def step(it, _):
-        first = it * 2 * PAIR
-        accumulate(jnp.maximum(first - PAIR, 0), k1)
-        distance(first + PAIR, s1)
-        evaluate(s0, k0)
-        accumulate(first, k0)
-        distance(first + 2 * PAIR, s0)
-        evaluate(s1, k1)
+        for turn in range(TURNS):
+            first = (it * TURNS + turn) * 2 * PAIR
+            accumulate(jnp.maximum(first - PAIR, 0), k1)
+            distance(first + PAIR, s1)
+            evaluate(s0, k0)
+            accumulate(first, k0)
+            distance(first + 2 * PAIR, s0)
+            evaluate(s1, k1)
         return 0
 
-    turns = (count + 2 * PAIR - 1) // (2 * PAIR)
+    turns = (count + TURNS * 2 * PAIR - 1) // (TURNS * 2 * PAIR)
     lax.fori_loop(0, turns, step, 0)
-    accumulate(jnp.maximum(turns * 2 * PAIR - PAIR, 0), k1)
+    accumulate(jnp.maximum(turns * TURNS * 2 * PAIR - PAIR, 0), k1)
 
 
 def load_columns(pack_ref, base, count, col_ref, val_ref):
@@ -169,11 +194,11 @@
 
 
 def near_local_kernel(
-    where_ref, scale_ref, offs_ref, cols_ref, points_ref, pack_ref,
+    scale_ref, offs_ref, cols_ref, points_ref, pack_ref,
     mine_ref, other_ref, row_ref, far_list, far_count,
     col_ref, val_ref, s0, s1, k0, k1, own_list,
 ):
-    device, half_id = where_ref[0], where_ref[1]
+    device, half_id = whole(scale_ref[3]), whole(scale_ref[4])
     leaves = offs_ref.shape[0]
     half = leaves // 2
     slots = cols_ref.shape[0]
@@ -297,8 +322,30 @@
     return jnp.where(low, pair, turned), jnp.where(low, turned, pair)
 
 
-def up_kernel(vec_ref, basis_ref, raw_ref, coef_ref, export_ref, move_ref, flat, pairs):
+def up_kernel(
+    vec_hbm, basis_hbm, raw_hbm, coef_ref, export_ref, move_ref,
+    vec_ref, basis_ref, raw_ref, flat, pairs, sems,
+):
     leaves = basis_ref.shape[0]
+    chunks = 4
+    per = leaves // chunks
+    wide = per * LEAF
+    deep = RANK // chunks
+    copies = fetch(
+        [
+            pair
+            for c in range(chunks)
+            for pair in (
+                (vec_hbm.at[:, c * wide : (c + 1) * wide], vec_ref.at[:, c * wide : (c + 1) * wide]),
+                (basis_hbm.at[c * per : (c + 1) * per], basis_ref.at[c * per : (c + 1) * per]),
+                (
+                    raw_hbm.at[:, c * deep : (c + 1) * deep],
+                    raw_ref.at[:, c * deep : (c + 1) * deep],
+                ),
+            )
+        ],
+        sems,
+    )
     levels = leaves.bit_length() - 1
 
     def keep(parent, first, second):
@@ -321,7 +368,10 @@
             keep(leaves // 2 - 1 + it * 4 + q, outs[2 * q], outs[2 * q + 1])
         return 0
 
-    lax.fori_loop(0, leaves // 8, leaf_step, 0)
+    for c in range(chunks):
+        for copy in copies[3 * c : 3 * c + 3]:
+            copy.wait()
+        lax.fori_loop(c * per // 8, (c + 1) * per // 8, leaf_step, 0)
     for depth in range(levels - 1, 0, -1):
         first = 2**depth - 1
         above = 2 ** (depth - 1) - 1
@@ -342,27 +392,39 @@
     move_ref[0] = move
     root = join_parts(mul_nt(pairs[0], move))
     coef_ref[0] = split_parts(side_by_side(root, root))
-    export_ref[0] = coef_ref[0:EXPORT]
+    export_ref[...] = coef_ref[0:EXPORT]
 
 
 def couple_kernel(
-    where_ref, partners_ref, coef_ref, raw_ref, local_ref, wide_ref, thin_ref, wide, thin
+    scale_ref, partners_ref, coef_ref, raw_hbm, local_ref, wide_ref, thin_ref,
+    raw_ref, wide, thin, sems,
 ):
-    device = where_ref[0]
+    device = whole(scale_ref[3])
     total = raw_ref.shape[3]
+    chunks = 4
+    deep = RANK // chunks
+    copies = fetch(
+        [
+            (raw_hbm.at[:, c * deep : (c + 1) * deep], raw_ref.at[:, c * deep : (c + 1) * deep])
+            for c in range(chunks)
+        ],
+        sems,
+    )
     span = total + 1
     levels = span.bit_length() - 2
     low = lax.broadcasted_iota(jnp.int32, (16, 2 * RANK), 1) < RANK
 
     def turn(i, _):
-        for q in range(2):
-            r = i * 2 + q
+        for q in range(4):
+            r = i * 4 + q
             block = jnp.concatenate([raw_ref[0, r], raw_ref[1, r]], axis=0).astype(F32)
             store_turned(wide, r, block)
             store_turned(thin, r, raw_ref[2, r].astype(F32))
         return 0
 
-    lax.fori_loop(0, RANK // 2, turn, 0)
+    for c in range(chunks):
+        copies[c].wait()
+        lax.fori_loop(c * deep // 4, (c + 1) * deep // 4, turn, 0)
     for node in range(EXPORT):
         wide_ref[node] = load_node(wide, node)
         thin_ref[node] = load_node(thin, node)
@@ -376,7 +438,7 @@
             for j in nodes:
                 for c in range(2):
                     node = first + 2 * j + c
-                    mates = [coef_ref[partners_ref[node, f] + shift] for f in range(3)]
+                    mates = [coef_ref[partners_ref[f, node] + shift] for f in range(3)]
                     left = jnp.where(low, mates[0], mates[1])
                     outs.append(
                         mul_nt(left, load_node(wide, node))
@@ -390,16 +452,28 @@
                     join_parts(outs[2 * j]), join_parts(outs[2 * j + 1])
                 )
 
-        over_nodes(2 ** (depth - 1), 4, work)
+        over_nodes(2 ** (depth - 1), 8, work)
 
 
 def down_kernel(
-    dev_levels, where_ref, partners_ref, top_partners_ref, gather_ref, tops_ref, top_e, top_b,
-    wide_ref, thin_ref, local_ref, move_ref, out_ref, down, tree,
+    dev_levels, scale_ref, partners_ref, top_partners_ref, top_e, top_b, wide_ref, thin_ref,
+    local_ref, move_ref, *refs,
 ):
-    device = where_ref[0]
-    leaves = out_ref.shape[0]
+    exports, (basis_hbm, noise_hbm, vec_hbm, near_hbm, swap_hbm, out_hbm) = refs[:9], refs[9:15]
+    gather_ref, down, tree, low_ref, basis, noise, vec, near, swap, out, sems = refs[15:]
+    device = whole(scale_ref[3])
+    leaves = low_ref.shape[0]
     levels = leaves.bit_length() - 1
+    copies = fetch(
+        [
+            (basis_hbm, basis), (noise_hbm, noise), (vec_hbm, vec), (near_hbm, near),
+            (swap_hbm, swap),
+        ],
+        sems,
+    )
+    for i in range(2**SPAN):
+        gather_ref[i] = exports[i][...]
+    tops_ref = gather_ref if dev_levels == SPAN else exports[2**SPAN]
     low = lax.broadcasted_iota(jnp.int32, (16, 2 * RANK), 1) < RANK
 
     for level in range(dev_levels - 1, 1, -1):
@@ -421,7 +495,7 @@
     def near_root(node, depth):
         mates = []
         for f in range(3):
-            mate = partners_ref[node, f]
+            mate = partners_ref[f, node]
             at = ((mate >> depth) ^ device) & (2**SPAN - 1)
             mates.append(gather_ref[at, 2**depth - 1 + (mate & (2**depth - 1))])
         left = jnp.where(low, mates[0], mates[1])
@@ -458,8 +532,8 @@
                     base = local_ref[node]
                 pair = base + join_parts(out)
                 if depth == levels - 1:
-                    out_ref[2 * i] = pair[:, :RANK].astype(BF)
-                    out_ref[2 * i + 1] = pair[:, RANK:].astype(BF)
+                    low_ref[2 * i] = pair[:, :RANK].astype(BF)
+                    low_ref[2 * i + 1] = pair[:, RANK:].astype(BF)
                 else:
                     down[2 * node + 1] = split_parts(pair[:, :RANK])
                     down[2 * node + 2] = split_parts(pair[:, RANK:])
@@ -470,25 +544,37 @@
         else:
             over_nodes(2**depth, 8, work)
 
-
-def final_kernel(low_ref, basis_ref, noise_ref, vec_ref, mine_ref, got_ref, out_ref):
-    def work(nodes):
-        fars = [
-            jnp.dot(low_ref[n], basis_ref[n], preferred_element_type=F32) for n in nodes
-        ]
-        for n, far in zip(nodes, fars):
-            here = lanes(n)
-            near = mine_ref[:, here] + got_ref[:, here]
-            out_ref[:, here] = near + noise_ref[:, here] * vec_ref[:, here].astype(F32) + far
-
-    over_nodes(low_ref.shape[0], 8, work)
-
-
-def swap_bit(value, bit):
-    sub_bits = lax.axis_size("sub").bit_length() - 1
-    axis, apart = ("sub", 2**bit) if bit < sub_bits else ("leaf", 2 ** (bit - sub_bits))
-    pairs = [(i, i ^ apart) for i in range(lax.axis_size(axis))]
-    return lax.ppermute(value, axis, pairs)
+    for copy in copies:
+        copy.wait()
+    chunks = 4
+    per = leaves // chunks
+    wide = per * LEAF
+    sends = []
+    for c in range(chunks):
+
+        def last(nodes, c=c):
+            rows = [c * per + i for i in nodes]
+            fars = [jnp.dot(low_ref[n], basis[n], preferred_element_type=F32) for n in rows]
+            for n, far in zip(rows, fars):
+                here = lanes(n)
+                total = near[:, here] + swap[:, here]
+                out[:, here] = total + noise[:, here] * vec[:, here].astype(F32) + far
+
+        over_nodes(per, 8, last)
+        piece = slice(c * wide, (c + 1) * wide)
+        send = pltpu.make_async_copy(
+            out.at[:, piece], out_hbm.at[:, piece], sems.at[len(copies) + c]
+        )
+        send.start()
+        sends.append(send)
+    for send in sends:
+        send.wait()
+
+
+def swap_mask(value, mask):
+    leaf, sub = lax.axis_size("leaf"), lax.axis_size("sub")
+    pairs = [(i, i ^ mask) for i in range(leaf * sub)]
+    return lax.ppermute(value, ("leaf", "sub"), pairs)
 
 
 def body(
@@ -500,7 +586,7 @@
     dev_levels = count.bit_length() - 1
     device = lax.axis_index("leaf") * subs + lax.axis_index("sub")
     core = lax.axis_index("vec")
-    where = jnp.stack([device, core]).astype(jnp.int32)
+    scale = jnp.concatenate([inv_scale, jnp.stack([device, core]).astype(F32)])
     size = vectors.shape[1]
     leaves = near_offsets.shape[0]
     slots = near_cols.shape[0]
@@ -511,36 +597,40 @@
         VMEM((PAIR, LEAF, LEAF), BF), VMEM((PAIR, LEAF, LEAF), BF),
     ]
 
-    send = lax.dynamic_slice(vectors, (0, (1 - core) * half), (PART, half))
-    got = lax.ppermute(send, "vec", [(0, 1), (1, 0)])
-
+    got = lax.ppermute(vectors, "vec", [(0, 1), (1, 0)])
+
+    moves_raw = jnp.transpose(local_transfer, (1, 2, 3, 0))
     coef, export, moves = pl.pallas_call(
         up_kernel,
         name="up",
         out_shape=(
-            sds((2 * leaves - 1, 16, 2 * RANK), BF), sds((1, EXPORT, 16, 2 * RANK), BF),
+            sds((2 * leaves - 1, 16, 2 * RANK), BF), sds((EXPORT, 16, 2 * RANK), BF),
             sds((leaves - 1, RANK, 2 * RANK), BF),
         ),
-        in_specs=[vspec()] * 3,
+        in_specs=[hspec()] * 3,
         out_specs=(vspec(),) * 3,
         scratch_shapes=[
+            VMEM(vectors.shape, BF), VMEM(leaf_basis.shape, BF), VMEM(moves_raw.shape, BF),
             VMEM((leaves // 8, RANK * 8, 2 * RANK), F32), VMEM((leaves - 1, 16, 2 * RANK), BF),
+            pltpu.SemaphoreType.DMA((12,)),
         ],
         compiler_params=params(28),
         cost_estimate=pl.CostEstimate(
             flops=300 * 2 * 256 * 256 * 48, bytes_accessed=8 << 20, transcendentals=0
         ),
-    )(vectors, leaf_basis, jnp.transpose(local_transfer, (1, 2, 3, 0)))
-    gathered = jnp.concatenate([export, swap_bit(export, 0)], axis=0)
-
+    )(vectors, leaf_basis, moves_raw)
     pack = pl.pallas_call(
         pack_kernel,
         name="pack",
         out_shape=sds((24, half), BF),
-        in_specs=[sspec(), sspec(), vspec(), vspec(), vspec()],
+        in_specs=[sspec(), hspec(), hspec(), hspec()],
         out_specs=vspec(),
+        scratch_shapes=[
+            VMEM((3, half), F32), VMEM((PART, half), BF), VMEM((PART, half), BF),
+            pltpu.SemaphoreType.DMA((3,)),
+        ],
         compiler_params=params(16),
-    )(where, inv_scale, points, vectors, got)
+    )(scale, points, vectors, got)
     axes = ("leaf", "sub")
     left = lax.ppermute(pack, axes, [(i, i + 1) for i in range(count - 1)])
     right = lax.ppermute(pack, axes, [(i + 1, i) for i in range(count - 1)])
@@ -553,7 +643,7 @@
             sds((PART, size), F32), sds((PART, size), F32), sds((leaves, 32, LEAF), BF),
             sds((slots + PAD,), jnp.int32), sds((1,), jnp.int32),
         ),
-        in_specs=[sspec()] * 4 + [vspec()] * 2,
+        in_specs=[sspec()] * 3 + [vspec()] * 2,
         out_specs=(vspec(), vspec(), vspec(), sspec(), sspec()),
         scratch_shapes=[
             VMEM((leaves // 2 + 1, LEAF, 32), BF), VMEM((leaves // 2 + 1, 16, LEAF), BF),
@@ -563,10 +653,14 @@
         cost_estimate=pl.CostEstimate(
             flops=190 * 2 * 256 * 256 * 48, bytes_accessed=8 << 20, transcendentals=190 * 2**17
         ),
-    )(where, inv_scale, near_offsets, near_cols, points, pack)
-
-    far_list, gathered = lax.optimization_barrier((far_list, gathered))
-    gathered = jnp.concatenate([gathered, swap_bit(gathered, 1)], axis=0)
+    )(scale, near_offsets, near_cols, points, pack)
+
+    exports = [export] + [swap_mask(export, mask) for mask in range(1, 2**SPAN)]
+    tops = export[None]
+    for bit in range(SPAN, dev_levels):
+        if bit == SPAN:
+            tops = jnp.stack([part[0:1] for part in exports])
+        tops = jnp.concatenate([tops, swap_mask(tops, 2**bit)], axis=0)
     mine, other = pl.pallas_call(
         near_halo_kernel,
         name="near_halo",
@@ -584,12 +678,9 @@
     )(far_list, far_count, row_feat, left, right, mine, other)
     swapped = lax.ppermute(other, "vec", [(0, 1), (1, 0)])
 
-    _, coef_late, gathered = lax.optimization_barrier((mine, coef, gathered))
-    gathered = jnp.concatenate([gathered, swap_bit(gathered, 2)], axis=0)
-    tops = gathered
-    for bit in range(SPAN, dev_levels):
-        tops = tops[:, 0:1]
-        tops = jnp.concatenate([tops, swap_bit(tops, bit)], axis=0)
+    _, coef_late = lax.optimization_barrier((mine, coef))
+    ties_raw = jnp.transpose(local_coupling, (1, 2, 3, 0))
+    mates = jnp.transpose(local_partners)
     local, wide, thin = pl.pallas_call(
         couple_kernel,
         name="couple",
@@ -597,42 +688,40 @@
             sds((leaves - 1, PART, 2 * RANK), F32), sds((EXPORT, RANK, 2 * RANK), BF),
             sds((EXPORT, RANK, RANK), BF),
         ),
-        in_specs=[sspec()] * 2 + [vspec()] * 2,
+        in_specs=[sspec()] * 2 + [vspec(), hspec()],
         out_specs=(vspec(),) * 3,
         scratch_shapes=[
+            VMEM(ties_raw.shape, BF),
             VMEM((leaves // 4, RANK * 8, 2 * RANK), F32),
-            VMEM((leaves // 4, RANK * 8, RANK), F32),
+            VMEM((leaves // 4, RANK * 8, RANK), F32), pltpu.SemaphoreType.DMA((4,)),
         ],
         compiler_params=params(36),
         cost_estimate=pl.CostEstimate(
             flops=300 * 2 * 256 * 256 * 48, bytes_accessed=8 << 20, transcendentals=0
         ),
-    )(where, local_partners, coef_late, jnp.transpose(local_coupling, (1, 2, 3, 0)))
-
-    low = pl.pallas_call(
+    )(scale, mates, coef_late, ties_raw)
+
+    return pl.pallas_call(
         functools.partial(down_kernel, dev_levels),
         name="down",
-        out_shape=sds((leaves, PART, RANK), BF),
-        in_specs=[sspec()] * 3 + [vspec()] * 8,
-        out_specs=vspec(),
-        scratch_shapes=[VMEM((leaves - 1, 16, RANK), BF), VMEM((count, 16, RANK), BF)],
-        compiler_params=params(24),
+        out_shape=sds((PART, size), F32),
+        in_specs=[sspec()] * 3 + [vspec()] * 15 + [hspec()] * 5,
+        out_specs=hspec(),
+        scratch_shapes=[
+            VMEM((2**SPAN, EXPORT, 16, 2 * RANK), BF), VMEM((leaves - 1, 16, RANK), BF),
+            VMEM((count, 16, RANK), BF), VMEM((leaves, PART, RANK), BF),
+            VMEM(leaf_basis.shape, BF), VMEM((1, size), F32), VMEM(vectors.shape, BF),
+            VMEM((PART, size), F32), VMEM((PART, size), F32), VMEM((PART, size), F32),
+            pltpu.SemaphoreType.DMA((9,)),
+        ],
+        compiler_params=params(32),
         cost_estimate=pl.CostEstimate(
             flops=100 * 2 * 256 * 256 * 48, bytes_accessed=8 << 20, transcendentals=0
         ),
     )(
-        where, local_partners, top_partners, gathered, tops, top_transfer, top_coupling,
-        wide, thin, local, moves,
-    )
-
-    return pl.pallas_call(
-        final_kernel,
-        name="final",
-        out_shape=sds((PART, size), F32),
-        in_specs=[vspec()] * 6,
-        out_specs=vspec(),
-        compiler_params=params(16),
-    )(low, leaf_basis, noise.reshape(1, size), vectors, mine, swapped)
+        scale, mates, top_partners, top_transfer, top_coupling, wide, thin, local, moves,
+        *exports, tops, leaf_basis, noise.reshape(1, size), vectors, mine, swapped,
+    )
 
 
 def solution(mesh):

time: 130 us -> 97 us (0.75)
  waiting for transfers between devices: 22.2 us -> 0.97 us
  Pallas kernels: 80.7 us -> 69.7 us
  local copies, waits for them, and re-layouts: 11.1 us -> 5.92 us
  starting transfers between devices: 15.2 us -> 19.2 us
    ppermute x4 -> x8, waiting for transfers between devices: 22.2 us -> 0.96 us  [the longest x1 0.94 us: body(): got = lax.ppermute(vectors, 'vec', [(0, 1), (1, 0)])]
    pallas_call x1, Pallas kernels: 17.8 us -> 12.3 us  [body(): pl.pallas_call(couple_kernel, name='couple', out_shape=(sds((leaves - 1,...]
    pallas_call x1 -> x0, Pallas kernels: 4.74 us -> none  [body(): pl.pallas_call(final_kernel, name='final', out_shape=sds((PART, size), F3...]
    unnamed x43 -> x32, local copies, waits for them, and re-layouts: 10.1 us -> 5.92 us
    ppermute x4 -> x8, starting transfers between devices: 9.11 us -> 13.1 us  [the longest x7 12.7 us: swap_mask(): return lax.ppermute(value, ('leaf', 'sub'), pairs)]
    pallas_call x1, Pallas kernels: 35.4 us -> 32.7 us  [body(): pl.pallas_call(near_local_kernel, name='near_local', out_shape=(sds((PART...]
    pallas_call x1, Pallas kernels: 7.21 us -> 9.08 us  [body(): pl.pallas_call(functools.partial(down_kernel, dev_levels), name='down', o...]
    pallas_call x1, Pallas kernels: 5.08 us -> 3.74 us  [body(): pl.pallas_call(near_halo_kernel, name='near_halo', out_shape=(sds((PART,...]
  transfers between devices with their start and end apart: 7 -> 11, of which waited for: 3 -> 1; matrix products, arithmetic and copies ran while one was open for 0% -> 1% of each run, Pallas kernels for 54% -> 58%
where the time goes in v3:
time: 97 us; the launch traced here: 96.8 us
  Pallas kernels  69.7 us (72%)
  starting transfers between devices  19.2 us (20%)
  local copies, waits for them, and re-layouts  5.92 us (6%)
  waiting for transfers between devices  0.97 us (1%)
    pallas_call x1, Pallas kernels, body(): pl.pallas_call(near_local_kernel, name='near_local', out_shape=(sds((PART...  32.7 us
    ppermute x7, starting transfers between devices, swap_mask(): return lax.ppermute(value, ('leaf', 'sub'), pairs)  12.7 us
    pallas_call x1, Pallas kernels, body(): pl.pallas_call(couple_kernel, name='couple', out_shape=(sds((leaves - 1,...  12.3 us
    pallas_call x1, Pallas kernels, body(): pl.pallas_call(up_kernel, name='up', out_shape=(sds((2 * leaves - 1, 16,...  10.9 us
    pallas_call x1, Pallas kernels, body(): pl.pallas_call(functools.partial(down_kernel, dev_levels), name='down', o...  9.08 us
    unnamed x32, local copies, waits for them, and re-layouts  5.92 us
    ppermute x1, starting transfers between devices, body(): left = lax.ppermute(pack, axes, [(i, i + 1) for i in range(count - 1)])  4.81 us
    pallas_call x1, Pallas kernels, body(): pl.pallas_call(near_halo_kernel, name='near_halo', out_shape=(sds((PART,...  3.74 us
  transfers between devices with their start and end apart: 11, of which 1 were waited for; matrix products, arithmetic and copies ran while one was open for 1% of the time, Pallas kernels for 58%

profile of v3, /device:TPU:0, one launch (start us, length us, event | category | flops | bytes accessed | tf_op | source)
XLA Modules:
  0.0 96.8 jit_solution(9090103143018357081)
XLA Ops:
  0.0 0.5 collective-permute-start
  0.5 0.1 add_convert_fusion
  0.5 0.7 pad_maximum_fusion.scale_ref
  1.3 0.9 collective-permute-done.got_hbm
  2.2 1.0 %copy-done.2 = bf16[8,32768]{1,0:T(8,128)(2,1)S(1)} copy-done((bf16[8,32768]{1,0:T(8,128)(2,1)S(1)}, bf16[8,32768]{1,0:T(8,128)(2,1)}, u32[]{:S(2)}) %copy-start.2) | copy-done | bytes 524312
  3.2 1.0 %copy-done.4 = f32[3,32768]{1,0:T(4,128)S(1)} copy-done((f32[3,32768]{1,0:T(4,128)S(1)}, f32[3,32768]{1,0:T(4,128)}, u32[]{:S(2)}) %copy-start.4) | copy-done | bytes 393240
  4.3 0.9 pack.1.pack_ref
  5.2 4.8 %collective-permute-start.1 = (bf16[24,16384]{1,0:T(8,128)(2,1)S(1)}, bf16[24,16384]{1,0:T(8,128)(2,1)S(1)}, u32[]{:S(2)}, u32[]{:S(2)}) collective-permute-start(bf16[24,16384]{1,0:T(8,128)(2,1)S(1)} %pack.1.pack_ref), channel_id=1, source_target_pairs={{0,2},{2,4},{4,6},{6,8},{8,10},{10,12},{12,14},{1,3},{3,5},{5,7},{... | collective-permute-start | bytes 2359304 | tf_op jit(solution)/shard_map/ppermute | solution.py:635
  10.1 1.3 %collective-permute-start.2 = (bf16[24,16384]{1,0:T(8,128)(2,1)S(1)}, bf16[24,16384]{1,0:T(8,128)(2,1)S(1)}, u32[]{:S(2)}, u32[]{:S(2)}) collective-permute-start(bf16[24,16384]{1,0:T(8,128)(2,1)S(1)} %pack.1.pack_ref), channel_id=1, source_target_pairs={{2,0},{4,2},{6,4},{8,6},{10,8},{12,10},{14,12},{3,1},{5,3},{7,5},{... | collective-permute-start | bytes 2359304 | tf_op jit(solution)/shard_map/ppermute | solution.py:636
  11.4 2.2 %copy-done = bf16[128,64,256]{2,1,0:T(8,128)(2,1)S(1)} copy-done((bf16[128,64,256]{2,1,0:T(8,128)(2,1)S(1)}, bf16[128,64,256]{2,1,0:T(8,128)(2,1)}, u32[]{:S(2)}) %copy-start) | copy-done | bytes 4194328
  13.6 1.6 %copy-done.11 = bf16[127,2,64,64]{0,3,2,1:T(8,128)(2,1)S(1)} copy-done((bf16[127,2,64,64]{0,3,2,1:T(8,128)(2,1)S(1)}, bf16[127,2,64,64]{0,3,2,1:T(8,128)(2,1)}, u32[]{:S(2)}) %copy-start.11) | copy-done | bytes 2080792
  15.2 10.9 %up.1 = (bf16[255,16,128]{2,1,0:T(8,128)(2,1)S(1)}, bf16[7,16,128]{2,1,0:T(8,128)(2,1)S(1)}, bf16[127,64,128]{2,1,0:T(8,128)(2,1)S(1)}) custom-call(bf16[8,32768]{1,0:T(8,128)(2,1)S(1)} %copy-done.3, bf16[128,64,256]{2,1,0:T(8,128)(2,1)S(1)} %copy-done, bf16[2,64,64,127]{3,2,1,0:T(8,128)(2,1)S(1)} %bitcast.14), custom_call_target="tpu_custom_call" | custom-call | flops 1887436800 | bytes 8388608 | tf_op jit(solution)/shard_map/up/pallas_call | solution.py:603
  26.1 0.0 slice-start.1
  26.1 32.7 %near_local.1 = (f32[8,32768]{1,0:T(8,128)S(1)}, f32[8,32768]{1,0:T(8,128)S(1)}, bf16[128,32,256]{2,1,0:T(8,128)(2,1)S(1)}, s32[528]{0:T(1024)S(1)}, s32[1]{0:T(128)}) custom-call(f32[5]{0:T(128)S(1)} %pad_maximum_fusion.scale_ref, s32[128]{0:T(128)S(1)} %copy-done.13, s32[512]{0:T(512)S(1)} %copy-done.12, f32[3,32768]{1,0:T(4,128)S(1)} %copy-done.5, ...), custom_call_target="tpu_custom_call" | custom-call | flops 1195376640 | bytes 8388608 | tf_op jit(solution)/shard_map/near_local/pallas_call | solution.py:639
  58.8 3.7 %near_halo.1 = (f32[8,32768]{1,0:T(8,128)S(1)}, f32[8,32768]{1,0:T(8,128)S(1)}) custom-call(s32[528]{0:T(1024)S(1)} %get-tuple-element.22.far_list, s32[1]{0:T(128)} %get-tuple-element.23.far_count, bf16[128,32,256]{2,1,0:T(8,128)(2,1)S(1)} %get-tuple-element.24.row_ref, bf16[24,16384]{1,0:T(8,128)(2,1)S(1)} %collective-permute-done.1.left_ref, ...), custom_call_target="tpu_custom_call" | custom-call | flops 377487360 | bytes 8388608 | tf_op jit(solution)/shard_map/near_halo/pallas_call | solution.py:664
  62.6 1.9 %collective-permute-start.3 = (bf16[7,16,128]{2,1,0:T(8,128)(2,1)S(1)}, bf16[7,16,128]{2,1,0:T(8,128)(2,1)S(1)}, u32[]{:S(2)}, u32[]{:S(2)}) collective-permute-start(bf16[7,16,128]{2,1,0:T(8,128)(2,1)S(1)} %get-tuple-element.20.refs_0_), channel_id=1, source_target_pairs={{0,2},{2,0},{4,6},{6,4},{8,10},{10,8},{12,14},{14,12},{1,3},{3,1},... | collective-permute-start | bytes 86024 | tf_op jit(solution)/shard_map/ppermute | solution.py:577
  64.5 1.2 %collective-permute-start.4 = (bf16[7,16,128]{2,1,0:T(8,128)(2,1)S(1)}, bf16[7,16,128]{2,1,0:T(8,128)(2,1)S(1)}, u32[]{:S(2)}, u32[]{:S(2)}) collective-permute-start(bf16[7,16,128]{2,1,0:T(8,128)(2,1)S(1)} %get-tuple-element.20.refs_0_), channel_id=1, source_target_pairs={{0,4},{2,6},{4,0},{6,2},{8,12},{10,14},{12,8},{14,10},{1,5},{3,7},... | collective-permute-start | bytes 86024 | tf_op jit(solution)/shard_map/ppermute | solution.py:577
  65.7 1.2 %collective-permute-start.5 = (bf16[7,16,128]{2,1,0:T(8,128)(2,1)S(1)}, bf16[7,16,128]{2,1,0:T(8,128)(2,1)S(1)}, u32[]{:S(2)}, u32[]{:S(2)}) collective-permute-start(bf16[7,16,128]{2,1,0:T(8,128)(2,1)S(1)} %get-tuple-element.20.refs_0_), channel_id=1, source_target_pairs={{0,6},{2,4},{4,2},{6,0},{8,14},{10,12},{12,10},{14,8},{1,7},{3,5},... | collective-permute-start | bytes 86024 | tf_op jit(solution)/shard_map/ppermute | solution.py:577
  66.9 3.2 %collective-permute-start.6 = (bf16[7,16,128]{2,1,0:T(8,128)(2,1)S(1)}, bf16[7,16,128]{2,1,0:T(8,128)(2,1)S(1)}, u32[]{:S(2)}, u32[]{:S(2)}) collective-permute-start(bf16[7,16,128]{2,1,0:T(8,128)(2,1)S(1)} %get-tuple-element.20.refs_0_), channel_id=1, source_target_pairs={{0,8},{2,10},{4,12},{6,14},{8,0},{10,2},{12,4},{14,6},{1,9},{3,11}... | collective-permute-start | bytes 86024 | tf_op jit(solution)/shard_map/ppermute | solution.py:577
  70.1 0.4 collective-permute-start.7
  70.5 3.7 %collective-permute-start.8 = (bf16[7,16,128]{2,1,0:T(8,128)(2,1)S(1)}, bf16[7,16,128]{2,1,0:T(8,128)(2,1)S(1)}, u32[]{:S(2)}, u32[]{:S(2)}) collective-permute-start(bf16[7,16,128]{2,1,0:T(8,128)(2,1)S(1)} %get-tuple-element.20.refs_0_), channel_id=1, source_target_pairs={{0,12},{2,14},{4,8},{6,10},{8,4},{10,6},{12,0},{14,2},{1,13},{3,15... | collective-permute-start | bytes 86024 | tf_op jit(solution)/shard_map/ppermute | solution.py:577
  74.3 1.0 %collective-permute-start.9 = (bf16[7,16,128]{2,1,0:T(8,128)(2,1)S(1)}, bf16[7,16,128]{2,1,0:T(8,128)(2,1)S(1)}, u32[]{:S(2)}, u32[]{:S(2)}) collective-permute-start(bf16[7,16,128]{2,1,0:T(8,128)(2,1)S(1)} %get-tuple-element.20.refs_0_), channel_id=1, source_target_pairs={{0,14},{2,12},{4,10},{6,8},{8,6},{10,4},{12,2},{14,0},{1,15},{3,13... | collective-permute-start | bytes 86024 | tf_op jit(solution)/shard_map/ppermute | solution.py:577
  75.3 12.3 %couple.1 = (f32[127,8,128]{2,1,0:T(8,128)S(1)}, bf16[7,64,128]{2,1,0:T(8,128)(2,1)S(1)}, bf16[7,64,64]{2,1,0:T(8,128)(2,1)S(1)}) custom-call(f32[5]{0:T(128)S(1)} %pad_maximum_fusion.scale_ref, s32[3,255]{1,0:T(4,128)S(1)} %bitcast.12, bf16[255,16,128]{2,1,0:T(8,128)(2,1)S(1)} %get-tuple-element.29.coef_ref, bf16[3,64,64,255]{3,2,1,0:T(8,128)(2,1)S(1)} %bitcast.9), custom_call_target="tpu_custom_call" | custom-call | flops 1887436800 | bytes 8388608 | tf_op jit(solution)/shard_map/couple/pallas_call | solution.py:684
  87.8 9.1 %down.1 = f32[8,32768]{1,0:T(8,128)} custom-call(f32[5]{0:T(128)S(1)} %pad_maximum_fusion.scale_ref, s32[3,255]{1,0:T(4,128)S(1)} %bitcast.13, s32[4,3]{1,0:T(4,128)S(1)} %copy-done.10, bf16[4,2,64,64]{3,2,1,0:T(8,128)(2,1)S(1)} %copy-done.7, bf16[4,3,64,64]{3,2,1,0:T(8,128)(2,1)S(1)} %copy-done.6, bf16[7,64,128]{2,1,0:T(8,128)(2,1)S(1)} %get-tuple-element.30.wide_ref, ...), custom_call_target="tpu_custom_call" | custom-call | flops 629145600 | bytes 8388608 | tf_op jit(solution)/shard_map/down/pallas_call | solution.py:704
  (39 shorter events, 0.1 us)
Async XLA Ops:
  0.0 2.2 %collective-permute-start = (bf16[8,32768]{1,0:T(8,128)(2,1)}, bf16[8,32768]{1,0:T(8,128)(2,1)S(1)}, u32[]{:S(2)}, u32[]{:S(2)}) collective-permute-start(bf16[8,32768]{1,0:T(8,128)(2,1)} %refs_11_.1), channel_id=1, source_target_pairs={{0,1},{1,0},{2,3},{3,2},{4,5},{5,4},{6,7},{7,6},{8,9},{9,8},{10,11... | collective-permute-start | bytes 1572872 | tf_op jit(solution)/shard_map/ppermute | solution.py:600
  4.3 7.1 %copy-start.3 = (bf16[8,32768]{1,0:T(8,128)(2,1)S(1)}, bf16[8,32768]{1,0:T(8,128)(2,1)}, u32[]{:S(2)}) copy-start(bf16[8,32768]{1,0:T(8,128)(2,1)} %refs_11_.1) | copy-start | bytes 1572868
  5.2 53.6 %collective-permute-start.1 = (bf16[24,16384]{1,0:T(8,128)(2,1)S(1)}, bf16[24,16384]{1,0:T(8,128)(2,1)S(1)}, u32[]{:S(2)}, u32[]{:S(2)}) collective-permute-start(bf16[24,16384]{1,0:T(8,128)(2,1)S(1)} %pack.1.pack_ref), channel_id=1, source_target_pairs={{0,2},{2,4},{4,6},{6,8},{8,10},{10,12},{12,14},{1,3},{3,5},{5,7},{... | collective-permute-start | bytes 2359304 | tf_op jit(solution)/shard_map/ppermute | solution.py:635
  10.1 48.7 %collective-permute-start.2 = (bf16[24,16384]{1,0:T(8,128)(2,1)S(1)}, bf16[24,16384]{1,0:T(8,128)(2,1)S(1)}, u32[]{:S(2)}, u32[]{:S(2)}) collective-permute-start(bf16[24,16384]{1,0:T(8,128)(2,1)S(1)} %pack.1.pack_ref), channel_id=1, source_target_pairs={{2,0},{4,2},{6,4},{8,6},{10,8},{12,10},{14,12},{3,1},{5,3},{7,5},{... | collective-permute-start | bytes 2359304 | tf_op jit(solution)/shard_map/ppermute | solution.py:636
  11.4 2.2 %copy-start = (bf16[128,64,256]{2,1,0:T(8,128)(2,1)S(1)}, bf16[128,64,256]{2,1,0:T(8,128)(2,1)}, u32[]{:S(2)}) copy-start(bf16[128,64,256]{2,1,0:T(8,128)(2,1)} %refs_9_.1) | copy-start | bytes 12582916
  15.1 10.9 %copy-start.5 = (f32[3,32768]{1,0:T(4,128)S(1)}, f32[3,32768]{1,0:T(4,128)}, u32[]{:S(2)}) copy-start(f32[3,32768]{1,0:T(4,128)} %points_ref.1) | copy-start | bytes 1179652
  15.2 10.9 %copy-start.12 = (s32[512]{0:T(512)S(1)}, s32[512]{0:T(512)}, u32[]{:S(2)}) copy-start(s32[512]{0:T(512)} %cols_ref.1) | copy-start | bytes 6148
  15.2 10.9 %copy-start.13 = (s32[128]{0:T(128)S(1)}, s32[128]{0:T(128)}, u32[]{:S(2)}) copy-start(s32[128]{0:T(128)} %offs_ref.1) | copy-start | bytes 1540
  15.2 60.1 %slice-start = ((s8[6291456]{0:T(1024)(128)(4,1)}), s8[4194304]{0:T(1024)(128)(4,1)S(1)}, s32[]{:S(2)}) async-start(s8[6291456]{0:T(1024)(128)(4,1)} %bitcast.7), calls=%async_computation | async-start | bytes 8388608
  26.1 49.2 %slice-start.1 = ((s8[6291456]{0:T(1024)(128)(4,1)}), s8[2097152]{0:T(1024)(128)(4,1)S(1)}, s32[]{:S(2)}) async-start(s8[6291456]{0:T(1024)(128)(4,1)} %bitcast.7), calls=%async_computation.1 | async-start | bytes 4194304
  58.8 16.4 %copy-start.9 = (s32[255,3]{0,1:T(4,128)S(1)}, s32[255,3]{0,1:T(4,128)}, u32[]{:S(2)}) copy-start(s32[255,3]{0,1:T(4,128)} %param.22) | copy-start | bytes 9184
  62.6 25.1 %collective-permute-start.10 = (f32[8,32768]{1,0:T(8,128)S(1)}, f32[8,32768]{1,0:T(8,128)S(1)}, u32[]{:S(2)}, u32[]{:S(2)}) collective-permute-start(f32[8,32768]{1,0:T(8,128)S(1)} %get-tuple-element.34), channel_id=1, source_target_pairs={{0,1},{1,0},{2,3},{3,2},{4,5},{5,4},{6,7},{7,6},{8,9},{9,8},{10,11... | collective-permute-start | bytes 3145736 | tf_op jit(solution)/shard_map/ppermute | solution.py:679
  62.6 7.6 %collective-permute-start.3 = (bf16[7,16,128]{2,1,0:T(8,128)(2,1)S(1)}, bf16[7,16,128]{2,1,0:T(8,128)(2,1)S(1)}, u32[]{:S(2)}, u32[]{:S(2)}) collective-permute-start(bf16[7,16,128]{2,1,0:T(8,128)(2,1)S(1)} %get-tuple-element.20.refs_0_), channel_id=1, source_target_pairs={{0,2},{2,0},{4,6},{6,4},{8,10},{10,8},{12,14},{14,12},{1,3},{3,1},... | collective-permute-start | bytes 86024 | tf_op jit(solution)/shard_map/ppermute | solution.py:577
  64.5 6.0 %collective-permute-start.4 = (bf16[7,16,128]{2,1,0:T(8,128)(2,1)S(1)}, bf16[7,16,128]{2,1,0:T(8,128)(2,1)S(1)}, u32[]{:S(2)}, u32[]{:S(2)}) collective-permute-start(bf16[7,16,128]{2,1,0:T(8,128)(2,1)S(1)} %get-tuple-element.20.refs_0_), channel_id=1, source_target_pairs={{0,4},{2,6},{4,0},{6,2},{8,12},{10,14},{12,8},{14,10},{1,5},{3,7},... | collective-permute-start | bytes 86024 | tf_op jit(solution)/shard_map/ppermute | solution.py:577
  65.7 8.5 %collective-permute-start.5 = (bf16[7,16,128]{2,1,0:T(8,128)(2,1)S(1)}, bf16[7,16,128]{2,1,0:T(8,128)(2,1)S(1)}, u32[]{:S(2)}, u32[]{:S(2)}) collective-permute-start(bf16[7,16,128]{2,1,0:T(8,128)(2,1)S(1)} %get-tuple-element.20.refs_0_), channel_id=1, source_target_pairs={{0,6},{2,4},{4,2},{6,0},{8,14},{10,12},{12,10},{14,8},{1,7},{3,5},... | collective-permute-start | bytes 86024 | tf_op jit(solution)/shard_map/ppermute | solution.py:577
  66.9 20.7 %collective-permute-start.6 = (bf16[7,16,128]{2,1,0:T(8,128)(2,1)S(1)}, bf16[7,16,128]{2,1,0:T(8,128)(2,1)S(1)}, u32[]{:S(2)}, u32[]{:S(2)}) collective-permute-start(bf16[7,16,128]{2,1,0:T(8,128)(2,1)S(1)} %get-tuple-element.20.refs_0_), channel_id=1, source_target_pairs={{0,8},{2,10},{4,12},{6,14},{8,0},{10,2},{12,4},{14,6},{1,9},{3,11}... | collective-permute-start | bytes 86024 | tf_op jit(solution)/shard_map/ppermute | solution.py:577
  70.1 17.5 %collective-permute-start.7 = (bf16[7,16,128]{2,1,0:T(8,128)(2,1)S(1)}, bf16[7,16,128]{2,1,0:T(8,128)(2,1)S(1)}, u32[]{:S(2)}, u32[]{:S(2)}) collective-permute-start(bf16[7,16,128]{2,1,0:T(8,128)(2,1)S(1)} %get-tuple-element.20.refs_0_), channel_id=1, source_target_pairs={{0,10},{2,8},{4,14},{6,12},{8,2},{10,0},{12,6},{14,4},{1,11},{3,9}... | collective-permute-start | bytes 86024 | tf_op jit(solution)/shard_map/ppermute | solution.py:577
  70.5 17.1 %collective-permute-start.8 = (bf16[7,16,128]{2,1,0:T(8,128)(2,1)S(1)}, bf16[7,16,128]{2,1,0:T(8,128)(2,1)S(1)}, u32[]{:S(2)}, u32[]{:S(2)}) collective-permute-start(bf16[7,16,128]{2,1,0:T(8,128)(2,1)S(1)} %get-tuple-element.20.refs_0_), channel_id=1, source_target_pairs={{0,12},{2,14},{4,8},{6,10},{8,4},{10,6},{12,0},{14,2},{1,13},{3,15... | collective-permute-start | bytes 86024 | tf_op jit(solution)/shard_map/ppermute | solution.py:577
  74.3 13.4 %collective-permute-start.9 = (bf16[7,16,128]{2,1,0:T(8,128)(2,1)S(1)}, bf16[7,16,128]{2,1,0:T(8,128)(2,1)S(1)}, u32[]{:S(2)}, u32[]{:S(2)}) collective-permute-start(bf16[7,16,128]{2,1,0:T(8,128)(2,1)S(1)} %get-tuple-element.20.refs_0_), channel_id=1, source_target_pairs={{0,14},{2,12},{4,10},{6,8},{8,6},{10,4},{12,2},{14,0},{1,15},{3,13... | collective-permute-start | bytes 86024 | tf_op jit(solution)/shard_map/ppermute | solution.py:577
  75.3 12.5 %copy-start.1 = (bf16[128,64,256]{2,1,0:T(8,128)(2,1)S(1)}, bf16[128,64,256]{2,1,0:T(8,128)(2,1)}, u32[]{:S(2)}) copy-start(bf16[128,64,256]{2,1,0:T(8,128)(2,1)} %refs_9_.1) | copy-start | bytes 12582916
  75.3 12.5 %copy-start.6 = (bf16[4,3,64,64]{3,2,1,0:T(8,128)(2,1)S(1)}, bf16[4,3,64,64]{3,2,1,0:T(8,128)(2,1)}, u32[]{:S(2)}) copy-start(bf16[4,3,64,64]{3,2,1,0:T(8,128)(2,1)} %top_b.1) | copy-start | bytes 294916
  75.3 12.4 %copy-start.7 = (bf16[4,2,64,64]{3,2,1,0:T(8,128)(2,1)S(1)}, bf16[4,2,64,64]{3,2,1,0:T(8,128)(2,1)}, u32[]{:S(2)}) copy-start(bf16[4,2,64,64]{3,2,1,0:T(8,128)(2,1)} %top_e.1) | copy-start | bytes 196612
  75.3 12.4 %copy-start.8 = (f32[32768]{0:T(1024)S(1)}, f32[32768]{0:T(1024)}, u32[]{:S(2)}) copy-start(f32[32768]{0:T(1024)} %param.15) | copy-start | bytes 393220
  75.3 12.4 %copy-start.10 = (s32[4,3]{1,0:T(4,128)S(1)}, s32[4,3]{1,0:T(4,128)}, u32[]{:S(2)}) copy-start(s32[4,3]{1,0:T(4,128)} %top_partners_ref.1) | copy-start | bytes 148
  (3 other events, 3.7 us)

commit v4 on v3

--- a/solution.py
+++ b/solution.py
@@ -14,7 +14,8 @@
 RANK = 64
 SPAN = 3
 PART = 8
-EXPORT = 2**SPAN - 1
+ALL = 2 * PART
+EXPORT = 2**SPAN
 NEG_LOG2E = -1.0 / math.log(2.0)
 ROOT3 = math.sqrt(3.0)
 TINY = 1e-12
@@ -131,9 +132,9 @@
     def step(i, _):
         here = pl.ds(pl.multiple_of(i * 2048, 2048), 2048)
         rows = coordinate_rows(points[:, here], scale_ref)
-        out_ref[:, here] = jnp.concatenate(
-            [mine[:, here].astype(F32), got[:, here].astype(F32), rows], axis=0
-        ).astype(BF)
+        one, two = mine[:, here].astype(F32), got[:, here].astype(F32)
+        first, second = jnp.where(core == 0, one, two), jnp.where(core == 0, two, one)
+        out_ref[:, here] = jnp.concatenate([first, second, rows], axis=0).astype(BF)
         return 0
 
     lax.fori_loop(0, half // 2048, step, 0)
@@ -241,10 +242,11 @@
 
 
 def near_halo_kernel(
-    far_list, far_count, row_ref, left_ref, right_ref, mine_in, other_in,
+    scale_ref, far_list, far_count, row_ref, left_ref, right_ref, first_in, second_in,
     mine_ref, other_ref,
-    col_ref, val_ref, s0, s1, k0, k1,
+    first, second, col_ref, val_ref, s0, s1, k0, k1,
 ):
+    core = whole(scale_ref[4])
     half = left_ref.shape[1] // LEAF
     bits = half.bit_length() - 1
     count = far_count[0]
@@ -263,13 +265,23 @@
             col_ref[place(code)] = col_features(rows.astype(F32))
         return 0
 
-    mine_ref[...] = mine_in[...]
-    other_ref[...] = other_in[...]
+    first[...] = first_in[...]
+    second[...] = second_in[...]
     lax.fori_loop(0, (count + 3) // 4, load, 0)
     val_ref[2 * half] = jnp.zeros((16, LEAF), BF)
     col_ref[2 * half] = jnp.zeros(col_ref.shape[1:], BF)
-    sums = (mine_ref, other_ref)
+    sums = (first, second)
     block_loop(count, place, far_list, row_ref, col_ref, val_ref, sums, s0, s1, k0, k1)
+
+    @pl.when(core == 0)
+    def _():
+        mine_ref[...] = first[...]
+        other_ref[...] = second[...]
+
+    @pl.when(core == 1)
+    def _():
+        mine_ref[...] = second[...]
+        other_ref[...] = first[...]
 
 
 def split_parts(value):
@@ -278,7 +290,7 @@
 
 
 def join_parts(value):
-    return value[0:8] + value[8:16]
+    return value[0:ALL] + value[ALL : 2 * ALL]
 
 
 def mul_nt(left, right):
@@ -323,21 +335,24 @@
 
 
 def up_kernel(
-    vec_hbm, basis_hbm, raw_hbm, coef_ref, export_ref, move_ref,
-    vec_ref, basis_ref, raw_ref, flat, pairs, sems,
+    scale_ref, pack_ref, basis_hbm, raw_hbm, coef_ref, export_ref, move_ref,
+    basis_ref, raw_ref, flat, pairs, sems,
 ):
+    core = whole(scale_ref[4])
     leaves = basis_ref.shape[0]
+    levels = leaves.bit_length() - 1
     chunks = 4
     per = leaves // chunks
-    wide = per * LEAF
     deep = RANK // chunks
     copies = fetch(
         [
             pair
             for c in range(chunks)
             for pair in (
-                (vec_hbm.at[:, c * wide : (c + 1) * wide], vec_ref.at[:, c * wide : (c + 1) * wide]),
-                (basis_hbm.at[c * per : (c + 1) * per], basis_ref.at[c * per : (c + 1) * per]),
+                (
+                    basis_hbm.at[pl.ds(core * leaves + c * per, per)],
+                    basis_ref.at[c * per : (c + 1) * per],
+                ),
                 (
                     raw_hbm.at[:, c * deep : (c + 1) * deep],
                     raw_ref.at[:, c * deep : (c + 1) * deep],
@@ -346,7 +361,6 @@
         ],
         sems,
     )
-    levels = leaves.bit_length() - 1
 
     def keep(parent, first, second):
         pair = side_by_side(first, second)
@@ -359,9 +373,9 @@
         outs = []
         for q in range(8):
             leaf = it * 8 + q
-            outs.append(mul_nt(vec_ref[:, lanes(leaf)], basis_ref[leaf]))
-        for q in range(4):
-            r = it * 4 + q
+            outs.append(mul_nt(pack_ref[0:ALL, lanes(leaf)], basis_ref[leaf]))
+        for q in range(8):
+            r = it * 8 + q
             block = jnp.concatenate([raw_ref[0, r], raw_ref[1, r]], axis=0).astype(F32)
             store_turned(flat, r, block)
         for q in range(4):
@@ -369,38 +383,47 @@
         return 0
 
     for c in range(chunks):
-        for copy in copies[3 * c : 3 * c + 3]:
+        for copy in copies[2 * c : 2 * c + 2]:
             copy.wait()
         lax.fori_loop(c * per // 8, (c + 1) * per // 8, leaf_step, 0)
+    root_move = load_node(flat, 0)
+    move_ref[leaves - 1] = root_move
     for depth in range(levels - 1, 0, -1):
         first = 2**depth - 1
         above = 2 ** (depth - 1) - 1
-
-        def work(nodes, first=first, above=above):
+        start = 2 ** (depth + 1) - 1 + core * 2**depth
+
+        def work(nodes, first=first, above=above, start=start):
             outs = []
             for j in nodes:
                 for c in range(2):
-                    node = first + 2 * j + c
-                    move = load_node(flat, node)
-                    move_ref[node] = move
-                    outs.append(mul_nt(pairs[node], move))
+                    move = load_node(flat, start + 2 * j + c)
+                    move_ref[first + 2 * j + c] = move
+                    outs.append(mul_nt(pairs[first + 2 * j + c], move))
             for j, i in enumerate(nodes):
                 keep(above + i, join_parts(outs[2 * j]), join_parts(outs[2 * j + 1]))
 
         over_nodes(2 ** (depth - 1), 8, work)
-    move = load_node(flat, 0)
+    move = load_node(flat, 1 + core)
     move_ref[0] = move
-    root = join_parts(mul_nt(pairs[0], move))
-    coef_ref[0] = split_parts(side_by_side(root, root))
-    export_ref[...] = coef_ref[0:EXPORT]
+    crown = join_parts(mul_nt(pairs[0], move))
+    crown = split_parts(side_by_side(crown, crown))
+    coef_ref[0] = crown
+    side = lax.broadcasted_iota(jnp.int32, crown.shape, 1) // RANK
+    root = join_parts(mul_nt(jnp.where(side == core, crown.astype(F32), 0.0).astype(BF), root_move))
+    export_ref[0] = split_parts(side_by_side(root, root))
+    export_ref[1:EXPORT] = coef_ref[0 : EXPORT - 1]
+
+
+def joint(first, second, third):
+    return jnp.concatenate([first, second, third], axis=1)
 
 
 def couple_kernel(
-    scale_ref, partners_ref, coef_ref, raw_hbm, local_ref, wide_ref, thin_ref,
-    raw_ref, wide, thin, sems,
+    scale_ref, partners_ref, coef_ref, raw_hbm, local_ref, tie_ref, raw_ref, wide, thin, sems,
 ):
-    device = whole(scale_ref[3])
-    total = raw_ref.shape[3]
+    device, core = whole(scale_ref[3]), whole(scale_ref[4])
+    levels = (raw_ref.shape[3] + 1).bit_length() - 2
     chunks = 4
     deep = RANK // chunks
     copies = fetch(
@@ -410,13 +433,11 @@
         ],
         sems,
     )
-    span = total + 1
-    levels = span.bit_length() - 2
-    low = lax.broadcasted_iota(jnp.int32, (16, 2 * RANK), 1) < RANK
+    low = lax.broadcasted_iota(jnp.int32, (2 * ALL, 2 * RANK), 1) < RANK
 
     def turn(i, _):
-        for q in range(4):
-            r = i * 4 + q
+        for q in range(8):
+            r = i * 8 + q
             block = jnp.concatenate([raw_ref[0, r], raw_ref[1, r]], axis=0).astype(F32)
             store_turned(wide, r, block)
             store_turned(thin, r, raw_ref[2, r].astype(F32))
@@ -424,87 +445,84 @@
 
     for c in range(chunks):
         copies[c].wait()
-        lax.fori_loop(c * deep // 4, (c + 1) * deep // 4, turn, 0)
-    for node in range(EXPORT):
-        wide_ref[node] = load_node(wide, node)
-        thin_ref[node] = load_node(thin, node)
-    for depth in range(SPAN, levels + 1):
-        first = 2**depth - 1
-        above = 2 ** (depth - 1) - 1
-        shift = first - device * 2**depth
-
-        def work(nodes, first=first, above=above, shift=shift):
+        lax.fori_loop(c * deep // 8, (c + 1) * deep // 8, turn, 0)
+
+    def tie(node):
+        return jnp.concatenate([load_node(wide, node), load_node(thin, node)], axis=1)
+
+    tie_ref[0] = tie(0)
+    for depth in range(1, SPAN + 1):
+        for i in range(2 ** (depth - 1)):
+            tie_ref[2 ** (depth - 1) + i] = tie(2**depth - 1 + core * 2 ** (depth - 1) + i)
+    for depth in range(SPAN + 1, levels + 1):
+        half = 2 ** (depth - 1)
+        above = half // 2 - 1
+        start = 2**depth - 1 + core * half
+        shift = half - 1 - device * 2**depth - core * half
+
+        def work(nodes, above=above, start=start, shift=shift):
             outs = []
             for j in nodes:
                 for c in range(2):
-                    node = first + 2 * j + c
+                    node = start + 2 * j + c
                     mates = [coef_ref[partners_ref[f, node] + shift] for f in range(3)]
-                    left = jnp.where(low, mates[0], mates[1])
-                    outs.append(
-                        mul_nt(left, load_node(wide, node))
-                        + mul_nt(
-                            mates[2][:, :RANK],
-                            load_node(thin, node),
-                        )
+                    left = jnp.concatenate(
+                        [jnp.where(low, mates[0], mates[1]), mates[2][:, :RANK]], axis=1
                     )
+                    outs.append(mul_nt(left, tie(node)))
             for j, i in enumerate(nodes):
                 local_ref[above + i] = side_by_side(
                     join_parts(outs[2 * j]), join_parts(outs[2 * j + 1])
                 )
 
-        over_nodes(2 ** (depth - 1), 8, work)
+        over_nodes(half // 2, 8, work)
 
 
 def down_kernel(
-    dev_levels, scale_ref, partners_ref, top_partners_ref, top_e, top_b, wide_ref, thin_ref,
-    local_ref, move_ref, *refs,
+    dev_levels, scale_ref, partners_ref, top_partners_ref, top_e, top_b, tie_ref,
+    local_ref, move_ref, gather_ref, mine_ref, other_ref, down, tree,
 ):
-    exports, (basis_hbm, noise_hbm, vec_hbm, near_hbm, swap_hbm, out_hbm) = refs[:9], refs[9:15]
-    gather_ref, down, tree, low_ref, basis, noise, vec, near, swap, out, sems = refs[15:]
-    device = whole(scale_ref[3])
-    leaves = low_ref.shape[0]
+    device, core = whole(scale_ref[3]), whole(scale_ref[4])
+    leaves = mine_ref.shape[0]
     levels = leaves.bit_length() - 1
-    copies = fetch(
-        [
-            (basis_hbm, basis), (noise_hbm, noise), (vec_hbm, vec), (near_hbm, near),
-            (swap_hbm, swap),
-        ],
-        sems,
-    )
-    for i in range(2**SPAN):
-        gather_ref[i] = exports[i][...]
-    tops_ref = gather_ref if dev_levels == SPAN else exports[2**SPAN]
-    low = lax.broadcasted_iota(jnp.int32, (16, 2 * RANK), 1) < RANK
-
+    count = 2**dev_levels
+
+    def roots(nodes):
+        for i in nodes:
+            parts = join_parts(gather_ref[2 * i, 0].astype(F32)) + join_parts(
+                gather_ref[2 * i + 1, 0].astype(F32)
+            )
+            tree[count + i] = split_parts(parts[:, :RANK])
+
+    over_nodes(count, 8, roots)
     for level in range(dev_levels - 1, 1, -1):
 
         def work(nodes, level=level):
             outs = []
             for i in nodes:
                 row = 2**level - 4 + i
-                if level == dev_levels - 1:
-                    kids = [tops_ref[(2 * i + c) ^ device, 0][:, :RANK] for c in range(2)]
-                else:
-                    kids = [tree[2 ** (level + 1) + 2 * i + c] for c in range(2)]
+                kids = [tree[2 ** (level + 1) + 2 * i + c] for c in range(2)]
                 outs.append(mul_nt(kids[0], top_e[row, 0]) + mul_nt(kids[1], top_e[row, 1]))
             for i, out in zip(nodes, outs):
                 tree[2**level + i] = split_parts(join_parts(out))
 
         over_nodes(2**level, 4, work)
 
-    def near_root(node, depth):
-        mates = []
-        for f in range(3):
-            mate = partners_ref[f, node]
-            at = ((mate >> depth) ^ device) & (2**SPAN - 1)
-            mates.append(gather_ref[at, 2**depth - 1 + (mate & (2**depth - 1))])
-        left = jnp.where(low, mates[0], mates[1])
-        return join_parts(
-            mul_nt(left, wide_ref[node]) + mul_nt(mates[2][:, :RANK], thin_ref[node])
-        )
-
-    shallow = [near_root(node, (node + 1).bit_length() - 1) for node in range(EXPORT)]
-    pushed = jnp.zeros((PART, RANK), F32)
+    mates = [tree[count + partners_ref[f, 0]] for f in range(3)]
+    shallow = [join_parts(mul_nt(joint(*mates), tie_ref[0]))]
+    for depth in range(1, SPAN + 1):
+        half = 2 ** (depth - 1)
+        for i in range(half):
+            node = 2**depth - 1 + core * half + i
+            picks = []
+            for f in range(3):
+                mate = partners_ref[f, node]
+                picks.append(
+                    gather_ref[mate >> (depth - 1), half + (mate & (half - 1))][:, :RANK]
+                )
+            shallow.append(join_parts(mul_nt(joint(*picks), tie_ref[half + i])))
+
+    pushed = jnp.zeros((ALL, RANK), F32)
     for level in range(2, dev_levels):
         node = device >> (dev_levels - level)
         row = 2**level - 4 + node
@@ -515,7 +533,9 @@
         here = split_parts(join_parts(parts) + pushed)
         pushed = join_parts(jnp.dot(here, top_e[row, side], preferred_element_type=F32))
 
-    down[0] = split_parts(shallow[0] + pushed)
+    root = split_parts(shallow[0] + pushed)
+    both = join_parts(jnp.dot(root, move_ref[leaves - 1], preferred_element_type=F32))
+    down[0] = split_parts(shallow[1] + jnp.where(core == 0, both[:, :RANK], both[:, RANK:]))
     for depth in range(levels):
         first = 2**depth - 1
 
@@ -526,55 +546,61 @@
             ]
             for i, out in zip(nodes, outs):
                 node = first + i
-                if depth < SPAN - 1:
-                    base = side_by_side(shallow[2 * node + 1], shallow[2 * node + 2])
+                if depth + 2 <= SPAN:
+                    kid = 2 ** (depth + 1) + 2 * i
+                    base = side_by_side(shallow[kid], shallow[kid + 1])
                 else:
                     base = local_ref[node]
                 pair = base + join_parts(out)
                 if depth == levels - 1:
-                    low_ref[2 * i] = pair[:, :RANK].astype(BF)
-                    low_ref[2 * i + 1] = pair[:, RANK:].astype(BF)
+                    for c in range(2):
+                        value = pair[:, c * RANK : (c + 1) * RANK]
+                        one, two = value[:PART], value[PART:]
+                        mine_ref[2 * i + c] = jnp.where(core == 0, one, two).astype(BF)
+                        other_ref[2 * i + c] = jnp.where(core == 0, two, one).astype(BF)
                 else:
                     down[2 * node + 1] = split_parts(pair[:, :RANK])
                     down[2 * node + 2] = split_parts(pair[:, RANK:])
 
         if depth < SPAN:
-            first_nodes = list(range(2**depth))
-            work(first_nodes)
+            work(list(range(2**depth)))
         else:
             over_nodes(2**depth, 8, work)
 
-    for copy in copies:
-        copy.wait()
-    chunks = 4
+
+def final_kernel(
+    scale_ref, mine_ref, got_ref, basis, noise, vec, near, swap, out_hbm, out, sems
+):
+    core = whole(scale_ref[4])
+    leaves = mine_ref.shape[0]
+    chunks = 2
     per = leaves // chunks
     wide = per * LEAF
     sends = []
-    for c in range(chunks):
-
-        def last(nodes, c=c):
-            rows = [c * per + i for i in nodes]
-            fars = [jnp.dot(low_ref[n], basis[n], preferred_element_type=F32) for n in rows]
-            for n, far in zip(rows, fars):
-                here = lanes(n)
-                total = near[:, here] + swap[:, here]
-                out[:, here] = total + noise[:, here] * vec[:, here].astype(F32) + far
-
-        over_nodes(per, 8, last)
-        piece = slice(c * wide, (c + 1) * wide)
-        send = pltpu.make_async_copy(
-            out.at[:, piece], out_hbm.at[:, piece], sems.at[len(copies) + c]
-        )
-        send.start()
-        sends.append(send)
+    for part, low_ref in enumerate((mine_ref, got_ref)):
+        base = jnp.where(core == part, 0, leaves)
+        for c in range(chunks):
+
+            def last(nodes, c=c, low_ref=low_ref, base=base):
+                rows = [c * per + i for i in nodes]
+                fars = [
+                    jnp.dot(low_ref[n], basis[base + n], preferred_element_type=F32)
+                    for n in rows
+                ]
+                for n, far in zip(rows, fars):
+                    here = lanes(base + n)
+                    total = near[:, here] + swap[:, here]
+                    out[:, here] = total + noise[:, here] * vec[:, here].astype(F32) + far
+
+            over_nodes(per, 8, last)
+            piece = pl.ds(pl.multiple_of((base + c * per) * LEAF, wide), wide)
+            send = pltpu.make_async_copy(
+                out.at[:, piece], out_hbm.at[:, piece], sems.at[part * chunks + c]
+            )
+            send.start()
+            sends.append(send)
     for send in sends:
         send.wait()
-
-
-def swap_mask(value, mask):
-    leaf, sub = lax.axis_size("leaf"), lax.axis_size("sub")
-    pairs = [(i, i ^ mask) for i in range(leaf * sub)]
-    return lax.ppermute(value, ("leaf", "sub"), pairs)
 
 
 def body(
@@ -599,26 +625,6 @@
 
     got = lax.ppermute(vectors, "vec", [(0, 1), (1, 0)])
 
-    moves_raw = jnp.transpose(local_transfer, (1, 2, 3, 0))
-    coef, export, moves = pl.pallas_call(
-        up_kernel,
-        name="up",
-        out_shape=(
-            sds((2 * leaves - 1, 16, 2 * RANK), BF), sds((EXPORT, 16, 2 * RANK), BF),
-            sds((leaves - 1, RANK, 2 * RANK), BF),
-        ),
-        in_specs=[hspec()] * 3,
-        out_specs=(vspec(),) * 3,
-        scratch_shapes=[
-            VMEM(vectors.shape, BF), VMEM(leaf_basis.shape, BF), VMEM(moves_raw.shape, BF),
-            VMEM((leaves // 8, RANK * 8, 2 * RANK), F32), VMEM((leaves - 1, 16, 2 * RANK), BF),
-            pltpu.SemaphoreType.DMA((12,)),
-        ],
-        compiler_params=params(28),
-        cost_estimate=pl.CostEstimate(
-            flops=300 * 2 * 256 * 256 * 48, bytes_accessed=8 << 20, transcendentals=0
-        ),
-    )(vectors, leaf_basis, moves_raw)
     pack = pl.pallas_call(
         pack_kernel,
         name="pack",
@@ -635,8 +641,28 @@
     left = lax.ppermute(pack, axes, [(i, i + 1) for i in range(count - 1)])
     right = lax.ppermute(pack, axes, [(i + 1, i) for i in range(count - 1)])
 
+    moves_raw = jnp.transpose(local_transfer, (1, 2, 3, 0))
+    part = leaves // 2
+    coef, export, moves = pl.pallas_call(
+        up_kernel,
+        name="up",
+        out_shape=(
+            sds((2 * part - 1, 2 * ALL, 2 * RANK), BF), sds((EXPORT, 2 * ALL, 2 * RANK), BF),
+            sds((part, RANK, 2 * RANK), BF),
+        ),
+        in_specs=[sspec(), vspec(), hspec(), hspec()],
+        out_specs=(vspec(),) * 3,
+        scratch_shapes=[
+            VMEM((part, RANK, LEAF), BF), VMEM(moves_raw.shape, BF),
+            VMEM((leaves // 8, RANK * 8, 2 * RANK), F32),
+            VMEM((part - 1, 2 * ALL, 2 * RANK), BF), pltpu.SemaphoreType.DMA((8,)),
+        ],
+        compiler_params=params(28),
+        cost_estimate=pl.CostEstimate(flops=8 * 10**9, bytes_accessed=8 << 20, transcendentals=0),
+    )(scale, pack, leaf_basis, moves_raw)
+    gathered = lax.all_gather(export, ("leaf", "sub", "vec"))
     pack, _ = lax.optimization_barrier((pack, export))
-    mine, other, row_feat, far_list, far_count = pl.pallas_call(
+    first, second, row_feat, far_list, far_count = pl.pallas_call(
         near_local_kernel,
         name="near_local",
         out_shape=(
@@ -651,77 +677,72 @@
         ],
         compiler_params=params(28),
         cost_estimate=pl.CostEstimate(
-            flops=190 * 2 * 256 * 256 * 48, bytes_accessed=8 << 20, transcendentals=190 * 2**17
+            flops=36 * 10**9, bytes_accessed=8 << 20, transcendentals=190 * 2**17
         ),
     )(scale, near_offsets, near_cols, points, pack)
 
-    exports = [export] + [swap_mask(export, mask) for mask in range(1, 2**SPAN)]
-    tops = export[None]
-    for bit in range(SPAN, dev_levels):
-        if bit == SPAN:
-            tops = jnp.stack([part[0:1] for part in exports])
-        tops = jnp.concatenate([tops, swap_mask(tops, 2**bit)], axis=0)
     mine, other = pl.pallas_call(
         near_halo_kernel,
         name="near_halo",
         out_shape=(sds((PART, size), F32), sds((PART, size), F32)),
-        in_specs=[sspec(), sspec()] + [vspec()] * 5,
+        in_specs=[sspec()] * 3 + [vspec()] * 5,
         out_specs=(vspec(), vspec()),
         scratch_shapes=[
+            VMEM((PART, size), F32), VMEM((PART, size), F32),
             VMEM((leaves + 1, LEAF, 32), BF), VMEM((leaves + 1, 16, LEAF), BF),
             *scratch_blocks,
         ],
         compiler_params=params(36),
         cost_estimate=pl.CostEstimate(
-            flops=60 * 2 * 256 * 256 * 48, bytes_accessed=8 << 20, transcendentals=60 * 2**17
+            flops=4 * 10**9, bytes_accessed=8 << 20, transcendentals=60 * 2**17
         ),
-    )(far_list, far_count, row_feat, left, right, mine, other)
+    )(scale, far_list, far_count, row_feat, left, right, first, second)
     swapped = lax.ppermute(other, "vec", [(0, 1), (1, 0)])
 
     _, coef_late = lax.optimization_barrier((mine, coef))
     ties_raw = jnp.transpose(local_coupling, (1, 2, 3, 0))
     mates = jnp.transpose(local_partners)
-    local, wide, thin = pl.pallas_call(
+    local, ties = pl.pallas_call(
         couple_kernel,
         name="couple",
         out_shape=(
-            sds((leaves - 1, PART, 2 * RANK), F32), sds((EXPORT, RANK, 2 * RANK), BF),
-            sds((EXPORT, RANK, RANK), BF),
+            sds((part - 1, ALL, 2 * RANK), F32), sds((EXPORT, RANK, 3 * RANK), BF),
         ),
         in_specs=[sspec()] * 2 + [vspec(), hspec()],
-        out_specs=(vspec(),) * 3,
+        out_specs=(vspec(),) * 2,
         scratch_shapes=[
             VMEM(ties_raw.shape, BF),
             VMEM((leaves // 4, RANK * 8, 2 * RANK), F32),
             VMEM((leaves // 4, RANK * 8, RANK), F32), pltpu.SemaphoreType.DMA((4,)),
         ],
         compiler_params=params(36),
-        cost_estimate=pl.CostEstimate(
-            flops=300 * 2 * 256 * 256 * 48, bytes_accessed=8 << 20, transcendentals=0
-        ),
+        cost_estimate=pl.CostEstimate(flops=9 * 10**9, bytes_accessed=8 << 20, transcendentals=0),
     )(scale, mates, coef_late, ties_raw)
 
-    return pl.pallas_call(
+    low_mine, low_other = pl.pallas_call(
         functools.partial(down_kernel, dev_levels),
         name="down",
+        out_shape=(sds((part, PART, RANK), BF), sds((part, PART, RANK), BF)),
+        in_specs=[sspec()] * 3 + [vspec()] * 6,
+        out_specs=(vspec(), vspec()),
+        scratch_shapes=[
+            VMEM((part - 1, 2 * ALL, RANK), BF), VMEM((2 * count, 2 * ALL, RANK), BF),
+        ],
+        compiler_params=params(24),
+        cost_estimate=pl.CostEstimate(flops=4 * 10**9, bytes_accessed=4 << 20, transcendentals=0),
+    )(scale, mates, top_partners, top_transfer, top_coupling, ties, local, moves, gathered)
+    low_got = lax.ppermute(low_other, "vec", [(0, 1), (1, 0)])
+
+    return pl.pallas_call(
+        final_kernel,
+        name="final",
         out_shape=sds((PART, size), F32),
-        in_specs=[sspec()] * 3 + [vspec()] * 15 + [hspec()] * 5,
+        in_specs=[sspec()] + [vspec()] * 7,
         out_specs=hspec(),
-        scratch_shapes=[
-            VMEM((2**SPAN, EXPORT, 16, 2 * RANK), BF), VMEM((leaves - 1, 16, RANK), BF),
-            VMEM((count, 16, RANK), BF), VMEM((leaves, PART, RANK), BF),
-            VMEM(leaf_basis.shape, BF), VMEM((1, size), F32), VMEM(vectors.shape, BF),
-            VMEM((PART, size), F32), VMEM((PART, size), F32), VMEM((PART, size), F32),
-            pltpu.SemaphoreType.DMA((9,)),
-        ],
-        compiler_params=params(32),
-        cost_estimate=pl.CostEstimate(
-            flops=100 * 2 * 256 * 256 * 48, bytes_accessed=8 << 20, transcendentals=0
-        ),
-    )(
-        scale, mates, top_partners, top_transfer, top_coupling, wide, thin, local, moves,
-        *exports, tops, leaf_basis, noise.reshape(1, size), vectors, mine, swapped,
-    )
+        scratch_shapes=[VMEM((PART, size), F32), pltpu.SemaphoreType.DMA((4,))],
+        compiler_params=params(16),
+        cost_estimate=pl.CostEstimate(flops=2 * 10**9, bytes_accessed=4 << 20, transcendentals=0),
+    )(scale, low_mine, low_got, leaf_basis, noise.reshape(1, size), vectors, mine, swapped)
 
 
 def solution(mesh):

time: 97 us -> 103 us (1.062)
  between operations: 0.26 us -> 13.6 us
  local copies, waits for them, and re-layouts: 5.92 us -> 18.5 us
  starting transfers between devices: 19.2 us -> 7.16 us
  Pallas kernels: 69.7 us -> 60.2 us
    unnamed x32 -> x52, local copies, waits for them, and re-layouts: 5.92 us -> 18.5 us
    ppermute x7 -> x1, starting transfers between devices: 12.7 us -> 0.53 us  [body(): low_got = lax.ppermute(low_other, 'vec', [(0, 1), (1, 0)])]
    pallas_call x1, Pallas kernels: 9.08 us -> 3.61 us  [body(): pl.pallas_call(functools.partial(down_kernel, dev_levels), name='down', o...]
    pallas_call x2 -> x3, Pallas kernels: 23.2 us -> 17.8 us  [the longest x1 7.69 us: body(): pl.pallas_call(couple_kernel, name='couple', out_shape=(sds((part - 1, AL...]
    pallas_call x1, Pallas kernels: 3.74 us -> 5.04 us  [body(): pl.pallas_call(near_halo_kernel, name='near_halo', out_shape=(sds((PART,...]
  transfers between devices with their start and end apart: 11 -> 6, of which waited for: 1 -> 2; matrix products, arithmetic and copies ran while one was open for 1% -> 1% of each run, Pallas kernels for 58% -> 54%
where the time goes in v4:
time: 103 us; the launch traced here: 102 us
  Pallas kernels  60.2 us (58%)
  local copies, waits for them, and re-layouts  18.5 us (18%)
  between operations  13.6 us (13%)
  starting transfers between devices  7.16 us (7%)
  waiting for transfers between devices  1.95 us (2%)
    pallas_call x1, Pallas kernels, body(): pl.pallas_call(near_local_kernel, name='near_local', out_shape=(sds((PART...  32.7 us
    unnamed x52, local copies, waits for them, and re-layouts  18.5 us
    pallas_call x1, Pallas kernels, body(): pl.pallas_call(couple_kernel, name='couple', out_shape=(sds((part - 1, AL...  7.69 us
    pallas_call x1, Pallas kernels, body(): pl.pallas_call(up_kernel, name='up', out_shape=(sds((2 * part - 1, 2 * AL...  6.32 us
    pallas_call x1, Pallas kernels, body(): pl.pallas_call(near_halo_kernel, name='near_halo', out_shape=(sds((PART,...  5.04 us
    ppermute x1, starting transfers between devices, body(): left = lax.ppermute(pack, axes, [(i, i + 1) for i in range(count - 1)])  4.81 us
    pallas_call x1, Pallas kernels, body(): pl.pallas_call(final_kernel, name='final', out_shape=sds((PART, size), F3...  3.83 us
    pallas_call x1, Pallas kernels, body(): pl.pallas_call(functools.partial(down_kernel, dev_levels), name='down', o...  3.61 us
  transfers between devices with their start and end apart: 6, of which 2 were waited for; matrix products, arithmetic and copies ran while one was open for 1% of the time, Pallas kernels for 54%

profile of v4, /device:TPU:0, one launch (start us, length us, event | category | flops | bytes accessed | tf_op | source)
XLA Modules:
  0.0 102.3 jit_solution(7322450855192210032)
XLA Ops:
  7.8 0.9 collective-permute-done.got_hbm
  8.7 1.0 %copy-done.2 = bf16[8,32768]{1,0:T(8,128)(2,1)S(1)} copy-done((bf16[8,32768]{1,0:T(8,128)(2,1)S(1)}, bf16[8,32768]{1,0:T(8,128)(2,1)}, u32[]{:S(2)}) %copy-start.2) | copy-done | bytes 524312
  9.8 1.0 %copy-done.4 = f32[3,32768]{1,0:T(4,128)S(1)} copy-done((f32[3,32768]{1,0:T(4,128)S(1)}, f32[3,32768]{1,0:T(4,128)}, u32[]{:S(2)}) %copy-start.4) | copy-done | bytes 393240
  10.8 1.0 pack.1.pack_ref
  11.8 4.8 %collective-permute-start.1 = (bf16[24,16384]{1,0:T(8,128)(2,1)S(1)}, bf16[24,16384]{1,0:T(8,128)(2,1)S(1)}, u32[]{:S(2)}, u32[]{:S(2)}) collective-permute-start(bf16[24,16384]{1,0:T(8,128)(2,1)S(1)} %pack.1.pack_ref), channel_id=1, source_target_pairs={{0,2},{2,4},{4,6},{6,8},{8,10},{10,12},{12,14},{1,3},{3,5},{5,7},{... | collective-permute-start | bytes 2359304 | tf_op jit(solution)/shard_map/ppermute | solution.py:641
  16.6 1.3 %collective-permute-start.2 = (bf16[24,16384]{1,0:T(8,128)(2,1)S(1)}, bf16[24,16384]{1,0:T(8,128)(2,1)S(1)}, u32[]{:S(2)}, u32[]{:S(2)}) collective-permute-start(bf16[24,16384]{1,0:T(8,128)(2,1)S(1)} %pack.1.pack_ref), channel_id=1, source_target_pairs={{2,0},{4,2},{6,4},{8,6},{10,8},{12,10},{14,12},{3,1},{5,3},{7,5},{... | collective-permute-start | bytes 2359304 | tf_op jit(solution)/shard_map/ppermute | solution.py:642
  18.0 2.2 %copy-done = bf16[128,64,256]{2,1,0:T(8,128)(2,1)S(1)} copy-done((bf16[128,64,256]{2,1,0:T(8,128)(2,1)S(1)}, bf16[128,64,256]{2,1,0:T(8,128)(2,1)}, u32[]{:S(2)}) %copy-start) | copy-done | bytes 4194328
  20.1 1.6 %copy-done.8 = bf16[127,2,64,64]{0,3,2,1:T(8,128)(2,1)S(1)} copy-done((bf16[127,2,64,64]{0,3,2,1:T(8,128)(2,1)S(1)}, bf16[127,2,64,64]{0,3,2,1:T(8,128)(2,1)}, u32[]{:S(2)}) %copy-start.8) | copy-done | bytes 2080792
  21.7 6.3 %up.1 = (bf16[127,32,128]{2,1,0:T(8,128)(2,1)S(1)}, bf16[8,32,128]{2,1,0:T(8,128)(2,1)}, bf16[64,64,128]{2,1,0:T(8,128)(2,1)S(1)}) custom-call(f32[5]{0:T(128)S(1)} %pad_maximum_fusion.scale_ref, bf16[24,16384]{1,0:T(8,128)(2,1)S(1)} %pack.1.pack_ref, bf16[128,64,256]{2,1,0:T(8,128)(2,1)S(1)} %copy-done, bf16[2,64,64,127]{3,2,1,0:T(8,128)(2,1)S(1)} %bitcast.9), custom_call_target="tpu_custom_call" | custom-call | flops 8000000000 | bytes 8388608 | tf_op jit(solution)/shard_map/up/pallas_call | solution.py:646
  28.1 1.0 copy-done.18
  29.0 1.0 copy-done.22
  30.1 32.7 %near_local.1 = (f32[8,32768]{1,0:T(8,128)S(1)}, f32[8,32768]{1,0:T(8,128)S(1)}, bf16[128,32,256]{2,1,0:T(8,128)(2,1)S(1)}, s32[528]{0:T(1024)S(1)}, s32[1]{0:T(128)}) custom-call(f32[5]{0:T(128)S(1)} %pad_maximum_fusion.scale_ref, s32[128]{0:T(128)S(1)} %copy-done.17, s32[512]{0:T(512)S(1)} %copy-done.15, f32[3,32768]{1,0:T(4,128)S(1)} %copy-done.5, ...), custom_call_target="tpu_custom_call" | custom-call | flops 35999997952 | bytes 8388608 | tf_op jit(solution)/shard_map/near_local/pallas_call | solution.py:665
  62.8 0.9 copy-done.10
  63.7 1.1 %copy-done.11 = bf16[24,16384]{1,0:T(8,128)(2,1)S(1)} copy-done((bf16[24,16384]{1,0:T(8,128)(2,1)S(1)}, bf16[24,16384]{1,0:T(8,128)(2,1)}, u32[]{:S(2)}) %copy-start.11) | copy-done | bytes 786456
  64.8 5.0 %near_halo.1 = (f32[8,32768]{1,0:T(8,128)S(1)}, f32[8,32768]{1,0:T(8,128)S(1)}) custom-call(f32[5]{0:T(128)S(1)} %pad_maximum_fusion.scale_ref, s32[528]{0:T(1024)S(1)} %get-tuple-element.23.far_list, s32[1]{0:T(128)} %get-tuple-element.24.far_count, bf16[128,32,256]{2,1,0:T(8,128)(2,1)S(1)} %get-tuple-element.25.row_ref, ...), custom_call_target="tpu_custom_call" | custom-call | flops 4000000000 | bytes 8388608 | tf_op jit(solution)/shard_map/near_halo/pallas_call | solution.py:684
  70.0 2.8 %copy-done.7 = bf16[255,3,64,64]{0,3,2,1:T(8,128)(2,1)S(1)} copy-done((bf16[255,3,64,64]{0,3,2,1:T(8,128)(2,1)S(1)}, bf16[255,3,64,64]{0,3,2,1:T(8,128)(2,1)}, u32[]{:S(2)}) %copy-start.7) | copy-done | bytes 6266904
  72.8 7.7 %couple.1 = (f32[63,16,128]{2,1,0:T(8,128)S(1)}, bf16[8,64,192]{2,1,0:T(8,128)(2,1)S(1)}) custom-call(f32[5]{0:T(128)S(1)} %pad_maximum_fusion.scale_ref, s32[3,255]{1,0:T(4,128)S(1)} %bitcast.11, bf16[127,32,128]{2,1,0:T(8,128)(2,1)S(1)} %copy-done.23, bf16[3,64,64,255]{3,2,1,0:T(8,128)(2,1)S(1)} %bitcast.8), custom_call_target="tpu_custom_call" | custom-call | flops 8999999488 | bytes 8388608 | tf_op jit(solution)/shard_map/couple/pallas_call | solution.py:705
  82.0 1.2 %copy-done.9 = bf16[128,32,128]{2,1,0:T(8,128)(2,1)S(1)} copy-done((bf16[128,32,128]{2,1,0:T(8,128)(2,1)S(1)}, bf16[128,32,128]{2,1,0:T(8,128)(2,1)}, u32[]{:S(2)}) %copy-start.9) | copy-done | bytes 1048600
  83.2 1.2 %copy-done.19 = bf16[64,64,128]{2,1,0:T(8,128)(2,1)S(1)} copy-done((bf16[64,64,128]{2,1,0:T(8,128)(2,1)S(1)}, bf16[64,64,128]{2,1,0:T(8,128)(2,1)}, u32[]{:S(2)}) %copy-start.19) | copy-done | bytes 1048600
  84.4 1.0 %copy-done.21 = f32[63,16,128]{2,1,0:T(8,128)S(1)} copy-done((f32[63,16,128]{2,1,0:T(8,128)S(1)}, f32[63,16,128]{2,1,0:T(8,128)}, u32[]{:S(2)}) %copy-start.21) | copy-done | bytes 516120
  85.5 0.9 copy-done.25
  86.4 3.6 %down.1 = (bf16[64,8,64]{2,1,0:T(8,128)(2,1)S(1)}, bf16[64,8,64]{2,1,0:T(8,128)(2,1)S(1)}) custom-call(f32[5]{0:T(128)S(1)} %pad_maximum_fusion.scale_ref, s32[3,255]{1,0:T(4,128)S(1)} %bitcast.12, s32[4,3]{1,0:T(4,128)S(1)} %copy-done.16, bf16[4,2,64,64]{3,2,1,0:T(8,128)(2,1)S(1)} %copy-done.13, bf16[4,3,64,64]{3,2,1,0:T(8,128)(2,1)S(1)} %copy-done.12, ...), custom_call_target="tpu_custom_call" | custom-call | flops 4000000000 | bytes 4194304 | tf_op jit(solution)/shard_map/down/pallas_call | solution.py:722
  90.6 1.0 collective-permute-done.3.got_ref
  91.6 3.8 %final.1 = f32[8,32768]{1,0:T(8,128)} custom-call(f32[5]{0:T(128)S(1)} %pad_maximum_fusion.scale_ref, bf16[64,8,64]{2,1,0:T(8,128)(2,1)S(1)} %get-tuple-element.34.mine_ref, bf16[64,8,64]{2,1,0:T(8,128)(2,1)S(1)} %collective-permute-done.3.got_ref, bf16[128,64,256]{2,1,0:T(8,128)(2,1)S(1)} %copy-done.1, f32[1,32768]{1,0:T(1,128)S(1)} %bitcast.7, ...), custom_call_target="tpu_custom_call" | custom-call | flops 2000000000 | bytes 4194304 | tf_op jit(solution)/shard_map/final/pallas_call | solution.py:736
  (50 shorter events, 3.4 us)
Async XLA Ops:
  6.5 75.4 %all-gather.3.cloned.1.call-start = ((), (), s32[]{:S(2)}) async-start(), calls=%async_computation | async-start | bytes 1114112 | tf_op jit(solution)/shard_map/all_gather | solution.py:663
  6.5 2.2 %collective-permute-start = (bf16[8,32768]{1,0:T(8,128)(2,1)}, bf16[8,32768]{1,0:T(8,128)(2,1)S(1)}, u32[]{:S(2)}, u32[]{:S(2)}) collective-permute-start(bf16[8,32768]{1,0:T(8,128)(2,1)} %vec.1), channel_id=1, source_target_pairs={{0,1},{1,0},{2,3},{3,2},{4,5},{5,4},{6,7},{7,6},{8,9},{9,8},{10,11... | collective-permute-start | bytes 1572872 | tf_op jit(solution)/shard_map/ppermute | solution.py:626
  8.7 1.0 %copy-start.2 = (bf16[8,32768]{1,0:T(8,128)(2,1)S(1)}, bf16[8,32768]{1,0:T(8,128)(2,1)}, u32[]{:S(2)}) copy-start(bf16[8,32768]{1,0:T(8,128)(2,1)} %vec.1) | copy-start | bytes 1572868
  11.8 51.0 %collective-permute-start.1 = (bf16[24,16384]{1,0:T(8,128)(2,1)S(1)}, bf16[24,16384]{1,0:T(8,128)(2,1)S(1)}, u32[]{:S(2)}, u32[]{:S(2)}) collective-permute-start(bf16[24,16384]{1,0:T(8,128)(2,1)S(1)} %pack.1.pack_ref), channel_id=1, source_target_pairs={{0,2},{2,4},{4,6},{6,8},{8,10},{10,12},{12,14},{1,3},{3,5},{5,7},{... | collective-permute-start | bytes 2359304 | tf_op jit(solution)/shard_map/ppermute | solution.py:641
  16.6 46.1 %collective-permute-start.2 = (bf16[24,16384]{1,0:T(8,128)(2,1)S(1)}, bf16[24,16384]{1,0:T(8,128)(2,1)S(1)}, u32[]{:S(2)}, u32[]{:S(2)}) collective-permute-start(bf16[24,16384]{1,0:T(8,128)(2,1)S(1)} %pack.1.pack_ref), channel_id=1, source_target_pairs={{2,0},{4,2},{6,4},{8,6},{10,8},{12,10},{14,12},{3,1},{5,3},{7,5},{... | collective-permute-start | bytes 2359304 | tf_op jit(solution)/shard_map/ppermute | solution.py:642
  17.9 2.2 %copy-start = (bf16[128,64,256]{2,1,0:T(8,128)(2,1)S(1)}, bf16[128,64,256]{2,1,0:T(8,128)(2,1)}, u32[]{:S(2)}) copy-start(bf16[128,64,256]{2,1,0:T(8,128)(2,1)} %basis.1) | copy-start | bytes 12582916
  20.1 1.6 %copy-start.8 = (bf16[127,2,64,64]{0,3,2,1:T(8,128)(2,1)S(1)}, bf16[127,2,64,64]{0,3,2,1:T(8,128)(2,1)}, u32[]{:S(2)}) copy-start(bf16[127,2,64,64]{0,3,2,1:T(8,128)(2,1)} %param.18) | copy-start | bytes 6242308
  21.7 8.3 %copy-start.5 = (f32[3,32768]{1,0:T(4,128)S(1)}, f32[3,32768]{1,0:T(4,128)}, u32[]{:S(2)}) copy-start(f32[3,32768]{1,0:T(4,128)} %points_ref.1) | copy-start | bytes 1179652
  21.7 8.3 %copy-start.15 = (s32[512]{0:T(512)S(1)}, s32[512]{0:T(512)}, u32[]{:S(2)}) copy-start(s32[512]{0:T(512)} %cols_ref.1) | copy-start | bytes 6148
  21.7 8.3 %copy-start.17 = (s32[128]{0:T(128)S(1)}, s32[128]{0:T(128)}, u32[]{:S(2)}) copy-start(s32[128]{0:T(128)} %offs_ref.1) | copy-start | bytes 1540
  63.7 1.1 %copy-start.11 = (bf16[24,16384]{1,0:T(8,128)(2,1)S(1)}, bf16[24,16384]{1,0:T(8,128)(2,1)}, u32[]{:S(2)}) copy-start(bf16[24,16384]{1,0:T(8,128)(2,1)} %copy-done.10) | copy-start | bytes 2359300
  64.8 5.1 %copy-start.14 = (s32[255,3]{0,1:T(4,128)S(1)}, s32[255,3]{0,1:T(4,128)}, u32[]{:S(2)}) copy-start(s32[255,3]{0,1:T(4,128)} %param.22) | copy-start | bytes 9184
  64.8 5.1 %copy-start.23 = (bf16[127,32,128]{2,1,0:T(8,128)(2,1)S(1)}, bf16[127,32,128]{2,1,0:T(8,128)(2,1)}, u32[]{:S(2)}) copy-start(bf16[127,32,128]{2,1,0:T(8,128)(2,1)} %copy-done.22) | copy-start | bytes 3121156
  69.9 20.7 %collective-permute-start.4 = (f32[8,32768]{1,0:T(8,128)S(1)}, f32[8,32768]{1,0:T(8,128)S(1)}, u32[]{:S(2)}, u32[]{:S(2)}) collective-permute-start(f32[8,32768]{1,0:T(8,128)S(1)} %get-tuple-element.36), channel_id=1, source_target_pairs={{0,1},{1,0},{2,3},{3,2},{4,5},{5,4},{6,7},{7,6},{8,9},{9,8},{10,11... | collective-permute-start | bytes 3145736 | tf_op jit(solution)/shard_map/ppermute | solution.py:700
  70.0 2.8 %copy-start.7 = (bf16[255,3,64,64]{0,3,2,1:T(8,128)(2,1)S(1)}, bf16[255,3,64,64]{0,3,2,1:T(8,128)(2,1)}, u32[]{:S(2)}) copy-start(bf16[255,3,64,64]{0,3,2,1:T(8,128)(2,1)} %param.20) | copy-start | bytes 18800644
  72.8 9.2 %copy-start.12 = (bf16[4,3,64,64]{3,2,1,0:T(8,128)(2,1)S(1)}, bf16[4,3,64,64]{3,2,1,0:T(8,128)(2,1)}, u32[]{:S(2)}) copy-start(bf16[4,3,64,64]{3,2,1,0:T(8,128)(2,1)} %top_b.1) | copy-start | bytes 294916
  72.8 9.2 %copy-start.13 = (bf16[4,2,64,64]{3,2,1,0:T(8,128)(2,1)S(1)}, bf16[4,2,64,64]{3,2,1,0:T(8,128)(2,1)}, u32[]{:S(2)}) copy-start(bf16[4,2,64,64]{3,2,1,0:T(8,128)(2,1)} %top_e.1) | copy-start | bytes 196612
  72.8 9.2 %copy-start.16 = (s32[4,3]{1,0:T(4,128)S(1)}, s32[4,3]{1,0:T(4,128)}, u32[]{:S(2)}) copy-start(s32[4,3]{1,0:T(4,128)} %top_partners_ref.1) | copy-start | bytes 148
  82.0 1.2 %copy-start.9 = (bf16[128,32,128]{2,1,0:T(8,128)(2,1)S(1)}, bf16[128,32,128]{2,1,0:T(8,128)(2,1)}, u32[]{:S(2)}) copy-start(bf16[128,32,128]{2,1,0:T(8,128)(2,1)} %all-gather.3.cloned.1.call-done) | copy-start | bytes 3145732
  83.2 1.2 %copy-start.19 = (bf16[64,64,128]{2,1,0:T(8,128)(2,1)S(1)}, bf16[64,64,128]{2,1,0:T(8,128)(2,1)}, u32[]{:S(2)}) copy-start(bf16[64,64,128]{2,1,0:T(8,128)(2,1)} %copy-done.18) | copy-start | bytes 3145732
  86.4 5.1 %copy-start.1 = (bf16[128,64,256]{2,1,0:T(8,128)(2,1)S(1)}, bf16[128,64,256]{2,1,0:T(8,128)(2,1)}, u32[]{:S(2)}) copy-start(bf16[128,64,256]{2,1,0:T(8,128)(2,1)} %basis.1) | copy-start | bytes 12582916
  86.4 5.1 %copy-start.3 = (bf16[8,32768]{1,0:T(8,128)(2,1)S(1)}, bf16[8,32768]{1,0:T(8,128)(2,1)}, u32[]{:S(2)}) copy-start(bf16[8,32768]{1,0:T(8,128)(2,1)} %vec.1) | copy-start | bytes 1572868
  86.4 5.1 %copy-start.6 = (f32[32768]{0:T(1024)S(1)}, f32[32768]{0:T(1024)}, u32[]{:S(2)}) copy-start(f32[32768]{0:T(1024)} %param.15) | copy-start | bytes 393220
  90.0 1.5 %collective-permute-start.3 = (bf16[64,8,64]{2,1,0:T(8,128)(2,1)S(1)}, bf16[64,8,64]{2,1,0:T(8,128)(2,1)S(1)}, u32[]{:S(2)}, u32[]{:S(2)}) collective-permute-start(bf16[64,8,64]{2,1,0:T(8,128)(2,1)S(1)} %get-tuple-element.35), channel_id=1, source_target_pairs={{0,1},{1,0},{2,3},{3,2},{4,5},{5,4},{6,7},{7,6},{8,9},{9,8},{10,11... | collective-permute-start | bytes 196616 | tf_op jit(solution)/shard_map/ppermute | solution.py:734
  (8 other events, 7.4 us)
Sparse Core Ops, SparseCore 0:
  30.2 40.6 all-gather.2

commit v5 on v4

--- a/solution.py
+++ b/solution.py
@@ -480,17 +480,25 @@
 
 def down_kernel(
     dev_levels, scale_ref, partners_ref, top_partners_ref, top_e, top_b, tie_ref,
-    local_ref, move_ref, gather_ref, mine_ref, other_ref, down, tree,
+    local_ref, move_ref, own_ref, core_ref, next_ref, far_refs, tops_ref, mine_ref, other_ref,
+    gather_ref, down, tree,
 ):
     device, core = whole(scale_ref[3]), whole(scale_ref[4])
+    self_id = 2 * device + core
+    gather_ref[0] = own_ref[...]
+    gather_ref[1] = core_ref[...]
+    gather_ref[2:4, 0:4] = next_ref[...]
+    for i, far_ref in enumerate(far_refs):
+        gather_ref[4 * i + 4 : 4 * i + 8, 0:2] = far_ref[...]
+    root_ref = gather_ref if dev_levels == SPAN else tops_ref
     leaves = mine_ref.shape[0]
     levels = leaves.bit_length() - 1
     count = 2**dev_levels
 
     def roots(nodes):
         for i in nodes:
-            parts = join_parts(gather_ref[2 * i, 0].astype(F32)) + join_parts(
-                gather_ref[2 * i + 1, 0].astype(F32)
+            parts = join_parts(root_ref[(2 * i) ^ self_id, 0].astype(F32)) + join_parts(
+                root_ref[(2 * i + 1) ^ self_id, 0].astype(F32)
             )
             tree[count + i] = split_parts(parts[:, :RANK])
 
@@ -517,9 +525,8 @@
             picks = []
             for f in range(3):
                 mate = partners_ref[f, node]
-                picks.append(
-                    gather_ref[mate >> (depth - 1), half + (mate & (half - 1))][:, :RANK]
-                )
+                at = ((mate >> (depth - 1)) ^ self_id) & (2 * 2**SPAN - 1)
+                picks.append(gather_ref[at, half + (mate & (half - 1))][:, :RANK])
             shallow.append(join_parts(mul_nt(joint(*picks), tie_ref[half + i])))
 
     pushed = jnp.zeros((ALL, RANK), F32)
@@ -603,6 +610,15 @@
         send.wait()
 
 
+def swap_mask(value, mask):
+    total = lax.axis_size("leaf") * lax.axis_size("sub")
+    return lax.ppermute(value, ("leaf", "sub"), [(i, i ^ mask) for i in range(total)])
+
+
+def after(value, anchor):
+    return lax.optimization_barrier((value, anchor))[0]
+
+
 def body(
     points, inv_scale, noise, vectors, leaf_basis, local_transfer, top_transfer,
     local_coupling, top_coupling, local_partners, top_partners, near_offsets, near_cols,
@@ -660,7 +676,7 @@
         compiler_params=params(28),
         cost_estimate=pl.CostEstimate(flops=8 * 10**9, bytes_accessed=8 << 20, transcendentals=0),
     )(scale, pack, leaf_basis, moves_raw)
-    gathered = lax.all_gather(export, ("leaf", "sub", "vec"))
+    from_core = lax.ppermute(export, "vec", [(0, 1), (1, 0)])
     pack, _ = lax.optimization_barrier((pack, export))
     first, second, row_feat, far_list, far_count = pl.pallas_call(
         near_local_kernel,
@@ -681,25 +697,10 @@
         ),
     )(scale, near_offsets, near_cols, points, pack)
 
-    mine, other = pl.pallas_call(
-        near_halo_kernel,
-        name="near_halo",
-        out_shape=(sds((PART, size), F32), sds((PART, size), F32)),
-        in_specs=[sspec()] * 3 + [vspec()] * 5,
-        out_specs=(vspec(), vspec()),
-        scratch_shapes=[
-            VMEM((PART, size), F32), VMEM((PART, size), F32),
-            VMEM((leaves + 1, LEAF, 32), BF), VMEM((leaves + 1, 16, LEAF), BF),
-            *scratch_blocks,
-        ],
-        compiler_params=params(36),
-        cost_estimate=pl.CostEstimate(
-            flops=4 * 10**9, bytes_accessed=8 << 20, transcendentals=60 * 2**17
-        ),
-    )(scale, far_list, far_count, row_feat, left, right, first, second)
-    swapped = lax.ppermute(other, "vec", [(0, 1), (1, 0)])
-
-    _, coef_late = lax.optimization_barrier((mine, coef))
+    from_core = after(from_core, far_list)
+    near_pair = jnp.stack([export[0:4], from_core[0:4]])
+    from_next = swap_mask(near_pair, 1)
+    coef_late = after(coef, far_list)
     ties_raw = jnp.transpose(local_coupling, (1, 2, 3, 0))
     mates = jnp.transpose(local_partners)
     local, ties = pl.pallas_call(
@@ -719,18 +720,53 @@
         cost_estimate=pl.CostEstimate(flops=9 * 10**9, bytes_accessed=8 << 20, transcendentals=0),
     )(scale, mates, coef_late, ties_raw)
 
+    from_next = after(from_next, local)
+    quad = jnp.concatenate([near_pair[:, 0:2], from_next[:, 0:2]], axis=0)
+    from_far = [swap_mask(quad, mask) for mask in (2, 4, 6)]
+    first = after(first, local)
+    mine, other = pl.pallas_call(
+        near_halo_kernel,
+        name="near_halo",
+        out_shape=(sds((PART, size), F32), sds((PART, size), F32)),
+        in_specs=[sspec()] * 3 + [vspec()] * 5,
+        out_specs=(vspec(), vspec()),
+        scratch_shapes=[
+            VMEM((PART, size), F32), VMEM((PART, size), F32),
+            VMEM((leaves + 1, LEAF, 32), BF), VMEM((leaves + 1, 16, LEAF), BF),
+            *scratch_blocks,
+        ],
+        compiler_params=params(36),
+        cost_estimate=pl.CostEstimate(
+            flops=4 * 10**9, bytes_accessed=8 << 20, transcendentals=60 * 2**17
+        ),
+    )(scale, far_list, far_count, row_feat, left, right, first, second)
+    swapped = lax.ppermute(other, "vec", [(0, 1), (1, 0)])
+
+    tops = export[None, 0:1]
+    if dev_levels > SPAN:
+        tops = jnp.concatenate(
+            [export[None, 0:1], from_core[None, 0:1], from_next[:, 0:1]]
+            + [part[:, 0:1] for part in from_far],
+            axis=0,
+        )
+        for bit in range(SPAN, dev_levels):
+            tops = jnp.concatenate([tops, swap_mask(tops, 2**bit)], axis=0)
     low_mine, low_other = pl.pallas_call(
-        functools.partial(down_kernel, dev_levels),
+        lambda *refs: down_kernel(dev_levels, *refs[:11], refs[11:14], *refs[14:]),
         name="down",
         out_shape=(sds((part, PART, RANK), BF), sds((part, PART, RANK), BF)),
-        in_specs=[sspec()] * 3 + [vspec()] * 6,
+        in_specs=[sspec()] * 3 + [vspec()] * 12,
         out_specs=(vspec(), vspec()),
         scratch_shapes=[
+            VMEM((2 * 2**SPAN, EXPORT, 2 * ALL, 2 * RANK), BF),
             VMEM((part - 1, 2 * ALL, RANK), BF), VMEM((2 * count, 2 * ALL, RANK), BF),
         ],
         compiler_params=params(24),
         cost_estimate=pl.CostEstimate(flops=4 * 10**9, bytes_accessed=4 << 20, transcendentals=0),
-    )(scale, mates, top_partners, top_transfer, top_coupling, ties, local, moves, gathered)
+    )(
+        scale, mates, top_partners, top_transfer, top_coupling, ties, local, moves,
+        export, from_core, from_next, *from_far, tops,
+    )
     low_got = lax.ppermute(low_other, "vec", [(0, 1), (1, 0)])
 
     return pl.pallas_call(

time: 103 us -> 92.1 us (0.89)
  between operations: 13.6 us -> 0.29 us
  local copies, waits for them, and re-layouts: 18.5 us -> 5.94 us
  waiting for transfers between devices: 1.95 us -> 10.2 us
  starting transfers between devices: 7.16 us -> 15.3 us
  Pallas kernels: 60.2 us -> 58.7 us
    unnamed x52 -> x32, local copies, waits for them, and re-layouts: 18.5 us -> 5.92 us
    ppermute x0 -> x5, starting transfers between devices: none -> 8.55 us  [the longest x4 8.11 us: swap_mask(): lax.ppermute(value, ('leaf', 'sub'), [(i, i ^ mask) for i in range(total)])]
    ppermute x0 -> x5, waiting for transfers between devices: none -> 7.97 us  [the longest x4 7.96 us: swap_mask(): lax.ppermute(value, ('leaf', 'sub'), [(i, i ^ mask) for i in range(total)])]
  transfers between devices with their start and end apart: 6 -> 10, of which waited for: 2 -> 5; matrix products, arithmetic and copies ran while one was open for 1% -> 1% of each run, Pallas kernels for 54% -> 48%
where the time goes in v5:
time: 92.1 us; the launch traced here: 91.3 us
  Pallas kernels  58.7 us (64%)
  starting transfers between devices  15.3 us (17%)
  waiting for transfers between devices  10.2 us (11%)
  local copies, waits for them, and re-layouts  5.94 us (6%)
    pallas_call x1, Pallas kernels, body(): pl.pallas_call(near_local_kernel, name='near_local', out_shape=(sds((PART...  32.7 us
    ppermute x4, starting transfers between devices, swap_mask(): lax.ppermute(value, ('leaf', 'sub'), [(i, i ^ mask) for i in range(total)])  8.11 us
    ppermute x4, waiting for transfers between devices, swap_mask(): lax.ppermute(value, ('leaf', 'sub'), [(i, i ^ mask) for i in range(total)])  7.96 us
    pallas_call x1, Pallas kernels, body(): pl.pallas_call(couple_kernel, name='couple', out_shape=(sds((part - 1, AL...  7.7 us
    unnamed x32, local copies, waits for them, and re-layouts  5.92 us
    pallas_call x1, Pallas kernels, body(): pl.pallas_call(up_kernel, name='up', out_shape=(sds((2 * part - 1, 2 * AL...  5.71 us
    ppermute x1, starting transfers between devices, body(): left = lax.ppermute(pack, axes, [(i, i + 1) for i in range(count - 1)])  4.84 us
    pallas_call x1, Pallas kernels, body(): pl.pallas_call(near_halo_kernel, name='near_halo', out_shape=(sds((PART,...  4.1 us
  transfers between devices with their start and end apart: 10, of which 5 were waited for; matrix products, arithmetic and copies ran while one was open for 1% of the time, Pallas kernels for 48%

profile of v5, /device:TPU:0, one launch (start us, length us, event | category | flops | bytes accessed | tf_op | source)
XLA Modules:
  0.0 91.3 jit_solution(11316922161076557108)
XLA Ops:
  0.0 0.5 collective-permute-start
  0.5 0.7 pad_maximum_fusion.2.scale_ref.refs_0_
  1.3 0.9 %collective-permute-done.got_hbm = bf16[8,32768]{1,0:T(8,128)(2,1)S(1)} collective-permute-done((bf16[8,32768]{1,0:T(8,128)(2,1)}, bf16[8,32768]{1,0:T(8,128)(2,1)S(1)}, u32[]{:S(2)}, u32[]{:S(2)}) %collective-permute-start) | collective-permute-done | bytes 524320 | tf_op jit(solution)/shard_map/ppermute | solution.py:642
  2.2 1.0 %copy-done.2 = bf16[8,32768]{1,0:T(8,128)(2,1)S(1)} copy-done((bf16[8,32768]{1,0:T(8,128)(2,1)S(1)}, bf16[8,32768]{1,0:T(8,128)(2,1)}, u32[]{:S(2)}) %copy-start.2) | copy-done | bytes 524312
  3.2 1.0 %copy-done.4 = f32[3,32768]{1,0:T(4,128)S(1)} copy-done((f32[3,32768]{1,0:T(4,128)S(1)}, f32[3,32768]{1,0:T(4,128)}, u32[]{:S(2)}) %copy-start.4) | copy-done | bytes 393240
  4.3 1.0 %pack.1.pack_ref = bf16[24,16384]{1,0:T(8,128)(2,1)S(1)} custom-call(f32[5]{0:T(128)S(1)} %pad_maximum_fusion.2.scale_ref.refs_0_, f32[3,32768]{1,0:T(4,128)S(1)} %copy-done.4, bf16[8,32768]{1,0:T(8,128)(2,1)S(1)} %copy-done.2, bf16[8,32768]{1,0:T(8,128)(2,1)S(1)} %collective-permute-done.got_hbm), custom_call_target="tpu_custom_call" | custom-call | tf_op jit(solution)/shard_map/pack/pallas_call | solution.py:644
  5.3 2.2 %copy-done = bf16[128,64,256]{2,1,0:T(8,128)(2,1)S(1)} copy-done((bf16[128,64,256]{2,1,0:T(8,128)(2,1)S(1)}, bf16[128,64,256]{2,1,0:T(8,128)(2,1)}, u32[]{:S(2)}) %copy-start) | copy-done | bytes 4194328
  7.5 1.6 %copy-done.7 = bf16[127,2,64,64]{0,3,2,1:T(8,128)(2,1)S(1)} copy-done((bf16[127,2,64,64]{0,3,2,1:T(8,128)(2,1)S(1)}, bf16[127,2,64,64]{0,3,2,1:T(8,128)(2,1)}, u32[]{:S(2)}) %copy-start.7) | copy-done | bytes 2080792
  9.1 5.7 %up.1 = (bf16[127,32,128]{2,1,0:T(8,128)(2,1)S(1)}, bf16[8,32,128]{2,1,0:T(8,128)(2,1)S(1)}, bf16[64,64,128]{2,1,0:T(8,128)(2,1)S(1)}) custom-call(f32[5]{0:T(128)S(1)} %pad_maximum_fusion.2.scale_ref.refs_0_, bf16[24,16384]{1,0:T(8,128)(2,1)S(1)} %pack.1.pack_ref, bf16[128,64,256]{2,1,0:T(8,128)(2,1)S(1)} %copy-done, bf16[2,64,64,127]{3,2,1,0:T(8,128)(2,1)S(1)} %bitcast.16), custom_call_target="tpu_custom_call" | custom-call | flops 8000000000 | bytes 8388608 | tf_op jit(solution)/shard_map/up/pallas_call | solution.py:662
  15.3 4.8 %collective-permute-start.7 = (bf16[24,16384]{1,0:T(8,128)(2,1)S(1)}, bf16[24,16384]{1,0:T(8,128)(2,1)S(1)}, u32[]{:S(2)}, u32[]{:S(2)}) collective-permute-start(bf16[24,16384]{1,0:T(8,128)(2,1)S(1)} %pack.1.pack_ref), channel_id=1, source_target_pairs={{0,2},{2,4},{4,6},{6,8},{8,10},{10,12},{12,14},{1,3},{3,5},{5,7},{... | collective-permute-start | bytes 2359304 | tf_op jit(solution)/shard_map/ppermute | solution.py:657
  20.1 1.3 %collective-permute-start.8 = (bf16[24,16384]{1,0:T(8,128)(2,1)S(1)}, bf16[24,16384]{1,0:T(8,128)(2,1)S(1)}, u32[]{:S(2)}, u32[]{:S(2)}) collective-permute-start(bf16[24,16384]{1,0:T(8,128)(2,1)S(1)} %pack.1.pack_ref), channel_id=1, source_target_pairs={{2,0},{4,2},{6,4},{8,6},{10,8},{12,10},{14,12},{3,1},{5,3},{7,5},{... | collective-permute-start | bytes 2359304 | tf_op jit(solution)/shard_map/ppermute | solution.py:658
  21.4 32.7 %near_local.1 = (f32[8,32768]{1,0:T(8,128)S(1)}, f32[8,32768]{1,0:T(8,128)S(1)}, bf16[128,32,256]{2,1,0:T(8,128)(2,1)S(1)}, s32[528]{0:T(1024)S(1)}, s32[1]{0:T(128)}) custom-call(f32[5]{0:T(128)S(1)} %pad_maximum_fusion.2.scale_ref.refs_0_, s32[128]{0:T(128)S(1)} %copy-done.13, s32[512]{0:T(512)S(1)} %copy-done.11, f32[3,32768]{1,0:T(4,128)S(1)} %copy-done.5, ...), custom_call_target="tpu_custom_call" | custom-call | flops 35999997952 | bytes 8388608 | tf_op jit(solution)/shard_map/near_local/pallas_call | solution.py:681
  54.2 7.7 %couple.1 = (f32[63,16,128]{2,1,0:T(8,128)S(1)}, bf16[8,64,192]{2,1,0:T(8,128)(2,1)S(1)}) custom-call(f32[5]{0:T(128)S(1)} %pad_maximum_fusion.2.scale_ref.refs_0_, s32[3,255]{1,0:T(4,128)S(1)} %bitcast.17, bf16[127,32,128]{2,1,0:T(8,128)(2,1)S(1)} %get-tuple-element.28.coef_ref, bf16[3,64,64,255]{3,2,1,0:T(8,128)(2,1)S(1)} %bitcast.15), custom_call_target="tpu_custom_call" | custom-call | flops 8999999488 | bytes 8388608 | tf_op jit(solution)/shard_map/couple/pallas_call | solution.py:706
  62.0 4.1 %near_halo.1 = (f32[8,32768]{1,0:T(8,128)S(1)}, f32[8,32768]{1,0:T(8,128)S(1)}) custom-call(f32[5]{0:T(128)S(1)} %pad_maximum_fusion.2.scale_ref.refs_0_, s32[528]{0:T(1024)S(1)} %get-tuple-element.27.far_list, s32[1]{0:T(128)} %get-tuple-element.36.far_count, bf16[128,32,256]{2,1,0:T(8,128)(2,1)S(1)} %get-tuple-element.37.row_ref, ...), custom_call_target="tpu_custom_call" | custom-call | flops 4000000000 | bytes 8388608 | tf_op jit(solution)/shard_map/near_halo/pallas_call | solution.py:727
  66.2 2.7 %collective-permute-start.2 = (bf16[2,4,32,128]{3,2,1,0:T(8,128)(2,1)S(1)}, bf16[2,4,32,128]{3,2,1,0:T(8,128)(2,1)S(1)}, u32[]{:S(2)}, u32[]{:S(2)}) collective-permute-start(bf16[2,4,32,128]{3,2,1,0:T(8,128)(2,1)S(1)} %pad_maximum_fusion), channel_id=1, source_target_pairs={{0,2},{2,0},{4,6},{6,4},{8,10},{10,8},{12,14},{14,12},{1,3},{3,1},... | collective-permute-start | bytes 196616 | tf_op jit(solution)/shard_map/ppermute | solution.py:615
  68.9 2.7 %collective-permute-done.2.refs_10_ = bf16[2,4,32,128]{3,2,1,0:T(8,128)(2,1)S(1)} collective-permute-done((bf16[2,4,32,128]{3,2,1,0:T(8,128)(2,1)S(1)}, bf16[2,4,32,128]{3,2,1,0:T(8,128)(2,1)S(1)}, u32[]{:S(2)}, u32[]{:S(2)}) %collective-permute-start.2) | collective-permute-done | bytes 65568 | tf_op jit(solution)/shard_map/ppermute | solution.py:615
  71.7 2.5 %collective-permute-start.3 = (bf16[4,2,32,128]{3,2,1,0:T(8,128)(2,1)S(1)}, bf16[4,2,32,128]{3,2,1,0:T(8,128)(2,1)S(1)}, u32[]{:S(2)}, u32[]{:S(2)}) collective-permute-start(bf16[4,2,32,128]{3,2,1,0:T(8,128)(2,1)S(1)} %pad_maximum_fusion.1), channel_id=1, source_target_pairs={{0,4},{2,6},{4,0},{6,2},{8,12},{10,14},{12,8},{14,10},{1,5},{3,7},... | collective-permute-start | bytes 196616 | tf_op jit(solution)/shard_map/ppermute | solution.py:615
  74.1 2.0 %collective-permute-start.4 = (bf16[4,2,32,128]{3,2,1,0:T(8,128)(2,1)S(1)}, bf16[4,2,32,128]{3,2,1,0:T(8,128)(2,1)S(1)}, u32[]{:S(2)}, u32[]{:S(2)}) collective-permute-start(bf16[4,2,32,128]{3,2,1,0:T(8,128)(2,1)S(1)} %pad_maximum_fusion.1), channel_id=1, source_target_pairs={{0,8},{2,10},{4,12},{6,14},{8,0},{10,2},{12,4},{14,6},{1,9},{3,11}... | collective-permute-start | bytes 196616 | tf_op jit(solution)/shard_map/ppermute | solution.py:615
  76.1 0.9 %collective-permute-start.5 = (bf16[4,2,32,128]{3,2,1,0:T(8,128)(2,1)S(1)}, bf16[4,2,32,128]{3,2,1,0:T(8,128)(2,1)S(1)}, u32[]{:S(2)}, u32[]{:S(2)}) collective-permute-start(bf16[4,2,32,128]{3,2,1,0:T(8,128)(2,1)S(1)} %pad_maximum_fusion.1), channel_id=1, source_target_pairs={{0,12},{2,14},{4,8},{6,10},{8,4},{10,6},{12,0},{14,2},{1,13},{3,15... | collective-permute-start | bytes 196616 | tf_op jit(solution)/shard_map/ppermute | solution.py:615
  77.1 4.4 %collective-permute-done.4.refs_12_ = bf16[4,2,32,128]{3,2,1,0:T(8,128)(2,1)S(1)} collective-permute-done((bf16[4,2,32,128]{3,2,1,0:T(8,128)(2,1)S(1)}, bf16[4,2,32,128]{3,2,1,0:T(8,128)(2,1)S(1)}, u32[]{:S(2)}, u32[]{:S(2)}) %collective-permute-start.4) | collective-permute-done | bytes 65568 | tf_op jit(solution)/shard_map/ppermute | solution.py:615
  81.5 0.8 collective-permute-done.5.refs_13_
  82.3 3.7 %down.1 = (bf16[64,8,64]{2,1,0:T(8,128)(2,1)S(1)}, bf16[64,8,64]{2,1,0:T(8,128)(2,1)S(1)}) custom-call(f32[5]{0:T(128)S(1)} %pad_maximum_fusion.2.scale_ref.refs_0_, s32[3,255]{1,0:T(4,128)S(1)} %bitcast.18, s32[4,3]{1,0:T(4,128)S(1)} %copy-done.12, bf16[4,2,64,64]{3,2,1,0:T(8,128)(2,1)S(1)} %copy-done.9, bf16[4,3,64,64]{3,2,1,0:T(8,128)(2,1)S(1)} %copy-done.8, ...), custom_call_target="tpu_custom_call" | custom-call | flops 4000000000 | bytes 4194304 | tf_op jit(solution)/shard_map/down/pallas_call | solution.py:754
  86.1 1.3 %collective-permute-done.6.got_ref = bf16[64,8,64]{2,1,0:T(8,128)(2,1)S(1)} collective-permute-done((bf16[64,8,64]{2,1,0:T(8,128)(2,1)S(1)}, bf16[64,8,64]{2,1,0:T(8,128)(2,1)S(1)}, u32[]{:S(2)}, u32[]{:S(2)}) %collective-permute-start.6) | collective-permute-done | bytes 65568 | tf_op jit(solution)/shard_map/ppermute | solution.py:770
  87.4 3.8 %final.1 = f32[8,32768]{1,0:T(8,128)} custom-call(f32[5]{0:T(128)S(1)} %pad_maximum_fusion.2.scale_ref.refs_0_, bf16[64,8,64]{2,1,0:T(8,128)(2,1)S(1)} %get-tuple-element.34.mine_ref, bf16[64,8,64]{2,1,0:T(8,128)(2,1)S(1)} %collective-permute-done.6.got_ref, bf16[128,64,256]{2,1,0:T(8,128)(2,1)S(1)} %copy-done.1, f32[1,32768]{1,0:T(1,128)S(1)} %bitcast.12, ...), custom_call_target="tpu_custom_call" | custom-call | flops 2000000000 | bytes 4194304 | tf_op jit(solution)/shard_map/final/pallas_call | solution.py:772
  (45 shorter events, 0.8 us)
Async XLA Ops:
  0.0 2.2 %collective-permute-start = (bf16[8,32768]{1,0:T(8,128)(2,1)}, bf16[8,32768]{1,0:T(8,128)(2,1)S(1)}, u32[]{:S(2)}, u32[]{:S(2)}) collective-permute-start(bf16[8,32768]{1,0:T(8,128)(2,1)} %vec.1), channel_id=1, source_target_pairs={{0,1},{1,0},{2,3},{3,2},{4,5},{5,4},{6,7},{7,6},{8,9},{9,8},{10,11... | collective-permute-start | bytes 1572872 | tf_op jit(solution)/shard_map/ppermute | solution.py:642
  5.3 2.2 %copy-start = (bf16[128,64,256]{2,1,0:T(8,128)(2,1)S(1)}, bf16[128,64,256]{2,1,0:T(8,128)(2,1)}, u32[]{:S(2)}) copy-start(bf16[128,64,256]{2,1,0:T(8,128)(2,1)} %basis.1) | copy-start | bytes 12582916
  7.5 1.6 %copy-start.7 = (bf16[127,2,64,64]{0,3,2,1:T(8,128)(2,1)S(1)}, bf16[127,2,64,64]{0,3,2,1:T(8,128)(2,1)}, u32[]{:S(2)}) copy-start(bf16[127,2,64,64]{0,3,2,1:T(8,128)(2,1)} %param.18) | copy-start | bytes 6242308
  9.1 12.3 %copy-start.5 = (f32[3,32768]{1,0:T(4,128)S(1)}, f32[3,32768]{1,0:T(4,128)}, u32[]{:S(2)}) copy-start(f32[3,32768]{1,0:T(4,128)} %points_ref.1) | copy-start | bytes 1179652
  9.1 12.4 %copy-start.11 = (s32[512]{0:T(512)S(1)}, s32[512]{0:T(512)}, u32[]{:S(2)}) copy-start(s32[512]{0:T(512)} %cols_ref.1) | copy-start | bytes 6148
  9.1 12.4 %copy-start.13 = (s32[128]{0:T(128)S(1)}, s32[128]{0:T(128)}, u32[]{:S(2)}) copy-start(s32[128]{0:T(128)} %offs_ref.1) | copy-start | bytes 1540
  14.8 39.4 %slice-start = ((s8[6291456]{0:T(1024)(128)(4,1)}), s8[4194304]{0:T(1024)(128)(4,1)S(1)}, s32[]{:S(2)}) async-start(s8[6291456]{0:T(1024)(128)(4,1)} %bitcast.13), calls=%async_computation | async-start | bytes 8388608
  14.8 39.4 %slice-start.1 = ((s8[6291456]{0:T(1024)(128)(4,1)}), s8[2097152]{0:T(1024)(128)(4,1)S(1)}, s32[]{:S(2)}) async-start(s8[6291456]{0:T(1024)(128)(4,1)} %bitcast.13), calls=%async_computation.1 | async-start | bytes 4194304
  14.8 39.4 %copy-start.10 = (s32[255,3]{0,1:T(4,128)S(1)}, s32[255,3]{0,1:T(4,128)}, u32[]{:S(2)}) copy-start(s32[255,3]{0,1:T(4,128)} %param.22) | copy-start | bytes 9184
  14.8 47.1 %collective-permute-start.1 = (bf16[8,32,128]{2,1,0:T(8,128)(2,1)S(1)}, bf16[8,32,128]{2,1,0:T(8,128)(2,1)S(1)}, u32[]{:S(2)}, u32[]{:S(2)}) collective-permute-start(bf16[8,32,128]{2,1,0:T(8,128)(2,1)S(1)} %get-tuple-element.25.refs_8_), channel_id=1, source_target_pairs={{0,1},{1,0},{2,3},{3,2},{4,5},{5,4},{6,7},{7,6},{8,9},{9,8},{10,11... | collective-permute-start | bytes 196616 | tf_op jit(solution)/shard_map/ppermute | solution.py:679
  15.3 46.7 %collective-permute-start.7 = (bf16[24,16384]{1,0:T(8,128)(2,1)S(1)}, bf16[24,16384]{1,0:T(8,128)(2,1)S(1)}, u32[]{:S(2)}, u32[]{:S(2)}) collective-permute-start(bf16[24,16384]{1,0:T(8,128)(2,1)S(1)} %pack.1.pack_ref), channel_id=1, source_target_pairs={{0,2},{2,4},{4,6},{6,8},{8,10},{10,12},{12,14},{1,3},{3,5},{5,7},{... | collective-permute-start | bytes 2359304 | tf_op jit(solution)/shard_map/ppermute | solution.py:657
  20.1 41.8 %collective-permute-start.8 = (bf16[24,16384]{1,0:T(8,128)(2,1)S(1)}, bf16[24,16384]{1,0:T(8,128)(2,1)S(1)}, u32[]{:S(2)}, u32[]{:S(2)}) collective-permute-start(bf16[24,16384]{1,0:T(8,128)(2,1)S(1)} %pack.1.pack_ref), channel_id=1, source_target_pairs={{2,0},{4,2},{6,4},{8,6},{10,8},{12,10},{14,12},{3,1},{5,3},{7,5},{... | collective-permute-start | bytes 2359304 | tf_op jit(solution)/shard_map/ppermute | solution.py:658
  61.9 20.4 %copy-start.8 = (bf16[4,3,64,64]{3,2,1,0:T(8,128)(2,1)S(1)}, bf16[4,3,64,64]{3,2,1,0:T(8,128)(2,1)}, u32[]{:S(2)}) copy-start(bf16[4,3,64,64]{3,2,1,0:T(8,128)(2,1)} %refs_4_.1) | copy-start | bytes 294916
  62.0 20.3 %copy-start.9 = (bf16[4,2,64,64]{3,2,1,0:T(8,128)(2,1)S(1)}, bf16[4,2,64,64]{3,2,1,0:T(8,128)(2,1)}, u32[]{:S(2)}) copy-start(bf16[4,2,64,64]{3,2,1,0:T(8,128)(2,1)} %refs_3_.1) | copy-start | bytes 196612
  62.0 20.3 %copy-start.12 = (s32[4,3]{1,0:T(4,128)S(1)}, s32[4,3]{1,0:T(4,128)}, u32[]{:S(2)}) copy-start(s32[4,3]{1,0:T(4,128)} %refs_2_.1) | copy-start | bytes 148
  66.1 21.3 %collective-permute-start.9 = (f32[8,32768]{1,0:T(8,128)S(1)}, f32[8,32768]{1,0:T(8,128)S(1)}, u32[]{:S(2)}, u32[]{:S(2)}) collective-permute-start(f32[8,32768]{1,0:T(8,128)S(1)} %get-tuple-element.42), channel_id=1, source_target_pairs={{0,1},{1,0},{2,3},{3,2},{4,5},{5,4},{6,7},{7,6},{8,9},{9,8},{10,11... | collective-permute-start | bytes 3145736 | tf_op jit(solution)/shard_map/ppermute | solution.py:743
  66.2 5.4 %collective-permute-start.2 = (bf16[2,4,32,128]{3,2,1,0:T(8,128)(2,1)S(1)}, bf16[2,4,32,128]{3,2,1,0:T(8,128)(2,1)S(1)}, u32[]{:S(2)}, u32[]{:S(2)}) collective-permute-start(bf16[2,4,32,128]{3,2,1,0:T(8,128)(2,1)S(1)} %pad_maximum_fusion), channel_id=1, source_target_pairs={{0,2},{2,0},{4,6},{6,4},{8,10},{10,8},{12,14},{14,12},{1,3},{3,1},... | collective-permute-start | bytes 196616 | tf_op jit(solution)/shard_map/ppermute | solution.py:615
  71.7 5.4 %collective-permute-start.3 = (bf16[4,2,32,128]{3,2,1,0:T(8,128)(2,1)S(1)}, bf16[4,2,32,128]{3,2,1,0:T(8,128)(2,1)S(1)}, u32[]{:S(2)}, u32[]{:S(2)}) collective-permute-start(bf16[4,2,32,128]{3,2,1,0:T(8,128)(2,1)S(1)} %pad_maximum_fusion.1), channel_id=1, source_target_pairs={{0,4},{2,6},{4,0},{6,2},{8,12},{10,14},{12,8},{14,10},{1,5},{3,7},... | collective-permute-start | bytes 196616 | tf_op jit(solution)/shard_map/ppermute | solution.py:615
  74.1 7.3 %collective-permute-start.4 = (bf16[4,2,32,128]{3,2,1,0:T(8,128)(2,1)S(1)}, bf16[4,2,32,128]{3,2,1,0:T(8,128)(2,1)S(1)}, u32[]{:S(2)}, u32[]{:S(2)}) collective-permute-start(bf16[4,2,32,128]{3,2,1,0:T(8,128)(2,1)S(1)} %pad_maximum_fusion.1), channel_id=1, source_target_pairs={{0,8},{2,10},{4,12},{6,14},{8,0},{10,2},{12,4},{14,6},{1,9},{3,11}... | collective-permute-start | bytes 196616 | tf_op jit(solution)/shard_map/ppermute | solution.py:615
  76.1 6.2 %collective-permute-start.5 = (bf16[4,2,32,128]{3,2,1,0:T(8,128)(2,1)S(1)}, bf16[4,2,32,128]{3,2,1,0:T(8,128)(2,1)S(1)}, u32[]{:S(2)}, u32[]{:S(2)}) collective-permute-start(bf16[4,2,32,128]{3,2,1,0:T(8,128)(2,1)S(1)} %pad_maximum_fusion.1), channel_id=1, source_target_pairs={{0,12},{2,14},{4,8},{6,10},{8,4},{10,6},{12,0},{14,2},{1,13},{3,15... | collective-permute-start | bytes 196616 | tf_op jit(solution)/shard_map/ppermute | solution.py:615
  82.3 5.1 %copy-start.1 = (bf16[128,64,256]{2,1,0:T(8,128)(2,1)S(1)}, bf16[128,64,256]{2,1,0:T(8,128)(2,1)}, u32[]{:S(2)}) copy-start(bf16[128,64,256]{2,1,0:T(8,128)(2,1)} %basis.1) | copy-start | bytes 12582916
  82.3 5.1 %copy-start.3 = (bf16[8,32768]{1,0:T(8,128)(2,1)S(1)}, bf16[8,32768]{1,0:T(8,128)(2,1)}, u32[]{:S(2)}) copy-start(bf16[8,32768]{1,0:T(8,128)(2,1)} %vec.1) | copy-start | bytes 1572868
  82.3 5.1 %copy-start.6 = (f32[32768]{0:T(1024)S(1)}, f32[32768]{0:T(1024)}, u32[]{:S(2)}) copy-start(f32[32768]{0:T(1024)} %param.15) | copy-start | bytes 393220
  86.0 1.4 %collective-permute-start.6 = (bf16[64,8,64]{2,1,0:T(8,128)(2,1)S(1)}, bf16[64,8,64]{2,1,0:T(8,128)(2,1)S(1)}, u32[]{:S(2)}, u32[]{:S(2)}) collective-permute-start(bf16[64,8,64]{2,1,0:T(8,128)(2,1)S(1)} %get-tuple-element.35), channel_id=1, source_target_pairs={{0,1},{1,0},{2,3},{3,2},{4,5},{5,4},{6,7},{7,6},{8,9},{9,8},{10,11... | collective-permute-start | bytes 196616 | tf_op jit(solution)/shard_map/ppermute | solution.py:770
  (2 other events, 2.1 us)

commit v6 on v5

--- a/solution.py
+++ b/solution.py
@@ -576,36 +576,52 @@
 
 
 def final_kernel(
-    scale_ref, mine_ref, got_ref, basis, noise, vec, near, swap, out_hbm, out, sems
+    scale_ref, mine_ref, got_ref, basis, noise, vec, near_hbm, swap_hbm, out_hbm,
+    near, swap, out, sems,
 ):
     core = whole(scale_ref[4])
     leaves = mine_ref.shape[0]
-    chunks = 2
+    chunks = 4
     per = leaves // chunks
     wide = per * LEAF
-    sends = []
+    work = []
     for part, low_ref in enumerate((mine_ref, got_ref)):
         base = jnp.where(core == part, 0, leaves)
         for c in range(chunks):
-
-            def last(nodes, c=c, low_ref=low_ref, base=base):
-                rows = [c * per + i for i in nodes]
-                fars = [
-                    jnp.dot(low_ref[n], basis[base + n], preferred_element_type=F32)
-                    for n in rows
-                ]
-                for n, far in zip(rows, fars):
-                    here = lanes(base + n)
-                    total = near[:, here] + swap[:, here]
-                    out[:, here] = total + noise[:, here] * vec[:, here].astype(F32) + far
-
-            over_nodes(per, 8, last)
             piece = pl.ds(pl.multiple_of((base + c * per) * LEAF, wide), wide)
-            send = pltpu.make_async_copy(
-                out.at[:, piece], out_hbm.at[:, piece], sems.at[part * chunks + c]
+            work.append((low_ref, base, c * per, piece))
+    loads = fetch(
+        [
+            pair
+            for _, _, _, piece in work
+            for pair in (
+                (near_hbm.at[:, piece], near.at[:, piece]),
+                (swap_hbm.at[:, piece], swap.at[:, piece]),
             )
-            send.start()
-            sends.append(send)
+        ],
+        sems,
+    )
+    sends = []
+    for i, (low_ref, base, start, piece) in enumerate(work):
+        loads[2 * i].wait()
+        loads[2 * i + 1].wait()
+
+        def last(nodes, low_ref=low_ref, base=base, start=start):
+            rows = [start + n for n in nodes]
+            fars = [
+                jnp.dot(low_ref[n], basis[base + n], preferred_element_type=F32) for n in rows
+            ]
+            for n, far in zip(rows, fars):
+                here = lanes(base + n)
+                total = near[:, here] + swap[:, here]
+                out[:, here] = total + noise[:, here] * vec[:, here].astype(F32) + far
+
+        over_nodes(per, 8, last)
+        send = pltpu.make_async_copy(
+            out.at[:, piece], out_hbm.at[:, piece], sems.at[len(loads) + i]
+        )
+        send.start()
+        sends.append(send)
     for send in sends:
         send.wait()
 
@@ -651,7 +667,7 @@
             VMEM((3, half), F32), VMEM((PART, half), BF), VMEM((PART, half), BF),
             pltpu.SemaphoreType.DMA((3,)),
         ],
-        compiler_params=params(16),
+        compiler_params=params(60),
     )(scale, points, vectors, got)
     axes = ("leaf", "sub")
     left = lax.ppermute(pack, axes, [(i, i + 1) for i in range(count - 1)])
@@ -673,7 +689,7 @@
             VMEM((leaves // 8, RANK * 8, 2 * RANK), F32),
             VMEM((part - 1, 2 * ALL, 2 * RANK), BF), pltpu.SemaphoreType.DMA((8,)),
         ],
-        compiler_params=params(28),
+        compiler_params=params(60),
         cost_estimate=pl.CostEstimate(flops=8 * 10**9, bytes_accessed=8 << 20, transcendentals=0),
     )(scale, pack, leaf_basis, moves_raw)
     from_core = lax.ppermute(export, "vec", [(0, 1), (1, 0)])
@@ -691,7 +707,7 @@
             VMEM((leaves // 2 + 1, LEAF, 32), BF), VMEM((leaves // 2 + 1, 16, LEAF), BF),
             *scratch_blocks, SMEM((slots + PAD,), jnp.int32),
         ],
-        compiler_params=params(28),
+        compiler_params=params(22),
         cost_estimate=pl.CostEstimate(
             flops=36 * 10**9, bytes_accessed=8 << 20, transcendentals=190 * 2**17
         ),
@@ -699,8 +715,8 @@
 
     from_core = after(from_core, far_list)
     near_pair = jnp.stack([export[0:4], from_core[0:4]])
+    coef_late, near_pair = lax.optimization_barrier((coef, near_pair))
     from_next = swap_mask(near_pair, 1)
-    coef_late = after(coef, far_list)
     ties_raw = jnp.transpose(local_coupling, (1, 2, 3, 0))
     mates = jnp.transpose(local_partners)
     local, ties = pl.pallas_call(
@@ -717,13 +733,12 @@
             VMEM((leaves // 4, RANK * 8, RANK), F32), pltpu.SemaphoreType.DMA((4,)),
         ],
         compiler_params=params(36),
-        cost_estimate=pl.CostEstimate(flops=9 * 10**9, bytes_accessed=8 << 20, transcendentals=0),
+        cost_estimate=pl.CostEstimate(flops=16 * 10**9, bytes_accessed=8 << 20, transcendentals=0),
     )(scale, mates, coef_late, ties_raw)
 
-    from_next = after(from_next, local)
+    first, _, from_next = lax.optimization_barrier((first, local, from_next))
     quad = jnp.concatenate([near_pair[:, 0:2], from_next[:, 0:2]], axis=0)
     from_far = [swap_mask(quad, mask) for mask in (2, 4, 6)]
-    first = after(first, local)
     mine, other = pl.pallas_call(
         near_halo_kernel,
         name="near_halo",
@@ -735,9 +750,9 @@
             VMEM((leaves + 1, LEAF, 32), BF), VMEM((leaves + 1, 16, LEAF), BF),
             *scratch_blocks,
         ],
-        compiler_params=params(36),
+        compiler_params=params(26),
         cost_estimate=pl.CostEstimate(
-            flops=4 * 10**9, bytes_accessed=8 << 20, transcendentals=60 * 2**17
+            flops=20 * 10**9, bytes_accessed=8 << 20, transcendentals=60 * 2**17
         ),
     )(scale, far_list, far_count, row_feat, left, right, first, second)
     swapped = lax.ppermute(other, "vec", [(0, 1), (1, 0)])
@@ -761,8 +776,8 @@
             VMEM((2 * 2**SPAN, EXPORT, 2 * ALL, 2 * RANK), BF),
             VMEM((part - 1, 2 * ALL, RANK), BF), VMEM((2 * count, 2 * ALL, RANK), BF),
         ],
-        compiler_params=params(24),
-        cost_estimate=pl.CostEstimate(flops=4 * 10**9, bytes_accessed=4 << 20, transcendentals=0),
+        compiler_params=params(14),
+        cost_estimate=pl.CostEstimate(flops=40 * 10**9, bytes_accessed=4 << 20, transcendentals=0),
     )(
         scale, mates, top_partners, top_transfer, top_coupling, ties, local, moves,
         export, from_core, from_next, *from_far, tops,
@@ -773,10 +788,10 @@
         final_kernel,
         name="final",
         out_shape=sds((PART, size), F32),
-        in_specs=[sspec()] + [vspec()] * 7,
+        in_specs=[sspec()] + [vspec()] * 5 + [hspec()] * 2,
         out_specs=hspec(),
-        scratch_shapes=[VMEM((PART, size), F32), pltpu.SemaphoreType.DMA((4,))],
-        compiler_params=params(16),
+        scratch_shapes=[VMEM((PART, size), F32)] * 3 + [pltpu.SemaphoreType.DMA((24,))],
+        compiler_params=params(10),
         cost_estimate=pl.CostEstimate(flops=2 * 10**9, bytes_accessed=4 << 20, transcendentals=0),
     )(scale, low_mine, low_got, leaf_basis, noise.reshape(1, size), vectors, mine, swapped)
 

time: 92.1 us -> 88.2 us (0.958)
  Pallas kernels: 58.7 us -> 67.2 us
  waiting for transfers between devices: 10.2 us -> 2.84 us
  local copies, waits for them, and re-layouts: 5.94 us -> 2.5 us
  starting transfers between devices: 15.3 us -> 13.6 us
    ppermute x4, waiting for transfers between devices: 7.96 us -> 1.07 us  [swap_mask(): lax.ppermute(value, ('leaf', 'sub'), [(i, i ^ mask) for i in range(total)])]
    unnamed x32 -> x36, local copies, waits for them, and re-layouts: 5.92 us -> 0.88 us
    pallas_call x1, Pallas kernels: 5.71 us -> 8.66 us  [body(): pl.pallas_call(up_kernel, name='up', out_shape=(sds((2 * part - 1, 2 * AL...]
    pallas_call x1, Pallas kernels: 3.83 us -> 6.73 us  [body(): pl.pallas_call(final_kernel, name='final', out_shape=sds((PART, size), F3...]
    pallas_call x1, Pallas kernels: 1 us -> 3.06 us  [body(): pl.pallas_call(pack_kernel, name='pack', out_shape=sds((24, half), BF), i...]
    ppermute x4, starting transfers between devices: 8.11 us -> 6.4 us  [swap_mask(): lax.ppermute(value, ('leaf', 'sub'), [(i, i ^ mask) for i in range(total)])]
  transfers between devices with their start and end apart: 10 -> 10, of which waited for: 5 -> 3; matrix products, arithmetic and copies ran while one was open for 1% -> 3% of each run, Pallas kernels for 48% -> 56%
where the time goes in v6:
time: 88.2 us; the launch traced here: 87.8 us
  Pallas kernels  67.2 us (76%)
  starting transfers between devices  13.6 us (15%)
  waiting for transfers between devices  2.84 us (3%)
  local copies, waits for them, and re-layouts  2.5 us (3%)
  other arithmetic  1.34 us (2%)
    pallas_call x1, Pallas kernels, body(): pl.pallas_call(near_local_kernel, name='near_local', out_shape=(sds((PART...  33.5 us
    pallas_call x1, Pallas kernels, body(): pl.pallas_call(up_kernel, name='up', out_shape=(sds((2 * part - 1, 2 * AL...  8.66 us
    pallas_call x1, Pallas kernels, body(): pl.pallas_call(couple_kernel, name='couple', out_shape=(sds((part - 1, AL...  7.7 us
    pallas_call x1, Pallas kernels, body(): pl.pallas_call(final_kernel, name='final', out_shape=sds((PART, size), F3...  6.73 us
    ppermute x4, starting transfers between devices, swap_mask(): lax.ppermute(value, ('leaf', 'sub'), [(i, i ^ mask) for i in range(total)])  6.4 us
    ppermute x1, starting transfers between devices, body(): left = lax.ppermute(pack, axes, [(i, i + 1) for i in range(count - 1)])  4.85 us
    pallas_call x1, Pallas kernels, body(): pl.pallas_call(near_halo_kernel, name='near_halo', out_shape=(sds((PART,...  3.97 us
    pallas_call x1, Pallas kernels, body(): pl.pallas_call(lambda *refs: down_kernel(dev_levels, *refs[:11], refs[11:...  3.66 us
  transfers between devices with their start and end apart: 10, of which 3 were waited for; matrix products, arithmetic and copies ran while one was open for 3% of the time, Pallas kernels for 56%

profile of v6, /device:TPU:0, one launch (start us, length us, event | category | flops | bytes accessed | tf_op | source)
XLA Modules:
  0.0 87.8 jit_solution(16516468472903699537)
XLA Ops:
  0.0 0.5 collective-permute-start
  0.5 0.1 add_convert_fusion
  0.5 1.2 %pad_maximum_fusion.2.scale_ref.refs_0_ = f32[5]{0:T(128)} fusion(f32[2]{0:T(128)S(1)} %add_convert_fusion, f32[3]{0:T(128)} %param.14), kind=kLoop, calls=%fused_computation.6 | loop fusion | flops 5 | bytes 40 | tf_op jit(solution)/shard_map/concatenate | solution.py:647
  1.8 0.4 collective-permute-done.got_hbm
  2.2 0.8 copy-done.15
  3.0 3.1 %pack.1.pack_ref = bf16[24,16384]{1,0:T(8,128)(2,1)} custom-call(f32[5]{0:T(128)} %pad_maximum_fusion.2.scale_ref.refs_0_, f32[3,32768]{1,0:T(4,128)} %points_ref.1, bf16[8,32768]{1,0:T(8,128)(2,1)} %vec.1, bf16[8,32768]{1,0:T(8,128)(2,1)} %copy-done.15), custom_call_target="tpu_custom_call" | custom-call | tf_op jit(solution)/shard_map/pack/pallas_call | solution.py:660
  6.1 8.7 %up.1 = (bf16[127,32,128]{2,1,0:T(8,128)(2,1)}, bf16[8,32,128]{2,1,0:T(8,128)(2,1)}, bf16[64,64,128]{2,1,0:T(8,128)(2,1)}) custom-call(f32[5]{0:T(128)} %pad_maximum_fusion.2.scale_ref.refs_0_, bf16[24,16384]{1,0:T(8,128)(2,1)} %pack.1.pack_ref, bf16[128,64,256]{2,1,0:T(8,128)(2,1)} %basis.1, bf16[2,64,64,127]{3,2,1,0:T(8,128)(2,1)} %bitcast.18), custom_call_target="tpu_custom_call" | custom-call | flops 8000000000 | bytes 8388608 | tf_op jit(solution)/shard_map/up/pallas_call | solution.py:678
  14.8 0.4 collective-permute-start.1
  15.2 0.8 slice_bitcast_fusion.1
  16.0 0.8 slice_bitcast_fusion.2.refs_14_
  16.8 4.9 %collective-permute-start.7 = (bf16[24,16384]{1,0:T(8,128)(2,1)S(1)}, bf16[24,16384]{1,0:T(8,128)(2,1)S(1)}, u32[]{:S(2)}, u32[]{:S(2)}) collective-permute-start(bf16[24,16384]{1,0:T(8,128)(2,1)S(1)} %copy-done.2), channel_id=1, source_target_pairs={{0,2},{2,4},{4,6},{6,8},{8,10},{10,12},{12,14},{1,3},{3,5},{5,7},{... | collective-permute-start | bytes 2359304 | tf_op jit(solution)/shard_map/ppermute | solution.py:673
  21.7 1.3 %collective-permute-start.8 = (bf16[24,16384]{1,0:T(8,128)(2,1)S(1)}, bf16[24,16384]{1,0:T(8,128)(2,1)S(1)}, u32[]{:S(2)}, u32[]{:S(2)}) collective-permute-start(bf16[24,16384]{1,0:T(8,128)(2,1)S(1)} %copy-done.2), channel_id=1, source_target_pairs={{2,0},{4,2},{6,4},{8,6},{10,8},{12,10},{14,12},{3,1},{5,3},{7,5},{... | collective-permute-start | bytes 2359304 | tf_op jit(solution)/shard_map/ppermute | solution.py:674
  23.0 33.5 %near_local.1 = (f32[8,32768]{1,0:T(8,128)S(1)}, f32[8,32768]{1,0:T(8,128)S(1)}, bf16[128,32,256]{2,1,0:T(8,128)(2,1)S(1)}, s32[528]{0:T(1024)S(1)}, s32[1]{0:T(128)}) custom-call(f32[5]{0:T(128)S(1)} %copy-done.6, s32[128]{0:T(128)S(1)} %copy-done.12, s32[512]{0:T(512)S(1)} %copy-done.10, f32[3,32768]{1,0:T(4,128)S(1)} %copy-done.3, ...), custom_call_target="tpu_custom_call" | custom-call | flops 35999997952 | bytes 8388608 | tf_op jit(solution)/shard_map/near_local/pallas_call | solution.py:697
  56.5 2.0 %collective-permute-start.2 = (bf16[2,4,32,128]{3,2,1,0:T(8,128)(2,1)S(1)}, bf16[2,4,32,128]{3,2,1,0:T(8,128)(2,1)S(1)}, u32[]{:S(2)}, u32[]{:S(2)}) collective-permute-start(bf16[2,4,32,128]{3,2,1,0:T(8,128)(2,1)S(1)} %pad_maximum_fusion), channel_id=1, source_target_pairs={{0,2},{2,0},{4,6},{6,4},{8,10},{10,8},{12,14},{14,12},{1,3},{3,1},... | collective-permute-start | bytes 196616 | tf_op jit(solution)/shard_map/ppermute | solution.py:631
  58.5 7.7 %couple.1 = (f32[63,16,128]{2,1,0:T(8,128)S(1)}, bf16[8,64,192]{2,1,0:T(8,128)(2,1)S(1)}) custom-call(f32[5]{0:T(128)S(1)} %copy-done.6, s32[3,255]{1,0:T(4,128)S(1)} %bitcast.16, bf16[127,32,128]{2,1,0:T(8,128)(2,1)S(1)} %copy-done.14, bf16[3,64,64,255]{3,2,1,0:T(8,128)(2,1)S(1)} %bitcast.15), custom_call_target="tpu_custom_call" | custom-call | flops 16000000000 | bytes 8388608 | tf_op jit(solution)/shard_map/couple/pallas_call | solution.py:722
  66.3 0.8 collective-permute-start.3
  67.1 2.6 %collective-permute-start.4 = (bf16[4,2,32,128]{3,2,1,0:T(8,128)(2,1)S(1)}, bf16[4,2,32,128]{3,2,1,0:T(8,128)(2,1)S(1)}, u32[]{:S(2)}, u32[]{:S(2)}) collective-permute-start(bf16[4,2,32,128]{3,2,1,0:T(8,128)(2,1)S(1)} %pad_maximum_fusion.1), channel_id=1, source_target_pairs={{0,8},{2,10},{4,12},{6,14},{8,0},{10,2},{12,4},{14,6},{1,9},{3,11}... | collective-permute-start | bytes 196616 | tf_op jit(solution)/shard_map/ppermute | solution.py:631
  69.8 1.0 %collective-permute-start.5 = (bf16[4,2,32,128]{3,2,1,0:T(8,128)(2,1)S(1)}, bf16[4,2,32,128]{3,2,1,0:T(8,128)(2,1)S(1)}, u32[]{:S(2)}, u32[]{:S(2)}) collective-permute-start(bf16[4,2,32,128]{3,2,1,0:T(8,128)(2,1)S(1)} %pad_maximum_fusion.1), channel_id=1, source_target_pairs={{0,12},{2,14},{4,8},{6,10},{8,4},{10,6},{12,0},{14,2},{1,13},{3,15... | collective-permute-start | bytes 196616 | tf_op jit(solution)/shard_map/ppermute | solution.py:631
  70.8 4.0 %near_halo.1 = (f32[8,32768]{1,0:T(8,128)S(1)}, f32[8,32768]{1,0:T(8,128)S(1)}) custom-call(f32[5]{0:T(128)S(1)} %copy-done.6, s32[528]{0:T(1024)S(1)} %get-tuple-element.28.far_list, s32[1]{0:T(128)} %get-tuple-element.39.far_count, bf16[128,32,256]{2,1,0:T(8,128)(2,1)S(1)} %get-tuple-element.40.row_ref, ...), custom_call_target="tpu_custom_call" | custom-call | flops 20000000000 | bytes 8388608 | tf_op jit(solution)/shard_map/near_halo/pallas_call | solution.py:742
  74.8 0.1 collective-permute-start.9
  74.9 1.1 %collective-permute-done.5.refs_13_ = bf16[4,2,32,128]{3,2,1,0:T(8,128)(2,1)S(1)} collective-permute-done((bf16[4,2,32,128]{3,2,1,0:T(8,128)(2,1)S(1)}, bf16[4,2,32,128]{3,2,1,0:T(8,128)(2,1)S(1)}, u32[]{:S(2)}, u32[]{:S(2)}) %collective-permute-start.5) | collective-permute-done | bytes 65568 | tf_op jit(solution)/shard_map/ppermute | solution.py:631
  76.0 3.7 %down.1 = (bf16[64,8,64]{2,1,0:T(8,128)(2,1)S(1)}, bf16[64,8,64]{2,1,0:T(8,128)(2,1)S(1)}) custom-call(f32[5]{0:T(128)S(1)} %copy-done.6, s32[3,255]{1,0:T(4,128)S(1)} %bitcast.17, s32[4,3]{1,0:T(4,128)S(1)} %copy-done.11, bf16[4,2,64,64]{3,2,1,0:T(8,128)(2,1)S(1)} %copy-done.8, bf16[4,3,64,64]{3,2,1,0:T(8,128)(2,1)S(1)} %copy-done.7, ...), custom_call_target="tpu_custom_call" | custom-call | flops 40000000000 | bytes 4194304 | tf_op jit(solution)/shard_map/down/pallas_call | solution.py:769
  79.7 1.3 %collective-permute-done.6.got_ref = bf16[64,8,64]{2,1,0:T(8,128)(2,1)S(1)} collective-permute-done((bf16[64,8,64]{2,1,0:T(8,128)(2,1)S(1)}, bf16[64,8,64]{2,1,0:T(8,128)(2,1)S(1)}, u32[]{:S(2)}, u32[]{:S(2)}) %collective-permute-start.6) | collective-permute-done | bytes 65568 | tf_op jit(solution)/shard_map/ppermute | solution.py:785
  81.1 6.7 %final.1 = f32[8,32768]{1,0:T(8,128)} custom-call(f32[5]{0:T(128)S(1)} %copy-done.6, bf16[64,8,64]{2,1,0:T(8,128)(2,1)S(1)} %get-tuple-element.37.mine_ref, bf16[64,8,64]{2,1,0:T(8,128)(2,1)S(1)} %collective-permute-done.6.got_ref, bf16[128,64,256]{2,1,0:T(8,128)(2,1)S(1)} %copy-done, f32[1,32768]{1,0:T(1,128)S(1)} %bitcast.12, ...), custom_call_target="tpu_custom_call" | custom-call | flops 2000000000 | bytes 4194304 | tf_op jit(solution)/shard_map/final/pallas_call | solution.py:787
  (49 shorter events, 0.2 us)
Async XLA Ops:
  0.0 2.2 %collective-permute-start = (bf16[8,32768]{1,0:T(8,128)(2,1)}, bf16[8,32768]{1,0:T(8,128)(2,1)S(1)}, u32[]{:S(2)}, u32[]{:S(2)}) collective-permute-start(bf16[8,32768]{1,0:T(8,128)(2,1)} %vec.1), channel_id=1, source_target_pairs={{0,1},{1,0},{2,3},{3,2},{4,5},{5,4},{6,7},{7,6},{8,9},{9,8},{10,11... | collective-permute-start | bytes 1572872 | tf_op jit(solution)/shard_map/ppermute | solution.py:658
  6.1 10.8 %copy-start.2 = (bf16[24,16384]{1,0:T(8,128)(2,1)S(1)}, bf16[24,16384]{1,0:T(8,128)(2,1)}, u32[]{:S(2)}) copy-start(bf16[24,16384]{1,0:T(8,128)(2,1)} %pack.1.pack_ref) | copy-start | bytes 2359300
  6.1 16.9 %copy-start.3 = (f32[3,32768]{1,0:T(4,128)S(1)}, f32[3,32768]{1,0:T(4,128)}, u32[]{:S(2)}) copy-start(f32[3,32768]{1,0:T(4,128)} %points_ref.1) | copy-start | bytes 1179652
  6.1 16.9 %copy-start.6 = (f32[5]{0:T(128)S(1)}, f32[5]{0:T(128)}, u32[]{:S(2)}) copy-start(f32[5]{0:T(128)} %pad_maximum_fusion.2.scale_ref.refs_0_) | copy-start | bytes 64
  6.1 16.9 %copy-start.10 = (s32[512]{0:T(512)S(1)}, s32[512]{0:T(512)}, u32[]{:S(2)}) copy-start(s32[512]{0:T(512)} %cols_ref.1) | copy-start | bytes 6148
  6.1 16.9 %copy-start.12 = (s32[128]{0:T(128)S(1)}, s32[128]{0:T(128)}, u32[]{:S(2)}) copy-start(s32[128]{0:T(128)} %offs_ref.1) | copy-start | bytes 1540
  14.8 41.7 %collective-permute-start.1 = (bf16[8,32,128]{2,1,0:T(8,128)(2,1)}, bf16[8,32,128]{2,1,0:T(8,128)(2,1)S(1)}, u32[]{:S(2)}, u32[]{:S(2)}) collective-permute-start(bf16[8,32,128]{2,1,0:T(8,128)(2,1)} %get-tuple-element.26.refs_8_), channel_id=1, source_target_pairs={{0,1},{1,0},{2,3},{3,2},{4,5},{5,4},{6,7},{7,6},{8,9},{9,8},{10,11... | collective-permute-start | bytes 196616 | tf_op jit(solution)/shard_map/ppermute | solution.py:695
  16.0 42.5 %slice-start = ((s8[6291456]{0:T(1024)(128)(4,1)}), s8[4194304]{0:T(1024)(128)(4,1)S(1)}, s32[]{:S(2)}) async-start(s8[6291456]{0:T(1024)(128)(4,1)} %bitcast.13), calls=%async_computation | async-start | bytes 8388608
  16.8 41.7 %slice-start.1 = ((s8[6291456]{0:T(1024)(128)(4,1)}), s8[2097152]{0:T(1024)(128)(4,1)S(1)}, s32[]{:S(2)}) async-start(s8[6291456]{0:T(1024)(128)(4,1)} %bitcast.13), calls=%async_computation.1 | async-start | bytes 4194304
  16.8 41.7 %copy-start.9 = (s32[255,3]{0,1:T(4,128)S(1)}, s32[255,3]{0,1:T(4,128)}, u32[]{:S(2)}) copy-start(s32[255,3]{0,1:T(4,128)} %param.22) | copy-start | bytes 9184
  16.8 41.7 %copy-start.14 = (bf16[127,32,128]{2,1,0:T(8,128)(2,1)S(1)}, bf16[127,32,128]{2,1,0:T(8,128)(2,1)}, u32[]{:S(2)}) copy-start(bf16[127,32,128]{2,1,0:T(8,128)(2,1)} %get-tuple-element.30.coef_ref) | copy-start | bytes 3121156
  16.8 53.9 %collective-permute-start.7 = (bf16[24,16384]{1,0:T(8,128)(2,1)S(1)}, bf16[24,16384]{1,0:T(8,128)(2,1)S(1)}, u32[]{:S(2)}, u32[]{:S(2)}) collective-permute-start(bf16[24,16384]{1,0:T(8,128)(2,1)S(1)} %copy-done.2), channel_id=1, source_target_pairs={{0,2},{2,4},{4,6},{6,8},{8,10},{10,12},{12,14},{1,3},{3,5},{5,7},{... | collective-permute-start | bytes 2359304 | tf_op jit(solution)/shard_map/ppermute | solution.py:673
  21.7 49.0 %collective-permute-start.8 = (bf16[24,16384]{1,0:T(8,128)(2,1)S(1)}, bf16[24,16384]{1,0:T(8,128)(2,1)S(1)}, u32[]{:S(2)}, u32[]{:S(2)}) collective-permute-start(bf16[24,16384]{1,0:T(8,128)(2,1)S(1)} %copy-done.2), channel_id=1, source_target_pairs={{2,0},{4,2},{6,4},{8,6},{10,8},{12,10},{14,12},{3,1},{5,3},{7,5},{... | collective-permute-start | bytes 2359304 | tf_op jit(solution)/shard_map/ppermute | solution.py:674
  56.5 9.7 %collective-permute-start.2 = (bf16[2,4,32,128]{3,2,1,0:T(8,128)(2,1)S(1)}, bf16[2,4,32,128]{3,2,1,0:T(8,128)(2,1)S(1)}, u32[]{:S(2)}, u32[]{:S(2)}) collective-permute-start(bf16[2,4,32,128]{3,2,1,0:T(8,128)(2,1)S(1)} %pad_maximum_fusion), channel_id=1, source_target_pairs={{0,2},{2,0},{4,6},{6,4},{8,10},{10,8},{12,14},{14,12},{1,3},{3,1},... | collective-permute-start | bytes 196616 | tf_op jit(solution)/shard_map/ppermute | solution.py:631
  66.3 8.6 %collective-permute-start.3 = (bf16[4,2,32,128]{3,2,1,0:T(8,128)(2,1)S(1)}, bf16[4,2,32,128]{3,2,1,0:T(8,128)(2,1)S(1)}, u32[]{:S(2)}, u32[]{:S(2)}) collective-permute-start(bf16[4,2,32,128]{3,2,1,0:T(8,128)(2,1)S(1)} %pad_maximum_fusion.1), channel_id=1, source_target_pairs={{0,4},{2,6},{4,0},{6,2},{8,12},{10,14},{12,8},{14,10},{1,5},{3,7},... | collective-permute-start | bytes 196616 | tf_op jit(solution)/shard_map/ppermute | solution.py:631
  67.1 7.7 %collective-permute-start.4 = (bf16[4,2,32,128]{3,2,1,0:T(8,128)(2,1)S(1)}, bf16[4,2,32,128]{3,2,1,0:T(8,128)(2,1)S(1)}, u32[]{:S(2)}, u32[]{:S(2)}) collective-permute-start(bf16[4,2,32,128]{3,2,1,0:T(8,128)(2,1)S(1)} %pad_maximum_fusion.1), channel_id=1, source_target_pairs={{0,8},{2,10},{4,12},{6,14},{8,0},{10,2},{12,4},{14,6},{1,9},{3,11}... | collective-permute-start | bytes 196616 | tf_op jit(solution)/shard_map/ppermute | solution.py:631
  69.8 6.2 %collective-permute-start.5 = (bf16[4,2,32,128]{3,2,1,0:T(8,128)(2,1)S(1)}, bf16[4,2,32,128]{3,2,1,0:T(8,128)(2,1)S(1)}, u32[]{:S(2)}, u32[]{:S(2)}) collective-permute-start(bf16[4,2,32,128]{3,2,1,0:T(8,128)(2,1)S(1)} %pad_maximum_fusion.1), channel_id=1, source_target_pairs={{0,12},{2,14},{4,8},{6,10},{8,4},{10,6},{12,0},{14,2},{1,13},{3,15... | collective-permute-start | bytes 196616 | tf_op jit(solution)/shard_map/ppermute | solution.py:631
  70.7 5.2 %copy-start.5 = (bf16[8,32,128]{2,1,0:T(8,128)(2,1)S(1)}, bf16[8,32,128]{2,1,0:T(8,128)(2,1)}, u32[]{:S(2)}) copy-start(bf16[8,32,128]{2,1,0:T(8,128)(2,1)} %get-tuple-element.26.refs_8_) | copy-start | bytes 196612
  70.7 5.2 %copy-start.7 = (bf16[4,3,64,64]{3,2,1,0:T(8,128)(2,1)S(1)}, bf16[4,3,64,64]{3,2,1,0:T(8,128)(2,1)}, u32[]{:S(2)}) copy-start(bf16[4,3,64,64]{3,2,1,0:T(8,128)(2,1)} %refs_4_.1) | copy-start | bytes 294916
  70.8 5.2 %copy-start.8 = (bf16[4,2,64,64]{3,2,1,0:T(8,128)(2,1)S(1)}, bf16[4,2,64,64]{3,2,1,0:T(8,128)(2,1)}, u32[]{:S(2)}) copy-start(bf16[4,2,64,64]{3,2,1,0:T(8,128)(2,1)} %refs_3_.1) | copy-start | bytes 196612
  70.8 5.2 %copy-start.11 = (s32[4,3]{1,0:T(4,128)S(1)}, s32[4,3]{1,0:T(4,128)}, u32[]{:S(2)}) copy-start(s32[4,3]{1,0:T(4,128)} %refs_2_.1) | copy-start | bytes 148
  70.8 5.2 %copy-start.13 = (bf16[64,64,128]{2,1,0:T(8,128)(2,1)S(1)}, bf16[64,64,128]{2,1,0:T(8,128)(2,1)}, u32[]{:S(2)}) copy-start(bf16[64,64,128]{2,1,0:T(8,128)(2,1)} %get-tuple-element.33.refs_7_) | copy-start | bytes 3145732
  74.8 6.3 %collective-permute-start.9 = (f32[8,32768]{1,0:T(8,128)S(1)}, f32[8,32768]{1,0:T(8,128)S(1)}, u32[]{:S(2)}, u32[]{:S(2)}) collective-permute-start(f32[8,32768]{1,0:T(8,128)S(1)} %get-tuple-element.44), channel_id=1, source_target_pairs={{0,1},{1,0},{2,3},{3,2},{4,5},{5,4},{6,7},{7,6},{8,9},{9,8},{10,11... | collective-permute-start | bytes 3145736 | tf_op jit(solution)/shard_map/ppermute | solution.py:758
  79.7 1.4 %collective-permute-start.6 = (bf16[64,8,64]{2,1,0:T(8,128)(2,1)S(1)}, bf16[64,8,64]{2,1,0:T(8,128)(2,1)S(1)}, u32[]{:S(2)}, u32[]{:S(2)}) collective-permute-start(bf16[64,8,64]{2,1,0:T(8,128)(2,1)S(1)} %get-tuple-element.38), channel_id=1, source_target_pairs={{0,1},{1,0},{2,3},{3,2},{4,5},{5,4},{6,7},{7,6},{8,9},{9,8},{10,11... | collective-permute-start | bytes 196616 | tf_op jit(solution)/shard_map/ppermute | solution.py:785
  (4 other events, 16.1 us)

commit v7 on v5

--- a/solution.py
+++ b/solution.py
@@ -183,6 +183,53 @@
     accumulate(jnp.maximum(turns * TURNS * 2 * PAIR - PAIR, 0), k1)
 
 
+def diagonal_loop(first_leaf, count, row_ref, col_ref, val_ref, sums, s0, s1, k0, k1):
+    mid = LEAF // 2
+
+    def distance(first, out):
+        for q in range(PAIR):
+            col = jnp.minimum(first + q, count - 1)
+            rows = row_ref[first_leaf + col]
+            out[q, :mid] = jnp.dot(col_ref[col, :mid], rows, preferred_element_type=F32)
+            out[q, mid:, mid:] = jnp.dot(
+                col_ref[col, mid:], rows[:, mid:], preferred_element_type=F32
+            )
+
+    def evaluate(squared, kern):
+        for q in range(PAIR):
+            kern[q, :mid] = matern(squared[q, :mid])
+            kern[q, mid:, mid:] = matern(squared[q, mid:, mid:])
+
+    def accumulate(first, kern):
+        for q in range(PAIR):
+            col = jnp.maximum(first + q, 0)
+            values = val_ref[col]
+            part = jnp.dot(values[:, :mid], kern[q, :mid], preferred_element_type=F32)
+            left = mul_nt(values[:, mid:], kern[q, :mid, mid:])
+            right = jnp.dot(values[:, mid:], kern[q, mid:, mid:], preferred_element_type=F32)
+            part = part + jnp.concatenate([left, right], axis=1)
+            here = lanes(first_leaf + col)
+            sums[0][:, here] += part[:PART]
+            sums[1][:, here] += part[PART:]
+
+    k1[...] = jnp.zeros_like(k1)
+    distance(0, s0)
+
+    def step(it, _):
+        for turn in range(TURNS):
+            first = (it * TURNS + turn) * 2 * PAIR
+            accumulate(first - PAIR, k1)
+            distance(first + PAIR, s1)
+            evaluate(s0, k0)
+            accumulate(first, k0)
+            distance(first + 2 * PAIR, s0)
+            evaluate(s1, k1)
+        return 0
+
+    lax.fori_loop(0, count // (TURNS * 2 * PAIR), step, 0)
+    accumulate(count - PAIR, k1)
+
+
 def load_columns(pack_ref, base, count, col_ref, val_ref):
     def step(i, _):
         for q in range(4):
@@ -224,12 +271,12 @@
                 own_list[own] = code + (place - leaves)
                 far_list[far] = code + place
                 block = place >> half_bits
-                own = jnp.where(block == 2, own + 1, own)
+                own = jnp.where(block + jnp.where(begins, 8, 0) == 2, own + 1, own)
                 far = jnp.where((block & 3) == 0, far + 1, far)
         return row, code, own, far
 
     zero = jnp.int32(0)
-    _, _, own, far = lax.fori_loop(0, leaves // 2, rows_step, (zero, zero, zero, zero))
+    _, _, own, far = lax.fori_loop(0, leaves // 2, rows_step, (zero - 1, zero - CODE, zero, zero))
     for q in range(PAD):
         own_list[own + q] = half
         far_list[far + q] = 8 * half
@@ -238,6 +285,7 @@
     val_ref[half] = jnp.zeros((16, LEAF), BF)
     col_ref[half] = jnp.zeros(col_ref.shape[1:], BF)
     sums = (mine_ref, other_ref)
+    diagonal_loop(half_id * half, half, row_ref, col_ref, val_ref, sums, s0, s1, k0, k1)
     block_loop(own, lambda c: c, own_list, row_ref, col_ref, val_ref, sums, s0, s1, k0, k1)
 
 
@@ -335,7 +383,7 @@
 
 
 def up_kernel(
-    scale_ref, pack_ref, basis_hbm, raw_hbm, coef_ref, export_ref, move_ref,
+    scale_ref, pack_ref, basis_hbm, raw_hbm, coef_ref, export_ref, front_ref, move_ref,
     basis_ref, raw_ref, flat, pairs, sems,
 ):
     core = whole(scale_ref[4])
@@ -413,6 +461,7 @@
     root = join_parts(mul_nt(jnp.where(side == core, crown.astype(F32), 0.0).astype(BF), root_move))
     export_ref[0] = split_parts(side_by_side(root, root))
     export_ref[1:EXPORT] = coef_ref[0 : EXPORT - 1]
+    front_ref[0] = export_ref[0 : EXPORT // 2]
 
 
 def joint(first, second, third):
@@ -651,7 +700,7 @@
             VMEM((3, half), F32), VMEM((PART, half), BF), VMEM((PART, half), BF),
             pltpu.SemaphoreType.DMA((3,)),
         ],
-        compiler_params=params(16),
+        compiler_params=params(8),
     )(scale, points, vectors, got)
     axes = ("leaf", "sub")
     left = lax.ppermute(pack, axes, [(i, i + 1) for i in range(count - 1)])
@@ -659,21 +708,21 @@
 
     moves_raw = jnp.transpose(local_transfer, (1, 2, 3, 0))
     part = leaves // 2
-    coef, export, moves = pl.pallas_call(
+    coef, export, front, moves = pl.pallas_call(
         up_kernel,
         name="up",
         out_shape=(
             sds((2 * part - 1, 2 * ALL, 2 * RANK), BF), sds((EXPORT, 2 * ALL, 2 * RANK), BF),
-            sds((part, RANK, 2 * RANK), BF),
+            sds((1, EXPORT // 2, 2 * ALL, 2 * RANK), BF), sds((part, RANK, 2 * RANK), BF),
         ),
         in_specs=[sspec(), vspec(), hspec(), hspec()],
-        out_specs=(vspec(),) * 3,
+        out_specs=(vspec(),) * 4,
         scratch_shapes=[
             VMEM((part, RANK, LEAF), BF), VMEM(moves_raw.shape, BF),
             VMEM((leaves // 8, RANK * 8, 2 * RANK), F32),
             VMEM((part - 1, 2 * ALL, 2 * RANK), BF), pltpu.SemaphoreType.DMA((8,)),
         ],
-        compiler_params=params(28),
+        compiler_params=params(18),
         cost_estimate=pl.CostEstimate(flops=8 * 10**9, bytes_accessed=8 << 20, transcendentals=0),
     )(scale, pack, leaf_basis, moves_raw)
     from_core = lax.ppermute(export, "vec", [(0, 1), (1, 0)])
@@ -691,16 +740,16 @@
             VMEM((leaves // 2 + 1, LEAF, 32), BF), VMEM((leaves // 2 + 1, 16, LEAF), BF),
             *scratch_blocks, SMEM((slots + PAD,), jnp.int32),
         ],
-        compiler_params=params(28),
+        compiler_params=params(22),
         cost_estimate=pl.CostEstimate(
             flops=36 * 10**9, bytes_accessed=8 << 20, transcendentals=190 * 2**17
         ),
     )(scale, near_offsets, near_cols, points, pack)
 
     from_core = after(from_core, far_list)
-    near_pair = jnp.stack([export[0:4], from_core[0:4]])
+    near_pair = jnp.concatenate([front, from_core[None, 0 : EXPORT // 2]], axis=0)
+    coef_late, near_pair = lax.optimization_barrier((coef, near_pair))
     from_next = swap_mask(near_pair, 1)
-    coef_late = after(coef, far_list)
     ties_raw = jnp.transpose(local_coupling, (1, 2, 3, 0))
     mates = jnp.transpose(local_partners)
     local, ties = pl.pallas_call(
@@ -717,13 +766,12 @@
             VMEM((leaves // 4, RANK * 8, RANK), F32), pltpu.SemaphoreType.DMA((4,)),
         ],
         compiler_params=params(36),
-        cost_estimate=pl.CostEstimate(flops=9 * 10**9, bytes_accessed=8 << 20, transcendentals=0),
+        cost_estimate=pl.CostEstimate(flops=16 * 10**9, bytes_accessed=8 << 20, transcendentals=0),
     )(scale, mates, coef_late, ties_raw)
 
-    from_next = after(from_next, local)
+    first, _, from_next = lax.optimization_barrier((first, local, from_next))
     quad = jnp.concatenate([near_pair[:, 0:2], from_next[:, 0:2]], axis=0)
     from_far = [swap_mask(quad, mask) for mask in (2, 4, 6)]
-    first = after(first, local)
     mine, other = pl.pallas_call(
         near_halo_kernel,
         name="near_halo",
@@ -735,14 +783,14 @@
             VMEM((leaves + 1, LEAF, 32), BF), VMEM((leaves + 1, 16, LEAF), BF),
             *scratch_blocks,
         ],
-        compiler_params=params(36),
+        compiler_params=params(26),
         cost_estimate=pl.CostEstimate(
-            flops=4 * 10**9, bytes_accessed=8 << 20, transcendentals=60 * 2**17
+            flops=20 * 10**9, bytes_accessed=8 << 20, transcendentals=60 * 2**17
         ),
     )(scale, far_list, far_count, row_feat, left, right, first, second)
     swapped = lax.ppermute(other, "vec", [(0, 1), (1, 0)])
 
-    tops = export[None, 0:1]
+    tops = export
     if dev_levels > SPAN:
         tops = jnp.concatenate(
             [export[None, 0:1], from_core[None, 0:1], from_next[:, 0:1]]
@@ -761,8 +809,8 @@
             VMEM((2 * 2**SPAN, EXPORT, 2 * ALL, 2 * RANK), BF),
             VMEM((part - 1, 2 * ALL, RANK), BF), VMEM((2 * count, 2 * ALL, RANK), BF),
         ],
-        compiler_params=params(24),
-        cost_estimate=pl.CostEstimate(flops=4 * 10**9, bytes_accessed=4 << 20, transcendentals=0),
+        compiler_params=params(14),
+        cost_estimate=pl.CostEstimate(flops=40 * 10**9, bytes_accessed=4 << 20, transcendentals=0),
     )(
         scale, mates, top_partners, top_transfer, top_coupling, ties, local, moves,
         export, from_core, from_next, *from_far, tops,
@@ -776,7 +824,7 @@
         in_specs=[sspec()] + [vspec()] * 7,
         out_specs=hspec(),
         scratch_shapes=[VMEM((PART, size), F32), pltpu.SemaphoreType.DMA((4,))],
-        compiler_params=params(16),
+        compiler_params=params(10),
         cost_estimate=pl.CostEstimate(flops=2 * 10**9, bytes_accessed=4 << 20, transcendentals=0),
     )(scale, low_mine, low_got, leaf_basis, noise.reshape(1, size), vectors, mine, swapped)
 

time: 92.1 us -> 84.8 us (0.921)
  waiting for transfers between devices: 10.2 us -> 2.52 us
  Pallas kernels: 58.7 us -> 60.9 us
  starting transfers between devices: 15.3 us -> 14 us
    ppermute x4, waiting for transfers between devices: 7.96 us -> 0.37 us  [swap_mask(): lax.ppermute(value, ('leaf', 'sub'), [(i, i ^ mask) for i in range(total)])]
    ppermute x4, starting transfers between devices: 8.11 us -> 6.71 us  [swap_mask(): lax.ppermute(value, ('leaf', 'sub'), [(i, i ^ mask) for i in range(total)])]
    pallas_call x1, Pallas kernels: 32.7 us -> 34 us  [body(): pl.pallas_call(near_local_kernel, name='near_local', out_shape=(sds((PART...]
  transfers between devices with their start and end apart: 10 -> 10, of which waited for: 5 -> 3; matrix products, arithmetic and copies ran while one was open for 1% -> 1% of each run, Pallas kernels for 48% -> 60%
where the time goes in v7:
time: 84.8 us; the launch traced here: 84.4 us
  Pallas kernels  60.9 us (72%)
  starting transfers between devices  14 us (17%)
  local copies, waits for them, and re-layouts  5.93 us (7%)
  waiting for transfers between devices  2.52 us (3%)
    pallas_call x1, Pallas kernels, body(): pl.pallas_call(near_local_kernel, name='near_local', out_shape=(sds((PART...  34 us
    pallas_call x1, Pallas kernels, body(): pl.pallas_call(couple_kernel, name='couple', out_shape=(sds((part - 1, AL...  7.7 us
    ppermute x4, starting transfers between devices, swap_mask(): lax.ppermute(value, ('leaf', 'sub'), [(i, i ^ mask) for i in range(total)])  6.71 us
    unnamed x32, local copies, waits for them, and re-layouts  5.92 us
    pallas_call x1, Pallas kernels, body(): pl.pallas_call(up_kernel, name='up', out_shape=(sds((2 * part - 1, 2 * AL...  5.7 us
    pallas_call x1, Pallas kernels, body(): pl.pallas_call(near_halo_kernel, name='near_halo', out_shape=(sds((PART,...  5.02 us
    ppermute x1, starting transfers between devices, body(): left = lax.ppermute(pack, axes, [(i, i + 1) for i in range(count - 1)])  4.84 us
    pallas_call x1, Pallas kernels, body(): pl.pallas_call(final_kernel, name='final', out_shape=sds((PART, size), F3...  3.83 us
  transfers between devices with their start and end apart: 10, of which 3 were waited for; matrix products, arithmetic and copies ran while one was open for 1% of the time, Pallas kernels for 60%

profile of v7, /device:TPU:0, one launch (start us, length us, event | category | flops | bytes accessed | tf_op | source)
XLA Modules:
  0.0 84.4 jit_solution(8622119691287092127)
XLA Ops:
  0.0 0.5 collective-permute-start
  0.5 0.7 pad_maximum_fusion.2.scale_ref.refs_0_
  1.3 0.9 %collective-permute-done.got_hbm = bf16[8,32768]{1,0:T(8,128)(2,1)S(1)} collective-permute-done((bf16[8,32768]{1,0:T(8,128)(2,1)}, bf16[8,32768]{1,0:T(8,128)(2,1)S(1)}, u32[]{:S(2)}, u32[]{:S(2)}) %collective-permute-start) | collective-permute-done | bytes 524320 | tf_op jit(solution)/shard_map/ppermute | solution.py:691
  2.2 1.0 %copy-done.2 = bf16[8,32768]{1,0:T(8,128)(2,1)S(1)} copy-done((bf16[8,32768]{1,0:T(8,128)(2,1)S(1)}, bf16[8,32768]{1,0:T(8,128)(2,1)}, u32[]{:S(2)}) %copy-start.2) | copy-done | bytes 524312
  3.2 1.0 %copy-done.4 = f32[3,32768]{1,0:T(4,128)S(1)} copy-done((f32[3,32768]{1,0:T(4,128)S(1)}, f32[3,32768]{1,0:T(4,128)}, u32[]{:S(2)}) %copy-start.4) | copy-done | bytes 393240
  4.3 1.0 %pack.1.pack_ref = bf16[24,16384]{1,0:T(8,128)(2,1)S(1)} custom-call(f32[5]{0:T(128)S(1)} %pad_maximum_fusion.2.scale_ref.refs_0_, f32[3,32768]{1,0:T(4,128)S(1)} %copy-done.4, bf16[8,32768]{1,0:T(8,128)(2,1)S(1)} %copy-done.2, bf16[8,32768]{1,0:T(8,128)(2,1)S(1)} %collective-permute-done.got_hbm), custom_call_target="tpu_custom_call" | custom-call | tf_op jit(solution)/shard_map/pack/pallas_call | solution.py:693
  5.3 2.2 %copy-done = bf16[128,64,256]{2,1,0:T(8,128)(2,1)S(1)} copy-done((bf16[128,64,256]{2,1,0:T(8,128)(2,1)S(1)}, bf16[128,64,256]{2,1,0:T(8,128)(2,1)}, u32[]{:S(2)}) %copy-start) | copy-done | bytes 4194328
  7.5 1.6 %copy-done.7 = bf16[127,2,64,64]{0,3,2,1:T(8,128)(2,1)S(1)} copy-done((bf16[127,2,64,64]{0,3,2,1:T(8,128)(2,1)S(1)}, bf16[127,2,64,64]{0,3,2,1:T(8,128)(2,1)}, u32[]{:S(2)}) %copy-start.7) | copy-done | bytes 2080792
  9.1 5.7 %up.1 = (bf16[127,32,128]{2,1,0:T(8,128)(2,1)S(1)}, bf16[8,32,128]{2,1,0:T(8,128)(2,1)S(1)}, bf16[1,4,32,128]{3,2,1,0:T(8,128)(2,1)S(1)}, bf16[64,64,128]{2,1,0:T(8,128)(2,1)S(1)}) custom-call(f32[5]{0:T(128)S(1)} %pad_maximum_fusion.2.scale_ref.refs_0_, bf16[24,16384]{1,0:T(8,128)(2,1)S(1)} %pack.1.pack_ref, bf16[128,64,256]{2,1,0:T(8,128)(2,1)S(1)} %copy-done, ...), custom_call_target="tpu_custom_call" | custom-call | flops 8000000000 | bytes 8388608 | tf_op jit(solution)/shard_map/up/pallas_call | solution.py:711
  14.8 0.4 collective-permute-start.1
  15.3 4.8 %collective-permute-start.7 = (bf16[24,16384]{1,0:T(8,128)(2,1)S(1)}, bf16[24,16384]{1,0:T(8,128)(2,1)S(1)}, u32[]{:S(2)}, u32[]{:S(2)}) collective-permute-start(bf16[24,16384]{1,0:T(8,128)(2,1)S(1)} %pack.1.pack_ref), channel_id=1, source_target_pairs={{0,2},{2,4},{4,6},{6,8},{8,10},{10,12},{12,14},{1,3},{3,5},{5,7},{... | collective-permute-start | bytes 2359304 | tf_op jit(solution)/shard_map/ppermute | solution.py:706
  20.1 1.3 %collective-permute-start.8 = (bf16[24,16384]{1,0:T(8,128)(2,1)S(1)}, bf16[24,16384]{1,0:T(8,128)(2,1)S(1)}, u32[]{:S(2)}, u32[]{:S(2)}) collective-permute-start(bf16[24,16384]{1,0:T(8,128)(2,1)S(1)} %pack.1.pack_ref), channel_id=1, source_target_pairs={{2,0},{4,2},{6,4},{8,6},{10,8},{12,10},{14,12},{3,1},{5,3},{7,5},{... | collective-permute-start | bytes 2359304 | tf_op jit(solution)/shard_map/ppermute | solution.py:707
  21.4 34.0 %near_local.1 = (f32[8,32768]{1,0:T(8,128)S(1)}, f32[8,32768]{1,0:T(8,128)S(1)}, bf16[128,32,256]{2,1,0:T(8,128)(2,1)S(1)}, s32[528]{0:T(1024)S(1)}, s32[1]{0:T(128)}) custom-call(f32[5]{0:T(128)S(1)} %pad_maximum_fusion.2.scale_ref.refs_0_, s32[128]{0:T(128)S(1)} %copy-done.13, s32[512]{0:T(512)S(1)} %copy-done.11, f32[3,32768]{1,0:T(4,128)S(1)} %copy-done.5, ...), custom_call_target="tpu_custom_call" | custom-call | flops 35999997952 | bytes 8388608 | tf_op jit(solution)/shard_map/near_local/pallas_call | solution.py:730
  55.5 1.9 %collective-permute-start.2 = (bf16[2,4,32,128]{3,2,1,0:T(8,128)(2,1)S(1)}, bf16[2,4,32,128]{3,2,1,0:T(8,128)(2,1)S(1)}, u32[]{:S(2)}, u32[]{:S(2)}) collective-permute-start(bf16[2,4,32,128]{3,2,1,0:T(8,128)(2,1)S(1)} %pad_maximum_fusion), channel_id=1, source_target_pairs={{0,2},{2,0},{4,6},{6,4},{8,10},{10,8},{12,14},{14,12},{1,3},{3,1},... | collective-permute-start | bytes 196616 | tf_op jit(solution)/shard_map/ppermute | solution.py:664
  57.4 7.7 %couple.1 = (f32[63,16,128]{2,1,0:T(8,128)S(1)}, bf16[8,64,192]{2,1,0:T(8,128)(2,1)S(1)}) custom-call(f32[5]{0:T(128)S(1)} %pad_maximum_fusion.2.scale_ref.refs_0_, s32[3,255]{1,0:T(4,128)S(1)} %bitcast.13, bf16[127,32,128]{2,1,0:T(8,128)(2,1)S(1)} %get-tuple-element.32.coef_ref, bf16[3,64,64,255]{3,2,1,0:T(8,128)(2,1)S(1)} %bitcast.11), custom_call_target="tpu_custom_call" | custom-call | flops 16000000000 | bytes 8388608 | tf_op jit(solution)/shard_map/couple/pallas_call | solution.py:755
  65.2 1.6 %collective-permute-start.3 = (bf16[4,2,32,128]{3,2,1,0:T(8,128)(2,1)S(1)}, bf16[4,2,32,128]{3,2,1,0:T(8,128)(2,1)S(1)}, u32[]{:S(2)}, u32[]{:S(2)}) collective-permute-start(bf16[4,2,32,128]{3,2,1,0:T(8,128)(2,1)S(1)} %pad_maximum_fusion.1), channel_id=1, source_target_pairs={{0,4},{2,6},{4,0},{6,2},{8,12},{10,14},{12,8},{14,10},{1,5},{3,7},... | collective-permute-start | bytes 196616 | tf_op jit(solution)/shard_map/ppermute | solution.py:664
  66.7 2.6 %collective-permute-start.4 = (bf16[4,2,32,128]{3,2,1,0:T(8,128)(2,1)S(1)}, bf16[4,2,32,128]{3,2,1,0:T(8,128)(2,1)S(1)}, u32[]{:S(2)}, u32[]{:S(2)}) collective-permute-start(bf16[4,2,32,128]{3,2,1,0:T(8,128)(2,1)S(1)} %pad_maximum_fusion.1), channel_id=1, source_target_pairs={{0,8},{2,10},{4,12},{6,14},{8,0},{10,2},{12,4},{14,6},{1,9},{3,11}... | collective-permute-start | bytes 196616 | tf_op jit(solution)/shard_map/ppermute | solution.py:664
  69.4 0.6 collective-permute-start.5
  70.0 5.0 %near_halo.1 = (f32[8,32768]{1,0:T(8,128)S(1)}, f32[8,32768]{1,0:T(8,128)S(1)}) custom-call(f32[5]{0:T(128)S(1)} %pad_maximum_fusion.2.scale_ref.refs_0_, s32[528]{0:T(1024)S(1)} %get-tuple-element.30.far_list, s32[1]{0:T(128)} %get-tuple-element.41.far_count, bf16[128,32,256]{2,1,0:T(8,128)(2,1)S(1)} %get-tuple-element.42.row_ref, ...), custom_call_target="tpu_custom_call" | custom-call | flops 20000000000 | bytes 8388608 | tf_op jit(solution)/shard_map/near_halo/pallas_call | solution.py:775
  75.1 0.4 collective-permute-done.5.refs_13_
  75.5 3.7 %down.1 = (bf16[64,8,64]{2,1,0:T(8,128)(2,1)S(1)}, bf16[64,8,64]{2,1,0:T(8,128)(2,1)S(1)}) custom-call(f32[5]{0:T(128)S(1)} %pad_maximum_fusion.2.scale_ref.refs_0_, s32[3,255]{1,0:T(4,128)S(1)} %bitcast.14, s32[4,3]{1,0:T(4,128)S(1)} %copy-done.12, bf16[4,2,64,64]{3,2,1,0:T(8,128)(2,1)S(1)} %copy-done.9, bf16[4,3,64,64]{3,2,1,0:T(8,128)(2,1)S(1)} %copy-done.8, ...), custom_call_target="tpu_custom_call" | custom-call | flops 40000000000 | bytes 4194304 | tf_op jit(solution)/shard_map/down/pallas_call | solution.py:802
  79.2 0.2 collective-permute-start.6
  79.4 1.2 %collective-permute-done.6.got_ref = bf16[64,8,64]{2,1,0:T(8,128)(2,1)S(1)} collective-permute-done((bf16[64,8,64]{2,1,0:T(8,128)(2,1)S(1)}, bf16[64,8,64]{2,1,0:T(8,128)(2,1)S(1)}, u32[]{:S(2)}, u32[]{:S(2)}) %collective-permute-start.6) | collective-permute-done | bytes 65568 | tf_op jit(solution)/shard_map/ppermute | solution.py:818
  80.6 3.8 %final.1 = f32[8,32768]{1,0:T(8,128)} custom-call(f32[5]{0:T(128)S(1)} %pad_maximum_fusion.2.scale_ref.refs_0_, bf16[64,8,64]{2,1,0:T(8,128)(2,1)S(1)} %get-tuple-element.39.mine_ref, bf16[64,8,64]{2,1,0:T(8,128)(2,1)S(1)} %collective-permute-done.6.got_ref, bf16[128,64,256]{2,1,0:T(8,128)(2,1)S(1)} %copy-done.1, f32[1,32768]{1,0:T(1,128)S(1)} %bitcast.8, ...), custom_call_target="tpu_custom_call" | custom-call | flops 2000000000 | bytes 4194304 | tf_op jit(solution)/shard_map/final/pallas_call | solution.py:820
  (43 shorter events, 0.3 us)
Async XLA Ops:
  0.0 2.2 %collective-permute-start = (bf16[8,32768]{1,0:T(8,128)(2,1)}, bf16[8,32768]{1,0:T(8,128)(2,1)S(1)}, u32[]{:S(2)}, u32[]{:S(2)}) collective-permute-start(bf16[8,32768]{1,0:T(8,128)(2,1)} %vec.1), channel_id=1, source_target_pairs={{0,1},{1,0},{2,3},{3,2},{4,5},{5,4},{6,7},{7,6},{8,9},{9,8},{10,11... | collective-permute-start | bytes 1572872 | tf_op jit(solution)/shard_map/ppermute | solution.py:691
  5.3 2.2 %copy-start = (bf16[128,64,256]{2,1,0:T(8,128)(2,1)S(1)}, bf16[128,64,256]{2,1,0:T(8,128)(2,1)}, u32[]{:S(2)}) copy-start(bf16[128,64,256]{2,1,0:T(8,128)(2,1)} %basis.1) | copy-start | bytes 12582916
  7.5 1.6 %copy-start.7 = (bf16[127,2,64,64]{0,3,2,1:T(8,128)(2,1)S(1)}, bf16[127,2,64,64]{0,3,2,1:T(8,128)(2,1)}, u32[]{:S(2)}) copy-start(bf16[127,2,64,64]{0,3,2,1:T(8,128)(2,1)} %param.18) | copy-start | bytes 6242308
  9.1 12.3 %copy-start.5 = (f32[3,32768]{1,0:T(4,128)S(1)}, f32[3,32768]{1,0:T(4,128)}, u32[]{:S(2)}) copy-start(f32[3,32768]{1,0:T(4,128)} %points_ref.1) | copy-start | bytes 1179652
  9.1 12.4 %copy-start.11 = (s32[512]{0:T(512)S(1)}, s32[512]{0:T(512)}, u32[]{:S(2)}) copy-start(s32[512]{0:T(512)} %cols_ref.1) | copy-start | bytes 6148
  9.1 12.4 %copy-start.13 = (s32[128]{0:T(128)S(1)}, s32[128]{0:T(128)}, u32[]{:S(2)}) copy-start(s32[128]{0:T(128)} %offs_ref.1) | copy-start | bytes 1540
  14.8 42.6 %slice-start = ((s8[6291456]{0:T(1024)(128)(4,1)}), s8[4194304]{0:T(1024)(128)(4,1)S(1)}, s32[]{:S(2)}) async-start(s8[6291456]{0:T(1024)(128)(4,1)} %bitcast.9), calls=%async_computation | async-start | bytes 8388608
  14.8 42.6 %slice-start.1 = ((s8[6291456]{0:T(1024)(128)(4,1)}), s8[2097152]{0:T(1024)(128)(4,1)S(1)}, s32[]{:S(2)}) async-start(s8[6291456]{0:T(1024)(128)(4,1)} %bitcast.9), calls=%async_computation.1 | async-start | bytes 4194304
  14.8 42.6 %copy-start.10 = (s32[255,3]{0,1:T(4,128)S(1)}, s32[255,3]{0,1:T(4,128)}, u32[]{:S(2)}) copy-start(s32[255,3]{0,1:T(4,128)} %param.22) | copy-start | bytes 9184
  14.8 40.6 %collective-permute-start.1 = (bf16[8,32,128]{2,1,0:T(8,128)(2,1)S(1)}, bf16[8,32,128]{2,1,0:T(8,128)(2,1)S(1)}, u32[]{:S(2)}, u32[]{:S(2)}) collective-permute-start(bf16[8,32,128]{2,1,0:T(8,128)(2,1)S(1)} %get-tuple-element.28.refs_8_.refs_14_), channel_id=1, source_target_pairs={{0,1},{1,0},{2,3},{3,2},{4,5},{5,4},{6,7},{7,6},{8,9},{9,8},{10,11... | collective-permute-start | bytes 196616 | tf_op jit(solution)/shard_map/ppermute | solution.py:728
  15.3 54.7 %collective-permute-start.7 = (bf16[24,16384]{1,0:T(8,128)(2,1)S(1)}, bf16[24,16384]{1,0:T(8,128)(2,1)S(1)}, u32[]{:S(2)}, u32[]{:S(2)}) collective-permute-start(bf16[24,16384]{1,0:T(8,128)(2,1)S(1)} %pack.1.pack_ref), channel_id=1, source_target_pairs={{0,2},{2,4},{4,6},{6,8},{8,10},{10,12},{12,14},{1,3},{3,5},{5,7},{... | collective-permute-start | bytes 2359304 | tf_op jit(solution)/shard_map/ppermute | solution.py:706
  20.1 49.9 %collective-permute-start.8 = (bf16[24,16384]{1,0:T(8,128)(2,1)S(1)}, bf16[24,16384]{1,0:T(8,128)(2,1)S(1)}, u32[]{:S(2)}, u32[]{:S(2)}) collective-permute-start(bf16[24,16384]{1,0:T(8,128)(2,1)S(1)} %pack.1.pack_ref), channel_id=1, source_target_pairs={{2,0},{4,2},{6,4},{8,6},{10,8},{12,10},{14,12},{3,1},{5,3},{7,5},{... | collective-permute-start | bytes 2359304 | tf_op jit(solution)/shard_map/ppermute | solution.py:707
  55.5 9.7 %collective-permute-start.2 = (bf16[2,4,32,128]{3,2,1,0:T(8,128)(2,1)S(1)}, bf16[2,4,32,128]{3,2,1,0:T(8,128)(2,1)S(1)}, u32[]{:S(2)}, u32[]{:S(2)}) collective-permute-start(bf16[2,4,32,128]{3,2,1,0:T(8,128)(2,1)S(1)} %pad_maximum_fusion), channel_id=1, source_target_pairs={{0,2},{2,0},{4,6},{6,4},{8,10},{10,8},{12,14},{14,12},{1,3},{3,1},... | collective-permute-start | bytes 196616 | tf_op jit(solution)/shard_map/ppermute | solution.py:664
  65.2 9.9 %collective-permute-start.3 = (bf16[4,2,32,128]{3,2,1,0:T(8,128)(2,1)S(1)}, bf16[4,2,32,128]{3,2,1,0:T(8,128)(2,1)S(1)}, u32[]{:S(2)}, u32[]{:S(2)}) collective-permute-start(bf16[4,2,32,128]{3,2,1,0:T(8,128)(2,1)S(1)} %pad_maximum_fusion.1), channel_id=1, source_target_pairs={{0,4},{2,6},{4,0},{6,2},{8,12},{10,14},{12,8},{14,10},{1,5},{3,7},... | collective-permute-start | bytes 196616 | tf_op jit(solution)/shard_map/ppermute | solution.py:664
  66.7 8.4 %collective-permute-start.4 = (bf16[4,2,32,128]{3,2,1,0:T(8,128)(2,1)S(1)}, bf16[4,2,32,128]{3,2,1,0:T(8,128)(2,1)S(1)}, u32[]{:S(2)}, u32[]{:S(2)}) collective-permute-start(bf16[4,2,32,128]{3,2,1,0:T(8,128)(2,1)S(1)} %pad_maximum_fusion.1), channel_id=1, source_target_pairs={{0,8},{2,10},{4,12},{6,14},{8,0},{10,2},{12,4},{14,6},{1,9},{3,11}... | collective-permute-start | bytes 196616 | tf_op jit(solution)/shard_map/ppermute | solution.py:664
  69.4 6.1 %collective-permute-start.5 = (bf16[4,2,32,128]{3,2,1,0:T(8,128)(2,1)S(1)}, bf16[4,2,32,128]{3,2,1,0:T(8,128)(2,1)S(1)}, u32[]{:S(2)}, u32[]{:S(2)}) collective-permute-start(bf16[4,2,32,128]{3,2,1,0:T(8,128)(2,1)S(1)} %pad_maximum_fusion.1), channel_id=1, source_target_pairs={{0,12},{2,14},{4,8},{6,10},{8,4},{10,6},{12,0},{14,2},{1,13},{3,15... | collective-permute-start | bytes 196616 | tf_op jit(solution)/shard_map/ppermute | solution.py:664
  70.0 5.5 %copy-start.8 = (bf16[4,3,64,64]{3,2,1,0:T(8,128)(2,1)S(1)}, bf16[4,3,64,64]{3,2,1,0:T(8,128)(2,1)}, u32[]{:S(2)}) copy-start(bf16[4,3,64,64]{3,2,1,0:T(8,128)(2,1)} %refs_4_.1) | copy-start | bytes 294916
  70.0 5.5 %copy-start.9 = (bf16[4,2,64,64]{3,2,1,0:T(8,128)(2,1)S(1)}, bf16[4,2,64,64]{3,2,1,0:T(8,128)(2,1)}, u32[]{:S(2)}) copy-start(bf16[4,2,64,64]{3,2,1,0:T(8,128)(2,1)} %refs_3_.1) | copy-start | bytes 196612
  70.0 5.5 %copy-start.12 = (s32[4,3]{1,0:T(4,128)S(1)}, s32[4,3]{1,0:T(4,128)}, u32[]{:S(2)}) copy-start(s32[4,3]{1,0:T(4,128)} %refs_2_.1) | copy-start | bytes 148
  75.0 5.6 %collective-permute-start.9 = (f32[8,32768]{1,0:T(8,128)S(1)}, f32[8,32768]{1,0:T(8,128)S(1)}, u32[]{:S(2)}, u32[]{:S(2)}) collective-permute-start(f32[8,32768]{1,0:T(8,128)S(1)} %get-tuple-element.46), channel_id=1, source_target_pairs={{0,1},{1,0},{2,3},{3,2},{4,5},{5,4},{6,7},{7,6},{8,9},{9,8},{10,11... | collective-permute-start | bytes 3145736 | tf_op jit(solution)/shard_map/ppermute | solution.py:791
  75.5 5.1 %copy-start.1 = (bf16[128,64,256]{2,1,0:T(8,128)(2,1)S(1)}, bf16[128,64,256]{2,1,0:T(8,128)(2,1)}, u32[]{:S(2)}) copy-start(bf16[128,64,256]{2,1,0:T(8,128)(2,1)} %basis.1) | copy-start | bytes 12582916
  75.5 5.1 %copy-start.3 = (bf16[8,32768]{1,0:T(8,128)(2,1)S(1)}, bf16[8,32768]{1,0:T(8,128)(2,1)}, u32[]{:S(2)}) copy-start(bf16[8,32768]{1,0:T(8,128)(2,1)} %vec.1) | copy-start | bytes 1572868
  75.5 5.1 %copy-start.6 = (f32[32768]{0:T(1024)S(1)}, f32[32768]{0:T(1024)}, u32[]{:S(2)}) copy-start(f32[32768]{0:T(1024)} %param.15) | copy-start | bytes 393220
  79.2 1.4 %collective-permute-start.6 = (bf16[64,8,64]{2,1,0:T(8,128)(2,1)S(1)}, bf16[64,8,64]{2,1,0:T(8,128)(2,1)S(1)}, u32[]{:S(2)}, u32[]{:S(2)}) collective-permute-start(bf16[64,8,64]{2,1,0:T(8,128)(2,1)S(1)} %get-tuple-element.40), channel_id=1, source_target_pairs={{0,1},{1,0},{2,3},{3,2},{4,5},{5,4},{6,7},{7,6},{8,9},{9,8},{10,11... | collective-permute-start | bytes 196616 | tf_op jit(solution)/shard_map/ppermute | solution.py:818
  (2 other events, 2.1 us)

commit v8 on v7

--- a/solution.py
+++ b/solution.py
@@ -20,7 +20,6 @@
 ROOT3 = math.sqrt(3.0)
 TINY = 1e-12
 PAIR = 2
-PAD = 16
 TURNS = 2
 CODE_BITS = 10
 CODE = 2**CODE_BITS
@@ -140,10 +139,56 @@
     lax.fori_loop(0, half // 2048, step, 0)
 
 
-def block_loop(count, place, list_ref, row_ref, col_ref, val_ref, sums, s0, s1, k0, k1):
+def plan_kernel(scale_ref, offs_ref, cols_ref, out_ref):
+    device, half_id = whole(scale_ref[3]), whole(scale_ref[4])
+    leaves = offs_ref.shape[1]
+    slots = cols_ref.shape[1]
+    room = out_ref.shape[1]
+    half = leaves // 2
+    half_bits = half.bit_length() - 1
+    begins = jnp.broadcast_to(offs_ref[...].astype(F32), (8, leaves)).T[:, 0:1]
+    slot = lax.broadcasted_iota(jnp.int32, (leaves, slots), 1).astype(F32)
+    row = jnp.sum(jnp.where(begins <= slot, 1.0, 0.0), axis=0, keepdims=True) - 1.0
+    first = jnp.sum(jnp.where(begins == slot, 1.0, 0.0), axis=0, keepdims=True)
+    place = cols_ref[...] - (device * leaves - leaves + half_id * half)
+    block = place >> half_bits
+    own = jnp.where(block == 2, 1.0 - first, 0.0)
+    far = jnp.where((block & 3) == 0, 1.0, 0.0)
+    kinds = jnp.concatenate([own, far, jnp.zeros((6, slots), F32)], axis=0)
+    earlier = lax.broadcasted_iota(jnp.int32, (slots, slots), 0)
+    later = lax.broadcasted_iota(jnp.int32, (slots, slots), 1)
+    upto = jnp.where(earlier <= later, 1.0, 0.0).astype(BF)
+    rank = jnp.dot(kinds.astype(BF), upto, preferred_element_type=F32)
+    turned = rank.T
+    target = lax.broadcasted_iota(jnp.int32, (slots, room), 1).astype(F32) + 1.0
+    at = lax.broadcasted_iota(jnp.int32, (1, room), 1).astype(F32)
+    upper, lower = (place >> 4).astype(F32), (place & 15).astype(F32)
+    lists = []
+    for kind, (mask, shift, spare) in enumerate(
+        ((own, float(leaves), float(half)), (far, 0.0, 8.0 * half))
+    ):
+        parts = jnp.concatenate(
+            [row * mask, upper * mask, lower * mask, jnp.zeros((5, slots), F32)], axis=0
+        )
+        hits = jnp.where(turned[:, kind : kind + 1] == target, 1.0, 0.0).astype(BF)
+        got = jnp.dot(parts.astype(BF), hits, preferred_element_type=F32)
+        code = got[0:1] * float(CODE) + got[1:2] * 16.0 + got[2:3] - shift
+        total = rank[kind : kind + 1, slots - 1 : slots]
+        lists.append((jnp.where(at < total, code, spare), total))
+    out_ref[...] = jnp.concatenate(
+        [
+            lists[0][0], lists[1][0],
+            jnp.broadcast_to(lists[0][1], (1, room)), jnp.broadcast_to(lists[1][1], (1, room)),
+            jnp.zeros((4, room), F32),
+        ],
+        axis=0,
+    ).astype(jnp.int32)
+
+
+def block_loop(kind, place, plan_ref, row_ref, col_ref, val_ref, sums, s0, s1, k0, k1):
     def accumulate(first, kern):
         for q in range(PAIR):
-            code = list_ref[first + q]
+            code = plan_ref[kind, first + q]
             here = lanes(code >> CODE_BITS)
             part = jnp.dot(
                 val_ref[place(code & (CODE - 1))], kern[q], preferred_element_type=F32
@@ -153,7 +198,7 @@
 
     def distance(first, out):
         for q in range(PAIR):
-            code = list_ref[first + q]
+            code = plan_ref[kind, first + q]
             out[q] = jnp.dot(
                 col_ref[place(code & (CODE - 1))],
                 row_ref[code >> CODE_BITS],
@@ -178,6 +223,7 @@
             evaluate(s1, k1)
         return 0
 
+    count = plan_ref[2 + kind, 0]
     turns = (count + TURNS * 2 * PAIR - 1) // (TURNS * 2 * PAIR)
     lax.fori_loop(0, turns, step, 0)
     accumulate(jnp.maximum(turns * TURNS * 2 * PAIR - PAIR, 0), k1)
@@ -242,69 +288,47 @@
 
 
 def near_local_kernel(
-    scale_ref, offs_ref, cols_ref, points_ref, pack_ref,
-    mine_ref, other_ref, row_ref, far_list, far_count,
-    col_ref, val_ref, s0, s1, k0, k1, own_list,
+    scale_ref, plan_ref, points_ref, pack_ref,
+    mine_ref, other_ref, row_ref,
+    col_ref, val_ref, s0, s1, k0, k1,
 ):
-    device, half_id = whole(scale_ref[3]), whole(scale_ref[4])
-    leaves = offs_ref.shape[0]
+    half_id = whole(scale_ref[4])
+    leaves = row_ref.shape[0]
     half = leaves // 2
-    slots = cols_ref.shape[0]
-    each = slots // leaves
-
-    far_base = device * leaves - leaves + half_id * half
-    half_bits = half.bit_length() - 1
-
-    def rows_step(i, carry):
-        row, code, own, far = carry
-        for q in range(2):
-            leaf = i * 2 + q
+
+    def rows_step(i, _):
+        for q in range(4):
+            leaf = i * 4 + q
             row_ref[leaf] = row_features(coordinate_rows(points_ref[:, lanes(leaf)], scale_ref))
             mine_ref[:, lanes(leaf)] = jnp.zeros((PART, LEAF), F32)
             other_ref[:, lanes(leaf)] = jnp.zeros((PART, LEAF), F32)
-            for w in range(each):
-                slot = leaf * each + w
-                begins = offs_ref[jnp.minimum(row + 1, leaves - 1)] == slot
-                row = jnp.where(begins, row + 1, row)
-                code = jnp.where(begins, code + CODE, code)
-                place = cols_ref[slot] - far_base
-                own_list[own] = code + (place - leaves)
-                far_list[far] = code + place
-                block = place >> half_bits
-                own = jnp.where(block + jnp.where(begins, 8, 0) == 2, own + 1, own)
-                far = jnp.where((block & 3) == 0, far + 1, far)
-        return row, code, own, far
-
-    zero = jnp.int32(0)
-    _, _, own, far = lax.fori_loop(0, leaves // 2, rows_step, (zero - 1, zero - CODE, zero, zero))
-    for q in range(PAD):
-        own_list[own + q] = half
-        far_list[far + q] = 8 * half
-    far_count[0] = far
+        return 0
+
+    lax.fori_loop(0, leaves // 4, rows_step, 0)
     load_columns(pack_ref, 0, half, col_ref, val_ref)
     val_ref[half] = jnp.zeros((16, LEAF), BF)
     col_ref[half] = jnp.zeros(col_ref.shape[1:], BF)
     sums = (mine_ref, other_ref)
     diagonal_loop(half_id * half, half, row_ref, col_ref, val_ref, sums, s0, s1, k0, k1)
-    block_loop(own, lambda c: c, own_list, row_ref, col_ref, val_ref, sums, s0, s1, k0, k1)
+    block_loop(0, lambda c: c, plan_ref, row_ref, col_ref, val_ref, sums, s0, s1, k0, k1)
 
 
 def near_halo_kernel(
-    scale_ref, far_list, far_count, row_ref, left_ref, right_ref, first_in, second_in,
+    scale_ref, plan_ref, row_ref, left_ref, right_ref, first_in, second_in,
     mine_ref, other_ref,
     first, second, col_ref, val_ref, s0, s1, k0, k1,
 ):
     core = whole(scale_ref[4])
     half = left_ref.shape[1] // LEAF
     bits = half.bit_length() - 1
-    count = far_count[0]
+    count = plan_ref[3, 0]
 
     def place(code):
         return (code & (half - 1)) | ((code >> (bits + 2)) << bits)
 
     def load(i, _):
         for q in range(4):
-            code = far_list[i * 4 + q] & (CODE - 1)
+            code = plan_ref[1, i * 4 + q] & (CODE - 1)
             here = lanes(code & (half - 1))
             after = code >= 4 * half
             values = jnp.where(after, right_ref[0:16, here], left_ref[0:16, here])
@@ -319,7 +343,7 @@
     val_ref[2 * half] = jnp.zeros((16, LEAF), BF)
     col_ref[2 * half] = jnp.zeros(col_ref.shape[1:], BF)
     sums = (first, second)
-    block_loop(count, place, far_list, row_ref, col_ref, val_ref, sums, s0, s1, k0, k1)
+    block_loop(1, place, plan_ref, row_ref, col_ref, val_ref, sums, s0, s1, k0, k1)
 
     @pl.when(core == 0)
     def _():
@@ -690,6 +714,15 @@
 
     got = lax.ppermute(vectors, "vec", [(0, 1), (1, 0)])
 
+    plan = pl.pallas_call(
+        plan_kernel,
+        name="plan",
+        out_shape=sds((8, slots + 128), jnp.int32),
+        in_specs=[sspec(), vspec(), vspec()],
+        out_specs=vspec(),
+        compiler_params=params(16),
+    )(scale, near_offsets.reshape(1, leaves), near_cols.reshape(1, slots))
+
     pack = pl.pallas_call(
         pack_kernel,
         name="pack",
@@ -727,26 +760,25 @@
     )(scale, pack, leaf_basis, moves_raw)
     from_core = lax.ppermute(export, "vec", [(0, 1), (1, 0)])
     pack, _ = lax.optimization_barrier((pack, export))
-    first, second, row_feat, far_list, far_count = pl.pallas_call(
+    first, second, row_feat = pl.pallas_call(
         near_local_kernel,
         name="near_local",
         out_shape=(
             sds((PART, size), F32), sds((PART, size), F32), sds((leaves, 32, LEAF), BF),
-            sds((slots + PAD,), jnp.int32), sds((1,), jnp.int32),
         ),
-        in_specs=[sspec()] * 3 + [vspec()] * 2,
-        out_specs=(vspec(), vspec(), vspec(), sspec(), sspec()),
+        in_specs=[sspec()] * 2 + [vspec()] * 2,
+        out_specs=(vspec(), vspec(), vspec()),
         scratch_shapes=[
             VMEM((leaves // 2 + 1, LEAF, 32), BF), VMEM((leaves // 2 + 1, 16, LEAF), BF),
-            *scratch_blocks, SMEM((slots + PAD,), jnp.int32),
+            *scratch_blocks,
         ],
         compiler_params=params(22),
         cost_estimate=pl.CostEstimate(
             flops=36 * 10**9, bytes_accessed=8 << 20, transcendentals=190 * 2**17
         ),
-    )(scale, near_offsets, near_cols, points, pack)
-
-    from_core = after(from_core, far_list)
+    )(scale, plan, points, pack)
+
+    from_core = after(from_core, first)
     near_pair = jnp.concatenate([front, from_core[None, 0 : EXPORT // 2]], axis=0)
     coef_late, near_pair = lax.optimization_barrier((coef, near_pair))
     from_next = swap_mask(near_pair, 1)
@@ -776,7 +808,7 @@
         near_halo_kernel,
         name="near_halo",
         out_shape=(sds((PART, size), F32), sds((PART, size), F32)),
-        in_specs=[sspec()] * 3 + [vspec()] * 5,
+        in_specs=[sspec()] * 2 + [vspec()] * 5,
         out_specs=(vspec(), vspec()),
         scratch_shapes=[
             VMEM((PART, size), F32), VMEM((PART, size), F32),
@@ -787,7 +819,7 @@
         cost_estimate=pl.CostEstimate(
             flops=20 * 10**9, bytes_accessed=8 << 20, transcendentals=60 * 2**17
         ),
-    )(scale, far_list, far_count, row_feat, left, right, first, second)
+    )(scale, plan, row_feat, left, right, first, second)
     swapped = lax.ppermute(other, "vec", [(0, 1), (1, 0)])
 
     tops = export

time: 84.8 us -> 82.8 us (0.976)
  Pallas kernels: 60.9 us -> 57 us
  local copies, waits for them, and re-layouts: 5.93 us -> 7.26 us
  waiting for transfers between devices: 2.52 us -> 3.42 us
    pallas_call x1, Pallas kernels: 34 us -> 29.9 us  [body(): pl.pallas_call(near_local_kernel, name='near_local', out_shape=(sds((PART...]
    ppermute x4, waiting for transfers between devices: 0.37 us -> 2.07 us  [swap_mask(): lax.ppermute(value, ('leaf', 'sub'), [(i, i ^ mask) for i in range(total)])]
    pallas_call x0 -> x1, Pallas kernels: none -> 1.57 us  [body(): pl.pallas_call(plan_kernel, name='plan', out_shape=sds((8, slots + 128),...]
    unnamed x32, local copies, waits for them, and re-layouts: 5.92 us -> 7.24 us
    pallas_call x1, Pallas kernels: 5.02 us -> 3.7 us  [body(): pl.pallas_call(near_halo_kernel, name='near_halo', out_shape=(sds((PART,...]
    ppermute x1, waiting for transfers between devices: 0.94 us -> 0.01 us  [body(): got = lax.ppermute(vectors, 'vec', [(0, 1), (1, 0)])]
  transfers between devices with their start and end apart: 10 -> 10, of which waited for: 3 -> 2; matrix products, arithmetic and copies ran while one was open for 1% -> 1% of each run, Pallas kernels for 60% -> 56%
where the time goes in v8:
time: 82.8 us; the launch traced here: 82.7 us
  Pallas kernels  57 us (69%)
  starting transfers between devices  13.9 us (17%)
  local copies, waits for them, and re-layouts  7.26 us (9%)
  waiting for transfers between devices  3.42 us (4%)
    pallas_call x1, Pallas kernels, body(): pl.pallas_call(near_local_kernel, name='near_local', out_shape=(sds((PART...  29.9 us
    pallas_call x1, Pallas kernels, body(): pl.pallas_call(couple_kernel, name='couple', out_shape=(sds((part - 1, AL...  7.7 us
    unnamed x32, local copies, waits for them, and re-layouts  7.24 us
    ppermute x4, starting transfers between devices, swap_mask(): lax.ppermute(value, ('leaf', 'sub'), [(i, i ^ mask) for i in range(total)])  6.73 us
    pallas_call x1, Pallas kernels, body(): pl.pallas_call(up_kernel, name='up', out_shape=(sds((2 * part - 1, 2 * AL...  5.7 us
    ppermute x1, starting transfers between devices, body(): left = lax.ppermute(pack, axes, [(i, i + 1) for i in range(count - 1)])  5.14 us
    pallas_call x1, Pallas kernels, body(): pl.pallas_call(final_kernel, name='final', out_shape=sds((PART, size), F3...  3.84 us
    pallas_call x1, Pallas kernels, body(): pl.pallas_call(near_halo_kernel, name='near_halo', out_shape=(sds((PART,...  3.7 us
  transfers between devices with their start and end apart: 10, of which 2 were waited for; matrix products, arithmetic and copies ran while one was open for 1% of the time, Pallas kernels for 56%

profile of v8, /device:TPU:0, one launch (start us, length us, event | category | flops | bytes accessed | tf_op | source)
XLA Modules:
  0.0 82.7 jit_solution(10875488252336771603)
XLA Ops:
  0.0 0.5 collective-permute-start
  0.5 0.7 pad_maximum_fusion.2.scale_ref.refs_0_
  1.3 0.7 copy-done.7
  1.9 0.7 copy-done.8
  2.6 1.6 %plan.1.plan_ref = s32[8,640]{1,0:T(8,128)S(1)} custom-call(f32[5]{0:T(128)S(1)} %pad_maximum_fusion.2.scale_ref.refs_0_, s32[1,128]{1,0:T(1,128)S(1)} %bitcast.12, s32[1,512]{1,0:T(1,128)S(1)} %bitcast.11), custom_call_target="tpu_custom_call" | custom-call | tf_op jit(solution)/shard_map/plan/pallas_call | solution.py:717
  4.2 1.0 %copy-done.2 = bf16[8,32768]{1,0:T(8,128)(2,1)S(1)} copy-done((bf16[8,32768]{1,0:T(8,128)(2,1)S(1)}, bf16[8,32768]{1,0:T(8,128)(2,1)}, u32[]{:S(2)}) %copy-start.2) | copy-done | bytes 524312
  5.2 1.0 %copy-done.4 = f32[3,32768]{1,0:T(4,128)S(1)} copy-done((f32[3,32768]{1,0:T(4,128)S(1)}, f32[3,32768]{1,0:T(4,128)}, u32[]{:S(2)}) %copy-start.4) | copy-done | bytes 393240
  6.3 1.0 %pack.1.pack_ref = bf16[24,16384]{1,0:T(8,128)(2,1)S(1)} custom-call(f32[5]{0:T(128)S(1)} %pad_maximum_fusion.2.scale_ref.refs_0_, f32[3,32768]{1,0:T(4,128)S(1)} %copy-done.4, bf16[8,32768]{1,0:T(8,128)(2,1)S(1)} %copy-done.2, bf16[8,32768]{1,0:T(8,128)(2,1)S(1)} %collective-permute-done.got_hbm), custom_call_target="tpu_custom_call" | custom-call | tf_op jit(solution)/shard_map/pack/pallas_call | solution.py:726
  7.3 2.2 %copy-done = bf16[128,64,256]{2,1,0:T(8,128)(2,1)S(1)} copy-done((bf16[128,64,256]{2,1,0:T(8,128)(2,1)S(1)}, bf16[128,64,256]{2,1,0:T(8,128)(2,1)}, u32[]{:S(2)}) %copy-start) | copy-done | bytes 4194328
  9.5 1.6 %copy-done.9 = bf16[127,2,64,64]{0,3,2,1:T(8,128)(2,1)S(1)} copy-done((bf16[127,2,64,64]{0,3,2,1:T(8,128)(2,1)S(1)}, bf16[127,2,64,64]{0,3,2,1:T(8,128)(2,1)}, u32[]{:S(2)}) %copy-start.9) | copy-done | bytes 2080792
  11.1 5.7 %up.1 = (bf16[127,32,128]{2,1,0:T(8,128)(2,1)S(1)}, bf16[8,32,128]{2,1,0:T(8,128)(2,1)S(1)}, bf16[1,4,32,128]{3,2,1,0:T(8,128)(2,1)S(1)}, bf16[64,64,128]{2,1,0:T(8,128)(2,1)S(1)}) custom-call(f32[5]{0:T(128)S(1)} %pad_maximum_fusion.2.scale_ref.refs_0_, bf16[24,16384]{1,0:T(8,128)(2,1)S(1)} %pack.1.pack_ref, bf16[128,64,256]{2,1,0:T(8,128)(2,1)S(1)} %copy-done, ...), custom_call_target="tpu_custom_call" | custom-call | flops 8000000000 | bytes 8388608 | tf_op jit(solution)/shard_map/up/pallas_call | solution.py:744
  16.9 5.1 %collective-permute-start.7 = (bf16[24,16384]{1,0:T(8,128)(2,1)S(1)}, bf16[24,16384]{1,0:T(8,128)(2,1)S(1)}, u32[]{:S(2)}, u32[]{:S(2)}) collective-permute-start(bf16[24,16384]{1,0:T(8,128)(2,1)S(1)} %pack.1.pack_ref), channel_id=1, source_target_pairs={{0,2},{2,4},{4,6},{6,8},{8,10},{10,12},{12,14},{1,3},{3,5},{5,7},{... | collective-permute-start | bytes 2359304 | tf_op jit(solution)/shard_map/ppermute | solution.py:739
  22.1 1.3 %collective-permute-start.8 = (bf16[24,16384]{1,0:T(8,128)(2,1)S(1)}, bf16[24,16384]{1,0:T(8,128)(2,1)S(1)}, u32[]{:S(2)}, u32[]{:S(2)}) collective-permute-start(bf16[24,16384]{1,0:T(8,128)(2,1)S(1)} %pack.1.pack_ref), channel_id=1, source_target_pairs={{2,0},{4,2},{6,4},{8,6},{10,8},{12,10},{14,12},{3,1},{5,3},{7,5},{... | collective-permute-start | bytes 2359304 | tf_op jit(solution)/shard_map/ppermute | solution.py:740
  23.4 29.9 %near_local.1 = (f32[8,32768]{1,0:T(8,128)S(1)}, f32[8,32768]{1,0:T(8,128)S(1)}, bf16[128,32,256]{2,1,0:T(8,128)(2,1)S(1)}) custom-call(f32[5]{0:T(128)S(1)} %pad_maximum_fusion.2.scale_ref.refs_0_, s32[8,640]{1,0:T(8,128)S(1)} %plan.1.plan_ref, f32[3,32768]{1,0:T(4,128)S(1)} %copy-done.5, bf16[24,16384]{1,0:T(8,128)(2,1)S(1)} %pack.1.pack_ref), custom_call_target="tpu_custom_call" | custom-call | flops 35999997952 | bytes 8388608 | tf_op jit(solution)/shard_map/near_local/pallas_call | solution.py:763
  53.3 1.1 %collective-permute-start.2 = (bf16[2,4,32,128]{3,2,1,0:T(8,128)(2,1)S(1)}, bf16[2,4,32,128]{3,2,1,0:T(8,128)(2,1)S(1)}, u32[]{:S(2)}, u32[]{:S(2)}) collective-permute-start(bf16[2,4,32,128]{3,2,1,0:T(8,128)(2,1)S(1)} %pad_maximum_fusion), channel_id=1, source_target_pairs={{0,2},{2,0},{4,6},{6,4},{8,10},{10,8},{12,14},{14,12},{1,3},{3,1},... | collective-permute-start | bytes 196616 | tf_op jit(solution)/shard_map/ppermute | solution.py:688
  54.5 7.7 %couple.1 = (f32[63,16,128]{2,1,0:T(8,128)S(1)}, bf16[8,64,192]{2,1,0:T(8,128)(2,1)S(1)}) custom-call(f32[5]{0:T(128)S(1)} %pad_maximum_fusion.2.scale_ref.refs_0_, s32[3,255]{1,0:T(4,128)S(1)} %bitcast.17, bf16[127,32,128]{2,1,0:T(8,128)(2,1)S(1)} %get-tuple-element.30.coef_ref, bf16[3,64,64,255]{3,2,1,0:T(8,128)(2,1)S(1)} %bitcast.15), custom_call_target="tpu_custom_call" | custom-call | flops 16000000000 | bytes 8388608 | tf_op jit(solution)/shard_map/couple/pallas_call | solution.py:787
  62.2 3.2 %collective-permute-start.3 = (bf16[4,2,32,128]{3,2,1,0:T(8,128)(2,1)S(1)}, bf16[4,2,32,128]{3,2,1,0:T(8,128)(2,1)S(1)}, u32[]{:S(2)}, u32[]{:S(2)}) collective-permute-start(bf16[4,2,32,128]{3,2,1,0:T(8,128)(2,1)S(1)} %pad_maximum_fusion.1), channel_id=1, source_target_pairs={{0,4},{2,6},{4,0},{6,2},{8,12},{10,14},{12,8},{14,10},{1,5},{3,7},... | collective-permute-start | bytes 196616 | tf_op jit(solution)/shard_map/ppermute | solution.py:688
  65.4 2.0 %collective-permute-start.4 = (bf16[4,2,32,128]{3,2,1,0:T(8,128)(2,1)S(1)}, bf16[4,2,32,128]{3,2,1,0:T(8,128)(2,1)S(1)}, u32[]{:S(2)}, u32[]{:S(2)}) collective-permute-start(bf16[4,2,32,128]{3,2,1,0:T(8,128)(2,1)S(1)} %pad_maximum_fusion.1), channel_id=1, source_target_pairs={{0,8},{2,10},{4,12},{6,14},{8,0},{10,2},{12,4},{14,6},{1,9},{3,11}... | collective-permute-start | bytes 196616 | tf_op jit(solution)/shard_map/ppermute | solution.py:688
  67.4 0.4 collective-permute-start.5
  67.9 3.7 %near_halo.1 = (f32[8,32768]{1,0:T(8,128)S(1)}, f32[8,32768]{1,0:T(8,128)S(1)}) custom-call(f32[5]{0:T(128)S(1)} %pad_maximum_fusion.2.scale_ref.refs_0_, s32[8,640]{1,0:T(8,128)S(1)} %plan.1.plan_ref, bf16[128,32,256]{2,1,0:T(8,128)(2,1)S(1)} %get-tuple-element.38.row_ref, bf16[24,16384]{1,0:T(8,128)(2,1)S(1)} %collective-permute-done.7.left_ref, ...), custom_call_target="tpu_custom_call" | custom-call | flops 20000000000 | bytes 8388608 | tf_op jit(solution)/shard_map/near_halo/pallas_call | solution.py:807
  71.7 2.1 %collective-permute-done.4.refs_12_ = bf16[4,2,32,128]{3,2,1,0:T(8,128)(2,1)S(1)} collective-permute-done((bf16[4,2,32,128]{3,2,1,0:T(8,128)(2,1)S(1)}, bf16[4,2,32,128]{3,2,1,0:T(8,128)(2,1)S(1)}, u32[]{:S(2)}, u32[]{:S(2)}) %collective-permute-start.4) | collective-permute-done | bytes 65568 | tf_op jit(solution)/shard_map/ppermute | solution.py:688
  73.8 3.6 %down.1 = (bf16[64,8,64]{2,1,0:T(8,128)(2,1)S(1)}, bf16[64,8,64]{2,1,0:T(8,128)(2,1)S(1)}) custom-call(f32[5]{0:T(128)S(1)} %pad_maximum_fusion.2.scale_ref.refs_0_, s32[3,255]{1,0:T(4,128)S(1)} %bitcast.18, s32[4,3]{1,0:T(4,128)S(1)} %copy-done.13, bf16[4,2,64,64]{3,2,1,0:T(8,128)(2,1)S(1)} %copy-done.11, bf16[4,3,64,64]{3,2,1,0:T(8,128)(2,1)S(1)} %copy-done.10, ...), custom_call_target="tpu_custom_call" | custom-call | flops 40000000000 | bytes 4194304 | tf_op jit(solution)/shard_map/down/pallas_call | solution.py:834
  77.5 1.3 %collective-permute-done.6.got_ref = bf16[64,8,64]{2,1,0:T(8,128)(2,1)S(1)} collective-permute-done((bf16[64,8,64]{2,1,0:T(8,128)(2,1)S(1)}, bf16[64,8,64]{2,1,0:T(8,128)(2,1)S(1)}, u32[]{:S(2)}, u32[]{:S(2)}) %collective-permute-start.6) | collective-permute-done | bytes 65568 | tf_op jit(solution)/shard_map/ppermute | solution.py:850
  78.8 3.8 %final.1 = f32[8,32768]{1,0:T(8,128)} custom-call(f32[5]{0:T(128)S(1)} %pad_maximum_fusion.2.scale_ref.refs_0_, bf16[64,8,64]{2,1,0:T(8,128)(2,1)S(1)} %get-tuple-element.36.mine_ref, bf16[64,8,64]{2,1,0:T(8,128)(2,1)S(1)} %collective-permute-done.6.got_ref, bf16[128,64,256]{2,1,0:T(8,128)(2,1)S(1)} %copy-done.1, f32[1,32768]{1,0:T(1,128)S(1)} %bitcast.10, ...), custom_call_target="tpu_custom_call" | custom-call | flops 2000000000 | bytes 4194304 | tf_op jit(solution)/shard_map/final/pallas_call | solution.py:852
  (44 shorter events, 0.5 us)
Async XLA Ops:
  0.0 4.2 %collective-permute-start = (bf16[8,32768]{1,0:T(8,128)(2,1)}, bf16[8,32768]{1,0:T(8,128)(2,1)S(1)}, u32[]{:S(2)}, u32[]{:S(2)}) collective-permute-start(bf16[8,32768]{1,0:T(8,128)(2,1)} %vec.1), channel_id=1, source_target_pairs={{0,1},{1,0},{2,3},{3,2},{4,5},{5,4},{6,7},{7,6},{8,9},{9,8},{10,11... | collective-permute-start | bytes 1572872 | tf_op jit(solution)/shard_map/ppermute | solution.py:715
  4.2 1.0 %copy-start.2 = (bf16[8,32768]{1,0:T(8,128)(2,1)S(1)}, bf16[8,32768]{1,0:T(8,128)(2,1)}, u32[]{:S(2)}) copy-start(bf16[8,32768]{1,0:T(8,128)(2,1)} %vec.1) | copy-start | bytes 1572868
  5.2 1.0 %copy-start.4 = (f32[3,32768]{1,0:T(4,128)S(1)}, f32[3,32768]{1,0:T(4,128)}, u32[]{:S(2)}) copy-start(f32[3,32768]{1,0:T(4,128)} %points_ref.1) | copy-start | bytes 1179652
  7.3 2.2 %copy-start = (bf16[128,64,256]{2,1,0:T(8,128)(2,1)S(1)}, bf16[128,64,256]{2,1,0:T(8,128)(2,1)}, u32[]{:S(2)}) copy-start(bf16[128,64,256]{2,1,0:T(8,128)(2,1)} %basis.1) | copy-start | bytes 12582916
  9.5 1.6 %copy-start.9 = (bf16[127,2,64,64]{0,3,2,1:T(8,128)(2,1)S(1)}, bf16[127,2,64,64]{0,3,2,1:T(8,128)(2,1)}, u32[]{:S(2)}) copy-start(bf16[127,2,64,64]{0,3,2,1:T(8,128)(2,1)} %param.18) | copy-start | bytes 6242308
  11.1 12.3 %copy-start.5 = (f32[3,32768]{1,0:T(4,128)S(1)}, f32[3,32768]{1,0:T(4,128)}, u32[]{:S(2)}) copy-start(f32[3,32768]{1,0:T(4,128)} %points_ref.1) | copy-start | bytes 1179652
  16.8 37.7 %slice-start = ((s8[6291456]{0:T(1024)(128)(4,1)}), s8[4194304]{0:T(1024)(128)(4,1)S(1)}, s32[]{:S(2)}) async-start(s8[6291456]{0:T(1024)(128)(4,1)} %bitcast.13), calls=%async_computation | async-start | bytes 8388608
  16.8 37.7 %slice-start.1 = ((s8[6291456]{0:T(1024)(128)(4,1)}), s8[2097152]{0:T(1024)(128)(4,1)S(1)}, s32[]{:S(2)}) async-start(s8[6291456]{0:T(1024)(128)(4,1)} %bitcast.13), calls=%async_computation.1 | async-start | bytes 4194304
  16.8 37.7 %copy-start.12 = (s32[255,3]{0,1:T(4,128)S(1)}, s32[255,3]{0,1:T(4,128)}, u32[]{:S(2)}) copy-start(s32[255,3]{0,1:T(4,128)} %param.22) | copy-start | bytes 9184
  16.8 36.5 %collective-permute-start.1 = (bf16[8,32,128]{2,1,0:T(8,128)(2,1)S(1)}, bf16[8,32,128]{2,1,0:T(8,128)(2,1)S(1)}, u32[]{:S(2)}, u32[]{:S(2)}) collective-permute-start(bf16[8,32,128]{2,1,0:T(8,128)(2,1)S(1)} %get-tuple-element.26.refs_8_.refs_14_), channel_id=1, source_target_pairs={{0,1},{1,0},{2,3},{3,2},{4,5},{5,4},{6,7},{7,6},{8,9},{9,8},{10,11... | collective-permute-start | bytes 196616 | tf_op jit(solution)/shard_map/ppermute | solution.py:761
  16.9 50.9 %collective-permute-start.7 = (bf16[24,16384]{1,0:T(8,128)(2,1)S(1)}, bf16[24,16384]{1,0:T(8,128)(2,1)S(1)}, u32[]{:S(2)}, u32[]{:S(2)}) collective-permute-start(bf16[24,16384]{1,0:T(8,128)(2,1)S(1)} %pack.1.pack_ref), channel_id=1, source_target_pairs={{0,2},{2,4},{4,6},{6,8},{8,10},{10,12},{12,14},{1,3},{3,5},{5,7},{... | collective-permute-start | bytes 2359304 | tf_op jit(solution)/shard_map/ppermute | solution.py:739
  22.1 45.7 %collective-permute-start.8 = (bf16[24,16384]{1,0:T(8,128)(2,1)S(1)}, bf16[24,16384]{1,0:T(8,128)(2,1)S(1)}, u32[]{:S(2)}, u32[]{:S(2)}) collective-permute-start(bf16[24,16384]{1,0:T(8,128)(2,1)S(1)} %pack.1.pack_ref), channel_id=1, source_target_pairs={{2,0},{4,2},{6,4},{8,6},{10,8},{12,10},{14,12},{3,1},{5,3},{7,5},{... | collective-permute-start | bytes 2359304 | tf_op jit(solution)/shard_map/ppermute | solution.py:740
  53.3 8.9 %collective-permute-start.2 = (bf16[2,4,32,128]{3,2,1,0:T(8,128)(2,1)S(1)}, bf16[2,4,32,128]{3,2,1,0:T(8,128)(2,1)S(1)}, u32[]{:S(2)}, u32[]{:S(2)}) collective-permute-start(bf16[2,4,32,128]{3,2,1,0:T(8,128)(2,1)S(1)} %pad_maximum_fusion), channel_id=1, source_target_pairs={{0,2},{2,0},{4,6},{6,4},{8,10},{10,8},{12,14},{14,12},{1,3},{3,1},... | collective-permute-start | bytes 196616 | tf_op jit(solution)/shard_map/ppermute | solution.py:688
  62.2 9.4 %collective-permute-start.3 = (bf16[4,2,32,128]{3,2,1,0:T(8,128)(2,1)S(1)}, bf16[4,2,32,128]{3,2,1,0:T(8,128)(2,1)S(1)}, u32[]{:S(2)}, u32[]{:S(2)}) collective-permute-start(bf16[4,2,32,128]{3,2,1,0:T(8,128)(2,1)S(1)} %pad_maximum_fusion.1), channel_id=1, source_target_pairs={{0,4},{2,6},{4,0},{6,2},{8,12},{10,14},{12,8},{14,10},{1,5},{3,7},... | collective-permute-start | bytes 196616 | tf_op jit(solution)/shard_map/ppermute | solution.py:688
  65.4 8.3 %collective-permute-start.4 = (bf16[4,2,32,128]{3,2,1,0:T(8,128)(2,1)S(1)}, bf16[4,2,32,128]{3,2,1,0:T(8,128)(2,1)S(1)}, u32[]{:S(2)}, u32[]{:S(2)}) collective-permute-start(bf16[4,2,32,128]{3,2,1,0:T(8,128)(2,1)S(1)} %pad_maximum_fusion.1), channel_id=1, source_target_pairs={{0,8},{2,10},{4,12},{6,14},{8,0},{10,2},{12,4},{14,6},{1,9},{3,11}... | collective-permute-start | bytes 196616 | tf_op jit(solution)/shard_map/ppermute | solution.py:688
  67.4 6.3 %collective-permute-start.5 = (bf16[4,2,32,128]{3,2,1,0:T(8,128)(2,1)S(1)}, bf16[4,2,32,128]{3,2,1,0:T(8,128)(2,1)S(1)}, u32[]{:S(2)}, u32[]{:S(2)}) collective-permute-start(bf16[4,2,32,128]{3,2,1,0:T(8,128)(2,1)S(1)} %pad_maximum_fusion.1), channel_id=1, source_target_pairs={{0,12},{2,14},{4,8},{6,10},{8,4},{10,6},{12,0},{14,2},{1,13},{3,15... | collective-permute-start | bytes 196616 | tf_op jit(solution)/shard_map/ppermute | solution.py:688
  67.8 5.9 %copy-start.10 = (bf16[4,3,64,64]{3,2,1,0:T(8,128)(2,1)S(1)}, bf16[4,3,64,64]{3,2,1,0:T(8,128)(2,1)}, u32[]{:S(2)}) copy-start(bf16[4,3,64,64]{3,2,1,0:T(8,128)(2,1)} %refs_4_.1) | copy-start | bytes 294916
  67.8 5.9 %copy-start.11 = (bf16[4,2,64,64]{3,2,1,0:T(8,128)(2,1)S(1)}, bf16[4,2,64,64]{3,2,1,0:T(8,128)(2,1)}, u32[]{:S(2)}) copy-start(bf16[4,2,64,64]{3,2,1,0:T(8,128)(2,1)} %refs_3_.1) | copy-start | bytes 196612
  67.8 5.9 %copy-start.13 = (s32[4,3]{1,0:T(4,128)S(1)}, s32[4,3]{1,0:T(4,128)}, u32[]{:S(2)}) copy-start(s32[4,3]{1,0:T(4,128)} %refs_2_.1) | copy-start | bytes 148
  71.6 7.2 %collective-permute-start.9 = (f32[8,32768]{1,0:T(8,128)S(1)}, f32[8,32768]{1,0:T(8,128)S(1)}, u32[]{:S(2)}, u32[]{:S(2)}) collective-permute-start(f32[8,32768]{1,0:T(8,128)S(1)} %get-tuple-element.42), channel_id=1, source_target_pairs={{0,1},{1,0},{2,3},{3,2},{4,5},{5,4},{6,7},{7,6},{8,9},{9,8},{10,11... | collective-permute-start | bytes 3145736 | tf_op jit(solution)/shard_map/ppermute | solution.py:823
  73.7 5.1 %copy-start.1 = (bf16[128,64,256]{2,1,0:T(8,128)(2,1)S(1)}, bf16[128,64,256]{2,1,0:T(8,128)(2,1)}, u32[]{:S(2)}) copy-start(bf16[128,64,256]{2,1,0:T(8,128)(2,1)} %basis.1) | copy-start | bytes 12582916
  73.8 5.1 %copy-start.3 = (bf16[8,32768]{1,0:T(8,128)(2,1)S(1)}, bf16[8,32768]{1,0:T(8,128)(2,1)}, u32[]{:S(2)}) copy-start(bf16[8,32768]{1,0:T(8,128)(2,1)} %vec.1) | copy-start | bytes 1572868
  73.8 5.1 %copy-start.6 = (f32[32768]{0:T(1024)S(1)}, f32[32768]{0:T(1024)}, u32[]{:S(2)}) copy-start(f32[32768]{0:T(1024)} %param.15) | copy-start | bytes 393220
  77.4 1.4 %collective-permute-start.6 = (bf16[64,8,64]{2,1,0:T(8,128)(2,1)S(1)}, bf16[64,8,64]{2,1,0:T(8,128)(2,1)S(1)}, u32[]{:S(2)}, u32[]{:S(2)}) collective-permute-start(bf16[64,8,64]{2,1,0:T(8,128)(2,1)S(1)} %get-tuple-element.37), channel_id=1, source_target_pairs={{0,1},{1,0},{2,3},{3,2},{4,5},{5,4},{6,7},{7,6},{8,9},{9,8},{10,11... | collective-permute-start | bytes 196616 | tf_op jit(solution)/shard_map/ppermute | solution.py:850
  (2 other events, 1.3 us)

commit v9 on v8

--- a/solution.py
+++ b/solution.py
@@ -40,16 +40,6 @@
     return pl.BlockSpec(memory_space=pltpu.HBM)
 
 
-def fetch(pairs, sems):
-    copies = [
-        pltpu.make_async_copy(source, target, sems.at[i])
-        for i, (source, target) in enumerate(pairs)
-    ]
-    for copy in copies:
-        copy.start()
-    return copies
-
-
 def params(mib):
     return pltpu.CompilerParams(vmem_limit_bytes=mib << 20)
 
@@ -114,24 +104,15 @@
     return ((1.0 + dist) * jnp.exp2(dist * NEG_LOG2E)).astype(BF)
 
 
-def pack_kernel(scale_ref, points_hbm, vec_hbm, got_hbm, out_ref, points, mine, got, sems):
+def pack_kernel(scale_ref, points, mine, got, out_ref):
     half = out_ref.shape[1]
     core = whole(scale_ref[4])
-    there = pl.ds(pl.multiple_of(core * half, half), half)
-    copies = fetch(
-        [
-            (points_hbm.at[:, there], points), (vec_hbm.at[:, there], mine),
-            (got_hbm.at[:, there], got),
-        ],
-        sems,
-    )
-    for copy in copies:
-        copy.wait()
 
     def step(i, _):
         here = pl.ds(pl.multiple_of(i * 2048, 2048), 2048)
-        rows = coordinate_rows(points[:, here], scale_ref)
-        one, two = mine[:, here].astype(F32), got[:, here].astype(F32)
+        there = pl.ds(pl.multiple_of(core * half + i * 2048, 2048), 2048)
+        rows = coordinate_rows(points[:, there], scale_ref)
+        one, two = mine[:, there].astype(F32), got[:, there].astype(F32)
         first, second = jnp.where(core == 0, one, two), jnp.where(core == 0, two, one)
         out_ref[:, here] = jnp.concatenate([first, second, rows], axis=0).astype(BF)
         return 0
@@ -314,12 +295,13 @@
 
 
 def near_halo_kernel(
-    scale_ref, plan_ref, row_ref, left_ref, right_ref, first_in, second_in,
+    scale_ref, plan_ref, row_ref, inner_ref, outer_ref, first_in, second_in,
     mine_ref, other_ref,
     first, second, col_ref, val_ref, s0, s1, k0, k1,
 ):
     core = whole(scale_ref[4])
-    half = left_ref.shape[1] // LEAF
+    half = inner_ref.shape[1] // LEAF
+    odd = whole(scale_ref[3]) & 1
     bits = half.bit_length() - 1
     count = plan_ref[3, 0]
 
@@ -330,9 +312,9 @@
         for q in range(4):
             code = plan_ref[1, i * 4 + q] & (CODE - 1)
             here = lanes(code & (half - 1))
-            after = code >= 4 * half
-            values = jnp.where(after, right_ref[0:16, here], left_ref[0:16, here])
-            rows = jnp.where(after, right_ref[16:24, here], left_ref[16:24, here])
+            paired = (code >> (bits + 2)) + odd == 1
+            values = jnp.where(paired, inner_ref[0:16, here], outer_ref[0:16, here])
+            rows = jnp.where(paired, inner_ref[16:24, here], outer_ref[16:24, here])
             val_ref[place(code)] = values
             col_ref[place(code)] = col_features(rows.astype(F32))
         return 0
@@ -407,32 +389,13 @@
 
 
 def up_kernel(
-    scale_ref, pack_ref, basis_hbm, raw_hbm, coef_ref, export_ref, front_ref, move_ref,
-    basis_ref, raw_ref, flat, pairs, sems,
+    scale_ref, pack_ref, basis_ref, raw_ref, coef_ref, export_ref, front_ref, move_ref,
+    flat, pairs,
 ):
     core = whole(scale_ref[4])
-    leaves = basis_ref.shape[0]
+    leaves = move_ref.shape[0]
     levels = leaves.bit_length() - 1
-    chunks = 4
-    per = leaves // chunks
-    deep = RANK // chunks
-    copies = fetch(
-        [
-            pair
-            for c in range(chunks)
-            for pair in (
-                (
-                    basis_hbm.at[pl.ds(core * leaves + c * per, per)],
-                    basis_ref.at[c * per : (c + 1) * per],
-                ),
-                (
-                    raw_hbm.at[:, c * deep : (c + 1) * deep],
-                    raw_ref.at[:, c * deep : (c + 1) * deep],
-                ),
-            )
-        ],
-        sems,
-    )
+    base = core * leaves
 
     def keep(parent, first, second):
         pair = side_by_side(first, second)
@@ -445,7 +408,7 @@
         outs = []
         for q in range(8):
             leaf = it * 8 + q
-            outs.append(mul_nt(pack_ref[0:ALL, lanes(leaf)], basis_ref[leaf]))
+            outs.append(mul_nt(pack_ref[0:ALL, lanes(leaf)], basis_ref[base + leaf]))
         for q in range(8):
             r = it * 8 + q
             block = jnp.concatenate([raw_ref[0, r], raw_ref[1, r]], axis=0).astype(F32)
@@ -454,10 +417,7 @@
             keep(leaves // 2 - 1 + it * 4 + q, outs[2 * q], outs[2 * q + 1])
         return 0
 
-    for c in range(chunks):
-        for copy in copies[2 * c : 2 * c + 2]:
-            copy.wait()
-        lax.fori_loop(c * per // 8, (c + 1) * per // 8, leaf_step, 0)
+    lax.fori_loop(0, leaves // 8, leaf_step, 0)
     root_move = load_node(flat, 0)
     move_ref[leaves - 1] = root_move
     for depth in range(levels - 1, 0, -1):
@@ -493,19 +453,10 @@
 
 
 def couple_kernel(
-    scale_ref, partners_ref, coef_ref, raw_hbm, local_ref, tie_ref, raw_ref, wide, thin, sems,
+    scale_ref, partners_ref, coef_ref, raw_ref, local_ref, tie_ref, wide, thin,
 ):
     device, core = whole(scale_ref[3]), whole(scale_ref[4])
     levels = (raw_ref.shape[3] + 1).bit_length() - 2
-    chunks = 4
-    deep = RANK // chunks
-    copies = fetch(
-        [
-            (raw_hbm.at[:, c * deep : (c + 1) * deep], raw_ref.at[:, c * deep : (c + 1) * deep])
-            for c in range(chunks)
-        ],
-        sems,
-    )
     low = lax.broadcasted_iota(jnp.int32, (2 * ALL, 2 * RANK), 1) < RANK
 
     def turn(i, _):
@@ -516,9 +467,7 @@
             store_turned(thin, r, raw_ref[2, r].astype(F32))
         return 0
 
-    for c in range(chunks):
-        copies[c].wait()
-        lax.fori_loop(c * deep // 8, (c + 1) * deep // 8, turn, 0)
+    lax.fori_loop(0, RANK // 8, turn, 0)
 
     def tie(node):
         return jnp.concatenate([load_node(wide, node), load_node(thin, node)], axis=1)
@@ -720,24 +669,24 @@
         out_shape=sds((8, slots + 128), jnp.int32),
         in_specs=[sspec(), vspec(), vspec()],
         out_specs=vspec(),
-        compiler_params=params(16),
+        compiler_params=params(8),
+        cost_estimate=pl.CostEstimate(flops=3 * 10**9, bytes_accessed=1 << 16, transcendentals=0),
     )(scale, near_offsets.reshape(1, leaves), near_cols.reshape(1, slots))
 
     pack = pl.pallas_call(
         pack_kernel,
         name="pack",
         out_shape=sds((24, half), BF),
-        in_specs=[sspec(), hspec(), hspec(), hspec()],
+        in_specs=[sspec(), vspec(), vspec(), vspec()],
         out_specs=vspec(),
-        scratch_shapes=[
-            VMEM((3, half), F32), VMEM((PART, half), BF), VMEM((PART, half), BF),
-            pltpu.SemaphoreType.DMA((3,)),
-        ],
         compiler_params=params(8),
+        cost_estimate=pl.CostEstimate(flops=2 * 10**9, bytes_accessed=2 << 20, transcendentals=0),
     )(scale, points, vectors, got)
     axes = ("leaf", "sub")
-    left = lax.ppermute(pack, axes, [(i, i + 1) for i in range(count - 1)])
-    right = lax.ppermute(pack, axes, [(i + 1, i) for i in range(count - 1)])
+    inner = lax.ppermute(pack, axes, [(i, i ^ 1) for i in range(count)])
+    outer = lax.ppermute(
+        pack, axes, [(i, ((i + 1) ^ 1) - 1) for i in range(1, count - 1)]
+    )
 
     moves_raw = jnp.transpose(local_transfer, (1, 2, 3, 0))
     part = leaves // 2
@@ -748,12 +697,11 @@
             sds((2 * part - 1, 2 * ALL, 2 * RANK), BF), sds((EXPORT, 2 * ALL, 2 * RANK), BF),
             sds((1, EXPORT // 2, 2 * ALL, 2 * RANK), BF), sds((part, RANK, 2 * RANK), BF),
         ),
-        in_specs=[sspec(), vspec(), hspec(), hspec()],
+        in_specs=[sspec(), vspec(), vspec(), vspec()],
         out_specs=(vspec(),) * 4,
         scratch_shapes=[
-            VMEM((part, RANK, LEAF), BF), VMEM(moves_raw.shape, BF),
             VMEM((leaves // 8, RANK * 8, 2 * RANK), F32),
-            VMEM((part - 1, 2 * ALL, 2 * RANK), BF), pltpu.SemaphoreType.DMA((8,)),
+            VMEM((part - 1, 2 * ALL, 2 * RANK), BF),
         ],
         compiler_params=params(18),
         cost_estimate=pl.CostEstimate(flops=8 * 10**9, bytes_accessed=8 << 20, transcendentals=0),
@@ -790,14 +738,13 @@
         out_shape=(
             sds((part - 1, ALL, 2 * RANK), F32), sds((EXPORT, RANK, 3 * RANK), BF),
         ),
-        in_specs=[sspec()] * 2 + [vspec(), hspec()],
+        in_specs=[sspec()] * 2 + [vspec(), vspec()],
         out_specs=(vspec(),) * 2,
         scratch_shapes=[
-            VMEM(ties_raw.shape, BF),
             VMEM((leaves // 4, RANK * 8, 2 * RANK), F32),
-            VMEM((leaves // 4, RANK * 8, RANK), F32), pltpu.SemaphoreType.DMA((4,)),
+            VMEM((leaves // 4, RANK * 8, RANK), F32),
         ],
-        compiler_params=params(36),
+        compiler_params=params(30),
         cost_estimate=pl.CostEstimate(flops=16 * 10**9, bytes_accessed=8 << 20, transcendentals=0),
     )(scale, mates, coef_late, ties_raw)
 
@@ -819,7 +766,7 @@
         cost_estimate=pl.CostEstimate(
             flops=20 * 10**9, bytes_accessed=8 << 20, transcendentals=60 * 2**17
         ),
-    )(scale, plan, row_feat, left, right, first, second)
+    )(scale, plan, row_feat, inner, outer, first, second)
     swapped = lax.ppermute(other, "vec", [(0, 1), (1, 0)])
 
     tops = export

time: 82.8 us -> 76 us (0.918)
  local copies, waits for them, and re-layouts: 7.26 us -> 3.31 us
  starting transfers between devices: 13.9 us -> 11.9 us
    unnamed x32 -> x26, local copies, waits for them, and re-layouts: 7.24 us -> 3.29 us
    ppermute x2, starting transfers between devices: 6.44 us -> 3.64 us  [the longest x1 2.94 us: body(): inner = lax.ppermute(pack, axes, [(i, i ^ 1) for i in range(count)])]
    ppermute x4, starting transfers between devices: 6.73 us -> 7.58 us  [swap_mask(): lax.ppermute(value, ('leaf', 'sub'), [(i, i ^ mask) for i in range(total)])]
  transfers between devices with their start and end apart: 10 -> 10, of which waited for: 2 -> 2; matrix products, arithmetic and copies ran while one was open for 1% -> 1% of each run, Pallas kernels for 56% -> 61%
where the time goes in v9:
time: 76 us; the launch traced here: 76.2 us
  Pallas kernels  56.6 us (74%)
  starting transfers between devices  11.9 us (16%)
  local copies, waits for them, and re-layouts  3.31 us (4%)
  waiting for transfers between devices  3.31 us (4%)
  other arithmetic  0.82 us (1%)
    pallas_call x1, Pallas kernels, body(): pl.pallas_call(near_local_kernel, name='near_local', out_shape=(sds((PART...  30.6 us
    ppermute x4, starting transfers between devices, swap_mask(): lax.ppermute(value, ('leaf', 'sub'), [(i, i ^ mask) for i in range(total)])  7.58 us
    pallas_call x1, Pallas kernels, body(): pl.pallas_call(couple_kernel, name='couple', out_shape=(sds((part - 1, AL...  7.05 us
    pallas_call x1, Pallas kernels, body(): pl.pallas_call(up_kernel, name='up', out_shape=(sds((2 * part - 1, 2 * AL...  5.36 us
    pallas_call x1, Pallas kernels, body(): pl.pallas_call(final_kernel, name='final', out_shape=sds((PART, size), F3...  3.84 us
    pallas_call x1, Pallas kernels, body(): pl.pallas_call(lambda *refs: down_kernel(dev_levels, *refs[:11], refs[11:...  3.66 us
    pallas_call x1, Pallas kernels, body(): pl.pallas_call(near_halo_kernel, name='near_halo', out_shape=(sds((PART,...  3.53 us
    unnamed x26, local copies, waits for them, and re-layouts  3.29 us
  transfers between devices with their start and end apart: 10, of which 2 were waited for; matrix products, arithmetic and copies ran while one was open for 1% of the time, Pallas kernels for 61%

profile of v9, /device:TPU:0, one launch (start us, length us, event | category | flops | bytes accessed | tf_op | source)
XLA Modules:
  0.0 76.2 jit_solution(9911112933423045089)
XLA Ops:
  0.0 0.5 collective-permute-start
  0.5 0.1 add_convert_fusion
  0.5 0.7 pad_maximum_fusion.2.scale_ref.refs_0_
  1.3 0.7 copy-done.8
  1.9 0.7 copy-done.10
  2.6 1.6 %plan.1.plan_ref = s32[8,640]{1,0:T(8,128)S(1)} custom-call(f32[5]{0:T(128)S(1)} %pad_maximum_fusion.2.scale_ref.refs_0_, s32[1,128]{1,0:T(1,128)S(1)} %bitcast.18, s32[1,512]{1,0:T(1,128)S(1)} %bitcast.17), custom_call_target="tpu_custom_call" | custom-call | flops 3000000000 | bytes 65536 | tf_op jit(solution)/shard_map/plan/pallas_call | solution.py:666
  4.2 0.9 %pack.1.pack_ref = bf16[24,16384]{1,0:T(8,128)(2,1)S(1)} custom-call(f32[5]{0:T(128)S(1)} %pad_maximum_fusion.2.scale_ref.refs_0_, f32[3,32768]{1,0:T(4,128)S(1)} %copy-done.4, bf16[8,32768]{1,0:T(8,128)(2,1)S(1)} %copy-done.1, bf16[8,32768]{1,0:T(8,128)(2,1)S(1)} %collective-permute-done.got), custom_call_target="tpu_custom_call" | custom-call | flops 2000000000 | bytes 2097152 | tf_op jit(solution)/shard_map/pack/pallas_call | solution.py:676
  5.1 1.2 %copy-done = bf16[128,64,256]{2,1,0:T(8,128)(2,1)S(1)} copy-done((bf16[128,64,256]{2,1,0:T(8,128)(2,1)S(1)}, bf16[128,64,256]{2,1,0:T(8,128)(2,1)}, u32[]{:S(2)}) %copy-start) | copy-done | bytes 4194328
  6.4 0.7 copy-done.3
  7.0 5.4 %up.1 = (bf16[127,32,128]{2,1,0:T(8,128)(2,1)S(1)}, bf16[8,32,128]{2,1,0:T(8,128)(2,1)S(1)}, bf16[1,4,32,128]{3,2,1,0:T(8,128)(2,1)S(1)}, bf16[64,64,128]{2,1,0:T(8,128)(2,1)S(1)}) custom-call(f32[5]{0:T(128)S(1)} %pad_maximum_fusion.2.scale_ref.refs_0_, bf16[24,16384]{1,0:T(8,128)(2,1)S(1)} %pack.1.pack_ref, bf16[128,64,256]{2,1,0:T(8,128)(2,1)S(1)} %copy-done, ...), custom_call_target="tpu_custom_call" | custom-call | flops 8000000000 | bytes 8388608 | tf_op jit(solution)/shard_map/up/pallas_call | solution.py:693
  12.4 0.1 collective-permute-start.1
  12.6 2.9 %collective-permute-start.7 = (bf16[24,16384]{1,0:T(8,128)(2,1)S(1)}, bf16[24,16384]{1,0:T(8,128)(2,1)S(1)}, u32[]{:S(2)}, u32[]{:S(2)}) collective-permute-start(bf16[24,16384]{1,0:T(8,128)(2,1)S(1)} %pack.1.pack_ref), channel_id=1, source_target_pairs={{0,2},{2,0},{4,6},{6,4},{8,10},{10,8},{12,14},{14,12},{1,3},{3,1},... | collective-permute-start | bytes 2359304 | tf_op jit(solution)/shard_map/ppermute | solution.py:686
  15.5 0.7 collective-permute-start.8
  16.2 30.6 %near_local.1 = (f32[8,32768]{1,0:T(8,128)S(1)}, f32[8,32768]{1,0:T(8,128)S(1)}, bf16[128,32,256]{2,1,0:T(8,128)(2,1)S(1)}) custom-call(f32[5]{0:T(128)S(1)} %pad_maximum_fusion.2.scale_ref.refs_0_, s32[8,640]{1,0:T(8,128)S(1)} %plan.1.plan_ref, f32[3,32768]{1,0:T(4,128)S(1)} %copy-done.4, bf16[24,16384]{1,0:T(8,128)(2,1)S(1)} %pack.1.pack_ref), custom_call_target="tpu_custom_call" | custom-call | flops 35999997952 | bytes 8388608 | tf_op jit(solution)/shard_map/near_local/pallas_call | solution.py:711
  46.9 1.2 %collective-permute-start.2 = (bf16[2,4,32,128]{3,2,1,0:T(8,128)(2,1)S(1)}, bf16[2,4,32,128]{3,2,1,0:T(8,128)(2,1)S(1)}, u32[]{:S(2)}, u32[]{:S(2)}) collective-permute-start(bf16[2,4,32,128]{3,2,1,0:T(8,128)(2,1)S(1)} %pad_maximum_fusion), channel_id=1, source_target_pairs={{0,2},{2,0},{4,6},{6,4},{8,10},{10,8},{12,14},{14,12},{1,3},{3,1},... | collective-permute-start | bytes 196616 | tf_op jit(solution)/shard_map/ppermute | solution.py:637
  48.1 7.0 %couple.1 = (f32[63,16,128]{2,1,0:T(8,128)S(1)}, bf16[8,64,192]{2,1,0:T(8,128)(2,1)S(1)}) custom-call(f32[5]{0:T(128)S(1)} %pad_maximum_fusion.2.scale_ref.refs_0_, s32[3,255]{1,0:T(4,128)S(1)} %bitcast.15, bf16[127,32,128]{2,1,0:T(8,128)(2,1)S(1)} %get-tuple-element.30.coef_ref, bf16[3,64,64,255]{3,2,1,0:T(8,128)(2,1)S(1)} %bitcast.13), custom_call_target="tpu_custom_call" | custom-call | flops 16000000000 | bytes 8388608 | tf_op jit(solution)/shard_map/couple/pallas_call | solution.py:735
  55.2 4.0 %collective-permute-start.3 = (bf16[4,2,32,128]{3,2,1,0:T(8,128)(2,1)S(1)}, bf16[4,2,32,128]{3,2,1,0:T(8,128)(2,1)S(1)}, u32[]{:S(2)}, u32[]{:S(2)}) collective-permute-start(bf16[4,2,32,128]{3,2,1,0:T(8,128)(2,1)S(1)} %pad_maximum_fusion.1), channel_id=1, source_target_pairs={{0,4},{2,6},{4,0},{6,2},{8,12},{10,14},{12,8},{14,10},{1,5},{3,7},... | collective-permute-start | bytes 196616 | tf_op jit(solution)/shard_map/ppermute | solution.py:637
  59.2 2.4 %collective-permute-start.5 = (bf16[4,2,32,128]{3,2,1,0:T(8,128)(2,1)S(1)}, bf16[4,2,32,128]{3,2,1,0:T(8,128)(2,1)S(1)}, u32[]{:S(2)}, u32[]{:S(2)}) collective-permute-start(bf16[4,2,32,128]{3,2,1,0:T(8,128)(2,1)S(1)} %pad_maximum_fusion.1), channel_id=1, source_target_pairs={{0,12},{2,14},{4,8},{6,10},{8,4},{10,6},{12,0},{14,2},{1,13},{3,15... | collective-permute-start | bytes 196616 | tf_op jit(solution)/shard_map/ppermute | solution.py:637
  61.7 3.5 %near_halo.1 = (f32[8,32768]{1,0:T(8,128)S(1)}, f32[8,32768]{1,0:T(8,128)S(1)}) custom-call(f32[5]{0:T(128)S(1)} %pad_maximum_fusion.2.scale_ref.refs_0_, s32[8,640]{1,0:T(8,128)S(1)} %plan.1.plan_ref, bf16[128,32,256]{2,1,0:T(8,128)(2,1)S(1)} %get-tuple-element.38.row_ref, bf16[24,16384]{1,0:T(8,128)(2,1)S(1)} %collective-permute-done.7.inner_ref, ...), custom_call_target="tpu_custom_call" | custom-call | flops 20000000000 | bytes 8388608 | tf_op jit(solution)/shard_map/near_halo/pallas_call | solution.py:754
  65.2 0.1 collective-permute-start.9
  65.3 1.9 %collective-permute-done.4.refs_12_ = bf16[4,2,32,128]{3,2,1,0:T(8,128)(2,1)S(1)} collective-permute-done((bf16[4,2,32,128]{3,2,1,0:T(8,128)(2,1)S(1)}, bf16[4,2,32,128]{3,2,1,0:T(8,128)(2,1)S(1)}, u32[]{:S(2)}, u32[]{:S(2)}) %collective-permute-start.4) | collective-permute-done | bytes 65568 | tf_op jit(solution)/shard_map/ppermute | solution.py:637
  67.3 3.7 %down.1 = (bf16[64,8,64]{2,1,0:T(8,128)(2,1)S(1)}, bf16[64,8,64]{2,1,0:T(8,128)(2,1)S(1)}) custom-call(f32[5]{0:T(128)S(1)} %pad_maximum_fusion.2.scale_ref.refs_0_, s32[3,255]{1,0:T(4,128)S(1)} %bitcast.16, s32[4,3]{1,0:T(4,128)S(1)} %copy-done.9, bf16[4,2,64,64]{3,2,1,0:T(8,128)(2,1)S(1)} %copy-done.6, bf16[4,3,64,64]{3,2,1,0:T(8,128)(2,1)S(1)} %copy-done.5, ...), custom_call_target="tpu_custom_call" | custom-call | flops 40000000000 | bytes 4194304 | tf_op jit(solution)/shard_map/down/pallas_call | solution.py:781
  71.0 1.3 %collective-permute-done.6.got_ref = bf16[64,8,64]{2,1,0:T(8,128)(2,1)S(1)} collective-permute-done((bf16[64,8,64]{2,1,0:T(8,128)(2,1)S(1)}, bf16[64,8,64]{2,1,0:T(8,128)(2,1)S(1)}, u32[]{:S(2)}, u32[]{:S(2)}) %collective-permute-start.6) | collective-permute-done | bytes 65568 | tf_op jit(solution)/shard_map/ppermute | solution.py:797
  72.3 3.8 %final.1 = f32[8,32768]{1,0:T(8,128)} custom-call(f32[5]{0:T(128)S(1)} %pad_maximum_fusion.2.scale_ref.refs_0_, bf16[64,8,64]{2,1,0:T(8,128)(2,1)S(1)} %get-tuple-element.36.mine_ref, bf16[64,8,64]{2,1,0:T(8,128)(2,1)S(1)} %collective-permute-done.6.got_ref, bf16[128,64,256]{2,1,0:T(8,128)(2,1)S(1)} %copy-done, f32[1,32768]{1,0:T(1,128)S(1)} %bitcast.10, ...), custom_call_target="tpu_custom_call" | custom-call | flops 2000000000 | bytes 4194304 | tf_op jit(solution)/shard_map/final/pallas_call | solution.py:799
  (38 shorter events, 0.2 us)
Async XLA Ops:
  0.0 4.2 %collective-permute-start = (bf16[8,32768]{1,0:T(8,128)(2,1)}, bf16[8,32768]{1,0:T(8,128)(2,1)S(1)}, u32[]{:S(2)}, u32[]{:S(2)}) collective-permute-start(bf16[8,32768]{1,0:T(8,128)(2,1)} %vec.1), channel_id=1, source_target_pairs={{0,1},{1,0},{2,3},{3,2},{4,5},{5,4},{6,7},{7,6},{8,9},{9,8},{10,11... | collective-permute-start | bytes 1572872 | tf_op jit(solution)/shard_map/ppermute | solution.py:664
  1.3 0.7 copy-start.8
  1.9 0.7 copy-start.10
  2.6 1.6 %copy-start.1 = (bf16[8,32768]{1,0:T(8,128)(2,1)S(1)}, bf16[8,32768]{1,0:T(8,128)(2,1)}, u32[]{:S(2)}) copy-start(bf16[8,32768]{1,0:T(8,128)(2,1)} %vec.1) | copy-start | bytes 1572868
  2.6 1.6 %copy-start.4 = (f32[3,32768]{1,0:T(4,128)S(1)}, f32[3,32768]{1,0:T(4,128)}, u32[]{:S(2)}) copy-start(f32[3,32768]{1,0:T(4,128)} %points_ref.1) | copy-start | bytes 1179652
  4.2 2.2 %copy-start = (bf16[128,64,256]{2,1,0:T(8,128)(2,1)S(1)}, bf16[128,64,256]{2,1,0:T(8,128)(2,1)}, u32[]{:S(2)}) copy-start(bf16[128,64,256]{2,1,0:T(8,128)(2,1)} %basis.1) | copy-start | bytes 12582916
  4.2 2.9 %copy-start.3 = (bf16[127,2,64,64]{0,3,2,1:T(8,128)(2,1)S(1)}, bf16[127,2,64,64]{0,3,2,1:T(8,128)(2,1)}, u32[]{:S(2)}) copy-start(bf16[127,2,64,64]{0,3,2,1:T(8,128)(2,1)} %param.18) | copy-start | bytes 6242308
  12.4 35.7 %slice-start = ((s8[6291456]{0:T(1024)(128)(4,1)}), s8[4194304]{0:T(1024)(128)(4,1)S(1)}, s32[]{:S(2)}) async-start(s8[6291456]{0:T(1024)(128)(4,1)} %bitcast.11), calls=%async_computation | async-start | bytes 8388608
  12.4 35.7 %slice-start.1 = ((s8[6291456]{0:T(1024)(128)(4,1)}), s8[2097152]{0:T(1024)(128)(4,1)S(1)}, s32[]{:S(2)}) async-start(s8[6291456]{0:T(1024)(128)(4,1)} %bitcast.11), calls=%async_computation.1 | async-start | bytes 4194304
  12.4 35.7 %copy-start.7 = (s32[255,3]{0,1:T(4,128)S(1)}, s32[255,3]{0,1:T(4,128)}, u32[]{:S(2)}) copy-start(s32[255,3]{0,1:T(4,128)} %param.22) | copy-start | bytes 9184
  12.4 34.4 %collective-permute-start.1 = (bf16[8,32,128]{2,1,0:T(8,128)(2,1)S(1)}, bf16[8,32,128]{2,1,0:T(8,128)(2,1)S(1)}, u32[]{:S(2)}, u32[]{:S(2)}) collective-permute-start(bf16[8,32,128]{2,1,0:T(8,128)(2,1)S(1)} %get-tuple-element.26.refs_8_.refs_14_), channel_id=1, source_target_pairs={{0,1},{1,0},{2,3},{3,2},{4,5},{5,4},{6,7},{7,6},{8,9},{9,8},{10,11... | collective-permute-start | bytes 196616 | tf_op jit(solution)/shard_map/ppermute | solution.py:709
  12.6 49.1 %collective-permute-start.7 = (bf16[24,16384]{1,0:T(8,128)(2,1)S(1)}, bf16[24,16384]{1,0:T(8,128)(2,1)S(1)}, u32[]{:S(2)}, u32[]{:S(2)}) collective-permute-start(bf16[24,16384]{1,0:T(8,128)(2,1)S(1)} %pack.1.pack_ref), channel_id=1, source_target_pairs={{0,2},{2,0},{4,6},{6,4},{8,10},{10,8},{12,14},{14,12},{1,3},{3,1},... | collective-permute-start | bytes 2359304 | tf_op jit(solution)/shard_map/ppermute | solution.py:686
  15.5 46.1 %collective-permute-start.8 = (bf16[24,16384]{1,0:T(8,128)(2,1)S(1)}, bf16[24,16384]{1,0:T(8,128)(2,1)S(1)}, u32[]{:S(2)}, u32[]{:S(2)}) collective-permute-start(bf16[24,16384]{1,0:T(8,128)(2,1)S(1)} %pack.1.pack_ref), channel_id=1, source_target_pairs={{2,4},{4,2},{6,8},{8,6},{10,12},{12,10},{3,5},{5,3},{7,9},{9,7},{1... | collective-permute-start | bytes 2359304 | tf_op jit(solution)/shard_map/ppermute | solution.py:687
  46.9 8.3 %collective-permute-start.2 = (bf16[2,4,32,128]{3,2,1,0:T(8,128)(2,1)S(1)}, bf16[2,4,32,128]{3,2,1,0:T(8,128)(2,1)S(1)}, u32[]{:S(2)}, u32[]{:S(2)}) collective-permute-start(bf16[2,4,32,128]{3,2,1,0:T(8,128)(2,1)S(1)} %pad_maximum_fusion), channel_id=1, source_target_pairs={{0,2},{2,0},{4,6},{6,4},{8,10},{10,8},{12,14},{14,12},{1,3},{3,1},... | collective-permute-start | bytes 196616 | tf_op jit(solution)/shard_map/ppermute | solution.py:637
  55.2 10.1 %collective-permute-start.3 = (bf16[4,2,32,128]{3,2,1,0:T(8,128)(2,1)S(1)}, bf16[4,2,32,128]{3,2,1,0:T(8,128)(2,1)S(1)}, u32[]{:S(2)}, u32[]{:S(2)}) collective-permute-start(bf16[4,2,32,128]{3,2,1,0:T(8,128)(2,1)S(1)} %pad_maximum_fusion.1), channel_id=1, source_target_pairs={{0,4},{2,6},{4,0},{6,2},{8,12},{10,14},{12,8},{14,10},{1,5},{3,7},... | collective-permute-start | bytes 196616 | tf_op jit(solution)/shard_map/ppermute | solution.py:637
  59.2 8.0 %collective-permute-start.4 = (bf16[4,2,32,128]{3,2,1,0:T(8,128)(2,1)S(1)}, bf16[4,2,32,128]{3,2,1,0:T(8,128)(2,1)S(1)}, u32[]{:S(2)}, u32[]{:S(2)}) collective-permute-start(bf16[4,2,32,128]{3,2,1,0:T(8,128)(2,1)S(1)} %pad_maximum_fusion.1), channel_id=1, source_target_pairs={{0,8},{2,10},{4,12},{6,14},{8,0},{10,2},{12,4},{14,6},{1,9},{3,11}... | collective-permute-start | bytes 196616 | tf_op jit(solution)/shard_map/ppermute | solution.py:637
  59.2 8.0 %collective-permute-start.5 = (bf16[4,2,32,128]{3,2,1,0:T(8,128)(2,1)S(1)}, bf16[4,2,32,128]{3,2,1,0:T(8,128)(2,1)S(1)}, u32[]{:S(2)}, u32[]{:S(2)}) collective-permute-start(bf16[4,2,32,128]{3,2,1,0:T(8,128)(2,1)S(1)} %pad_maximum_fusion.1), channel_id=1, source_target_pairs={{0,12},{2,14},{4,8},{6,10},{8,4},{10,6},{12,0},{14,2},{1,13},{3,15... | collective-permute-start | bytes 196616 | tf_op jit(solution)/shard_map/ppermute | solution.py:637
  61.6 5.6 %copy-start.5 = (bf16[4,3,64,64]{3,2,1,0:T(8,128)(2,1)S(1)}, bf16[4,3,64,64]{3,2,1,0:T(8,128)(2,1)}, u32[]{:S(2)}) copy-start(bf16[4,3,64,64]{3,2,1,0:T(8,128)(2,1)} %refs_4_.1) | copy-start | bytes 294916
  61.6 5.6 %copy-start.6 = (bf16[4,2,64,64]{3,2,1,0:T(8,128)(2,1)S(1)}, bf16[4,2,64,64]{3,2,1,0:T(8,128)(2,1)}, u32[]{:S(2)}) copy-start(bf16[4,2,64,64]{3,2,1,0:T(8,128)(2,1)} %refs_3_.1) | copy-start | bytes 196612
  61.6 5.6 %copy-start.9 = (s32[4,3]{1,0:T(4,128)S(1)}, s32[4,3]{1,0:T(4,128)}, u32[]{:S(2)}) copy-start(s32[4,3]{1,0:T(4,128)} %refs_2_.1) | copy-start | bytes 148
  65.2 7.1 %collective-permute-start.9 = (f32[8,32768]{1,0:T(8,128)S(1)}, f32[8,32768]{1,0:T(8,128)S(1)}, u32[]{:S(2)}, u32[]{:S(2)}) collective-permute-start(f32[8,32768]{1,0:T(8,128)S(1)} %get-tuple-element.42), channel_id=1, source_target_pairs={{0,1},{1,0},{2,3},{3,2},{4,5},{5,4},{6,7},{7,6},{8,9},{9,8},{10,11... | collective-permute-start | bytes 3145736 | tf_op jit(solution)/shard_map/ppermute | solution.py:770
  67.3 5.1 %copy-start.2 = (f32[32768]{0:T(1024)S(1)}, f32[32768]{0:T(1024)}, u32[]{:S(2)}) copy-start(f32[32768]{0:T(1024)} %param.15) | copy-start | bytes 393220
  70.9 1.4 %collective-permute-start.6 = (bf16[64,8,64]{2,1,0:T(8,128)(2,1)S(1)}, bf16[64,8,64]{2,1,0:T(8,128)(2,1)S(1)}, u32[]{:S(2)}, u32[]{:S(2)}) collective-permute-start(bf16[64,8,64]{2,1,0:T(8,128)(2,1)S(1)} %get-tuple-element.37), channel_id=1, source_target_pairs={{0,1},{1,0},{2,3},{3,2},{4,5},{5,4},{6,7},{7,6},{8,9},{9,8},{10,11... | collective-permute-start | bytes 196616 | tf_op jit(solution)/shard_map/ppermute | solution.py:797

commit v10 on v9

--- a/solution.py
+++ b/solution.py
@@ -166,106 +166,94 @@
     ).astype(jnp.int32)
 
 
-def block_loop(kind, place, plan_ref, row_ref, col_ref, val_ref, sums, s0, s1, k0, k1):
-    def accumulate(first, kern):
+def pipeline(turns, unroll, ahead_first, accumulate, distance, evaluate, s0, s1, k0, k1):
+    def half_turn(first, near, ahead, ready, filled):
         for q in range(PAIR):
-            code = plan_ref[kind, first + q]
-            here = lanes(code >> CODE_BITS)
-            part = jnp.dot(
-                val_ref[place(code & (CODE - 1))], kern[q], preferred_element_type=F32
-            )
-            sums[0][:, here] += part[:PART]
-            sums[1][:, here] += part[PART:]
-
-    def distance(first, out):
-        for q in range(PAIR):
-            code = plan_ref[kind, first + q]
-            out[q] = jnp.dot(
-                col_ref[place(code & (CODE - 1))],
-                row_ref[code >> CODE_BITS],
-                preferred_element_type=F32,
-            )
+            if ahead_first:
+                distance(first + PAIR + q, ahead.at[q])
+            accumulate(first - PAIR + q, ready.at[q])
+            if not ahead_first:
+                distance(first + PAIR + q, ahead.at[q])
+            evaluate(near.at[q], filled.at[q])
+
+    k1[...] = jnp.zeros_like(k1)
+    for q in range(PAIR):
+        distance(q, s0.at[q])
+
+    def step(it, _):
+        for turn in range(unroll):
+            first = (it * unroll + turn) * 2 * PAIR
+            half_turn(first, s0, s1, k1, k0)
+            half_turn(first + PAIR, s1, s0, k0, k1)
+        return 0
+
+    lax.fori_loop(0, turns, step, 0)
+    for q in range(PAIR):
+        accumulate(turns * unroll * 2 * PAIR - PAIR + q, k1.at[q])
+
+
+def block_loop(kind, unroll, place, plan_ref, row_ref, col_ref, val_ref, sums, s0, s1, k0, k1):
+    def accumulate(slot, kern):
+        code = plan_ref[kind, jnp.maximum(slot, 0)]
+        here = lanes(code >> CODE_BITS)
+        part = jnp.dot(val_ref[place(code & (CODE - 1))], kern[...], preferred_element_type=F32)
+        sums[0][:, here] += part[:PART]
+        sums[1][:, here] += part[PART:]
+
+    def distance(slot, out):
+        code = plan_ref[kind, slot]
+        out[...] = jnp.dot(
+            col_ref[place(code & (CODE - 1))],
+            row_ref[code >> CODE_BITS],
+            preferred_element_type=F32,
+        )
 
     def evaluate(squared, kern):
-        for q in range(PAIR):
-            kern[q] = matern(squared[q])
-
-    k1[...] = jnp.zeros_like(k1)
-    distance(0, s0)
-
-    def step(it, _):
-        for turn in range(TURNS):
-            first = (it * TURNS + turn) * 2 * PAIR
-            accumulate(jnp.maximum(first - PAIR, 0), k1)
-            distance(first + PAIR, s1)
-            evaluate(s0, k0)
-            accumulate(first, k0)
-            distance(first + 2 * PAIR, s0)
-            evaluate(s1, k1)
-        return 0
+        kern[...] = matern(squared[...])
+
 
     count = plan_ref[2 + kind, 0]
-    turns = (count + TURNS * 2 * PAIR - 1) // (TURNS * 2 * PAIR)
-    lax.fori_loop(0, turns, step, 0)
-    accumulate(jnp.maximum(turns * TURNS * 2 * PAIR - PAIR, 0), k1)
+    turns = (count + unroll * 2 * PAIR - 1) // (unroll * 2 * PAIR)
+    pipeline(turns, unroll, True, accumulate, distance, evaluate, s0, s1, k0, k1)
 
 
 def diagonal_loop(first_leaf, count, row_ref, col_ref, val_ref, sums, s0, s1, k0, k1):
     mid = LEAF // 2
 
-    def distance(first, out):
-        for q in range(PAIR):
-            col = jnp.minimum(first + q, count - 1)
-            rows = row_ref[first_leaf + col]
-            out[q, :mid] = jnp.dot(col_ref[col, :mid], rows, preferred_element_type=F32)
-            out[q, mid:, mid:] = jnp.dot(
-                col_ref[col, mid:], rows[:, mid:], preferred_element_type=F32
-            )
+    def distance(slot, out):
+        col = jnp.minimum(slot, count - 1)
+        rows = row_ref[first_leaf + col]
+        out[:mid] = jnp.dot(col_ref[col, :mid], rows, preferred_element_type=F32)
+        out[mid:, mid:] = jnp.dot(col_ref[col, mid:], rows[:, mid:], preferred_element_type=F32)
 
     def evaluate(squared, kern):
-        for q in range(PAIR):
-            kern[q, :mid] = matern(squared[q, :mid])
-            kern[q, mid:, mid:] = matern(squared[q, mid:, mid:])
-
-    def accumulate(first, kern):
-        for q in range(PAIR):
-            col = jnp.maximum(first + q, 0)
-            values = val_ref[col]
-            part = jnp.dot(values[:, :mid], kern[q, :mid], preferred_element_type=F32)
-            left = mul_nt(values[:, mid:], kern[q, :mid, mid:])
-            right = jnp.dot(values[:, mid:], kern[q, mid:, mid:], preferred_element_type=F32)
-            part = part + jnp.concatenate([left, right], axis=1)
-            here = lanes(first_leaf + col)
-            sums[0][:, here] += part[:PART]
-            sums[1][:, here] += part[PART:]
-
-    k1[...] = jnp.zeros_like(k1)
-    distance(0, s0)
-
-    def step(it, _):
-        for turn in range(TURNS):
-            first = (it * TURNS + turn) * 2 * PAIR
-            accumulate(first - PAIR, k1)
-            distance(first + PAIR, s1)
-            evaluate(s0, k0)
-            accumulate(first, k0)
-            distance(first + 2 * PAIR, s0)
-            evaluate(s1, k1)
-        return 0
-
-    lax.fori_loop(0, count // (TURNS * 2 * PAIR), step, 0)
-    accumulate(count - PAIR, k1)
+        kern[:mid] = matern(squared[:mid])
+        kern[mid:, mid:] = matern(squared[mid:, mid:])
+
+    def accumulate(slot, kern):
+        col = jnp.maximum(slot, 0)
+        values = val_ref[col]
+        part = jnp.dot(values[:, :mid], kern[:mid], preferred_element_type=F32)
+        left = mul_nt(values[:, mid:], kern[:mid, mid:])
+        right = jnp.dot(values[:, mid:], kern[mid:, mid:], preferred_element_type=F32)
+        part = part + jnp.concatenate([left, right], axis=1)
+        here = lanes(first_leaf + col)
+        sums[0][:, here] += part[:PART]
+        sums[1][:, here] += part[PART:]
+
+    turns = count // (TURNS * 2 * PAIR)
+    pipeline(turns, TURNS, False, accumulate, distance, evaluate, s0, s1, k0, k1)
 
 
 def load_columns(pack_ref, base, count, col_ref, val_ref):
     def step(i, _):
-        for q in range(4):
-            leaf = i * 4 + q
+        for q in range(8):
+            leaf = i * 8 + q
             val_ref[base + leaf] = pack_ref[0:16, lanes(leaf)]
             col_ref[base + leaf] = col_features(pack_ref[16:24, lanes(leaf)].astype(F32))
         return 0
 
-    lax.fori_loop(0, count // 4, step, 0)
+    lax.fori_loop(0, count // 8, step, 0)
 
 
 def near_local_kernel(
@@ -291,7 +279,7 @@
     col_ref[half] = jnp.zeros(col_ref.shape[1:], BF)
     sums = (mine_ref, other_ref)
     diagonal_loop(half_id * half, half, row_ref, col_ref, val_ref, sums, s0, s1, k0, k1)
-    block_loop(0, lambda c: c, plan_ref, row_ref, col_ref, val_ref, sums, s0, s1, k0, k1)
+    block_loop(0, TURNS, lambda c: c, plan_ref, row_ref, col_ref, val_ref, sums, s0, s1, k0, k1)
 
 
 def near_halo_kernel(
@@ -325,7 +313,7 @@
     val_ref[2 * half] = jnp.zeros((16, LEAF), BF)
     col_ref[2 * half] = jnp.zeros(col_ref.shape[1:], BF)
     sums = (first, second)
-    block_loop(1, place, plan_ref, row_ref, col_ref, val_ref, sums, s0, s1, k0, k1)
+    block_loop(1, 1, place, plan_ref, row_ref, col_ref, val_ref, sums, s0, s1, k0, k1)
 
     @pl.when(core == 0)
     def _():

time: 76 us -> 71.6 us (0.942)
  Pallas kernels: 56.6 us -> 53.4 us
  waiting for transfers between devices: 3.31 us -> 1.6 us
    pallas_call x1, Pallas kernels: 30.6 us -> 27 us  [body(): pl.pallas_call(near_local_kernel, name='near_local', out_shape=(sds((PART...]
    ppermute x4, waiting for transfers between devices: 1.96 us -> 0.38 us  [swap_mask(): lax.ppermute(value, ('leaf', 'sub'), [(i, i ^ mask) for i in range(total)])]
where the time goes in v10:
time: 71.6 us; the launch traced here: 71.3 us
  Pallas kernels  53.4 us (75%)
  starting transfers between devices  11.9 us (17%)
  local copies, waits for them, and re-layouts  3.31 us (5%)
  waiting for transfers between devices  1.6 us (2%)
  other arithmetic  0.82 us (1%)
    pallas_call x1, Pallas kernels, body(): pl.pallas_call(near_local_kernel, name='near_local', out_shape=(sds((PART...  27 us
    ppermute x4, starting transfers between devices, swap_mask(): lax.ppermute(value, ('leaf', 'sub'), [(i, i ^ mask) for i in range(total)])  7.41 us
    pallas_call x1, Pallas kernels, body(): pl.pallas_call(couple_kernel, name='couple', out_shape=(sds((part - 1, AL...  7.05 us
    pallas_call x1, Pallas kernels, body(): pl.pallas_call(up_kernel, name='up', out_shape=(sds((2 * part - 1, 2 * AL...  5.36 us
    pallas_call x1, Pallas kernels, body(): pl.pallas_call(near_halo_kernel, name='near_halo', out_shape=(sds((PART,...  4.07 us
    pallas_call x1, Pallas kernels, body(): pl.pallas_call(final_kernel, name='final', out_shape=sds((PART, size), F3...  3.84 us
    pallas_call x1, Pallas kernels, body(): pl.pallas_call(lambda *refs: down_kernel(dev_levels, *refs[:11], refs[11:...  3.66 us
    unnamed x26, local copies, waits for them, and re-layouts  3.29 us
  transfers between devices with their start and end apart: 10, of which 2 were waited for; matrix products, arithmetic and copies ran while one was open for 1% of the time, Pallas kernels for 61%

profile of v10, /device:TPU:0, one launch (start us, length us, event | category | flops | bytes accessed | tf_op | source)
XLA Modules:
  0.0 71.3 jit_solution(9285709955406454354)
XLA Ops:
  0.0 0.5 collective-permute-start
  0.5 0.7 %pad_maximum_fusion.2.scale_ref.refs_0_ = f32[5]{0:T(128)S(1)} fusion(f32[2]{0:T(128)S(1)} %add_convert_fusion, f32[3]{0:T(128)} %param.14), kind=kLoop, calls=%fused_computation.4 | loop fusion | flops 5 | bytes 40 | tf_op jit(solution)/shard_map/concatenate | solution.py:641
  1.3 0.7 copy-done.8
  1.9 0.7 copy-done.10
  2.6 1.6 %plan.1.plan_ref = s32[8,640]{1,0:T(8,128)S(1)} custom-call(f32[5]{0:T(128)S(1)} %pad_maximum_fusion.2.scale_ref.refs_0_, s32[1,128]{1,0:T(1,128)S(1)} %bitcast.18, s32[1,512]{1,0:T(1,128)S(1)} %bitcast.17), custom_call_target="tpu_custom_call" | custom-call | flops 3000000000 | bytes 65536 | tf_op jit(solution)/shard_map/plan/pallas_call | solution.py:654
  4.2 0.9 %pack.1.pack_ref = bf16[24,16384]{1,0:T(8,128)(2,1)S(1)} custom-call(f32[5]{0:T(128)S(1)} %pad_maximum_fusion.2.scale_ref.refs_0_, f32[3,32768]{1,0:T(4,128)S(1)} %copy-done.4, bf16[8,32768]{1,0:T(8,128)(2,1)S(1)} %copy-done.1, bf16[8,32768]{1,0:T(8,128)(2,1)S(1)} %collective-permute-done.got), custom_call_target="tpu_custom_call" | custom-call | flops 2000000000 | bytes 2097152 | tf_op jit(solution)/shard_map/pack/pallas_call | solution.py:664
  5.1 1.2 %copy-done = bf16[128,64,256]{2,1,0:T(8,128)(2,1)S(1)} copy-done((bf16[128,64,256]{2,1,0:T(8,128)(2,1)S(1)}, bf16[128,64,256]{2,1,0:T(8,128)(2,1)}, u32[]{:S(2)}) %copy-start) | copy-done | bytes 4194328
  6.4 0.7 copy-done.3
  7.0 5.4 %up.1 = (bf16[127,32,128]{2,1,0:T(8,128)(2,1)S(1)}, bf16[8,32,128]{2,1,0:T(8,128)(2,1)S(1)}, bf16[1,4,32,128]{3,2,1,0:T(8,128)(2,1)S(1)}, bf16[64,64,128]{2,1,0:T(8,128)(2,1)S(1)}) custom-call(f32[5]{0:T(128)S(1)} %pad_maximum_fusion.2.scale_ref.refs_0_, bf16[24,16384]{1,0:T(8,128)(2,1)S(1)} %pack.1.pack_ref, bf16[128,64,256]{2,1,0:T(8,128)(2,1)S(1)} %copy-done, ...), custom_call_target="tpu_custom_call" | custom-call | flops 8000000000 | bytes 8388608 | tf_op jit(solution)/shard_map/up/pallas_call | solution.py:681
  12.4 0.1 collective-permute-start.1
  12.6 2.9 %collective-permute-start.7 = (bf16[24,16384]{1,0:T(8,128)(2,1)S(1)}, bf16[24,16384]{1,0:T(8,128)(2,1)S(1)}, u32[]{:S(2)}, u32[]{:S(2)}) collective-permute-start(bf16[24,16384]{1,0:T(8,128)(2,1)S(1)} %pack.1.pack_ref), channel_id=1, source_target_pairs={{0,2},{2,0},{4,6},{6,4},{8,10},{10,8},{12,14},{14,12},{1,3},{3,1},... | collective-permute-start | bytes 2359304 | tf_op jit(solution)/shard_map/ppermute | solution.py:674
  15.5 0.7 collective-permute-start.8
  16.2 27.0 %near_local.1 = (f32[8,32768]{1,0:T(8,128)S(1)}, f32[8,32768]{1,0:T(8,128)S(1)}, bf16[128,32,256]{2,1,0:T(8,128)(2,1)S(1)}) custom-call(f32[5]{0:T(128)S(1)} %pad_maximum_fusion.2.scale_ref.refs_0_, s32[8,640]{1,0:T(8,128)S(1)} %plan.1.plan_ref, f32[3,32768]{1,0:T(4,128)S(1)} %copy-done.4, bf16[24,16384]{1,0:T(8,128)(2,1)S(1)} %pack.1.pack_ref), custom_call_target="tpu_custom_call" | custom-call | flops 35999997952 | bytes 8388608 | tf_op jit(solution)/shard_map/near_local/pallas_call | solution.py:699
  43.2 3.0 %collective-permute-start.2 = (bf16[2,4,32,128]{3,2,1,0:T(8,128)(2,1)S(1)}, bf16[2,4,32,128]{3,2,1,0:T(8,128)(2,1)S(1)}, u32[]{:S(2)}, u32[]{:S(2)}) collective-permute-start(bf16[2,4,32,128]{3,2,1,0:T(8,128)(2,1)S(1)} %pad_maximum_fusion), channel_id=1, source_target_pairs={{0,2},{2,0},{4,6},{6,4},{8,10},{10,8},{12,14},{14,12},{1,3},{3,1},... | collective-permute-start | bytes 196616 | tf_op jit(solution)/shard_map/ppermute | solution.py:625
  46.2 7.0 %couple.1 = (f32[63,16,128]{2,1,0:T(8,128)S(1)}, bf16[8,64,192]{2,1,0:T(8,128)(2,1)S(1)}) custom-call(f32[5]{0:T(128)S(1)} %pad_maximum_fusion.2.scale_ref.refs_0_, s32[3,255]{1,0:T(4,128)S(1)} %bitcast.15, bf16[127,32,128]{2,1,0:T(8,128)(2,1)S(1)} %get-tuple-element.30.coef_ref, bf16[3,64,64,255]{3,2,1,0:T(8,128)(2,1)S(1)} %bitcast.13), custom_call_target="tpu_custom_call" | custom-call | flops 16000000000 | bytes 8388608 | tf_op jit(solution)/shard_map/couple/pallas_call | solution.py:723
  53.3 1.6 %collective-permute-start.3 = (bf16[4,2,32,128]{3,2,1,0:T(8,128)(2,1)S(1)}, bf16[4,2,32,128]{3,2,1,0:T(8,128)(2,1)S(1)}, u32[]{:S(2)}, u32[]{:S(2)}) collective-permute-start(bf16[4,2,32,128]{3,2,1,0:T(8,128)(2,1)S(1)} %pad_maximum_fusion.1), channel_id=1, source_target_pairs={{0,4},{2,6},{4,0},{6,2},{8,12},{10,14},{12,8},{14,10},{1,5},{3,7},... | collective-permute-start | bytes 196616 | tf_op jit(solution)/shard_map/ppermute | solution.py:625
  55.0 1.1 %collective-permute-start.4 = (bf16[4,2,32,128]{3,2,1,0:T(8,128)(2,1)S(1)}, bf16[4,2,32,128]{3,2,1,0:T(8,128)(2,1)S(1)}, u32[]{:S(2)}, u32[]{:S(2)}) collective-permute-start(bf16[4,2,32,128]{3,2,1,0:T(8,128)(2,1)S(1)} %pad_maximum_fusion.1), channel_id=1, source_target_pairs={{0,8},{2,10},{4,12},{6,14},{8,0},{10,2},{12,4},{14,6},{1,9},{3,11}... | collective-permute-start | bytes 196616 | tf_op jit(solution)/shard_map/ppermute | solution.py:625
  56.1 1.7 %collective-permute-start.5 = (bf16[4,2,32,128]{3,2,1,0:T(8,128)(2,1)S(1)}, bf16[4,2,32,128]{3,2,1,0:T(8,128)(2,1)S(1)}, u32[]{:S(2)}, u32[]{:S(2)}) collective-permute-start(bf16[4,2,32,128]{3,2,1,0:T(8,128)(2,1)S(1)} %pad_maximum_fusion.1), channel_id=1, source_target_pairs={{0,12},{2,14},{4,8},{6,10},{8,4},{10,6},{12,0},{14,2},{1,13},{3,15... | collective-permute-start | bytes 196616 | tf_op jit(solution)/shard_map/ppermute | solution.py:625
  57.8 4.1 %near_halo.1 = (f32[8,32768]{1,0:T(8,128)S(1)}, f32[8,32768]{1,0:T(8,128)S(1)}) custom-call(f32[5]{0:T(128)S(1)} %pad_maximum_fusion.2.scale_ref.refs_0_, s32[8,640]{1,0:T(8,128)S(1)} %plan.1.plan_ref, bf16[128,32,256]{2,1,0:T(8,128)(2,1)S(1)} %get-tuple-element.38.row_ref, bf16[24,16384]{1,0:T(8,128)(2,1)S(1)} %collective-permute-done.7.inner_ref, ...), custom_call_target="tpu_custom_call" | custom-call | flops 20000000000 | bytes 8388608 | tf_op jit(solution)/shard_map/near_halo/pallas_call | solution.py:742
  62.0 0.4 collective-permute-done.4.refs_12_
  62.4 3.7 %down.1 = (bf16[64,8,64]{2,1,0:T(8,128)(2,1)S(1)}, bf16[64,8,64]{2,1,0:T(8,128)(2,1)S(1)}) custom-call(f32[5]{0:T(128)S(1)} %pad_maximum_fusion.2.scale_ref.refs_0_, s32[3,255]{1,0:T(4,128)S(1)} %bitcast.16, s32[4,3]{1,0:T(4,128)S(1)} %copy-done.9, bf16[4,2,64,64]{3,2,1,0:T(8,128)(2,1)S(1)} %copy-done.6, bf16[4,3,64,64]{3,2,1,0:T(8,128)(2,1)S(1)} %copy-done.5, ...), custom_call_target="tpu_custom_call" | custom-call | flops 40000000000 | bytes 4194304 | tf_op jit(solution)/shard_map/down/pallas_call | solution.py:769
  66.0 0.2 collective-permute-start.6
  66.2 1.2 %collective-permute-done.6.got_ref = bf16[64,8,64]{2,1,0:T(8,128)(2,1)S(1)} collective-permute-done((bf16[64,8,64]{2,1,0:T(8,128)(2,1)S(1)}, bf16[64,8,64]{2,1,0:T(8,128)(2,1)S(1)}, u32[]{:S(2)}, u32[]{:S(2)}) %collective-permute-start.6) | collective-permute-done | bytes 65568 | tf_op jit(solution)/shard_map/ppermute | solution.py:785
  67.4 3.8 %final.1 = f32[8,32768]{1,0:T(8,128)} custom-call(f32[5]{0:T(128)S(1)} %pad_maximum_fusion.2.scale_ref.refs_0_, bf16[64,8,64]{2,1,0:T(8,128)(2,1)S(1)} %get-tuple-element.36.mine_ref, bf16[64,8,64]{2,1,0:T(8,128)(2,1)S(1)} %collective-permute-done.6.got_ref, bf16[128,64,256]{2,1,0:T(8,128)(2,1)S(1)} %copy-done, f32[1,32768]{1,0:T(1,128)S(1)} %bitcast.10, ...), custom_call_target="tpu_custom_call" | custom-call | flops 2000000000 | bytes 4194304 | tf_op jit(solution)/shard_map/final/pallas_call | solution.py:787
  (38 shorter events, 0.3 us)
Async XLA Ops:
  0.0 4.2 %collective-permute-start = (bf16[8,32768]{1,0:T(8,128)(2,1)}, bf16[8,32768]{1,0:T(8,128)(2,1)S(1)}, u32[]{:S(2)}, u32[]{:S(2)}) collective-permute-start(bf16[8,32768]{1,0:T(8,128)(2,1)} %vec.1), channel_id=1, source_target_pairs={{0,1},{1,0},{2,3},{3,2},{4,5},{5,4},{6,7},{7,6},{8,9},{9,8},{10,11... | collective-permute-start | bytes 1572872 | tf_op jit(solution)/shard_map/ppermute | solution.py:652
  1.3 0.7 copy-start.8
  1.9 0.7 copy-start.10
  2.6 1.6 %copy-start.1 = (bf16[8,32768]{1,0:T(8,128)(2,1)S(1)}, bf16[8,32768]{1,0:T(8,128)(2,1)}, u32[]{:S(2)}) copy-start(bf16[8,32768]{1,0:T(8,128)(2,1)} %vec.1) | copy-start | bytes 1572868
  2.6 1.6 %copy-start.4 = (f32[3,32768]{1,0:T(4,128)S(1)}, f32[3,32768]{1,0:T(4,128)}, u32[]{:S(2)}) copy-start(f32[3,32768]{1,0:T(4,128)} %points_ref.1) | copy-start | bytes 1179652
  4.2 2.2 %copy-start = (bf16[128,64,256]{2,1,0:T(8,128)(2,1)S(1)}, bf16[128,64,256]{2,1,0:T(8,128)(2,1)}, u32[]{:S(2)}) copy-start(bf16[128,64,256]{2,1,0:T(8,128)(2,1)} %basis.1) | copy-start | bytes 12582916
  4.2 2.9 %copy-start.3 = (bf16[127,2,64,64]{0,3,2,1:T(8,128)(2,1)S(1)}, bf16[127,2,64,64]{0,3,2,1:T(8,128)(2,1)}, u32[]{:S(2)}) copy-start(bf16[127,2,64,64]{0,3,2,1:T(8,128)(2,1)} %param.18) | copy-start | bytes 6242308
  12.4 33.8 %slice-start = ((s8[6291456]{0:T(1024)(128)(4,1)}), s8[4194304]{0:T(1024)(128)(4,1)S(1)}, s32[]{:S(2)}) async-start(s8[6291456]{0:T(1024)(128)(4,1)} %bitcast.11), calls=%async_computation | async-start | bytes 8388608
  12.4 33.8 %slice-start.1 = ((s8[6291456]{0:T(1024)(128)(4,1)}), s8[2097152]{0:T(1024)(128)(4,1)S(1)}, s32[]{:S(2)}) async-start(s8[6291456]{0:T(1024)(128)(4,1)} %bitcast.11), calls=%async_computation.1 | async-start | bytes 4194304
  12.4 33.8 %copy-start.7 = (s32[255,3]{0,1:T(4,128)S(1)}, s32[255,3]{0,1:T(4,128)}, u32[]{:S(2)}) copy-start(s32[255,3]{0,1:T(4,128)} %param.22) | copy-start | bytes 9184
  12.4 30.7 %collective-permute-start.1 = (bf16[8,32,128]{2,1,0:T(8,128)(2,1)S(1)}, bf16[8,32,128]{2,1,0:T(8,128)(2,1)S(1)}, u32[]{:S(2)}, u32[]{:S(2)}) collective-permute-start(bf16[8,32,128]{2,1,0:T(8,128)(2,1)S(1)} %get-tuple-element.26.refs_8_.refs_14_), channel_id=1, source_target_pairs={{0,1},{1,0},{2,3},{3,2},{4,5},{5,4},{6,7},{7,6},{8,9},{9,8},{10,11... | collective-permute-start | bytes 196616 | tf_op jit(solution)/shard_map/ppermute | solution.py:697
  12.6 45.2 %collective-permute-start.7 = (bf16[24,16384]{1,0:T(8,128)(2,1)S(1)}, bf16[24,16384]{1,0:T(8,128)(2,1)S(1)}, u32[]{:S(2)}, u32[]{:S(2)}) collective-permute-start(bf16[24,16384]{1,0:T(8,128)(2,1)S(1)} %pack.1.pack_ref), channel_id=1, source_target_pairs={{0,2},{2,0},{4,6},{6,4},{8,10},{10,8},{12,14},{14,12},{1,3},{3,1},... | collective-permute-start | bytes 2359304 | tf_op jit(solution)/shard_map/ppermute | solution.py:674
  15.5 42.3 %collective-permute-start.8 = (bf16[24,16384]{1,0:T(8,128)(2,1)S(1)}, bf16[24,16384]{1,0:T(8,128)(2,1)S(1)}, u32[]{:S(2)}, u32[]{:S(2)}) collective-permute-start(bf16[24,16384]{1,0:T(8,128)(2,1)S(1)} %pack.1.pack_ref), channel_id=1, source_target_pairs={{2,4},{4,2},{6,8},{8,6},{10,12},{12,10},{3,5},{5,3},{7,9},{9,7},{1... | collective-permute-start | bytes 2359304 | tf_op jit(solution)/shard_map/ppermute | solution.py:675
  43.2 10.1 %collective-permute-start.2 = (bf16[2,4,32,128]{3,2,1,0:T(8,128)(2,1)S(1)}, bf16[2,4,32,128]{3,2,1,0:T(8,128)(2,1)S(1)}, u32[]{:S(2)}, u32[]{:S(2)}) collective-permute-start(bf16[2,4,32,128]{3,2,1,0:T(8,128)(2,1)S(1)} %pad_maximum_fusion), channel_id=1, source_target_pairs={{0,2},{2,0},{4,6},{6,4},{8,10},{10,8},{12,14},{14,12},{1,3},{3,1},... | collective-permute-start | bytes 196616 | tf_op jit(solution)/shard_map/ppermute | solution.py:625
  53.3 8.6 %collective-permute-start.3 = (bf16[4,2,32,128]{3,2,1,0:T(8,128)(2,1)S(1)}, bf16[4,2,32,128]{3,2,1,0:T(8,128)(2,1)S(1)}, u32[]{:S(2)}, u32[]{:S(2)}) collective-permute-start(bf16[4,2,32,128]{3,2,1,0:T(8,128)(2,1)S(1)} %pad_maximum_fusion.1), channel_id=1, source_target_pairs={{0,4},{2,6},{4,0},{6,2},{8,12},{10,14},{12,8},{14,10},{1,5},{3,7},... | collective-permute-start | bytes 196616 | tf_op jit(solution)/shard_map/ppermute | solution.py:625
  55.0 7.4 %collective-permute-start.4 = (bf16[4,2,32,128]{3,2,1,0:T(8,128)(2,1)S(1)}, bf16[4,2,32,128]{3,2,1,0:T(8,128)(2,1)S(1)}, u32[]{:S(2)}, u32[]{:S(2)}) collective-permute-start(bf16[4,2,32,128]{3,2,1,0:T(8,128)(2,1)S(1)} %pad_maximum_fusion.1), channel_id=1, source_target_pairs={{0,8},{2,10},{4,12},{6,14},{8,0},{10,2},{12,4},{14,6},{1,9},{3,11}... | collective-permute-start | bytes 196616 | tf_op jit(solution)/shard_map/ppermute | solution.py:625
  56.1 6.3 %collective-permute-start.5 = (bf16[4,2,32,128]{3,2,1,0:T(8,128)(2,1)S(1)}, bf16[4,2,32,128]{3,2,1,0:T(8,128)(2,1)S(1)}, u32[]{:S(2)}, u32[]{:S(2)}) collective-permute-start(bf16[4,2,32,128]{3,2,1,0:T(8,128)(2,1)S(1)} %pad_maximum_fusion.1), channel_id=1, source_target_pairs={{0,12},{2,14},{4,8},{6,10},{8,4},{10,6},{12,0},{14,2},{1,13},{3,15... | collective-permute-start | bytes 196616 | tf_op jit(solution)/shard_map/ppermute | solution.py:625
  57.8 4.6 %copy-start.5 = (bf16[4,3,64,64]{3,2,1,0:T(8,128)(2,1)S(1)}, bf16[4,3,64,64]{3,2,1,0:T(8,128)(2,1)}, u32[]{:S(2)}) copy-start(bf16[4,3,64,64]{3,2,1,0:T(8,128)(2,1)} %refs_4_.1) | copy-start | bytes 294916
  57.8 4.6 %copy-start.6 = (bf16[4,2,64,64]{3,2,1,0:T(8,128)(2,1)S(1)}, bf16[4,2,64,64]{3,2,1,0:T(8,128)(2,1)}, u32[]{:S(2)}) copy-start(bf16[4,2,64,64]{3,2,1,0:T(8,128)(2,1)} %refs_3_.1) | copy-start | bytes 196612
  57.8 4.6 %copy-start.9 = (s32[4,3]{1,0:T(4,128)S(1)}, s32[4,3]{1,0:T(4,128)}, u32[]{:S(2)}) copy-start(s32[4,3]{1,0:T(4,128)} %refs_2_.1) | copy-start | bytes 148
  61.9 5.5 %collective-permute-start.9 = (f32[8,32768]{1,0:T(8,128)S(1)}, f32[8,32768]{1,0:T(8,128)S(1)}, u32[]{:S(2)}, u32[]{:S(2)}) collective-permute-start(f32[8,32768]{1,0:T(8,128)S(1)} %get-tuple-element.42), channel_id=1, source_target_pairs={{0,1},{1,0},{2,3},{3,2},{4,5},{5,4},{6,7},{7,6},{8,9},{9,8},{10,11... | collective-permute-start | bytes 3145736 | tf_op jit(solution)/shard_map/ppermute | solution.py:758
  62.4 5.1 %copy-start.2 = (f32[32768]{0:T(1024)S(1)}, f32[32768]{0:T(1024)}, u32[]{:S(2)}) copy-start(f32[32768]{0:T(1024)} %param.15) | copy-start | bytes 393220
  66.0 1.4 %collective-permute-start.6 = (bf16[64,8,64]{2,1,0:T(8,128)(2,1)S(1)}, bf16[64,8,64]{2,1,0:T(8,128)(2,1)S(1)}, u32[]{:S(2)}, u32[]{:S(2)}) collective-permute-start(bf16[64,8,64]{2,1,0:T(8,128)(2,1)S(1)} %get-tuple-element.37), channel_id=1, source_target_pairs={{0,1},{1,0},{2,3},{3,2},{4,5},{5,4},{6,7},{7,6},{8,9},{9,8},{10,11... | collective-permute-start | bytes 196616 | tf_op jit(solution)/shard_map/ppermute | solution.py:785

commit v11 on v10

--- a/solution.py
+++ b/solution.py
@@ -692,7 +692,7 @@
             VMEM((part - 1, 2 * ALL, 2 * RANK), BF),
         ],
         compiler_params=params(18),
-        cost_estimate=pl.CostEstimate(flops=8 * 10**9, bytes_accessed=8 << 20, transcendentals=0),
+        cost_estimate=pl.CostEstimate(flops=1 * 10**9, bytes_accessed=8 << 20, transcendentals=0),
     )(scale, pack, leaf_basis, moves_raw)
     from_core = lax.ppermute(export, "vec", [(0, 1), (1, 0)])
     pack, _ = lax.optimization_barrier((pack, export))
@@ -710,7 +710,7 @@
         ],
         compiler_params=params(22),
         cost_estimate=pl.CostEstimate(
-            flops=36 * 10**9, bytes_accessed=8 << 20, transcendentals=190 * 2**17
+            flops=1 * 10**9, bytes_accessed=8 << 20, transcendentals=190 * 2**17
         ),
     )(scale, plan, points, pack)
 
@@ -733,7 +733,7 @@
             VMEM((leaves // 4, RANK * 8, RANK), F32),
         ],
         compiler_params=params(30),
-        cost_estimate=pl.CostEstimate(flops=16 * 10**9, bytes_accessed=8 << 20, transcendentals=0),
+        cost_estimate=pl.CostEstimate(flops=1 * 10**9, bytes_accessed=8 << 20, transcendentals=0),
     )(scale, mates, coef_late, ties_raw)
 
     first, _, from_next = lax.optimization_barrier((first, local, from_next))

time: 71.6 us -> 73.1 us (1.021)
  waiting for transfers between devices: 1.6 us -> 3.71 us
  Pallas kernels: 53.4 us -> 52.1 us
    ppermute x4, waiting for transfers between devices: 0.38 us -> 1.42 us  [swap_mask(): lax.ppermute(value, ('leaf', 'sub'), [(i, i ^ mask) for i in range(total)])]
    ppermute x1, waiting for transfers between devices: 0.01 us -> 0.94 us  [body(): got = lax.ppermute(vectors, 'vec', [(0, 1), (1, 0)])]
    pallas_call x1, Pallas kernels: 27 us -> 26.2 us  [body(): pl.pallas_call(near_local_kernel, name='near_local', out_shape=(sds((PART...]
    unnamed x26 -> x30, local copies, waits for them, and re-layouts: 3.29 us -> 3.42 us
  transfers between devices with their start and end apart: 10 -> 10, of which waited for: 2 -> 3; matrix products, arithmetic and copies ran while one was open for 1% -> 1% of each run, Pallas kernels for 61% -> 65%
where the time goes in v11:
time: 73.1 us; the launch traced here: 72.7 us
  Pallas kernels  52.1 us (71%)
  starting transfers between devices  12.4 us (17%)
  waiting for transfers between devices  3.71 us (5%)
  local copies, waits for them, and re-layouts  3.44 us (5%)
  other arithmetic  0.82 us (1%)
    pallas_call x1, Pallas kernels, body(): pl.pallas_call(near_local_kernel, name='near_local', out_shape=(sds((PART...  26.2 us
    ppermute x4, starting transfers between devices, swap_mask(): lax.ppermute(value, ('leaf', 'sub'), [(i, i ^ mask) for i in range(total)])  8.11 us
    pallas_call x1, Pallas kernels, body(): pl.pallas_call(couple_kernel, name='couple', out_shape=(sds((part - 1, AL...  7.05 us
    pallas_call x1, Pallas kernels, body(): pl.pallas_call(up_kernel, name='up', out_shape=(sds((2 * part - 1, 2 * AL...  5.35 us
    pallas_call x1, Pallas kernels, body(): pl.pallas_call(final_kernel, name='final', out_shape=sds((PART, size), F3...  3.85 us
    pallas_call x1, Pallas kernels, body(): pl.pallas_call(lambda *refs: down_kernel(dev_levels, *refs[:11], refs[11:...  3.64 us
    pallas_call x1, Pallas kernels, body(): pl.pallas_call(near_halo_kernel, name='near_halo', out_shape=(sds((PART,...  3.54 us
    unnamed x30, local copies, waits for them, and re-layouts  3.42 us
  transfers between devices with their start and end apart: 10, of which 3 were waited for; matrix products, arithmetic and copies ran while one was open for 1% of the time, Pallas kernels for 65%

profile of v11, /device:TPU:0, one launch (start us, length us, event | category | flops | bytes accessed | tf_op | source)
XLA Modules:
  0.0 72.7 jit_solution(16664640818977232744)
XLA Ops:
  0.0 0.5 collective-permute-start
  0.5 0.1 add_convert_fusion
  0.5 0.7 %pad_maximum_fusion.2.scale_ref.refs_0_ = f32[5]{0:T(128)S(1)} fusion(f32[2]{0:T(128)S(1)} %add_convert_fusion, f32[3]{0:T(128)} %param.14), kind=kLoop, calls=%fused_computation.4 | loop fusion | flops 5 | bytes 40 | tf_op jit(solution)/shard_map/concatenate | solution.py:641
  1.3 0.9 %collective-permute-done.got = bf16[8,32768]{1,0:T(8,128)(2,1)S(1)} collective-permute-done((bf16[8,32768]{1,0:T(8,128)(2,1)}, bf16[8,32768]{1,0:T(8,128)(2,1)S(1)}, u32[]{:S(2)}, u32[]{:S(2)}) %collective-permute-start) | collective-permute-done | bytes 524320 | tf_op jit(solution)/shard_map/ppermute | solution.py:652
  2.2 1.0 %copy-done.2 = bf16[8,32768]{1,0:T(8,128)(2,1)S(1)} copy-done((bf16[8,32768]{1,0:T(8,128)(2,1)S(1)}, bf16[8,32768]{1,0:T(8,128)(2,1)}, u32[]{:S(2)}) %copy-start.2) | copy-done | bytes 524312
  3.2 1.0 %copy-done.6 = f32[3,32768]{1,0:T(4,128)S(1)} copy-done((f32[3,32768]{1,0:T(4,128)S(1)}, f32[3,32768]{1,0:T(4,128)}, u32[]{:S(2)}) %copy-start.6) | copy-done | bytes 393240
  4.3 0.9 %pack.1.pack_ref = bf16[24,16384]{1,0:T(8,128)(2,1)S(1)} custom-call(f32[5]{0:T(128)S(1)} %pad_maximum_fusion.2.scale_ref.refs_0_, f32[3,32768]{1,0:T(4,128)S(1)} %copy-done.6, bf16[8,32768]{1,0:T(8,128)(2,1)S(1)} %copy-done.2, bf16[8,32768]{1,0:T(8,128)(2,1)S(1)} %collective-permute-done.got), custom_call_target="tpu_custom_call" | custom-call | flops 2000000000 | bytes 2097152 | tf_op jit(solution)/shard_map/pack/pallas_call | solution.py:664
  5.2 2.9 %collective-permute-start.7 = (bf16[24,16384]{1,0:T(8,128)(2,1)S(1)}, bf16[24,16384]{1,0:T(8,128)(2,1)S(1)}, u32[]{:S(2)}, u32[]{:S(2)}) collective-permute-start(bf16[24,16384]{1,0:T(8,128)(2,1)S(1)} %pack.1.pack_ref), channel_id=1, source_target_pairs={{0,2},{2,0},{4,6},{6,4},{8,10},{10,8},{12,14},{14,12},{1,3},{3,1},... | collective-permute-start | bytes 2359304 | tf_op jit(solution)/shard_map/ppermute | solution.py:674
  8.1 0.7 collective-permute-start.8
  8.9 1.6 %plan.1.plan_ref = s32[8,640]{1,0:T(8,128)S(1)} custom-call(f32[5]{0:T(128)S(1)} %pad_maximum_fusion.2.scale_ref.refs_0_, s32[1,128]{1,0:T(1,128)S(1)} %bitcast.18, s32[1,512]{1,0:T(1,128)S(1)} %bitcast.17), custom_call_target="tpu_custom_call" | custom-call | flops 3000000000 | bytes 65536 | tf_op jit(solution)/shard_map/plan/pallas_call | solution.py:654
  10.5 0.6 copy-done
  11.0 0.7 copy-done.1
  11.7 5.3 %up.1 = (bf16[127,32,128]{2,1,0:T(8,128)(2,1)S(1)}, bf16[8,32,128]{2,1,0:T(8,128)(2,1)S(1)}, bf16[1,4,32,128]{3,2,1,0:T(8,128)(2,1)S(1)}, bf16[64,64,128]{2,1,0:T(8,128)(2,1)S(1)}) custom-call(f32[5]{0:T(128)S(1)} %pad_maximum_fusion.2.scale_ref.refs_0_, bf16[24,16384]{1,0:T(8,128)(2,1)S(1)} %pack.1.pack_ref, bf16[128,64,256]{2,1,0:T(8,128)(2,1)S(1)} %copy-done, ...), custom_call_target="tpu_custom_call" | custom-call | flops 1000000000 | bytes 8388608 | tf_op jit(solution)/shard_map/up/pallas_call | solution.py:681
  17.2 26.2 %near_local.1 = (f32[8,32768]{1,0:T(8,128)S(1)}, f32[8,32768]{1,0:T(8,128)S(1)}, bf16[128,32,256]{2,1,0:T(8,128)(2,1)S(1)}) custom-call(f32[5]{0:T(128)S(1)} %pad_maximum_fusion.2.scale_ref.refs_0_, s32[8,640]{1,0:T(8,128)S(1)} %plan.1.plan_ref, f32[3,32768]{1,0:T(4,128)S(1)} %copy-done.7, bf16[24,16384]{1,0:T(8,128)(2,1)S(1)} %pack.1.pack_ref), custom_call_target="tpu_custom_call" | custom-call | flops 1000000000 | bytes 8388608 | tf_op jit(solution)/shard_map/near_local/pallas_call | solution.py:699
  43.4 3.7 %collective-permute-start.2 = (bf16[2,4,32,128]{3,2,1,0:T(8,128)(2,1)S(1)}, bf16[2,4,32,128]{3,2,1,0:T(8,128)(2,1)S(1)}, u32[]{:S(2)}, u32[]{:S(2)}) collective-permute-start(bf16[2,4,32,128]{3,2,1,0:T(8,128)(2,1)S(1)} %pad_maximum_fusion), channel_id=1, source_target_pairs={{0,2},{2,0},{4,6},{6,4},{8,10},{10,8},{12,14},{14,12},{1,3},{3,1},... | collective-permute-start | bytes 196616 | tf_op jit(solution)/shard_map/ppermute | solution.py:625
  47.1 7.0 %couple.1 = (f32[63,16,128]{2,1,0:T(8,128)S(1)}, bf16[8,64,192]{2,1,0:T(8,128)(2,1)S(1)}) custom-call(f32[5]{0:T(128)S(1)} %pad_maximum_fusion.2.scale_ref.refs_0_, s32[3,255]{1,0:T(4,128)S(1)} %bitcast.15, bf16[127,32,128]{2,1,0:T(8,128)(2,1)S(1)} %get-tuple-element.30.coef_ref, bf16[3,64,64,255]{3,2,1,0:T(8,128)(2,1)S(1)} %bitcast.12), custom_call_target="tpu_custom_call" | custom-call | flops 1000000000 | bytes 8388608 | tf_op jit(solution)/shard_map/couple/pallas_call | solution.py:723
  54.2 1.0 %collective-permute-start.3 = (bf16[4,2,32,128]{3,2,1,0:T(8,128)(2,1)S(1)}, bf16[4,2,32,128]{3,2,1,0:T(8,128)(2,1)S(1)}, u32[]{:S(2)}, u32[]{:S(2)}) collective-permute-start(bf16[4,2,32,128]{3,2,1,0:T(8,128)(2,1)S(1)} %pad_maximum_fusion.1), channel_id=1, source_target_pairs={{0,4},{2,6},{4,0},{6,2},{8,12},{10,14},{12,8},{14,10},{1,5},{3,7},... | collective-permute-start | bytes 196616 | tf_op jit(solution)/shard_map/ppermute | solution.py:625
  55.2 1.1 %collective-permute-start.4 = (bf16[4,2,32,128]{3,2,1,0:T(8,128)(2,1)S(1)}, bf16[4,2,32,128]{3,2,1,0:T(8,128)(2,1)S(1)}, u32[]{:S(2)}, u32[]{:S(2)}) collective-permute-start(bf16[4,2,32,128]{3,2,1,0:T(8,128)(2,1)S(1)} %pad_maximum_fusion.1), channel_id=1, source_target_pairs={{0,8},{2,10},{4,12},{6,14},{8,0},{10,2},{12,4},{14,6},{1,9},{3,11}... | collective-permute-start | bytes 196616 | tf_op jit(solution)/shard_map/ppermute | solution.py:625
  56.3 2.4 %collective-permute-start.5 = (bf16[4,2,32,128]{3,2,1,0:T(8,128)(2,1)S(1)}, bf16[4,2,32,128]{3,2,1,0:T(8,128)(2,1)S(1)}, u32[]{:S(2)}, u32[]{:S(2)}) collective-permute-start(bf16[4,2,32,128]{3,2,1,0:T(8,128)(2,1)S(1)} %pad_maximum_fusion.1), channel_id=1, source_target_pairs={{0,12},{2,14},{4,8},{6,10},{8,4},{10,6},{12,0},{14,2},{1,13},{3,15... | collective-permute-start | bytes 196616 | tf_op jit(solution)/shard_map/ppermute | solution.py:625
  58.7 3.5 %near_halo.1 = (f32[8,32768]{1,0:T(8,128)S(1)}, f32[8,32768]{1,0:T(8,128)S(1)}) custom-call(f32[5]{0:T(128)S(1)} %pad_maximum_fusion.2.scale_ref.refs_0_, s32[8,640]{1,0:T(8,128)S(1)} %plan.1.plan_ref, bf16[128,32,256]{2,1,0:T(8,128)(2,1)S(1)} %get-tuple-element.38.row_ref, bf16[24,16384]{1,0:T(8,128)(2,1)S(1)} %collective-permute-done.7.inner_ref, ...), custom_call_target="tpu_custom_call" | custom-call | flops 20000000000 | bytes 8388608 | tf_op jit(solution)/shard_map/near_halo/pallas_call | solution.py:742
  62.4 1.4 %collective-permute-done.4.refs_12_ = bf16[4,2,32,128]{3,2,1,0:T(8,128)(2,1)S(1)} collective-permute-done((bf16[4,2,32,128]{3,2,1,0:T(8,128)(2,1)S(1)}, bf16[4,2,32,128]{3,2,1,0:T(8,128)(2,1)S(1)}, u32[]{:S(2)}, u32[]{:S(2)}) %collective-permute-start.4) | collective-permute-done | bytes 65568 | tf_op jit(solution)/shard_map/ppermute | solution.py:625
  63.8 3.6 %down.1 = (bf16[64,8,64]{2,1,0:T(8,128)(2,1)S(1)}, bf16[64,8,64]{2,1,0:T(8,128)(2,1)S(1)}) custom-call(f32[5]{0:T(128)S(1)} %pad_maximum_fusion.2.scale_ref.refs_0_, s32[3,255]{1,0:T(4,128)S(1)} %bitcast.16, s32[4,3]{1,0:T(4,128)S(1)} %copy-done.11, bf16[4,2,64,64]{3,2,1,0:T(8,128)(2,1)S(1)} %copy-done.9, bf16[4,3,64,64]{3,2,1,0:T(8,128)(2,1)S(1)} %copy-done.8, ...), custom_call_target="tpu_custom_call" | custom-call | flops 40000000000 | bytes 4194304 | tf_op jit(solution)/shard_map/down/pallas_call | solution.py:769
  67.5 1.3 %collective-permute-done.6.got_ref = bf16[64,8,64]{2,1,0:T(8,128)(2,1)S(1)} collective-permute-done((bf16[64,8,64]{2,1,0:T(8,128)(2,1)S(1)}, bf16[64,8,64]{2,1,0:T(8,128)(2,1)S(1)}, u32[]{:S(2)}, u32[]{:S(2)}) %collective-permute-start.6) | collective-permute-done | bytes 65568 | tf_op jit(solution)/shard_map/ppermute | solution.py:785
  68.9 3.8 %final.1 = f32[8,32768]{1,0:T(8,128)} custom-call(f32[5]{0:T(128)S(1)} %pad_maximum_fusion.2.scale_ref.refs_0_, bf16[64,8,64]{2,1,0:T(8,128)(2,1)S(1)} %get-tuple-element.36.mine_ref, bf16[64,8,64]{2,1,0:T(8,128)(2,1)S(1)} %collective-permute-done.6.got_ref, bf16[128,64,256]{2,1,0:T(8,128)(2,1)S(1)} %copy-done, f32[1,32768]{1,0:T(1,128)S(1)} %bitcast.14, ...), custom_call_target="tpu_custom_call" | custom-call | flops 2000000000 | bytes 4194304 | tf_op jit(solution)/shard_map/final/pallas_call | solution.py:787
  (42 shorter events, 0.3 us)
Async XLA Ops:
  0.0 8.8 %copy-start.12 = (s32[128]{0:T(128)S(1)}, s32[128]{0:T(128)}, u32[]{:S(2)}) copy-start(s32[128]{0:T(128)} %param.24) | copy-start | bytes 1540
  0.0 8.8 %copy-start.10 = (s32[512]{0:T(512)S(1)}, s32[512]{0:T(512)}, u32[]{:S(2)}) copy-start(s32[512]{0:T(512)} %param.25) | copy-start | bytes 6148
  0.0 2.2 %collective-permute-start = (bf16[8,32768]{1,0:T(8,128)(2,1)}, bf16[8,32768]{1,0:T(8,128)(2,1)S(1)}, u32[]{:S(2)}, u32[]{:S(2)}) collective-permute-start(bf16[8,32768]{1,0:T(8,128)(2,1)} %vec.1), channel_id=1, source_target_pairs={{0,1},{1,0},{2,3},{3,2},{4,5},{5,4},{6,7},{7,6},{8,9},{9,8},{10,11... | collective-permute-start | bytes 1572872 | tf_op jit(solution)/shard_map/ppermute | solution.py:652
  2.2 1.0 %copy-start.2 = (bf16[8,32768]{1,0:T(8,128)(2,1)S(1)}, bf16[8,32768]{1,0:T(8,128)(2,1)}, u32[]{:S(2)}) copy-start(bf16[8,32768]{1,0:T(8,128)(2,1)} %vec.1) | copy-start | bytes 1572868
  5.2 53.5 %collective-permute-start.7 = (bf16[24,16384]{1,0:T(8,128)(2,1)S(1)}, bf16[24,16384]{1,0:T(8,128)(2,1)S(1)}, u32[]{:S(2)}, u32[]{:S(2)}) collective-permute-start(bf16[24,16384]{1,0:T(8,128)(2,1)S(1)} %pack.1.pack_ref), channel_id=1, source_target_pairs={{0,2},{2,0},{4,6},{6,4},{8,10},{10,8},{12,14},{14,12},{1,3},{3,1},... | collective-permute-start | bytes 2359304 | tf_op jit(solution)/shard_map/ppermute | solution.py:674
  8.1 50.6 %collective-permute-start.8 = (bf16[24,16384]{1,0:T(8,128)(2,1)S(1)}, bf16[24,16384]{1,0:T(8,128)(2,1)S(1)}, u32[]{:S(2)}, u32[]{:S(2)}) collective-permute-start(bf16[24,16384]{1,0:T(8,128)(2,1)S(1)} %pack.1.pack_ref), channel_id=1, source_target_pairs={{2,4},{4,2},{6,8},{8,6},{10,12},{12,10},{3,5},{5,3},{7,9},{9,7},{1... | collective-permute-start | bytes 2359304 | tf_op jit(solution)/shard_map/ppermute | solution.py:675
  8.9 2.2 %copy-start = (bf16[128,64,256]{2,1,0:T(8,128)(2,1)S(1)}, bf16[128,64,256]{2,1,0:T(8,128)(2,1)}, u32[]{:S(2)}) copy-start(bf16[128,64,256]{2,1,0:T(8,128)(2,1)} %basis.1) | copy-start | bytes 12582916
  8.9 2.9 %copy-start.1 = (bf16[127,2,64,64]{0,3,2,1:T(8,128)(2,1)S(1)}, bf16[127,2,64,64]{0,3,2,1:T(8,128)(2,1)}, u32[]{:S(2)}) copy-start(bf16[127,2,64,64]{0,3,2,1:T(8,128)(2,1)} %param.18) | copy-start | bytes 6242308
  10.5 6.8 %copy-start.7 = (f32[3,32768]{1,0:T(4,128)S(1)}, f32[3,32768]{1,0:T(4,128)}, u32[]{:S(2)}) copy-start(f32[3,32768]{1,0:T(4,128)} %points_ref.1) | copy-start | bytes 1179652
  17.1 30.0 %slice-start = ((s8[6291456]{0:T(1024)(128)(4,1)}), s8[4194304]{0:T(1024)(128)(4,1)S(1)}, s32[]{:S(2)}) async-start(s8[6291456]{0:T(1024)(128)(4,1)} %bitcast.10), calls=%async_computation | async-start | bytes 8388608
  17.1 30.0 %slice-start.1 = ((s8[6291456]{0:T(1024)(128)(4,1)}), s8[2097152]{0:T(1024)(128)(4,1)S(1)}, s32[]{:S(2)}) async-start(s8[6291456]{0:T(1024)(128)(4,1)} %bitcast.10), calls=%async_computation.1 | async-start | bytes 4194304
  17.1 30.0 %copy-start.5 = (s32[255,3]{0,1:T(4,128)S(1)}, s32[255,3]{0,1:T(4,128)}, u32[]{:S(2)}) copy-start(s32[255,3]{0,1:T(4,128)} %param.22) | copy-start | bytes 9184
  17.1 26.3 %collective-permute-start.1 = (bf16[8,32,128]{2,1,0:T(8,128)(2,1)S(1)}, bf16[8,32,128]{2,1,0:T(8,128)(2,1)S(1)}, u32[]{:S(2)}, u32[]{:S(2)}) collective-permute-start(bf16[8,32,128]{2,1,0:T(8,128)(2,1)S(1)} %get-tuple-element.26.refs_8_.refs_14_), channel_id=1, source_target_pairs={{0,1},{1,0},{2,3},{3,2},{4,5},{5,4},{6,7},{7,6},{8,9},{9,8},{10,11... | collective-permute-start | bytes 196616 | tf_op jit(solution)/shard_map/ppermute | solution.py:697
  43.4 10.8 %collective-permute-start.2 = (bf16[2,4,32,128]{3,2,1,0:T(8,128)(2,1)S(1)}, bf16[2,4,32,128]{3,2,1,0:T(8,128)(2,1)S(1)}, u32[]{:S(2)}, u32[]{:S(2)}) collective-permute-start(bf16[2,4,32,128]{3,2,1,0:T(8,128)(2,1)S(1)} %pad_maximum_fusion), channel_id=1, source_target_pairs={{0,2},{2,0},{4,6},{6,4},{8,10},{10,8},{12,14},{14,12},{1,3},{3,1},... | collective-permute-start | bytes 196616 | tf_op jit(solution)/shard_map/ppermute | solution.py:625
  54.2 8.1 %collective-permute-start.3 = (bf16[4,2,32,128]{3,2,1,0:T(8,128)(2,1)S(1)}, bf16[4,2,32,128]{3,2,1,0:T(8,128)(2,1)S(1)}, u32[]{:S(2)}, u32[]{:S(2)}) collective-permute-start(bf16[4,2,32,128]{3,2,1,0:T(8,128)(2,1)S(1)} %pad_maximum_fusion.1), channel_id=1, source_target_pairs={{0,4},{2,6},{4,0},{6,2},{8,12},{10,14},{12,8},{14,10},{1,5},{3,7},... | collective-permute-start | bytes 196616 | tf_op jit(solution)/shard_map/ppermute | solution.py:625
  55.2 8.6 %collective-permute-start.4 = (bf16[4,2,32,128]{3,2,1,0:T(8,128)(2,1)S(1)}, bf16[4,2,32,128]{3,2,1,0:T(8,128)(2,1)S(1)}, u32[]{:S(2)}, u32[]{:S(2)}) collective-permute-start(bf16[4,2,32,128]{3,2,1,0:T(8,128)(2,1)S(1)} %pad_maximum_fusion.1), channel_id=1, source_target_pairs={{0,8},{2,10},{4,12},{6,14},{8,0},{10,2},{12,4},{14,6},{1,9},{3,11}... | collective-permute-start | bytes 196616 | tf_op jit(solution)/shard_map/ppermute | solution.py:625
  56.3 7.5 %collective-permute-start.5 = (bf16[4,2,32,128]{3,2,1,0:T(8,128)(2,1)S(1)}, bf16[4,2,32,128]{3,2,1,0:T(8,128)(2,1)S(1)}, u32[]{:S(2)}, u32[]{:S(2)}) collective-permute-start(bf16[4,2,32,128]{3,2,1,0:T(8,128)(2,1)S(1)} %pad_maximum_fusion.1), channel_id=1, source_target_pairs={{0,12},{2,14},{4,8},{6,10},{8,4},{10,6},{12,0},{14,2},{1,13},{3,15... | collective-permute-start | bytes 196616 | tf_op jit(solution)/shard_map/ppermute | solution.py:625
  58.7 5.1 %copy-start.8 = (bf16[4,3,64,64]{3,2,1,0:T(8,128)(2,1)S(1)}, bf16[4,3,64,64]{3,2,1,0:T(8,128)(2,1)}, u32[]{:S(2)}) copy-start(bf16[4,3,64,64]{3,2,1,0:T(8,128)(2,1)} %refs_4_.1) | copy-start | bytes 294916
  58.7 5.1 %copy-start.9 = (bf16[4,2,64,64]{3,2,1,0:T(8,128)(2,1)S(1)}, bf16[4,2,64,64]{3,2,1,0:T(8,128)(2,1)}, u32[]{:S(2)}) copy-start(bf16[4,2,64,64]{3,2,1,0:T(8,128)(2,1)} %refs_3_.1) | copy-start | bytes 196612
  58.7 5.1 %copy-start.11 = (s32[4,3]{1,0:T(4,128)S(1)}, s32[4,3]{1,0:T(4,128)}, u32[]{:S(2)}) copy-start(s32[4,3]{1,0:T(4,128)} %refs_2_.1) | copy-start | bytes 148
  62.3 6.6 %collective-permute-start.9 = (f32[8,32768]{1,0:T(8,128)S(1)}, f32[8,32768]{1,0:T(8,128)S(1)}, u32[]{:S(2)}, u32[]{:S(2)}) collective-permute-start(f32[8,32768]{1,0:T(8,128)S(1)} %get-tuple-element.42), channel_id=1, source_target_pairs={{0,1},{1,0},{2,3},{3,2},{4,5},{5,4},{6,7},{7,6},{8,9},{9,8},{10,11... | collective-permute-start | bytes 3145736 | tf_op jit(solution)/shard_map/ppermute | solution.py:758
  63.8 5.1 %copy-start.3 = (bf16[8,32768]{1,0:T(8,128)(2,1)S(1)}, bf16[8,32768]{1,0:T(8,128)(2,1)}, u32[]{:S(2)}) copy-start(bf16[8,32768]{1,0:T(8,128)(2,1)} %vec.1) | copy-start | bytes 1572868
  63.8 5.1 %copy-start.4 = (f32[32768]{0:T(1024)S(1)}, f32[32768]{0:T(1024)}, u32[]{:S(2)}) copy-start(f32[32768]{0:T(1024)} %param.15) | copy-start | bytes 393220
  67.5 1.4 %collective-permute-start.6 = (bf16[64,8,64]{2,1,0:T(8,128)(2,1)S(1)}, bf16[64,8,64]{2,1,0:T(8,128)(2,1)S(1)}, u32[]{:S(2)}, u32[]{:S(2)}) collective-permute-start(bf16[64,8,64]{2,1,0:T(8,128)(2,1)S(1)} %get-tuple-element.37), channel_id=1, source_target_pairs={{0,1},{1,0},{2,3},{3,2},{4,5},{5,4},{6,7},{7,6},{8,9},{9,8},{10,11... | collective-permute-start | bytes 196616 | tf_op jit(solution)/shard_map/ppermute | solution.py:785
  (1 other events, 1.0 us)

commit v12 on v10

--- a/solution.py
+++ b/solution.py
@@ -120,18 +120,18 @@
     lax.fori_loop(0, half // 2048, step, 0)
 
 
-def plan_kernel(scale_ref, offs_ref, cols_ref, out_ref):
+def plan_kernel(leaves, scale_ref, ids_ref, out_ref):
     device, half_id = whole(scale_ref[3]), whole(scale_ref[4])
-    leaves = offs_ref.shape[1]
-    slots = cols_ref.shape[1]
+    slots = ids_ref.shape[1] - leaves
+    offs, cols = ids_ref[:, :leaves], ids_ref[:, leaves:]
     room = out_ref.shape[1]
     half = leaves // 2
     half_bits = half.bit_length() - 1
-    begins = jnp.broadcast_to(offs_ref[...].astype(F32), (8, leaves)).T[:, 0:1]
+    begins = jnp.broadcast_to(offs.astype(F32), (8, leaves)).T[:, 0:1]
     slot = lax.broadcasted_iota(jnp.int32, (leaves, slots), 1).astype(F32)
     row = jnp.sum(jnp.where(begins <= slot, 1.0, 0.0), axis=0, keepdims=True) - 1.0
     first = jnp.sum(jnp.where(begins == slot, 1.0, 0.0), axis=0, keepdims=True)
-    place = cols_ref[...] - (device * leaves - leaves + half_id * half)
+    place = cols - (device * leaves - leaves + half_id * half)
     block = place >> half_bits
     own = jnp.where(block == 2, 1.0 - first, 0.0)
     far = jnp.where((block & 3) == 0, 1.0, 0.0)
@@ -586,36 +586,40 @@
 
 
 def final_kernel(
-    scale_ref, mine_ref, got_ref, basis, noise, vec, near, swap, out_hbm, out, sems
+    scale_ref, mine_ref, got_ref, basis, noise, vec, near_hbm, swap_hbm, out_hbm,
+    near, swap, out, sems,
 ):
     core = whole(scale_ref[4])
     leaves = mine_ref.shape[0]
-    chunks = 2
-    per = leaves // chunks
-    wide = per * LEAF
-    sends = []
+    loads = [
+        pltpu.make_async_copy(near_hbm, near, sems.at[0]),
+        pltpu.make_async_copy(swap_hbm, swap, sems.at[1]),
+    ]
+    for load in loads:
+        load.start()
     for part, low_ref in enumerate((mine_ref, got_ref)):
         base = jnp.where(core == part, 0, leaves)
-        for c in range(chunks):
-
-            def last(nodes, c=c, low_ref=low_ref, base=base):
-                rows = [c * per + i for i in nodes]
-                fars = [
-                    jnp.dot(low_ref[n], basis[base + n], preferred_element_type=F32)
-                    for n in rows
-                ]
-                for n, far in zip(rows, fars):
-                    here = lanes(base + n)
-                    total = near[:, here] + swap[:, here]
-                    out[:, here] = total + noise[:, here] * vec[:, here].astype(F32) + far
-
-            over_nodes(per, 8, last)
-            piece = pl.ds(pl.multiple_of((base + c * per) * LEAF, wide), wide)
-            send = pltpu.make_async_copy(
-                out.at[:, piece], out_hbm.at[:, piece], sems.at[part * chunks + c]
-            )
-            send.start()
-            sends.append(send)
+
+        def last(nodes, low_ref=low_ref, base=base):
+            fars = [
+                jnp.dot(low_ref[n], basis[base + n], preferred_element_type=F32) for n in nodes
+            ]
+            for n, far in zip(nodes, fars):
+                here = lanes(base + n)
+                out[:, here] = noise[:, here] * vec[:, here].astype(F32) + far
+
+        over_nodes(leaves, 8, last)
+    for load in loads:
+        load.wait()
+    chunks = 4
+    wide = out.shape[1] // chunks
+    sends = []
+    for c in range(chunks):
+        piece = slice(c * wide, (c + 1) * wide)
+        out[:, piece] += near[:, piece] + swap[:, piece]
+        send = pltpu.make_async_copy(out.at[:, piece], out_hbm.at[:, piece], sems.at[2 + c])
+        send.start()
+        sends.append(send)
     for send in sends:
         send.wait()
 
@@ -652,14 +656,14 @@
     got = lax.ppermute(vectors, "vec", [(0, 1), (1, 0)])
 
     plan = pl.pallas_call(
-        plan_kernel,
+        functools.partial(plan_kernel, leaves),
         name="plan",
         out_shape=sds((8, slots + 128), jnp.int32),
-        in_specs=[sspec(), vspec(), vspec()],
+        in_specs=[sspec(), vspec()],
         out_specs=vspec(),
         compiler_params=params(8),
         cost_estimate=pl.CostEstimate(flops=3 * 10**9, bytes_accessed=1 << 16, transcendentals=0),
-    )(scale, near_offsets.reshape(1, leaves), near_cols.reshape(1, slots))
+    )(scale, jnp.concatenate([near_offsets, near_cols]).reshape(1, leaves + slots))
 
     pack = pl.pallas_call(
         pack_kernel,
@@ -788,9 +792,9 @@
         final_kernel,
         name="final",
         out_shape=sds((PART, size), F32),
-        in_specs=[sspec()] + [vspec()] * 7,
+        in_specs=[sspec()] + [vspec()] * 5 + [hspec()] * 2,
         out_specs=hspec(),
-        scratch_shapes=[VMEM((PART, size), F32), pltpu.SemaphoreType.DMA((4,))],
+        scratch_shapes=[VMEM((PART, size), F32)] * 3 + [pltpu.SemaphoreType.DMA((6,))],
         compiler_params=params(10),
         cost_estimate=pl.CostEstimate(flops=2 * 10**9, bytes_accessed=4 << 20, transcendentals=0),
     )(scale, low_mine, low_got, leaf_basis, noise.reshape(1, size), vectors, mine, swapped)

time: 71.6 us -> 71.7 us (level)
  waiting for transfers between devices: 1.6 us -> 3.5 us
  Pallas kernels: 53.4 us -> 51.7 us
  local copies, waits for them, and re-layouts: 3.31 us -> 1.98 us
    ppermute x4, waiting for transfers between devices: 0.38 us -> 2.16 us  [swap_mask(): lax.ppermute(value, ('leaf', 'sub'), [(i, i ^ mask) for i in range(total)])]
    pallas_call x1, Pallas kernels: 4.07 us -> 2.53 us  [body(): pl.pallas_call(near_halo_kernel, name='near_halo', out_shape=(sds((PART,...]
    unnamed x26 -> x22, local copies, waits for them, and re-layouts: 3.29 us -> 1.96 us
  transfers between devices with their start and end apart: 10 -> 10, of which waited for: 2 -> 2; matrix products, arithmetic and copies ran while one was open for 1% -> 2% of each run, Pallas kernels for 61% -> 58%
where the time goes in v12:
time: 71.7 us; the launch traced here: 71.3 us
  Pallas kernels  51.7 us (72%)
  starting transfers between devices  12.4 us (17%)
  waiting for transfers between devices  3.5 us (5%)
  local copies, waits for them, and re-layouts  1.98 us (3%)
  other arithmetic  1.52 us (2%)
    pallas_call x1, Pallas kernels, body(): pl.pallas_call(near_local_kernel, name='near_local', out_shape=(sds((PART...  26.3 us
    ppermute x4, starting transfers between devices, swap_mask(): lax.ppermute(value, ('leaf', 'sub'), [(i, i ^ mask) for i in range(total)])  8.09 us
    pallas_call x1, Pallas kernels, body(): pl.pallas_call(couple_kernel, name='couple', out_shape=(sds((part - 1, AL...  7.05 us
    pallas_call x1, Pallas kernels, body(): pl.pallas_call(up_kernel, name='up', out_shape=(sds((2 * part - 1, 2 * AL...  5.36 us
    pallas_call x1, Pallas kernels, body(): pl.pallas_call(final_kernel, name='final', out_shape=sds((PART, size), F3...  4.3 us
    pallas_call x1, Pallas kernels, body(): pl.pallas_call(lambda *refs: down_kernel(dev_levels, *refs[:11], refs[11:...  3.66 us
    ppermute x1, starting transfers between devices, body(): inner = lax.ppermute(pack, axes, [(i, i ^ 1) for i in range(count)])  2.94 us
    pallas_call x1, Pallas kernels, body(): pl.pallas_call(near_halo_kernel, name='near_halo', out_shape=(sds((PART,...  2.53 us
  transfers between devices with their start and end apart: 10, of which 2 were waited for; matrix products, arithmetic and copies ran while one was open for 2% of the time, Pallas kernels for 58%

profile of v12, /device:TPU:0, one launch (start us, length us, event | category | flops | bytes accessed | tf_op | source)
XLA Modules:
  0.0 71.3 jit_solution(1560310519953790898)
XLA Ops:
  0.0 0.5 collective-permute-start
  0.5 0.7 pad_add_fusion
  1.2 0.1 add_convert_fusion
  1.2 0.7 %pad_maximum_fusion.2.scale_ref.refs_0_ = f32[5]{0:T(128)S(1)} fusion(f32[2]{0:T(128)S(1)} %add_convert_fusion, f32[3]{0:T(128)} %param.14), kind=kLoop, calls=%fused_computation.5 | loop fusion | flops 5 | bytes 40 | tf_op jit(solution)/shard_map/concatenate | solution.py:645
  2.0 1.6 %plan.1.plan_ref = s32[8,640]{1,0:T(8,128)S(1)} custom-call(f32[5]{0:T(128)S(1)} %pad_maximum_fusion.2.scale_ref.refs_0_, s32[1,640]{1,0:T(1,128)S(1)} %reshape.6.ids_ref), custom_call_target="tpu_custom_call" | custom-call | flops 3000000000 | bytes 65536 | tf_op jit(solution)/shard_map/plan/pallas_call | solution.py:658
  3.6 0.9 %pack.1.pack_ref = bf16[24,16384]{1,0:T(8,128)(2,1)S(1)} custom-call(f32[5]{0:T(128)S(1)} %pad_maximum_fusion.2.scale_ref.refs_0_, f32[3,32768]{1,0:T(4,128)S(1)} %copy-done.4, bf16[8,32768]{1,0:T(8,128)(2,1)S(1)} %copy-done.1, bf16[8,32768]{1,0:T(8,128)(2,1)S(1)} %collective-permute-done.got), custom_call_target="tpu_custom_call" | custom-call | flops 2000000000 | bytes 2097152 | tf_op jit(solution)/shard_map/pack/pallas_call | solution.py:668
  4.5 1.2 %copy-done = bf16[128,64,256]{2,1,0:T(8,128)(2,1)S(1)} copy-done((bf16[128,64,256]{2,1,0:T(8,128)(2,1)S(1)}, bf16[128,64,256]{2,1,0:T(8,128)(2,1)}, u32[]{:S(2)}) %copy-start) | copy-done | bytes 4194328
  5.7 0.7 copy-done.3
  6.4 5.4 %up.1 = (bf16[127,32,128]{2,1,0:T(8,128)(2,1)S(1)}, bf16[8,32,128]{2,1,0:T(8,128)(2,1)S(1)}, bf16[1,4,32,128]{3,2,1,0:T(8,128)(2,1)S(1)}, bf16[64,64,128]{2,1,0:T(8,128)(2,1)S(1)}) custom-call(f32[5]{0:T(128)S(1)} %pad_maximum_fusion.2.scale_ref.refs_0_, bf16[24,16384]{1,0:T(8,128)(2,1)S(1)} %pack.1.pack_ref, bf16[128,64,256]{2,1,0:T(8,128)(2,1)S(1)} %copy-done, ...), custom_call_target="tpu_custom_call" | custom-call | flops 8000000000 | bytes 8388608 | tf_op jit(solution)/shard_map/up/pallas_call | solution.py:685
  11.8 0.1 collective-permute-start.1
  11.9 2.9 %collective-permute-start.7 = (bf16[24,16384]{1,0:T(8,128)(2,1)S(1)}, bf16[24,16384]{1,0:T(8,128)(2,1)S(1)}, u32[]{:S(2)}, u32[]{:S(2)}) collective-permute-start(bf16[24,16384]{1,0:T(8,128)(2,1)S(1)} %pack.1.pack_ref), channel_id=1, source_target_pairs={{0,2},{2,0},{4,6},{6,4},{8,10},{10,8},{12,14},{14,12},{1,3},{3,1},... | collective-permute-start | bytes 2359304 | tf_op jit(solution)/shard_map/ppermute | solution.py:678
  14.9 0.7 collective-permute-start.8
  15.6 26.3 %near_local.1 = (f32[8,32768]{1,0:T(8,128)S(1)}, f32[8,32768]{1,0:T(8,128)S(1)}, bf16[128,32,256]{2,1,0:T(8,128)(2,1)S(1)}) custom-call(f32[5]{0:T(128)S(1)} %pad_maximum_fusion.2.scale_ref.refs_0_, s32[8,640]{1,0:T(8,128)S(1)} %plan.1.plan_ref, f32[3,32768]{1,0:T(4,128)S(1)} %copy-done.4, bf16[24,16384]{1,0:T(8,128)(2,1)S(1)} %pack.1.pack_ref), custom_call_target="tpu_custom_call" | custom-call | flops 35999997952 | bytes 8388608 | tf_op jit(solution)/shard_map/near_local/pallas_call | solution.py:703
  41.9 3.6 %collective-permute-start.2 = (bf16[2,4,32,128]{3,2,1,0:T(8,128)(2,1)S(1)}, bf16[2,4,32,128]{3,2,1,0:T(8,128)(2,1)S(1)}, u32[]{:S(2)}, u32[]{:S(2)}) collective-permute-start(bf16[2,4,32,128]{3,2,1,0:T(8,128)(2,1)S(1)} %pad_maximum_fusion), channel_id=1, source_target_pairs={{0,2},{2,0},{4,6},{6,4},{8,10},{10,8},{12,14},{14,12},{1,3},{3,1},... | collective-permute-start | bytes 196616 | tf_op jit(solution)/shard_map/ppermute | solution.py:629
  45.6 7.0 %couple.1 = (f32[63,16,128]{2,1,0:T(8,128)S(1)}, bf16[8,64,192]{2,1,0:T(8,128)(2,1)S(1)}) custom-call(f32[5]{0:T(128)S(1)} %pad_maximum_fusion.2.scale_ref.refs_0_, s32[3,255]{1,0:T(4,128)S(1)} %bitcast.13, bf16[127,32,128]{2,1,0:T(8,128)(2,1)S(1)} %get-tuple-element.30.coef_ref, bf16[3,64,64,255]{3,2,1,0:T(8,128)(2,1)S(1)} %bitcast.11), custom_call_target="tpu_custom_call" | custom-call | flops 16000000000 | bytes 8388608 | tf_op jit(solution)/shard_map/couple/pallas_call | solution.py:727
  52.7 1.6 %collective-permute-start.3 = (bf16[4,2,32,128]{3,2,1,0:T(8,128)(2,1)S(1)}, bf16[4,2,32,128]{3,2,1,0:T(8,128)(2,1)S(1)}, u32[]{:S(2)}, u32[]{:S(2)}) collective-permute-start(bf16[4,2,32,128]{3,2,1,0:T(8,128)(2,1)S(1)} %pad_maximum_fusion.1), channel_id=1, source_target_pairs={{0,4},{2,6},{4,0},{6,2},{8,12},{10,14},{12,8},{14,10},{1,5},{3,7},... | collective-permute-start | bytes 196616 | tf_op jit(solution)/shard_map/ppermute | solution.py:629
  54.3 1.1 %collective-permute-start.4 = (bf16[4,2,32,128]{3,2,1,0:T(8,128)(2,1)S(1)}, bf16[4,2,32,128]{3,2,1,0:T(8,128)(2,1)S(1)}, u32[]{:S(2)}, u32[]{:S(2)}) collective-permute-start(bf16[4,2,32,128]{3,2,1,0:T(8,128)(2,1)S(1)} %pad_maximum_fusion.1), channel_id=1, source_target_pairs={{0,8},{2,10},{4,12},{6,14},{8,0},{10,2},{12,4},{14,6},{1,9},{3,11}... | collective-permute-start | bytes 196616 | tf_op jit(solution)/shard_map/ppermute | solution.py:629
  55.4 1.7 %collective-permute-start.5 = (bf16[4,2,32,128]{3,2,1,0:T(8,128)(2,1)S(1)}, bf16[4,2,32,128]{3,2,1,0:T(8,128)(2,1)S(1)}, u32[]{:S(2)}, u32[]{:S(2)}) collective-permute-start(bf16[4,2,32,128]{3,2,1,0:T(8,128)(2,1)S(1)} %pad_maximum_fusion.1), channel_id=1, source_target_pairs={{0,12},{2,14},{4,8},{6,10},{8,4},{10,6},{12,0},{14,2},{1,13},{3,15... | collective-permute-start | bytes 196616 | tf_op jit(solution)/shard_map/ppermute | solution.py:629
  57.2 2.5 %near_halo.1 = (f32[8,32768]{1,0:T(8,128)S(1)}, f32[8,32768]{1,0:T(8,128)S(1)}) custom-call(f32[5]{0:T(128)S(1)} %pad_maximum_fusion.2.scale_ref.refs_0_, s32[8,640]{1,0:T(8,128)S(1)} %plan.1.plan_ref, bf16[128,32,256]{2,1,0:T(8,128)(2,1)S(1)} %get-tuple-element.38.row_ref, bf16[24,16384]{1,0:T(8,128)(2,1)S(1)} %collective-permute-done.7.inner_ref, ...), custom_call_target="tpu_custom_call" | custom-call | flops 20000000000 | bytes 8388608 | tf_op jit(solution)/shard_map/near_halo/pallas_call | solution.py:746
  59.7 0.1 collective-permute-start.9
  59.8 2.1 %collective-permute-done.4.refs_12_ = bf16[4,2,32,128]{3,2,1,0:T(8,128)(2,1)S(1)} collective-permute-done((bf16[4,2,32,128]{3,2,1,0:T(8,128)(2,1)S(1)}, bf16[4,2,32,128]{3,2,1,0:T(8,128)(2,1)S(1)}, u32[]{:S(2)}, u32[]{:S(2)}) %collective-permute-start.4) | collective-permute-done | bytes 65568 | tf_op jit(solution)/shard_map/ppermute | solution.py:629
  62.0 3.7 %down.1 = (bf16[64,8,64]{2,1,0:T(8,128)(2,1)S(1)}, bf16[64,8,64]{2,1,0:T(8,128)(2,1)S(1)}) custom-call(f32[5]{0:T(128)S(1)} %pad_maximum_fusion.2.scale_ref.refs_0_, s32[3,255]{1,0:T(4,128)S(1)} %bitcast.14, s32[4,3]{1,0:T(4,128)S(1)} %copy-done.8, bf16[4,2,64,64]{3,2,1,0:T(8,128)(2,1)S(1)} %copy-done.6, bf16[4,3,64,64]{3,2,1,0:T(8,128)(2,1)S(1)} %copy-done.5, ...), custom_call_target="tpu_custom_call" | custom-call | flops 40000000000 | bytes 4194304 | tf_op jit(solution)/shard_map/down/pallas_call | solution.py:773
  65.7 1.3 %collective-permute-done.6.got_ref = bf16[64,8,64]{2,1,0:T(8,128)(2,1)S(1)} collective-permute-done((bf16[64,8,64]{2,1,0:T(8,128)(2,1)S(1)}, bf16[64,8,64]{2,1,0:T(8,128)(2,1)S(1)}, u32[]{:S(2)}, u32[]{:S(2)}) %collective-permute-start.6) | collective-permute-done | bytes 65568 | tf_op jit(solution)/shard_map/ppermute | solution.py:789
  67.0 4.3 %final.1 = f32[8,32768]{1,0:T(8,128)} custom-call(f32[5]{0:T(128)S(1)} %pad_maximum_fusion.2.scale_ref.refs_0_, bf16[64,8,64]{2,1,0:T(8,128)(2,1)S(1)} %get-tuple-element.36.mine_ref, bf16[64,8,64]{2,1,0:T(8,128)(2,1)S(1)} %collective-permute-done.6.got_ref, bf16[128,64,256]{2,1,0:T(8,128)(2,1)S(1)} %copy-done, f32[1,32768]{1,0:T(1,128)S(1)} %bitcast.8, ...), custom_call_target="tpu_custom_call" | custom-call | flops 2000000000 | bytes 4194304 | tf_op jit(solution)/shard_map/final/pallas_call | solution.py:791
  (36 shorter events, 0.2 us)
Async XLA Ops:
  0.0 3.6 %collective-permute-start = (bf16[8,32768]{1,0:T(8,128)(2,1)}, bf16[8,32768]{1,0:T(8,128)(2,1)S(1)}, u32[]{:S(2)}, u32[]{:S(2)}) collective-permute-start(bf16[8,32768]{1,0:T(8,128)(2,1)} %vec.1), channel_id=1, source_target_pairs={{0,1},{1,0},{2,3},{3,2},{4,5},{5,4},{6,7},{7,6},{8,9},{9,8},{10,11... | collective-permute-start | bytes 1572872 | tf_op jit(solution)/shard_map/ppermute | solution.py:656
  2.0 1.6 %copy-start.1 = (bf16[8,32768]{1,0:T(8,128)(2,1)S(1)}, bf16[8,32768]{1,0:T(8,128)(2,1)}, u32[]{:S(2)}) copy-start(bf16[8,32768]{1,0:T(8,128)(2,1)} %vec.1) | copy-start | bytes 1572868
  2.0 1.6 %copy-start.4 = (f32[3,32768]{1,0:T(4,128)S(1)}, f32[3,32768]{1,0:T(4,128)}, u32[]{:S(2)}) copy-start(f32[3,32768]{1,0:T(4,128)} %points_ref.1) | copy-start | bytes 1179652
  3.5 2.2 %copy-start = (bf16[128,64,256]{2,1,0:T(8,128)(2,1)S(1)}, bf16[128,64,256]{2,1,0:T(8,128)(2,1)}, u32[]{:S(2)}) copy-start(bf16[128,64,256]{2,1,0:T(8,128)(2,1)} %basis.1) | copy-start | bytes 12582916
  3.6 2.9 %copy-start.3 = (bf16[127,2,64,64]{0,3,2,1:T(8,128)(2,1)S(1)}, bf16[127,2,64,64]{0,3,2,1:T(8,128)(2,1)}, u32[]{:S(2)}) copy-start(bf16[127,2,64,64]{0,3,2,1:T(8,128)(2,1)} %param.18) | copy-start | bytes 6242308
  11.8 33.8 %slice-start = ((s8[6291456]{0:T(1024)(128)(4,1)}), s8[4194304]{0:T(1024)(128)(4,1)S(1)}, s32[]{:S(2)}) async-start(s8[6291456]{0:T(1024)(128)(4,1)} %bitcast.9), calls=%async_computation | async-start | bytes 8388608
  11.8 33.8 %slice-start.1 = ((s8[6291456]{0:T(1024)(128)(4,1)}), s8[2097152]{0:T(1024)(128)(4,1)S(1)}, s32[]{:S(2)}) async-start(s8[6291456]{0:T(1024)(128)(4,1)} %bitcast.9), calls=%async_computation.1 | async-start | bytes 4194304
  11.8 33.7 %copy-start.7 = (s32[255,3]{0,1:T(4,128)S(1)}, s32[255,3]{0,1:T(4,128)}, u32[]{:S(2)}) copy-start(s32[255,3]{0,1:T(4,128)} %param.22) | copy-start | bytes 9184
  11.8 30.1 %collective-permute-start.1 = (bf16[8,32,128]{2,1,0:T(8,128)(2,1)S(1)}, bf16[8,32,128]{2,1,0:T(8,128)(2,1)S(1)}, u32[]{:S(2)}, u32[]{:S(2)}) collective-permute-start(bf16[8,32,128]{2,1,0:T(8,128)(2,1)S(1)} %get-tuple-element.26.refs_8_.refs_14_), channel_id=1, source_target_pairs={{0,1},{1,0},{2,3},{3,2},{4,5},{5,4},{6,7},{7,6},{8,9},{9,8},{10,11... | collective-permute-start | bytes 196616 | tf_op jit(solution)/shard_map/ppermute | solution.py:701
  11.9 45.2 %collective-permute-start.7 = (bf16[24,16384]{1,0:T(8,128)(2,1)S(1)}, bf16[24,16384]{1,0:T(8,128)(2,1)S(1)}, u32[]{:S(2)}, u32[]{:S(2)}) collective-permute-start(bf16[24,16384]{1,0:T(8,128)(2,1)S(1)} %pack.1.pack_ref), channel_id=1, source_target_pairs={{0,2},{2,0},{4,6},{6,4},{8,10},{10,8},{12,14},{14,12},{1,3},{3,1},... | collective-permute-start | bytes 2359304 | tf_op jit(solution)/shard_map/ppermute | solution.py:678
  14.9 42.3 %collective-permute-start.8 = (bf16[24,16384]{1,0:T(8,128)(2,1)S(1)}, bf16[24,16384]{1,0:T(8,128)(2,1)S(1)}, u32[]{:S(2)}, u32[]{:S(2)}) collective-permute-start(bf16[24,16384]{1,0:T(8,128)(2,1)S(1)} %pack.1.pack_ref), channel_id=1, source_target_pairs={{2,4},{4,2},{6,8},{8,6},{10,12},{12,10},{3,5},{5,3},{7,9},{9,7},{1... | collective-permute-start | bytes 2359304 | tf_op jit(solution)/shard_map/ppermute | solution.py:679
  41.9 10.7 %collective-permute-start.2 = (bf16[2,4,32,128]{3,2,1,0:T(8,128)(2,1)S(1)}, bf16[2,4,32,128]{3,2,1,0:T(8,128)(2,1)S(1)}, u32[]{:S(2)}, u32[]{:S(2)}) collective-permute-start(bf16[2,4,32,128]{3,2,1,0:T(8,128)(2,1)S(1)} %pad_maximum_fusion), channel_id=1, source_target_pairs={{0,2},{2,0},{4,6},{6,4},{8,10},{10,8},{12,14},{14,12},{1,3},{3,1},... | collective-permute-start | bytes 196616 | tf_op jit(solution)/shard_map/ppermute | solution.py:629
  52.7 7.1 %collective-permute-start.3 = (bf16[4,2,32,128]{3,2,1,0:T(8,128)(2,1)S(1)}, bf16[4,2,32,128]{3,2,1,0:T(8,128)(2,1)S(1)}, u32[]{:S(2)}, u32[]{:S(2)}) collective-permute-start(bf16[4,2,32,128]{3,2,1,0:T(8,128)(2,1)S(1)} %pad_maximum_fusion.1), channel_id=1, source_target_pairs={{0,4},{2,6},{4,0},{6,2},{8,12},{10,14},{12,8},{14,10},{1,5},{3,7},... | collective-permute-start | bytes 196616 | tf_op jit(solution)/shard_map/ppermute | solution.py:629
  54.3 7.6 %collective-permute-start.4 = (bf16[4,2,32,128]{3,2,1,0:T(8,128)(2,1)S(1)}, bf16[4,2,32,128]{3,2,1,0:T(8,128)(2,1)S(1)}, u32[]{:S(2)}, u32[]{:S(2)}) collective-permute-start(bf16[4,2,32,128]{3,2,1,0:T(8,128)(2,1)S(1)} %pad_maximum_fusion.1), channel_id=1, source_target_pairs={{0,8},{2,10},{4,12},{6,14},{8,0},{10,2},{12,4},{14,6},{1,9},{3,11}... | collective-permute-start | bytes 196616 | tf_op jit(solution)/shard_map/ppermute | solution.py:629
  55.4 6.5 %collective-permute-start.5 = (bf16[4,2,32,128]{3,2,1,0:T(8,128)(2,1)S(1)}, bf16[4,2,32,128]{3,2,1,0:T(8,128)(2,1)S(1)}, u32[]{:S(2)}, u32[]{:S(2)}) collective-permute-start(bf16[4,2,32,128]{3,2,1,0:T(8,128)(2,1)S(1)} %pad_maximum_fusion.1), channel_id=1, source_target_pairs={{0,12},{2,14},{4,8},{6,10},{8,4},{10,6},{12,0},{14,2},{1,13},{3,15... | collective-permute-start | bytes 196616 | tf_op jit(solution)/shard_map/ppermute | solution.py:629
  57.1 4.8 %copy-start.5 = (bf16[4,3,64,64]{3,2,1,0:T(8,128)(2,1)S(1)}, bf16[4,3,64,64]{3,2,1,0:T(8,128)(2,1)}, u32[]{:S(2)}) copy-start(bf16[4,3,64,64]{3,2,1,0:T(8,128)(2,1)} %refs_4_.1) | copy-start | bytes 294916
  57.2 4.8 %copy-start.6 = (bf16[4,2,64,64]{3,2,1,0:T(8,128)(2,1)S(1)}, bf16[4,2,64,64]{3,2,1,0:T(8,128)(2,1)}, u32[]{:S(2)}) copy-start(bf16[4,2,64,64]{3,2,1,0:T(8,128)(2,1)} %refs_3_.1) | copy-start | bytes 196612
  57.2 4.8 %copy-start.8 = (s32[4,3]{1,0:T(4,128)S(1)}, s32[4,3]{1,0:T(4,128)}, u32[]{:S(2)}) copy-start(s32[4,3]{1,0:T(4,128)} %refs_2_.1) | copy-start | bytes 148
  59.7 7.3 %collective-permute-start.9 = (f32[8,32768]{1,0:T(8,128)S(1)}, f32[8,32768]{1,0:T(8,128)S(1)}, u32[]{:S(2)}, u32[]{:S(2)}) collective-permute-start(f32[8,32768]{1,0:T(8,128)S(1)} %get-tuple-element.42), channel_id=1, source_target_pairs={{0,1},{1,0},{2,3},{3,2},{4,5},{5,4},{6,7},{7,6},{8,9},{9,8},{10,11... | collective-permute-start | bytes 3145736 | tf_op jit(solution)/shard_map/ppermute | solution.py:762
  62.0 5.1 %copy-start.2 = (f32[32768]{0:T(1024)S(1)}, f32[32768]{0:T(1024)}, u32[]{:S(2)}) copy-start(f32[32768]{0:T(1024)} %param.15) | copy-start | bytes 393220
  65.6 1.4 %collective-permute-start.6 = (bf16[64,8,64]{2,1,0:T(8,128)(2,1)S(1)}, bf16[64,8,64]{2,1,0:T(8,128)(2,1)S(1)}, u32[]{:S(2)}, u32[]{:S(2)}) collective-permute-start(bf16[64,8,64]{2,1,0:T(8,128)(2,1)S(1)} %get-tuple-element.37), channel_id=1, source_target_pairs={{0,1},{1,0},{2,3},{3,2},{4,5},{5,4},{6,7},{7,6},{8,9},{9,8},{10,11... | collective-permute-start | bytes 196616 | tf_op jit(solution)/shard_map/ppermute | solution.py:789

commit v13 on v10

--- a/solution.py
+++ b/solution.py
@@ -120,18 +120,18 @@
     lax.fori_loop(0, half // 2048, step, 0)
 
 
-def plan_kernel(scale_ref, offs_ref, cols_ref, out_ref):
+def plan_kernel(leaves, scale_ref, ids_ref, out_ref):
     device, half_id = whole(scale_ref[3]), whole(scale_ref[4])
-    leaves = offs_ref.shape[1]
-    slots = cols_ref.shape[1]
+    slots = ids_ref.shape[1] - leaves
+    offs, cols = ids_ref[:, :leaves], ids_ref[:, leaves:]
     room = out_ref.shape[1]
     half = leaves // 2
     half_bits = half.bit_length() - 1
-    begins = jnp.broadcast_to(offs_ref[...].astype(F32), (8, leaves)).T[:, 0:1]
+    begins = jnp.broadcast_to(offs.astype(F32), (8, leaves)).T[:, 0:1]
     slot = lax.broadcasted_iota(jnp.int32, (leaves, slots), 1).astype(F32)
     row = jnp.sum(jnp.where(begins <= slot, 1.0, 0.0), axis=0, keepdims=True) - 1.0
     first = jnp.sum(jnp.where(begins == slot, 1.0, 0.0), axis=0, keepdims=True)
-    place = cols_ref[...] - (device * leaves - leaves + half_id * half)
+    place = cols - (device * leaves - leaves + half_id * half)
     block = place >> half_bits
     own = jnp.where(block == 2, 1.0 - first, 0.0)
     far = jnp.where((block & 3) == 0, 1.0, 0.0)
@@ -652,14 +652,14 @@
     got = lax.ppermute(vectors, "vec", [(0, 1), (1, 0)])
 
     plan = pl.pallas_call(
-        plan_kernel,
+        functools.partial(plan_kernel, leaves),
         name="plan",
         out_shape=sds((8, slots + 128), jnp.int32),
-        in_specs=[sspec(), vspec(), vspec()],
+        in_specs=[sspec(), vspec()],
         out_specs=vspec(),
         compiler_params=params(8),
         cost_estimate=pl.CostEstimate(flops=3 * 10**9, bytes_accessed=1 << 16, transcendentals=0),
-    )(scale, near_offsets.reshape(1, leaves), near_cols.reshape(1, slots))
+    )(scale, jnp.concatenate([near_offsets, near_cols]).reshape(1, leaves + slots))
 
     pack = pl.pallas_call(
         pack_kernel,

time: 71.6 us -> 71.1 us (level)
  Pallas kernels: 53.4 us -> 51.7 us
  local copies, waits for them, and re-layouts: 3.31 us -> 1.98 us
  starting transfers between devices: 11.9 us -> 13.1 us
    unnamed x26 -> x22, local copies, waits for them, and re-layouts: 3.29 us -> 1.96 us
    ppermute x4, starting transfers between devices: 7.41 us -> 8.72 us  [swap_mask(): lax.ppermute(value, ('leaf', 'sub'), [(i, i ^ mask) for i in range(total)])]
    pallas_call x1, Pallas kernels: 4.07 us -> 3.05 us  [body(): pl.pallas_call(near_halo_kernel, name='near_halo', out_shape=(sds((PART,...]
  transfers between devices with their start and end apart: 10 -> 10, of which waited for: 2 -> 2; matrix products, arithmetic and copies ran while one was open for 1% -> 2% of each run, Pallas kernels for 61% -> 59%
where the time goes in v13:
time: 71.1 us; the launch traced here: 70.6 us
  Pallas kernels  51.7 us (73%)
  starting transfers between devices  13.1 us (18%)
  waiting for transfers between devices  2.08 us (3%)
  local copies, waits for them, and re-layouts  1.98 us (3%)
  other arithmetic  1.52 us (2%)
    pallas_call x1, Pallas kernels, body(): pl.pallas_call(near_local_kernel, name='near_local', out_shape=(sds((PART...  26.3 us
    ppermute x4, starting transfers between devices, swap_mask(): lax.ppermute(value, ('leaf', 'sub'), [(i, i ^ mask) for i in range(total)])  8.72 us
    pallas_call x1, Pallas kernels, body(): pl.pallas_call(couple_kernel, name='couple', out_shape=(sds((part - 1, AL...  7.05 us
    pallas_call x1, Pallas kernels, body(): pl.pallas_call(up_kernel, name='up', out_shape=(sds((2 * part - 1, 2 * AL...  5.36 us
    pallas_call x1, Pallas kernels, body(): pl.pallas_call(final_kernel, name='final', out_shape=sds((PART, size), F3...  3.84 us
    pallas_call x1, Pallas kernels, body(): pl.pallas_call(lambda *refs: down_kernel(dev_levels, *refs[:11], refs[11:...  3.66 us
    pallas_call x1, Pallas kernels, body(): pl.pallas_call(near_halo_kernel, name='near_halo', out_shape=(sds((PART,...  3.05 us
    ppermute x1, starting transfers between devices, body(): inner = lax.ppermute(pack, axes, [(i, i ^ 1) for i in range(count)])  2.94 us
  transfers between devices with their start and end apart: 10, of which 2 were waited for; matrix products, arithmetic and copies ran while one was open for 2% of the time, Pallas kernels for 59%

profile of v13, /device:TPU:0, one launch (start us, length us, event | category | flops | bytes accessed | tf_op | source)
XLA Modules:
  0.0 70.6 jit_solution(15808025542194753533)
XLA Ops:
  0.0 0.5 collective-permute-start
  0.5 0.7 pad_add_fusion
  1.2 0.1 add_convert_fusion
  1.2 0.7 %pad_maximum_fusion.2.scale_ref.refs_0_ = f32[5]{0:T(128)S(1)} fusion(f32[2]{0:T(128)S(1)} %add_convert_fusion, f32[3]{0:T(128)} %param.14), kind=kLoop, calls=%fused_computation.5 | loop fusion | flops 5 | bytes 40 | tf_op jit(solution)/shard_map/concatenate | solution.py:641
  2.0 1.6 %plan.1.plan_ref = s32[8,640]{1,0:T(8,128)S(1)} custom-call(f32[5]{0:T(128)S(1)} %pad_maximum_fusion.2.scale_ref.refs_0_, s32[1,640]{1,0:T(1,128)S(1)} %reshape.6.ids_ref), custom_call_target="tpu_custom_call" | custom-call | flops 3000000000 | bytes 65536 | tf_op jit(solution)/shard_map/plan/pallas_call | solution.py:654
  3.6 0.9 %pack.1.pack_ref = bf16[24,16384]{1,0:T(8,128)(2,1)S(1)} custom-call(f32[5]{0:T(128)S(1)} %pad_maximum_fusion.2.scale_ref.refs_0_, f32[3,32768]{1,0:T(4,128)S(1)} %copy-done.4, bf16[8,32768]{1,0:T(8,128)(2,1)S(1)} %copy-done.1, bf16[8,32768]{1,0:T(8,128)(2,1)S(1)} %collective-permute-done.got), custom_call_target="tpu_custom_call" | custom-call | flops 2000000000 | bytes 2097152 | tf_op jit(solution)/shard_map/pack/pallas_call | solution.py:664
  4.5 1.2 %copy-done = bf16[128,64,256]{2,1,0:T(8,128)(2,1)S(1)} copy-done((bf16[128,64,256]{2,1,0:T(8,128)(2,1)S(1)}, bf16[128,64,256]{2,1,0:T(8,128)(2,1)}, u32[]{:S(2)}) %copy-start) | copy-done | bytes 4194328
  5.7 0.7 copy-done.3
  6.4 5.4 %up.1 = (bf16[127,32,128]{2,1,0:T(8,128)(2,1)S(1)}, bf16[8,32,128]{2,1,0:T(8,128)(2,1)S(1)}, bf16[1,4,32,128]{3,2,1,0:T(8,128)(2,1)S(1)}, bf16[64,64,128]{2,1,0:T(8,128)(2,1)S(1)}) custom-call(f32[5]{0:T(128)S(1)} %pad_maximum_fusion.2.scale_ref.refs_0_, bf16[24,16384]{1,0:T(8,128)(2,1)S(1)} %pack.1.pack_ref, bf16[128,64,256]{2,1,0:T(8,128)(2,1)S(1)} %copy-done, ...), custom_call_target="tpu_custom_call" | custom-call | flops 8000000000 | bytes 8388608 | tf_op jit(solution)/shard_map/up/pallas_call | solution.py:681
  11.8 0.1 collective-permute-start.1
  11.9 2.9 %collective-permute-start.7 = (bf16[24,16384]{1,0:T(8,128)(2,1)S(1)}, bf16[24,16384]{1,0:T(8,128)(2,1)S(1)}, u32[]{:S(2)}, u32[]{:S(2)}) collective-permute-start(bf16[24,16384]{1,0:T(8,128)(2,1)S(1)} %pack.1.pack_ref), channel_id=1, source_target_pairs={{0,2},{2,0},{4,6},{6,4},{8,10},{10,8},{12,14},{14,12},{1,3},{3,1},... | collective-permute-start | bytes 2359304 | tf_op jit(solution)/shard_map/ppermute | solution.py:674
  14.9 0.7 collective-permute-start.8
  15.6 26.3 %near_local.1 = (f32[8,32768]{1,0:T(8,128)S(1)}, f32[8,32768]{1,0:T(8,128)S(1)}, bf16[128,32,256]{2,1,0:T(8,128)(2,1)S(1)}) custom-call(f32[5]{0:T(128)S(1)} %pad_maximum_fusion.2.scale_ref.refs_0_, s32[8,640]{1,0:T(8,128)S(1)} %plan.1.plan_ref, f32[3,32768]{1,0:T(4,128)S(1)} %copy-done.4, bf16[24,16384]{1,0:T(8,128)(2,1)S(1)} %pack.1.pack_ref), custom_call_target="tpu_custom_call" | custom-call | flops 35999997952 | bytes 8388608 | tf_op jit(solution)/shard_map/near_local/pallas_call | solution.py:699
  41.9 4.3 %collective-permute-start.2 = (bf16[2,4,32,128]{3,2,1,0:T(8,128)(2,1)S(1)}, bf16[2,4,32,128]{3,2,1,0:T(8,128)(2,1)S(1)}, u32[]{:S(2)}, u32[]{:S(2)}) collective-permute-start(bf16[2,4,32,128]{3,2,1,0:T(8,128)(2,1)S(1)} %pad_maximum_fusion), channel_id=1, source_target_pairs={{0,2},{2,0},{4,6},{6,4},{8,10},{10,8},{12,14},{14,12},{1,3},{3,1},... | collective-permute-start | bytes 196616 | tf_op jit(solution)/shard_map/ppermute | solution.py:625
  46.2 7.0 %couple.1 = (f32[63,16,128]{2,1,0:T(8,128)S(1)}, bf16[8,64,192]{2,1,0:T(8,128)(2,1)S(1)}) custom-call(f32[5]{0:T(128)S(1)} %pad_maximum_fusion.2.scale_ref.refs_0_, s32[3,255]{1,0:T(4,128)S(1)} %bitcast.13, bf16[127,32,128]{2,1,0:T(8,128)(2,1)S(1)} %get-tuple-element.30.coef_ref, bf16[3,64,64,255]{3,2,1,0:T(8,128)(2,1)S(1)} %bitcast.11), custom_call_target="tpu_custom_call" | custom-call | flops 16000000000 | bytes 8388608 | tf_op jit(solution)/shard_map/couple/pallas_call | solution.py:723
  53.3 1.0 %collective-permute-start.3 = (bf16[4,2,32,128]{3,2,1,0:T(8,128)(2,1)S(1)}, bf16[4,2,32,128]{3,2,1,0:T(8,128)(2,1)S(1)}, u32[]{:S(2)}, u32[]{:S(2)}) collective-permute-start(bf16[4,2,32,128]{3,2,1,0:T(8,128)(2,1)S(1)} %pad_maximum_fusion.1), channel_id=1, source_target_pairs={{0,4},{2,6},{4,0},{6,2},{8,12},{10,14},{12,8},{14,10},{1,5},{3,7},... | collective-permute-start | bytes 196616 | tf_op jit(solution)/shard_map/ppermute | solution.py:625
  54.3 1.1 %collective-permute-start.4 = (bf16[4,2,32,128]{3,2,1,0:T(8,128)(2,1)S(1)}, bf16[4,2,32,128]{3,2,1,0:T(8,128)(2,1)S(1)}, u32[]{:S(2)}, u32[]{:S(2)}) collective-permute-start(bf16[4,2,32,128]{3,2,1,0:T(8,128)(2,1)S(1)} %pad_maximum_fusion.1), channel_id=1, source_target_pairs={{0,8},{2,10},{4,12},{6,14},{8,0},{10,2},{12,4},{14,6},{1,9},{3,11}... | collective-permute-start | bytes 196616 | tf_op jit(solution)/shard_map/ppermute | solution.py:625
  55.4 2.4 %collective-permute-start.5 = (bf16[4,2,32,128]{3,2,1,0:T(8,128)(2,1)S(1)}, bf16[4,2,32,128]{3,2,1,0:T(8,128)(2,1)S(1)}, u32[]{:S(2)}, u32[]{:S(2)}) collective-permute-start(bf16[4,2,32,128]{3,2,1,0:T(8,128)(2,1)S(1)} %pad_maximum_fusion.1), channel_id=1, source_target_pairs={{0,12},{2,14},{4,8},{6,10},{8,4},{10,6},{12,0},{14,2},{1,13},{3,15... | collective-permute-start | bytes 196616 | tf_op jit(solution)/shard_map/ppermute | solution.py:625
  57.8 3.1 %near_halo.1 = (f32[8,32768]{1,0:T(8,128)S(1)}, f32[8,32768]{1,0:T(8,128)S(1)}) custom-call(f32[5]{0:T(128)S(1)} %pad_maximum_fusion.2.scale_ref.refs_0_, s32[8,640]{1,0:T(8,128)S(1)} %plan.1.plan_ref, bf16[128,32,256]{2,1,0:T(8,128)(2,1)S(1)} %get-tuple-element.38.row_ref, bf16[24,16384]{1,0:T(8,128)(2,1)S(1)} %collective-permute-done.7.inner_ref, ...), custom_call_target="tpu_custom_call" | custom-call | flops 20000000000 | bytes 8388608 | tf_op jit(solution)/shard_map/near_halo/pallas_call | solution.py:742
  60.9 0.1 collective-permute-start.9
  61.0 0.7 %collective-permute-done.4.refs_12_ = bf16[4,2,32,128]{3,2,1,0:T(8,128)(2,1)S(1)} collective-permute-done((bf16[4,2,32,128]{3,2,1,0:T(8,128)(2,1)S(1)}, bf16[4,2,32,128]{3,2,1,0:T(8,128)(2,1)S(1)}, u32[]{:S(2)}, u32[]{:S(2)}) %collective-permute-start.4) | collective-permute-done | bytes 65568 | tf_op jit(solution)/shard_map/ppermute | solution.py:625
  61.7 3.7 %down.1 = (bf16[64,8,64]{2,1,0:T(8,128)(2,1)S(1)}, bf16[64,8,64]{2,1,0:T(8,128)(2,1)S(1)}) custom-call(f32[5]{0:T(128)S(1)} %pad_maximum_fusion.2.scale_ref.refs_0_, s32[3,255]{1,0:T(4,128)S(1)} %bitcast.14, s32[4,3]{1,0:T(4,128)S(1)} %copy-done.8, bf16[4,2,64,64]{3,2,1,0:T(8,128)(2,1)S(1)} %copy-done.6, bf16[4,3,64,64]{3,2,1,0:T(8,128)(2,1)S(1)} %copy-done.5, ...), custom_call_target="tpu_custom_call" | custom-call | flops 40000000000 | bytes 4194304 | tf_op jit(solution)/shard_map/down/pallas_call | solution.py:769
  65.4 1.3 %collective-permute-done.6.got_ref = bf16[64,8,64]{2,1,0:T(8,128)(2,1)S(1)} collective-permute-done((bf16[64,8,64]{2,1,0:T(8,128)(2,1)S(1)}, bf16[64,8,64]{2,1,0:T(8,128)(2,1)S(1)}, u32[]{:S(2)}, u32[]{:S(2)}) %collective-permute-start.6) | collective-permute-done | bytes 65568 | tf_op jit(solution)/shard_map/ppermute | solution.py:785
  66.8 3.8 %final.1 = f32[8,32768]{1,0:T(8,128)} custom-call(f32[5]{0:T(128)S(1)} %pad_maximum_fusion.2.scale_ref.refs_0_, bf16[64,8,64]{2,1,0:T(8,128)(2,1)S(1)} %get-tuple-element.36.mine_ref, bf16[64,8,64]{2,1,0:T(8,128)(2,1)S(1)} %collective-permute-done.6.got_ref, bf16[128,64,256]{2,1,0:T(8,128)(2,1)S(1)} %copy-done, f32[1,32768]{1,0:T(1,128)S(1)} %bitcast.8, ...), custom_call_target="tpu_custom_call" | custom-call | flops 2000000000 | bytes 4194304 | tf_op jit(solution)/shard_map/final/pallas_call | solution.py:787
  (36 shorter events, 0.2 us)
Async XLA Ops:
  0.0 3.6 %collective-permute-start = (bf16[8,32768]{1,0:T(8,128)(2,1)}, bf16[8,32768]{1,0:T(8,128)(2,1)S(1)}, u32[]{:S(2)}, u32[]{:S(2)}) collective-permute-start(bf16[8,32768]{1,0:T(8,128)(2,1)} %vec.1), channel_id=1, source_target_pairs={{0,1},{1,0},{2,3},{3,2},{4,5},{5,4},{6,7},{7,6},{8,9},{9,8},{10,11... | collective-permute-start | bytes 1572872 | tf_op jit(solution)/shard_map/ppermute | solution.py:652
  2.0 1.6 %copy-start.1 = (bf16[8,32768]{1,0:T(8,128)(2,1)S(1)}, bf16[8,32768]{1,0:T(8,128)(2,1)}, u32[]{:S(2)}) copy-start(bf16[8,32768]{1,0:T(8,128)(2,1)} %vec.1) | copy-start | bytes 1572868
  2.0 1.6 %copy-start.4 = (f32[3,32768]{1,0:T(4,128)S(1)}, f32[3,32768]{1,0:T(4,128)}, u32[]{:S(2)}) copy-start(f32[3,32768]{1,0:T(4,128)} %points_ref.1) | copy-start | bytes 1179652
  3.5 2.2 %copy-start = (bf16[128,64,256]{2,1,0:T(8,128)(2,1)S(1)}, bf16[128,64,256]{2,1,0:T(8,128)(2,1)}, u32[]{:S(2)}) copy-start(bf16[128,64,256]{2,1,0:T(8,128)(2,1)} %basis.1) | copy-start | bytes 12582916
  3.6 2.9 %copy-start.3 = (bf16[127,2,64,64]{0,3,2,1:T(8,128)(2,1)S(1)}, bf16[127,2,64,64]{0,3,2,1:T(8,128)(2,1)}, u32[]{:S(2)}) copy-start(bf16[127,2,64,64]{0,3,2,1:T(8,128)(2,1)} %param.18) | copy-start | bytes 6242308
  11.8 34.4 %slice-start = ((s8[6291456]{0:T(1024)(128)(4,1)}), s8[4194304]{0:T(1024)(128)(4,1)S(1)}, s32[]{:S(2)}) async-start(s8[6291456]{0:T(1024)(128)(4,1)} %bitcast.9), calls=%async_computation | async-start | bytes 8388608
  11.8 34.4 %slice-start.1 = ((s8[6291456]{0:T(1024)(128)(4,1)}), s8[2097152]{0:T(1024)(128)(4,1)S(1)}, s32[]{:S(2)}) async-start(s8[6291456]{0:T(1024)(128)(4,1)} %bitcast.9), calls=%async_computation.1 | async-start | bytes 4194304
  11.8 34.4 %copy-start.7 = (s32[255,3]{0,1:T(4,128)S(1)}, s32[255,3]{0,1:T(4,128)}, u32[]{:S(2)}) copy-start(s32[255,3]{0,1:T(4,128)} %param.22) | copy-start | bytes 9184
  11.8 30.1 %collective-permute-start.1 = (bf16[8,32,128]{2,1,0:T(8,128)(2,1)S(1)}, bf16[8,32,128]{2,1,0:T(8,128)(2,1)S(1)}, u32[]{:S(2)}, u32[]{:S(2)}) collective-permute-start(bf16[8,32,128]{2,1,0:T(8,128)(2,1)S(1)} %get-tuple-element.26.refs_8_.refs_14_), channel_id=1, source_target_pairs={{0,1},{1,0},{2,3},{3,2},{4,5},{5,4},{6,7},{7,6},{8,9},{9,8},{10,11... | collective-permute-start | bytes 196616 | tf_op jit(solution)/shard_map/ppermute | solution.py:697
  11.9 45.9 %collective-permute-start.7 = (bf16[24,16384]{1,0:T(8,128)(2,1)S(1)}, bf16[24,16384]{1,0:T(8,128)(2,1)S(1)}, u32[]{:S(2)}, u32[]{:S(2)}) collective-permute-start(bf16[24,16384]{1,0:T(8,128)(2,1)S(1)} %pack.1.pack_ref), channel_id=1, source_target_pairs={{0,2},{2,0},{4,6},{6,4},{8,10},{10,8},{12,14},{14,12},{1,3},{3,1},... | collective-permute-start | bytes 2359304 | tf_op jit(solution)/shard_map/ppermute | solution.py:674
  14.9 42.9 %collective-permute-start.8 = (bf16[24,16384]{1,0:T(8,128)(2,1)S(1)}, bf16[24,16384]{1,0:T(8,128)(2,1)S(1)}, u32[]{:S(2)}, u32[]{:S(2)}) collective-permute-start(bf16[24,16384]{1,0:T(8,128)(2,1)S(1)} %pack.1.pack_ref), channel_id=1, source_target_pairs={{2,4},{4,2},{6,8},{8,6},{10,12},{12,10},{3,5},{5,3},{7,9},{9,7},{1... | collective-permute-start | bytes 2359304 | tf_op jit(solution)/shard_map/ppermute | solution.py:675
  41.9 11.4 %collective-permute-start.2 = (bf16[2,4,32,128]{3,2,1,0:T(8,128)(2,1)S(1)}, bf16[2,4,32,128]{3,2,1,0:T(8,128)(2,1)S(1)}, u32[]{:S(2)}, u32[]{:S(2)}) collective-permute-start(bf16[2,4,32,128]{3,2,1,0:T(8,128)(2,1)S(1)} %pad_maximum_fusion), channel_id=1, source_target_pairs={{0,2},{2,0},{4,6},{6,4},{8,10},{10,8},{12,14},{14,12},{1,3},{3,1},... | collective-permute-start | bytes 196616 | tf_op jit(solution)/shard_map/ppermute | solution.py:625
  53.3 7.6 %collective-permute-start.3 = (bf16[4,2,32,128]{3,2,1,0:T(8,128)(2,1)S(1)}, bf16[4,2,32,128]{3,2,1,0:T(8,128)(2,1)S(1)}, u32[]{:S(2)}, u32[]{:S(2)}) collective-permute-start(bf16[4,2,32,128]{3,2,1,0:T(8,128)(2,1)S(1)} %pad_maximum_fusion.1), channel_id=1, source_target_pairs={{0,4},{2,6},{4,0},{6,2},{8,12},{10,14},{12,8},{14,10},{1,5},{3,7},... | collective-permute-start | bytes 196616 | tf_op jit(solution)/shard_map/ppermute | solution.py:625
  54.3 7.4 %collective-permute-start.4 = (bf16[4,2,32,128]{3,2,1,0:T(8,128)(2,1)S(1)}, bf16[4,2,32,128]{3,2,1,0:T(8,128)(2,1)S(1)}, u32[]{:S(2)}, u32[]{:S(2)}) collective-permute-start(bf16[4,2,32,128]{3,2,1,0:T(8,128)(2,1)S(1)} %pad_maximum_fusion.1), channel_id=1, source_target_pairs={{0,8},{2,10},{4,12},{6,14},{8,0},{10,2},{12,4},{14,6},{1,9},{3,11}... | collective-permute-start | bytes 196616 | tf_op jit(solution)/shard_map/ppermute | solution.py:625
  55.4 6.3 %collective-permute-start.5 = (bf16[4,2,32,128]{3,2,1,0:T(8,128)(2,1)S(1)}, bf16[4,2,32,128]{3,2,1,0:T(8,128)(2,1)S(1)}, u32[]{:S(2)}, u32[]{:S(2)}) collective-permute-start(bf16[4,2,32,128]{3,2,1,0:T(8,128)(2,1)S(1)} %pad_maximum_fusion.1), channel_id=1, source_target_pairs={{0,12},{2,14},{4,8},{6,10},{8,4},{10,6},{12,0},{14,2},{1,13},{3,15... | collective-permute-start | bytes 196616 | tf_op jit(solution)/shard_map/ppermute | solution.py:625
  57.8 3.9 %copy-start.5 = (bf16[4,3,64,64]{3,2,1,0:T(8,128)(2,1)S(1)}, bf16[4,3,64,64]{3,2,1,0:T(8,128)(2,1)}, u32[]{:S(2)}) copy-start(bf16[4,3,64,64]{3,2,1,0:T(8,128)(2,1)} %refs_4_.1) | copy-start | bytes 294916
  57.8 3.9 %copy-start.6 = (bf16[4,2,64,64]{3,2,1,0:T(8,128)(2,1)S(1)}, bf16[4,2,64,64]{3,2,1,0:T(8,128)(2,1)}, u32[]{:S(2)}) copy-start(bf16[4,2,64,64]{3,2,1,0:T(8,128)(2,1)} %refs_3_.1) | copy-start | bytes 196612
  57.8 3.9 %copy-start.8 = (s32[4,3]{1,0:T(4,128)S(1)}, s32[4,3]{1,0:T(4,128)}, u32[]{:S(2)}) copy-start(s32[4,3]{1,0:T(4,128)} %refs_2_.1) | copy-start | bytes 148
  60.9 5.9 %collective-permute-start.9 = (f32[8,32768]{1,0:T(8,128)S(1)}, f32[8,32768]{1,0:T(8,128)S(1)}, u32[]{:S(2)}, u32[]{:S(2)}) collective-permute-start(f32[8,32768]{1,0:T(8,128)S(1)} %get-tuple-element.42), channel_id=1, source_target_pairs={{0,1},{1,0},{2,3},{3,2},{4,5},{5,4},{6,7},{7,6},{8,9},{9,8},{10,11... | collective-permute-start | bytes 3145736 | tf_op jit(solution)/shard_map/ppermute | solution.py:758
  61.7 5.1 %copy-start.2 = (f32[32768]{0:T(1024)S(1)}, f32[32768]{0:T(1024)}, u32[]{:S(2)}) copy-start(f32[32768]{0:T(1024)} %param.15) | copy-start | bytes 393220
  65.4 1.4 %collective-permute-start.6 = (bf16[64,8,64]{2,1,0:T(8,128)(2,1)S(1)}, bf16[64,8,64]{2,1,0:T(8,128)(2,1)S(1)}, u32[]{:S(2)}, u32[]{:S(2)}) collective-permute-start(bf16[64,8,64]{2,1,0:T(8,128)(2,1)S(1)} %get-tuple-element.37), channel_id=1, source_target_pairs={{0,1},{1,0},{2,3},{3,2},{4,5},{5,4},{6,7},{7,6},{8,9},{9,8},{10,11... | collective-permute-start | bytes 196616 | tf_op jit(solution)/shard_map/ppermute | solution.py:785
